TPU v7x, 32 devices: a whole 2x2x4 slice. The times are simulated.
32 devices in a mesh: dp: 8 (over y, x, core), tensor: 4 (over z).
Axes of the slice: x: 2, y: 2, z: 4, core: 2. Of those that a mesh axis runs over, the one named last changes fastest.
Arguments:
- tokens: bfloat16 [16, 1024, 512], P('dp'), may hold values from -6 to 6
- cotangent: bfloat16 [16, 1024, 512], P('dp'), may hold values from -6 to 6
- lengths: int32 [16], replicated, may hold values from 1 to 1024, 12288 in all
- dealing: int32 [16], replicated, may hold values from 0 to 15, each once
- ln1_gain: float32 [512], replicated, may hold values from 0.5 to 1.5
- ln1_bias: float32 [512], replicated, may hold values from -2 to 2
- w_query: bfloat16 [512, 512], P(None, 'tensor'), may hold values from -0.25 to 0.25
- b_query: float32 [512], P('tensor'), may hold values from -3 to 3
- w_key: bfloat16 [512, 512], P(None, 'tensor'), may hold values from -0.25 to 0.25
- w_value: bfloat16 [512, 512], P(None, 'tensor'), may hold values from -0.25 to 0.25
- b_value: float32 [512], P('tensor'), may hold values from -3 to 3
- w_out: bfloat16 [512, 512], P('tensor'), may hold values from -1.5 to 1.5
- b_out: float32 [512], replicated, may hold values from -2 to 2
- ln2_gain: float32 [512], replicated, may hold values from 0.5 to 1.5
- ln2_bias: float32 [512], replicated, may hold values from -2 to 2
- w_up: bfloat16 [512, 2048], P(None, 'tensor'), may hold values from -0.25 to 0.25
- b_up: float32 [2048], P('tensor'), may hold values from -3 to 3
- w_down: bfloat16 [2048, 512], P('tensor'), may hold values from -0.125 to 0.125
- b_down: float32 [512], replicated, may hold values from -2 to 2
Outputs:
- output: bfloat16 [16, 1024, 512], P('dp')
- grad_tokens: bfloat16 [16, 1024, 512], P('dp')
- grad_ln1_gain: float32 [512], replicated
- grad_ln1_bias: float32 [512], replicated
- grad_w_query: float32 [512, 512], P(None, 'tensor')
- grad_b_query: float32 [512], P('tensor')
- grad_w_key: float32 [512, 512], P(None, 'tensor')
- grad_w_value: float32 [512, 512], P(None, 'tensor')
- grad_b_value: float32 [512], P('tensor')
- grad_w_out: float32 [512, 512], P('tensor')
- grad_b_out: float32 [512], replicated
- grad_ln2_gain: float32 [512], replicated
- grad_ln2_bias: float32 [512], replicated
- grad_w_up: float32 [512, 2048], P(None, 'tensor')
- grad_b_up: float32 [2048], P('tensor')
- grad_w_down: float32 [2048, 512], P('tensor')
- grad_b_down: float32 [512], replicated
Inputs may be any that keep to these rules, and one draw needn't show every extreme that they name: `lengths`: the live tokens of each input sequence; the longest has 1024. A permutation of the 16 sequence numbers; dealt slot p takes input sequence dealing[p], dealt slots lie along dp in order as the input sequences do.
All inputs are finite; a program needn't handle non-finite values.
Results may differ from a plain program's by a relative error of at most 0.03.
Values may be sent and summed in bfloat16 or wider, within the bound.
No kernel may reach another device: no remote copies, remote signals or barrier semaphores. Data moves between devices by JAX's collectives and lax.ppermute only.
A program may use at most 128 MiB of HBM per device.

v0:
```python
import jax
import jax.numpy as jnp
from jax import lax
from jax.sharding import PartitionSpec as P

HEAD_SIZE = 64
BLOCK = 16


eps_norm = 1e-05
inv_root_two = 0.7071067811865476
inv_root_tau = 0.3989422804014327


def level_groups(length):
    groups = []
    group_size = 2
    while length // group_size >= 2 * BLOCK:
        groups.append(group_size)
        group_size = group_size * 2
    return groups


def pool_sum(values, group_size):
    dims_in = values.shape
    return jnp.sum(
        values.reshape(dims_in[:-2] + (dims_in[-2] // group_size, group_size, dims_in[-1])), axis=-2
    )


def padded_rows(level_parts):
    dims_in = level_parts[0].shape
    padding = jnp.zeros(dims_in[:-2] + (2 * BLOCK, dims_in[-1]), jnp.float32)
    return jnp.concatenate(level_parts + [padding], axis=-2)


def block_view(stacked):
    dims_in = stacked.shape
    return stacked.reshape(dims_in[:-2] + (dims_in[-2] // 128, 128, dims_in[-1]))


def interpolate(stacked, length):
    fine_rows = stacked[..., 0, :, :]
    offset = 0
    for group_size in level_groups(length):
        level_rows = length // group_size
        fine_rows = fine_rows + jnp.repeat(
            stacked[..., 1, offset : offset + level_rows, :], group_size, axis=-2
        )
        offset = offset + level_rows
    return fine_rows


def tile_masks():
    token_positions = jnp.arange(128)
    same_pair = token_positions[:, None] // (2 * BLOCK) == token_positions[None, :] // (2 * BLOCK)
    halves_apart = token_positions[:, None] // BLOCK != token_positions[None, :] // BLOCK
    return jnp.stack([same_pair, same_pair & halves_apart]).astype(jnp.float32)[:, None]


def block_probs(stack_query, stack_key, key_weight_matrix, attention_score_scale):
    scores = (
        jnp.einsum(
            "...qe,...ke->...qk",
            block_view(stack_query),
            block_view(stack_key),
            preferred_element_type=jnp.float32,
        )
        * attention_score_scale
    )
    dims_in = key_weight_matrix.shape
    weight_tiles = key_weight_matrix.reshape(dims_in[:-1] + (dims_in[-1] // 128, 1, 128))
    return jnp.exp(scores) * tile_masks() * weight_tiles


def attention_forward_pass(
    query_rows, key_row_block, value_row_block, validity_mask, attention_score_scale
):
    length = query_rows.shape[-2]
    valid_column = validity_mask[..., None]
    live_low = valid_column.astype(jnp.bfloat16)
    keys_live = key_row_block * live_low
    values_live = value_row_block * live_low
    query_wide = query_rows.astype(jnp.float32)
    key_wide = keys_live.astype(jnp.float32)
    value_wide = values_live.astype(jnp.float32)
    coarse_query, coarse_key, coarse_value, coarse_block_count, floor_list = ([], [], [], [], [])
    for group_size in level_groups(length):
        counts = pool_sum(valid_column, group_size)
        floors = jnp.maximum(counts, 1.0)
        coarse_query.append(pool_sum(query_wide, group_size) / group_size)
        coarse_key.append(pool_sum(key_wide, group_size) / floors)
        coarse_value.append(pool_sum(value_wide, group_size) / floors)
        coarse_block_count.append(counts)
        floor_list.append(floors)
    stack_query = jnp.stack([query_rows, padded_rows(coarse_query).astype(jnp.bfloat16)], axis=-3)
    stack_key = jnp.stack([keys_live, padded_rows(coarse_key).astype(jnp.bfloat16)], axis=-3)
    stack_value = jnp.stack([values_live, padded_rows(coarse_value).astype(jnp.bfloat16)], axis=-3)
    key_weight_matrix = jnp.stack([validity_mask, padded_rows(coarse_block_count)[..., 0]], axis=-2)
    prob_rows = block_probs(stack_query, stack_key, key_weight_matrix, attention_score_scale)
    numerators = jnp.einsum(
        "...qk,...ke->...qe",
        prob_rows.astype(jnp.bfloat16),
        block_view(stack_value),
        preferred_element_type=jnp.float32,
    )
    totals = jnp.sum(prob_rows, axis=-1)
    numerators = numerators.reshape(stack_value.shape)
    totals = totals.reshape(stack_value.shape[:-1])
    fine_total = interpolate(totals[..., None], length)
    attention_mixture = interpolate(numerators, length) / fine_total
    kept = (
        stack_query,
        stack_key,
        stack_value,
        key_weight_matrix,
        fine_total,
        attention_mixture,
        floor_list,
        valid_column,
    )
    return (attention_mixture, kept)


def attend_backward(grad_rows, kept, attention_score_scale):
    (
        stack_query,
        stack_key,
        stack_value,
        key_weight_matrix,
        fine_total,
        attention_mixture,
        floor_list,
        valid_column,
    ) = kept
    length = attention_mixture.shape[-2]
    groups = level_groups(length)
    grad_numer = grad_rows / fine_total
    grad_total = -jnp.sum(grad_rows * attention_mixture, axis=-1, keepdims=True) / fine_total
    numer_stack = jnp.stack(
        [grad_numer, padded_rows([pool_sum(grad_numer, group_size) for group_size in groups])],
        axis=-3,
    ).astype(jnp.bfloat16)
    total_stack = jnp.stack(
        [grad_total, padded_rows([pool_sum(grad_total, group_size) for group_size in groups])],
        axis=-3,
    )
    prob_rows = block_probs(stack_query, stack_key, key_weight_matrix, attention_score_scale)
    numer_tiles = block_view(numer_stack)
    total_tiles = block_view(total_stack)
    grad_probs = (
        jnp.einsum(
            "...qe,...ke->...qk",
            numer_tiles,
            block_view(stack_value),
            preferred_element_type=jnp.float32,
        )
        + total_tiles
    )
    grad_values = jnp.einsum(
        "...qk,...qe->...ke",
        prob_rows.astype(jnp.bfloat16),
        numer_tiles,
        preferred_element_type=jnp.float32,
    )
    grad_scores = (grad_probs * prob_rows).astype(jnp.bfloat16)
    grad_queries = (
        jnp.einsum(
            "...qk,...ke->...qe",
            grad_scores,
            block_view(stack_key),
            preferred_element_type=jnp.float32,
        )
        * attention_score_scale
    )
    grad_keys = (
        jnp.einsum(
            "...qk,...qe->...ke",
            grad_scores,
            block_view(stack_query),
            preferred_element_type=jnp.float32,
        )
        * attention_score_scale
    )
    grad_queries = grad_queries.reshape(stack_query.shape)
    grad_keys = grad_keys.reshape(stack_key.shape)
    grad_values = grad_values.reshape(stack_value.shape)
    fine_queries = grad_queries[..., 0, :, :]
    fine_keys = grad_keys[..., 0, :, :]
    fine_values = grad_values[..., 0, :, :]
    offset = 0
    for group_size, floors in zip(groups, floor_list):
        level_rows = length // group_size
        fine_queries = (
            fine_queries
            + jnp.repeat(grad_queries[..., 1, offset : offset + level_rows, :], group_size, axis=-2)
            / group_size
        )
        fine_keys = fine_keys + jnp.repeat(
            grad_keys[..., 1, offset : offset + level_rows, :] / floors, group_size, axis=-2
        )
        fine_values = fine_values + jnp.repeat(
            grad_values[..., 1, offset : offset + level_rows, :] / floors, group_size, axis=-2
        )
        offset = offset + level_rows
    return (fine_queries, fine_keys * valid_column, fine_values * valid_column)


def norm_parts(values, gain, shift):
    centred = values - jnp.mean(values, axis=-1, keepdims=True)
    inverse = lax.rsqrt(jnp.mean(centred * centred, axis=-1, keepdims=True) + eps_norm)
    unit_rows = centred * inverse
    return (unit_rows * gain + shift, unit_rows, inverse)


def norm_back(grad_rows, unit_rows, inverse, gain):
    scaled = grad_rows * gain
    return inverse * (
        scaled
        - jnp.mean(scaled, axis=-1, keepdims=True)
        - unit_rows * jnp.mean(scaled * unit_rows, axis=-1, keepdims=True)
    )


def rows_product(left, right):
    return lax.dot_general(
        left, right, (((0,), (0,)), ((), ())), preferred_element_type=jnp.float32
    )


def cols_product(left, right):
    return lax.dot_general(
        left, right, (((1,), (1,)), ((), ())), preferred_element_type=jnp.float32
    )


def local(
    tokens,
    cotangent,
    lengths,
    dealing,
    ln1_gain,
    ln1_bias,
    w_query,
    b_query,
    w_key,
    w_value,
    b_value,
    w_out,
    b_out,
    ln2_gain,
    ln2_bias,
    w_up,
    b_up,
    w_down,
    b_down,
):
    seq_dev, length, model_width = tokens.shape
    dp_size = lax.axis_size("dp")
    dp_index = lax.axis_index("dp")
    piece_rows = length // dp_size
    own_ids = lax.dynamic_slice_in_dim(dealing, dp_index * seq_dev, seq_dev)
    dealt_tokens = lax.all_to_all(
        jnp.take(
            lax.all_to_all(
                tokens.reshape(seq_dev, dp_size, piece_rows, model_width),
                "dp",
                split_axis=1,
                concat_axis=0,
                tiled=True,
            ),
            dealing,
            axis=0,
        ),
        "dp",
        split_axis=0,
        concat_axis=1,
        tiled=True,
    )
    dealt_cotangent = lax.all_to_all(
        jnp.take(
            lax.all_to_all(
                cotangent.reshape(seq_dev, dp_size, piece_rows, model_width),
                "dp",
                split_axis=1,
                concat_axis=0,
                tiled=True,
            ),
            dealing,
            axis=0,
        ),
        "dp",
        split_axis=0,
        concat_axis=1,
        tiled=True,
    )
    dealt_tokens = dealt_tokens.reshape(seq_dev, length, model_width)
    dealt_cotangent = dealt_cotangent.reshape(seq_dev, length, model_width)
    own_lengths = jnp.take(lengths, own_ids)
    valid_mask = (jnp.arange(length, dtype=jnp.int32)[None, :] < own_lengths[:, None]).astype(
        jnp.float32
    )
    validity_mask = valid_mask[:, None, :]
    rows_all = seq_dev * length
    head_count = w_query.shape[1] // HEAD_SIZE
    attention_score_scale = HEAD_SIZE ** (-0.5)

    def split_into_heads(values):
        return values.reshape(seq_dev, length, head_count, HEAD_SIZE).transpose(0, 2, 1, 3)

    def join_heads(values):
        return values.transpose(0, 2, 1, 3).reshape(rows_all, head_count * HEAD_SIZE)

    input_tokens = dealt_tokens.reshape(rows_all, model_width).astype(jnp.float32)
    normed_one, unit_one, inverse_one = norm_parts(input_tokens, ln1_gain, ln1_bias)
    normed_low = normed_one.astype(jnp.bfloat16)
    query_rows = (
        jnp.dot(normed_low, w_query, preferred_element_type=jnp.float32) + b_query
    ).astype(jnp.bfloat16)
    key_row_block = jnp.dot(normed_low, w_key, preferred_element_type=jnp.float32).astype(
        jnp.bfloat16
    )
    value_row_block = (
        jnp.dot(normed_low, w_value, preferred_element_type=jnp.float32) + b_value
    ).astype(jnp.bfloat16)
    attention_mixture, kept = attention_forward_pass(
        split_into_heads(query_rows),
        split_into_heads(key_row_block),
        split_into_heads(value_row_block),
        validity_mask,
        attention_score_scale,
    )
    mixed_low = join_heads(attention_mixture).astype(jnp.bfloat16)
    attend_sum = lax.psum(jnp.dot(mixed_low, w_out, preferred_element_type=jnp.float32), "tensor")
    hidden = input_tokens + attend_sum + b_out
    normed_two, unit_two, inverse_two = norm_parts(hidden, ln2_gain, ln2_bias)
    normed_two_low = normed_two.astype(jnp.bfloat16)
    pre_act = jnp.dot(normed_two_low, w_up, preferred_element_type=jnp.float32) + b_up
    erf_part = lax.erf(pre_act * inv_root_two)
    activated_low = (0.5 * pre_act * (1.0 + erf_part)).astype(jnp.bfloat16)
    ffn_sum = lax.psum(
        jnp.dot(activated_low, w_down, preferred_element_type=jnp.float32).astype(jnp.bfloat16),
        "tensor",
    ).astype(jnp.float32)
    layer_output = (
        (hidden + ffn_sum + b_down).astype(jnp.bfloat16).reshape(seq_dev, length, model_width)
    )
    grad_out = dealt_cotangent.reshape(rows_all, model_width)
    grad_out_wide = grad_out.astype(jnp.float32)
    grad_w_down = rows_product(activated_low, grad_out)
    grad_b_down = jnp.sum(grad_out_wide, axis=0)
    grad_act = cols_product(grad_out, w_down)
    gelu_slope = 0.5 * (1.0 + erf_part) + pre_act * jnp.exp(-0.5 * pre_act * pre_act) * inv_root_tau
    grad_pre = (grad_act * gelu_slope).astype(jnp.bfloat16)
    grad_w_up = rows_product(normed_two_low, grad_pre)
    grad_b_up = jnp.sum(grad_pre.astype(jnp.float32), axis=0)
    grad_normed_two = lax.psum(cols_product(grad_pre, w_up).astype(jnp.bfloat16), "tensor").astype(
        jnp.float32
    )
    grad_ln2_gain = jnp.sum(grad_normed_two * unit_two, axis=0)
    grad_ln2_bias = jnp.sum(grad_normed_two, axis=0)
    grad_hidden = grad_out_wide + norm_back(grad_normed_two, unit_two, inverse_two, ln2_gain)
    ffn_summed = (grad_ln2_gain, grad_ln2_bias, grad_w_up, grad_b_up, grad_w_down, grad_b_down)
    grad_hidden_low = grad_hidden.astype(jnp.bfloat16)
    grad_w_out = rows_product(mixed_low, grad_hidden_low)
    grad_b_out = jnp.sum(grad_hidden, axis=0)
    grad_mixed = cols_product(grad_hidden_low, w_out).astype(jnp.bfloat16)
    grad_queries, grad_keys, grad_values = attend_backward(
        split_into_heads(grad_mixed).astype(jnp.float32), kept, attention_score_scale
    )
    queries_low = join_heads(grad_queries).astype(jnp.bfloat16)
    keys_low = join_heads(grad_keys).astype(jnp.bfloat16)
    values_low = join_heads(grad_values).astype(jnp.bfloat16)
    grad_w_query = rows_product(normed_low, queries_low)
    grad_b_query = jnp.sum(queries_low.astype(jnp.float32), axis=0)
    grad_w_key = rows_product(normed_low, keys_low)
    grad_w_value = rows_product(normed_low, values_low)
    grad_b_value = jnp.sum(values_low.astype(jnp.float32), axis=0)
    grad_terms = (
        cols_product(queries_low, w_query)
        + cols_product(keys_low, w_key)
        + cols_product(values_low, w_value)
    )
    grad_normed_one = lax.psum(grad_terms.astype(jnp.bfloat16), "tensor").astype(jnp.float32)
    grad_ln1_gain = jnp.sum(grad_normed_one * unit_one, axis=0)
    grad_ln1_bias = jnp.sum(grad_normed_one, axis=0)
    grad_inputs = grad_hidden + norm_back(grad_normed_one, unit_one, inverse_one, ln1_gain)
    grad_low = grad_inputs.astype(jnp.bfloat16).reshape(seq_dev, length, model_width)
    restore = jnp.argsort(dealing)
    grad_tokens = lax.all_to_all(
        jnp.take(
            lax.all_to_all(
                grad_low.reshape(seq_dev, dp_size, piece_rows, model_width),
                "dp",
                split_axis=1,
                concat_axis=0,
                tiled=True,
            ),
            restore,
            axis=0,
        ),
        "dp",
        split_axis=0,
        concat_axis=1,
        tiled=True,
    ).reshape(seq_dev, length, model_width)
    summed = (
        lax.psum(grad_ln1_gain.astype(jnp.bfloat16), "dp").astype(jnp.float32),
        lax.psum(grad_ln1_bias.astype(jnp.bfloat16), "dp").astype(jnp.float32),
        lax.psum(grad_w_query.astype(jnp.bfloat16), "dp").astype(jnp.float32),
        lax.psum(grad_b_query.astype(jnp.bfloat16), "dp").astype(jnp.float32),
        lax.psum(grad_w_key.astype(jnp.bfloat16), "dp").astype(jnp.float32),
        lax.psum(grad_w_value.astype(jnp.bfloat16), "dp").astype(jnp.float32),
        lax.psum(grad_b_value.astype(jnp.bfloat16), "dp").astype(jnp.float32),
        lax.psum(grad_w_out.astype(jnp.bfloat16), "dp").astype(jnp.float32),
        lax.psum(grad_b_out.astype(jnp.bfloat16), "dp").astype(jnp.float32),
        lax.psum(ffn_summed[0].astype(jnp.bfloat16), "dp").astype(jnp.float32),
        lax.psum(ffn_summed[1].astype(jnp.bfloat16), "dp").astype(jnp.float32),
        lax.psum(ffn_summed[2].astype(jnp.bfloat16), "dp").astype(jnp.float32),
        lax.psum(ffn_summed[3].astype(jnp.bfloat16), "dp").astype(jnp.float32),
        lax.psum(ffn_summed[4].astype(jnp.bfloat16), "dp").astype(jnp.float32),
        lax.psum(ffn_summed[5].astype(jnp.bfloat16), "dp").astype(jnp.float32),
    )
    return (
        layer_output,
        grad_tokens,
        summed[0],
        summed[1],
        summed[2],
        summed[3],
        summed[4],
        summed[5],
        summed[6],
        summed[7],
        summed[8],
        summed[9],
        summed[10],
        summed[11],
        summed[12],
        summed[13],
        summed[14],
    )


def solution(mesh):
    placed = (
        P("dp", None, None),
        P("dp", None, None),
        P(),
        P(),
        P(),
        P(),
        P(None, "tensor"),
        P("tensor"),
        P(None, "tensor"),
        P(None, "tensor"),
        P("tensor"),
        P("tensor", None),
        P(),
        P(),
        P(),
        P(None, "tensor"),
        P("tensor"),
        P("tensor", None),
        P(),
    )
    return jax.shard_map(
        local,
        mesh=mesh,
        in_specs=placed,
        out_specs=(
            P("dp", None, None),
            P("dp", None, None),
            P(),
            P(),
            P(None, "tensor"),
            P("tensor"),
            P(None, "tensor"),
            P(None, "tensor"),
            P("tensor"),
            P("tensor", None),
            P(),
            P(),
            P(),
            P(None, "tensor"),
            P("tensor"),
            P("tensor", None),
            P(),
        ),
        check_vma=False,
    )
```

profile of v0, /device:TPU:8, one launch (start us, length us, event | category | flops | bytes accessed | tf_op | source)
XLA Modules:
  0.0 1025.3 jit_solution(5581900220783864506)
XLA Ops:
  10.4 3.7 all-to-all-start
  17.3 23.4 %all-to-all-done = bf16[2,8,128,512]{3,2,0,1:T(8,128)(2,1)S(1)} async-done(((bf16[2,8,128,512]{3,2,0,1:T(8,128)(2,1)}), bf16[2,8,128,512]{3,2,0,1:T(8,128)(2,1)S(1)}, u32[]{:S(2)}, u32[]{:S(2)}) %all-to-all-start) | async-done | bytes 2097184 | tf_op jit(solution)/shard_map/all_to_all | solution.py:265
  40.7 4.3 all-to-all-start.2
  48.5 23.3 %all-to-all-done.2 = bf16[2,8,128,512]{3,2,0,1:T(8,128)(2,1)} async-done(((bf16[2,8,128,512]{3,2,0,1:T(8,128)(2,1)}), bf16[2,8,128,512]{3,2,0,1:T(8,128)(2,1)}, u32[]{:S(2)}, u32[]{:S(2)}) %all-to-all-start.2) | async-done | bytes 2097184 | tf_op jit(solution)/shard_map/all_to_all | solution.py:282
  71.7 3.7 gather_fusion.2
  75.5 4.0 fusion.32
  79.5 3.6 all-to-all-start.1
  87.0 22.7 %all-to-all-done.1 = bf16[16,1,128,512]{3,2,1,0:T(8,128)(2,1)S(1)} async-done(((bf16[16,1,128,512]{3,2,1,0:T(8,128)(2,1)}), bf16[16,1,128,512]{3,2,1,0:T(8,128)(2,1)S(1)}, u32[]{:S(2)}, u32[]{:S(2)}) %all-to-all-start.1) | async-done | bytes 2097184 | tf_op jit(solution)/shard_map/all_to_all | solution.py:263
  126.7 3.3 reshape.1588
  130.0 3.5 copy.452
  143.7 3.3 bitcast_reduce_fusion.3
  154.5 5.2 reduce_sum.505
  169.0 3.7 reduce_sum.532
  172.7 5.4 reduce_sum.530
  180.4 4.2 reduce_sum.510
  188.7 4.4 fusion.29
  194.6 3.6 convolution_bitcast_fusion
  217.5 3.2 copy.466
  238.1 4.2 convert_bitcast_fusion.1
  246.1 30.3 %all_to_all.93 = bf16[16,1,128,512]{3,2,1,0:T(8,128)(2,1)S(1)} all-to-all(bf16[16,1,128,512]{3,2,1,0:T(8,128)(2,1)} %get-tuple-element.90), channel_id=1, replica_groups=mesh['dp'=8,'tensor'=4] {'dp'}, dimensions={0} | all-to-all | bytes 4194304 | tf_op jit(solution)/shard_map/all_to_all | solution.py:280
  279.3 119.0 %all-reduce.8.cloned.1.call-done = f32[2048,512]{1,0:T(8,128)} async-done(((f32[2048,512]{1,0:T(8,128)}), f32[2048,512]{1,0:T(8,128)}) %all-reduce.8.cloned.1.call-update) | async-done | bytes 4194320 | tf_op jit(solution)/shard_map/psum | solution.py:334
  398.3 4.0 fusion.140
  405.2 5.4 multiply_convert_fusion.1
  410.6 3.5 fusion.143
  439.0 4.4 convolution_convert_fusion.1
  443.5 61.2 %all-reduce.10.cloned.1.call-done = bf16[2048,512]{1,0:T(8,128)(2,1)} async-done(((bf16[2048,512]{1,0:T(8,128)(2,1)}), bf16[2048,512]{1,0:T(8,128)(2,1)}) %all-reduce.10.cloned.1.call-update) | async-done | bytes 2097168 | tf_op jit(solution)/shard_map/psum | solution.py:357
  504.6 5.7 fusion.10
  554.3 3.3 reduce_sum.545
  560.8 3.5 fusion.66
  602.6 3.2 broadcast_in_dim.312
  611.3 3.2 broadcast_in_dim.307
  617.7 3.2 broadcast_in_dim.302
  632.7 3.2 copy.525
  637.5 3.2 copy.496
  656.1 3.2 copy.513
  673.2 3.7 fusion.73
  682.2 3.2 fusion.135
  701.3 151.8 %all-reduce.14.cloned.1.call-done = (bf16[2048,512]{1,0:T(8,128)(2,1)}, bf16[2048,512]{1,0:T(8,128)(2,1)}) async-done(((bf16[2048,512]{1,0:T(8,128)(2,1)}, bf16[2048,512]{1,0:T(8,128)(2,1)}), (bf16[2048,512]{1,0:T(8,128)(2,1)}, bf16[2048,512]{1,0:T(8,128)(2,1)})) %all-reduce.14.cloned.1.call-update) | async-done | bytes 4194320 | tf_op jit(solution)/shard_map/psum | solution.py:341
  853.2 4.8 fusion.16
  858.1 3.9 fusion.14
  863.5 4.7 all-to-all-start.4
  878.6 16.3 %all-to-all-done.4 = bf16[2,8,128,512]{3,2,0,1:T(8,128)(2,1)} async-done(((bf16[2,8,128,512]{3,2,0,1:T(8,128)(2,1)}), bf16[2,8,128,512]{3,2,0,1:T(8,128)(2,1)}, u32[]{:S(2)}, u32[]{:S(2)}) %all-to-all-start.4) | async-done | bytes 2097184 | tf_op jit(solution)/shard_map/all_to_all | solution.py:392
  894.9 3.6 gather_fusion.3
  901.7 4.5 all-to-all-start.5
  907.6 3.4 convolution_convert_fusion.6
  913.5 69.1 %all-reduce.12.cloned.1.call-done = (bf16[512,128]{1,0:T(8,128)(2,1)}, bf16[512,128]{1,0:T(8,128)(2,1)}, bf16[512,128]{1,0:T(8,128)(2,1)}, bf16[128,512]{1,0:T(8...) async-done(((bf16[512,128]{1,0:T(8,128)(2,1)}, bf16[512,128]{1,0:T(8,128)(2,1)}, bf16[512,128]{1,0:T(8,128)(2,1)}, bf16[128,512]{1,0:T(8,128)(2,1)}, ...) | async-done | bytes 1572880 | tf_op jit(solution)/shard_map/psum | solution.py:410
  993.0 12.1 %all-reduce = (bf16[512]{0:T(512)(128)(2,1)S(1)}, bf16[512]{0:T(512)(128)(2,1)S(1)}, bf16[128]{0:T(256)(128)(2,1)S(1)}, bf16[128]{0:T(256)(128)(2,1)S(1)}, bf16[...) all-reduce(bf16[512]{0:T(512)(128)(2,1)S(1)} %get-tuple-element.22,, ...), channel_id=1, replica_groups=mesh['dp'=8,'tensor'=4] {'dp'}, use_global_device_ids=true, to_apply=%region_46.48 | all-reduce | flops 3840 | bytes 15360 | tf_op jit(solution)/shard_map/psum | solution.py:408
  1010.3 4.9 add_convert_fusion.2
  (662 shorter events, 330.2 us)
Async XLA Ops:
  7.2 397.9 %copy-start = (bf16[512,512]{1,0:T(8,128)(2,1)S(1)}, bf16[512,512]{1,0:T(8,128)(2,1)}, u32[]{:S(2)}) copy-start(bf16[512,512]{1,0:T(8,128)(2,1)} %param.36) | copy-start | bytes 1572868
  10.4 30.4 %all-to-all-start = ((bf16[2,8,128,512]{3,2,0,1:T(8,128)(2,1)}), bf16[2,8,128,512]{3,2,0,1:T(8,128)(2,1)S(1)}, u32[]{:S(2)}, u32[]{:S(2)}) async-start(bf16[2,8,128,512]{3,2,0,1:T(8,128)(2,1)} %copy.423), calls=%async_computation | async-start | bytes 4194304 | tf_op jit(solution)/shard_map/all_to_all | solution.py:265
  17.3 27.8 %copy-start.2 = (s32[16]{0:T(128)S(1)}, s32[16]{0:T(128)}, u32[]{:S(2)}) copy-start(s32[16]{0:T(128)} %param.23) | copy-start | bytes 196
  40.7 31.0 %all-to-all-start.2 = ((bf16[2,8,128,512]{3,2,0,1:T(8,128)(2,1)}), bf16[2,8,128,512]{3,2,0,1:T(8,128)(2,1)}, u32[]{:S(2)}, u32[]{:S(2)}) async-start(bf16[2,8,128,512]{3,2,0,1:T(8,128)(2,1)} %copy.476), calls=%async_computation.2 | async-start | bytes 4194304 | tf_op jit(solution)/shard_map/all_to_all | solution.py:282
  79.5 30.2 %all-to-all-start.1 = ((bf16[16,1,128,512]{3,2,1,0:T(8,128)(2,1)}), bf16[16,1,128,512]{3,2,1,0:T(8,128)(2,1)S(1)}, u32[]{:S(2)}, u32[]{:S(2)}) async-start(bf16[16,1,128,512]{3,2,1,0:T(8,128)(2,1)} %get-tuple-element.91), calls=%async_computation.1 | async-start | bytes 4194304 | tf_op jit(solution)/shard_map/all_to_all | solution.py:263
  83.1 315.2 %all-reduce.8.cloned.1.call-start = ((), (), s32[]{:S(2)}) async-start(), calls=%async_computation.6 | async-start | bytes 8388608 | tf_op jit(solution)/shard_map/psum | solution.py:334
  83.3 111.3 %copy-start.100 = (f32[2,2,8,128]{3,2,1,0:T(8,128)}, f32[2,2,8,128]{3,2,1,0:T(8,128)S(1)}, u32[]{:S(2)}) copy-start(f32[2,2,8,128]{3,2,1,0:T(8,128)S(1)} %maximum_bitcast_fusion.1) | copy-start | bytes 49156
  126.7 6.8 copy-start.14
  126.7 6.8 copy-start.82
  166.8 22.0 %copy-start.36 = (bf16[2,2,1,8,128,64]{4,5,3,2,1,0:T(8,128)(2,1)}, bf16[2,2,1,8,128,64]{4,5,3,2,1,0:T(8,128)(2,1)S(1)}, u32[]{:S(2)}) copy-start(bf16[2,2,1,8,128,64]{4,5,3,2,1,0:T(8,128)(2,1)S(1)} %copy.439) | copy-start | bytes 1572868
  188.7 5.2 copy-start.42
  193.2 8.3 copy-start.111
  193.2 9.1 copy-start.129
  193.3 7.4 copy-start.108
  200.7 5.9 copy-start.119
  200.7 5.9 copy-start.117
  200.8 5.8 copy-start.65
  246.0 258.6 %all-reduce.10.cloned.1.call-start = ((), (), s32[]{:S(2)}) async-start(), calls=%async_computation.7 | async-start | bytes 4194304 | tf_op jit(solution)/shard_map/psum | solution.py:357
  277.8 120.5 %copy-start.159 = (f32[512]{0:T(512)S(1)}, f32[512]{0:T(512)}, u32[]{:S(2)}) copy-start(f32[512]{0:T(512)} %param.33) | copy-start | bytes 6148
  405.2 5.5 copy-start.27
  405.2 5.4 copy-start.18
  405.2 5.4 copy-start.167
  418.2 434.9 %all-reduce.14.cloned.1.call-start = ((), (), s32[]{:S(2)}) async-start(), calls=%async_computation.9 | async-start | bytes 8388608 | tf_op jit(solution)/shard_map/psum | solution.py:341
  428.4 5.3 copy-start.112
  429.3 6.8 copy-start.130
  430.3 7.6 copy-start.120
  439.0 71.3 %copy-start.19 = (bf16[2,8,1,128,512]{4,3,1,0,2:T(8,128)(2,1)S(1)}, bf16[2,8,1,128,512]{4,3,1,0,2:T(8,128)(2,1)}, u32[]{:S(2)}) copy-start(bf16[2,8,1,128,512]{4,3,1,0,2:T(8,128)(2,1)} %copy.478) | copy-start | bytes 6291460
  504.6 5.7 copy-start.4
  504.6 5.7 copy-start.17
  504.6 5.7 copy-start.143
  540.6 5.9 copy-start.113
  541.9 5.6 copy-start.131
  541.9 5.6 copy-start.155
  543.3 5.2 copy-start.43
  543.3 5.2 copy-start.44
  543.4 5.2 copy-start.121
  543.4 5.2 copy-start.144
  543.4 5.2 copy-start.145
  543.4 5.2 copy-start.146
  699.4 153.8 %copy-start.105 = (f32[2048]{0:T(1024)S(1)}, f32[2048]{0:T(1024)}, u32[]{:S(2)}) copy-start(f32[2048]{0:T(1024)} %copy-done.104) | copy-start | bytes 24580
  699.4 153.8 %copy-start.107 = (f32[2048]{0:T(1024)S(1)}, f32[2048]{0:T(1024)}, u32[]{:S(2)}) copy-start(f32[2048]{0:T(1024)} %copy-done.106) | copy-start | bytes 24580
  699.4 153.8 %copy-start.135 = (f32[512]{0:T(512)S(1)}, f32[512]{0:T(512)}, u32[]{:S(2)}) copy-start(f32[512]{0:T(512)} %param.25) | copy-start | bytes 6148
  863.5 31.4 %all-to-all-start.4 = ((bf16[2,8,128,512]{3,2,0,1:T(8,128)(2,1)}), bf16[2,8,128,512]{3,2,0,1:T(8,128)(2,1)}, u32[]{:S(2)}, u32[]{:S(2)}) async-start(bf16[2,8,128,512]{3,2,0,1:T(8,128)(2,1)} %copy.536), calls=%async_computation.4 | async-start | bytes 4194304 | tf_op jit(solution)/shard_map/all_to_all | solution.py:392
  901.7 113.5 %all-to-all-start.5 = ((bf16[16,1,128,512]{3,2,1,0:T(8,128)(2,1)}), bf16[16,1,128,512]{3,2,1,0:T(8,128)(2,1)}, u32[]{:S(2)}, u32[]{:S(2)}) async-start(bf16[16,1,128,512]{3,2,1,0:T(8,128)(2,1)} %fusion.31), calls=%async_computation.5 | async-start | bytes 4194304 | tf_op jit(solution)/shard_map/all_to_all | solution.py:390
  906.1 76.5 %all-reduce.12.cloned.1.call-start = ((), (), s32[]{:S(2)}) async-start(), calls=%async_computation.8 | async-start | bytes 3145728 | tf_op jit(solution)/shard_map/psum | solution.py:410
  982.7 8.9 copy-start.69
  984.4 8.3 copy-start.22
  991.5 18.7 %copy-start.161 = (f32[512]{0:T(512)S(1)}, f32[512]{0:T(512)}, u32[]{:S(2)}) copy-start(f32[512]{0:T(512)} %param.39) | copy-start | bytes 6148
  (130 other events, 363.3 us)
Sparse Core Ops, SparseCore 0:
  246.2 152.0 all-reduce.7
  418.3 86.2 all-reduce.9
  699.6 153.5 all-reduce.13
  912.3 70.3 all-reduce.11
where the time goes:
time: 1040 us; the launch traced here: 1030 us
  waiting for transfers between devices  487 us (47%)
  local copies, waits for them, and re-layouts  257 us (25%)
  other arithmetic  146 us (14%)
  matrix products  56.5 us (5%)
  blocking collectives  42.4 us (4%)
  starting transfers between devices  21.1 us (2%)
  between operations  16.4 us (2%)
    psum x1, waiting for transfers between devices, local(): lax.psum(jnp.dot(activated_low, w_down, preferred_element_type=jnp.float3...  152 us
    psum x1, waiting for transfers between devices, local(): lax.psum(jnp.dot(mixed_low, w_out, preferred_element_type=jnp.float32), '...  119 us
    psum x1, waiting for transfers between devices, local(): lax.psum(grad_w_query.astype(jnp.bfloat16), 'dp').astype(jnp.float32)  69.1 us
    psum x1, waiting for transfers between devices, local(): lax.psum(cols_product(grad_pre, w_up).astype(jnp.bfloat16), 'tensor')  61.2 us
    reduce_sum x27, other arithmetic, pool_sum(): jnp.sum(values.reshape(dims_in[:-2] + (dims_in[-2] // group_size, group_s...  49 us
    broadcast_in_dim x49, local copies, waits for them, and re-layouts, interpolate(): jnp.repeat(stacked[..., 1, offset:offset + level_rows, :], group_size, ax...  34.4 us
    all_to_all x1, blocking collectives, local(): lax.all_to_all(jnp.take(lax.all_to_all(cotangent.reshape(seq_dev, dp_size...  30.3 us
    all_to_all x1, waiting for transfers between devices, local(): lax.all_to_all(tokens.reshape(seq_dev, dp_size, piece_rows, model_width),...  23.4 us
  transfers between devices with their start and end apart: 9, of which 8 were waited for; matrix products, arithmetic and copies ran while one was open for 7% of the time, Pallas kernels for 0%

commit v1 on v0

v1 whole, which is shorter than its diff:
```python
import functools

import jax
import jax.numpy as jnp
from jax import lax
from jax.experimental import pallas as pl
from jax.experimental.pallas import tpu as pltpu
from jax.sharding import PartitionSpec as P

F32 = jnp.float32
BF16 = jnp.bfloat16
HEAD_SIZE = 64
BLOCK = 16
TILE = 128
EPS = 1e-05
INV_ROOT_TWO = 0.7071067811865476
INV_ROOT_TAU = 0.3989422804014327
SCALE = HEAD_SIZE ** (-0.5)


def mm(left, right):
    return lax.dot_general(left, right, (((1,), (0,)), ((), ())), preferred_element_type=F32)


def mm_nt(left, right):
    return lax.dot_general(left, right, (((1,), (1,)), ((), ())), preferred_element_type=F32)


def mm_tn(left, right):
    return lax.dot_general(left, right, (((0,), (0,)), ((), ())), preferred_element_type=F32)


def split_low(values):
    high = values.astype(BF16)
    return high, (values - high.astype(F32)).astype(BF16)


def mm_wide(left, values):
    high, low = split_low(values)
    return mm(left, high) + mm(left, low)


def iota(shape, axis):
    return lax.broadcasted_iota(jnp.int32, shape, axis)


def unit_rows(values):
    centred = values - jnp.mean(values, axis=-1, keepdims=True)
    inverse = lax.rsqrt(jnp.mean(centred * centred, axis=-1, keepdims=True) + EPS)
    return centred * inverse, inverse


def norm_back(grad, unit, inverse, gain):
    scaled = grad * gain
    return inverse * (
        scaled
        - jnp.mean(scaled, axis=-1, keepdims=True)
        - unit * jnp.mean(scaled * unit, axis=-1, keepdims=True)
    )


def level_shifts(rows):
    shifts = []
    shift = 1
    while (2 * rows) >> shift >= 2 * BLOCK:
        shifts.append(shift)
        shift += 1
    return shifts


def coarse_map(index, rows):
    shifts = level_shifts(rows)
    shift = jnp.zeros_like(index)
    start = jnp.zeros_like(index)
    offset = 0
    for s in shifts:
        here = index >= offset
        shift = jnp.where(here, s, shift)
        start = jnp.where(here, offset, start)
        offset += rows >> s
    other = index >= offset
    start = jnp.where(other, offset, start)
    return shift, index - start, other


def coarse_counts(index, rows, length, own, partner):
    shift, place, other = coarse_map(index, rows)
    base = jnp.where(other, partner, own)
    left = length - base - lax.shift_left(place, shift)
    return jnp.clip(left, 0, lax.shift_left(jnp.ones_like(shift), shift)).astype(F32), shift


def pool_matrix(rows):
    coarse = iota((rows, rows), 0)
    fine = iota((rows, rows), 1)
    shift, place, other = coarse_map(coarse, rows)
    hit = (lax.shift_right_logical(fine, shift) == place) & jnp.logical_not(other)
    return hit.astype(F32).astype(BF16)


def spread_matrix(rows):
    fine = iota((rows, rows), 0)
    coarse = iota((rows, rows), 1)
    shift, place, other = coarse_map(coarse, rows)
    hit = (lax.shift_right_logical(fine, shift) == place) & jnp.logical_not(other)
    return hit.astype(F32).astype(BF16)


def top_pool(rows):
    shift = level_shifts(rows)[-1]
    count = rows >> shift
    hit = lax.shift_right_logical(iota((count, rows), 1), shift) == iota((count, rows), 0)
    return hit.astype(F32).astype(BF16)


def head_masks(width=TILE):
    lane = iota((width, TILE), 1)
    first = (lane < HEAD_SIZE).astype(F32)
    return first.astype(BF16), (1.0 - first).astype(BF16)


def full_weight(ref, z, lanes):
    inner, outer = ref.shape[0], ref.shape[1]
    return jnp.concatenate(
        [ref[c, o, z, :, lanes] for o in range(outer) for c in range(inner)], axis=0
    )


def full_weight2(ref, z, which):
    inner, outer = ref.shape[0], ref.shape[1]
    return jnp.concatenate(
        [ref[c, o, z, which, :, :] for o in range(outer) for c in range(inner)], axis=0
    )


def norm_one_kernel(info, own_ref, other_ref, gain_ref, bias_ref, normed_ref, pooled_ref):
    rows = own_ref.shape[0]
    length, partner = info[0], info[2]
    gain, bias = gain_ref[...], bias_ref[...]
    unit, _ = unit_rows(own_ref[...].astype(F32))
    normed_ref[...] = (unit * gain + bias).astype(BF16)
    unit, _ = unit_rows(other_ref[...].astype(F32))
    normed = (unit * gain + bias).astype(BF16)
    pool = top_pool(rows)
    count = pool.shape[0]
    live = (iota((1, rows), 1) + partner < length).astype(F32)
    pool_live = (pool.astype(F32) * live).astype(BF16)
    sums = mm(pool_live, normed)
    counts = jnp.sum(pool_live.astype(F32), axis=-1, keepdims=True)
    mean_live = sums / jnp.maximum(counts, 1.0)
    mean_all = mm(pool, normed) * (count / rows)
    high, low = split_low(mean_all)
    pooled_ref[0 * count : 1 * count, :] = high
    pooled_ref[1 * count : 2 * count, :] = low
    high, low = split_low(mean_live)
    pooled_ref[2 * count : 3 * count, :] = high
    pooled_ref[3 * count : 4 * count, :] = low


def attend_kernel(
    info,
    normed_ref,
    pooled_ref,
    weight_ref,
    bias_ref,
    mixed_ref,
    mixed_wide_ref,
    total_ref,
    q_ref,
    k_ref,
    v_ref,
    prob_ref,
    pool_s,
    spread_s,
    weight_s,
    mask_s,
    numer_s,
):
    rows = normed_ref.shape[0]
    pairs = q_ref.shape[0]
    tiles = 2 * rows // TILE
    half_tiles = rows // TILE
    length, own, partner = info[0], info[1], info[2]
    pool_s[...] = pool_matrix(rows)
    spread_s[...] = spread_matrix(rows)
    lane = iota((1, 2 * TILE), 1) & (TILE - 1)
    for i in range(half_tiles):
        weight_s[i] = (lane + (own + i * TILE) < length).astype(F32)
        counts, _ = coarse_counts(lane + i * TILE, rows, length, own, partner)
        weight_s[half_tiles + i] = counts
    row_at = iota((TILE, 2 * TILE), 0)
    key_at = iota((TILE, 2 * TILE), 1) & (TILE - 1)
    pair_same = (row_at >> 5) == (key_at >> 5)
    apart = (row_at >> 4) != (key_at >> 4)
    mask_s[0] = pair_same.astype(F32)
    mask_s[1] = (pair_same & apart).astype(F32)
    live = (iota((rows, 1), 0) + own < length).astype(F32)
    counts, shift = coarse_counts(iota((rows, 1), 0), rows, length, own, partner)
    key_scale = 1.0 / jnp.maximum(counts, 1.0)
    query_scale = 1.0 / lax.shift_left(jnp.ones_like(shift), shift).astype(F32)
    top = pooled_ref.shape[0] // 4
    counts_other = counts[rows - top :]
    filled = counts_other / jnp.maximum(counts_other, 1.0)
    head_lane = (iota((TILE, TILE), 1) >= HEAD_SIZE).astype(F32)
    ones_second = head_lane.astype(BF16)
    ones_first = (1.0 - head_lane).astype(BF16)

    def one_pair(p, carry):
        weight = full_weight(weight_ref, p, slice(0, 3 * TILE))
        wide = mm(normed_ref[...], weight)
        bq = bias_ref[p, 0:1, :]
        bv = bias_ref[p, 1:2, :]
        query = (wide[:, :TILE] + bq).astype(BF16)
        key = (wide[:, TILE : 2 * TILE].astype(BF16).astype(F32) * live).astype(BF16)
        value = ((wide[:, 2 * TILE :] + bv).astype(BF16).astype(F32) * live).astype(BF16)
        extra = mm(pooled_ref[...], weight)
        q_other = extra[:top, :TILE] + extra[top : 2 * top, :TILE] + bq
        kv_other = extra[2 * top : 3 * top, TILE:] + extra[3 * top :, TILE:]
        k_other = kv_other[:, :TILE]
        v_other = kv_other[:, TILE:] + bv * filled
        q_ref[p, :rows, :] = query
        k_ref[p, :rows, :] = key
        v_ref[p, :rows, :] = value
        pool = pool_s[...]
        q_ref[p, rows:, :] = (mm(pool, query) * query_scale).astype(BF16)
        k_ref[p, rows:, :] = (mm(pool, key) * key_scale).astype(BF16)
        v_ref[p, rows:, :] = (mm(pool, value) * key_scale).astype(BF16)
        q_ref[p, 2 * rows - top :, :] = q_other.astype(BF16)
        k_ref[p, 2 * rows - top :, :] = k_other.astype(BF16)
        v_ref[p, 2 * rows - top :, :] = v_other.astype(BF16)

        def one_tile(i, inner):
            at = pl.ds(pl.multiple_of(i * TILE, TILE), TILE)
            q = q_ref[p, at, :]
            k = k_ref[p, at, :]
            v = v_ref[p, at, :]
            keys = jnp.concatenate([k * ones_first, k * ones_second], axis=0)
            score = mm_nt(q, keys) * SCALE
            mask = mask_s[jnp.where(i >= half_tiles, 1, 0)]
            prob = jnp.where(mask > 0.0, jnp.exp(score) * weight_s[i], 0.0).astype(BF16)
            prob_ref[p, i] = prob
            values = jnp.concatenate(
                [
                    jnp.concatenate([v * ones_first, ones_first], axis=1),
                    jnp.concatenate([v * ones_second, ones_second], axis=1),
                ],
                axis=0,
            )
            numer_s[at, :] = mm(prob, values)
            return inner

        lax.fori_loop(0, tiles, one_tile, 0, unroll=2)
        both = numer_s[:rows, :] + mm_wide(spread_s[...], numer_s[rows:, :])
        total = both[:, TILE:]
        mixed = both[:, :TILE] / total
        total_ref[p] = total
        mixed_wide_ref[p] = mixed
        mixed_ref[p] = mixed.astype(BF16)
        return carry

    lax.fori_loop(0, pairs, one_pair, 0)


def feed_kernel(
    own_ref,
    mixed_ref,
    weight_ref,
    ffn_ref,
    b_out_ref,
    gain_ref,
    shift_ref,
    b_up_ref,
    b_down_ref,
    out_ref,
    hidden_ref,
    normed_ref,
    act_ref,
    slope_ref,
):
    pairs = mixed_ref.shape[0]
    hidden = own_ref[...].astype(F32) + b_out_ref[...]
    for p in range(pairs):
        hidden = hidden + mm_nt(mixed_ref[p], full_weight(weight_ref, p, slice(3 * TILE, None)))
    hidden_ref[...] = hidden
    unit, _ = unit_rows(hidden)
    normed = (unit * gain_ref[...] + shift_ref[...]).astype(BF16)
    normed_ref[...] = normed
    result = hidden + b_down_ref[...]
    for z in range(pairs):
        pre = mm(normed, full_weight2(ffn_ref, z, 0)) + b_up_ref[z]
        half_erf = 0.5 + 0.5 * lax.erf(pre * INV_ROOT_TWO)
        act = (pre * half_erf).astype(BF16)
        act_ref[z] = act
        slope_ref[z] = (half_erf + pre * jnp.exp(-0.5 * pre * pre) * INV_ROOT_TAU).astype(BF16)
        result = result + mm(act, full_weight2(ffn_ref, z, 1))
    out_ref[...] = result.astype(BF16)


def feed_back_kernel(
    dy_ref,
    ffn_ref,
    weight_ref,
    slope_ref,
    hidden_ref,
    gain_ref,
    mixed_wide_ref,
    total_ref,
    grad_pre_ref,
    grad_hidden_ref,
    grad_hidden_low_ref,
    numer_ref,
    gtotal_ref,
    exchange_ref,
    vector_ref,
    b_up_ref,
):
    rows = dy_ref.shape[0]
    pairs = slope_ref.shape[0]
    dy = dy_ref[...]
    grad_normed = jnp.zeros((rows, dy.shape[1]), F32)
    for z in range(pairs):
        grad_act = mm_nt(dy, full_weight2(ffn_ref, z, 1))
        grad_pre = (grad_act * slope_ref[z].astype(F32)).astype(BF16)
        grad_pre_ref[z] = grad_pre
        b_up_ref[z] = jnp.sum(grad_pre.astype(F32), axis=0, keepdims=True)
        grad_normed = grad_normed + mm_nt(grad_pre, full_weight2(ffn_ref, z, 0))
    unit, inverse = unit_rows(hidden_ref[...])
    dy_wide = dy.astype(F32)
    vector_ref[0:1, :] = jnp.sum(grad_normed * unit, axis=0, keepdims=True)
    vector_ref[1:2, :] = jnp.sum(grad_normed, axis=0, keepdims=True)
    vector_ref[2:3, :] = jnp.sum(dy_wide, axis=0, keepdims=True)
    grad_hidden = dy_wide + norm_back(grad_normed, unit, inverse, gain_ref[...])
    vector_ref[3:4, :] = jnp.sum(grad_hidden, axis=0, keepdims=True)
    grad_hidden_ref[...] = grad_hidden
    low = grad_hidden.astype(BF16)
    grad_hidden_low_ref[...] = low
    pool = top_pool(rows)
    top = pool.shape[0]
    same = ((iota((TILE, TILE), 0) // HEAD_SIZE) == (iota((TILE, TILE), 1) // HEAD_SIZE)).astype(F32).astype(BF16)
    for p in range(pairs):
        grad_mixed = mm(low, full_weight(weight_ref, p, slice(3 * TILE, None))).astype(BF16).astype(F32)
        inv = 1.0 / total_ref[p]
        numer = grad_mixed * inv
        high, rest = split_low(grad_mixed * mixed_wide_ref[p])
        gtotal = -(mm(high, same) + mm(rest, same)) * inv
        numer_ref[p] = numer
        gtotal_ref[p] = gtotal
        exchange_ref[:top, p * TILE : (p + 1) * TILE] = mm_wide(pool, numer)
        exchange_ref[top:, p * TILE : (p + 1) * TILE] = mm_wide(pool, gtotal)


def feed_grads_kernel(normed_ref, act_ref, grad_pre_ref, dy_ref, out_ref):
    pairs = act_ref.shape[0]
    inner, outer, _, _, chunk, _ = out_ref.shape
    for z in range(pairs):
        up = mm_tn(normed_ref[...], grad_pre_ref[z]).astype(BF16)
        down = mm_tn(act_ref[z], dy_ref[...]).astype(BF16)
        for o in range(outer):
            for c in range(inner):
                at = (o * inner + c) * chunk
                out_ref[c, o, z, 0] = up[at : at + chunk]
                out_ref[c, o, z, 1] = down[at : at + chunk]


def attend_back_kernel(
    info,
    numer_ref,
    gtotal_ref,
    exchange_ref,
    q_ref,
    k_ref,
    v_ref,
    prob_ref,
    weight_ref,
    own_ref,
    gain_ref,
    grad_hidden_ref,
    grad_tokens_ref,
    grads_ref,
    vector_ref,
    b_qv_ref,
    pool_s,
    spread_s,
    numer_s,
    gtotal_s,
    gq_s,
    gk_s,
    gv_s,
    acc_s,
):
    rows = own_ref.shape[0]
    pairs = q_ref.shape[0]
    tiles = 2 * rows // TILE
    length, own, partner = info[0], info[1], info[2]
    pool_s[...] = pool_matrix(rows)
    spread_s[...] = spread_matrix(rows)
    live = (iota((rows, 1), 0) + own < length).astype(F32)
    counts, shift = coarse_counts(iota((rows, 1), 0), rows, length, own, partner)
    key_scale = SCALE / jnp.maximum(counts, 1.0)
    value_scale = 1.0 / jnp.maximum(counts, 1.0)
    query_scale = SCALE / lax.shift_left(jnp.ones_like(shift), shift).astype(F32)
    lane = iota((TILE, TILE), 1)
    second = (lane >= HEAD_SIZE).astype(F32)
    ones_second = second.astype(BF16)
    ones_first = (1.0 - second).astype(BF16)
    at_lane = lane & (HEAD_SIZE - 1)
    pick = (at_lane < 2).astype(F32)
    pick_first = (pick * (1.0 - second)).astype(BF16)
    pick_second = (pick * second).astype(BF16)
    is_low = at_lane == 1
    top = exchange_ref.shape[1] // 2
    acc_s[...] = jnp.zeros_like(acc_s)

    def one_pair(p, carry):
        pool = pool_s[...]
        numer = numer_ref[p]
        gtotal = gtotal_ref[p]
        numer_s[:rows, :] = numer.astype(BF16)
        numer_s[rows:, :] = mm_wide(pool, numer).astype(BF16)
        gtotal_s[:rows, :] = gtotal
        gtotal_s[rows:, :] = mm_wide(pool, gtotal)
        numer_s[2 * rows - top :, :] = exchange_ref[p, :top, :].astype(BF16)
        gtotal_s[2 * rows - top :, :] = exchange_ref[p, top:, :]

        def one_tile(i, inner):
            at = pl.ds(pl.multiple_of(i * TILE, TILE), TILE)
            q = q_ref[p, at, :]
            k = k_ref[p, at, :]
            v = v_ref[p, at, :]
            prob = prob_ref[p, i]
            numer = numer_s[at, :]
            gtotal = gtotal_s[at, :]
            high = gtotal.astype(BF16).astype(F32)
            mixed_total = jnp.where(is_low, gtotal - high, high).astype(BF16)
            left = jnp.concatenate([numer, mixed_total], axis=1)
            right = jnp.concatenate(
                [
                    jnp.concatenate([v * ones_first, pick_first], axis=1),
                    jnp.concatenate([v * ones_second, pick_second], axis=1),
                ],
                axis=0,
            )
            grad_prob = mm_nt(left, right)
            grad_score = (grad_prob * prob.astype(F32)).astype(BF16)
            keys = jnp.concatenate([k * ones_first, k * ones_second], axis=0)
            gq_s[at, :] = mm(grad_score, keys)
            gk = mm_tn(grad_score, q)
            gk_s[at, :] = jnp.where(lane < HEAD_SIZE, gk[:TILE], gk[TILE:])
            gv = mm_tn(prob, numer)
            gv_s[at, :] = jnp.where(lane < HEAD_SIZE, gv[:TILE], gv[TILE:])
            return inner

        lax.fori_loop(0, tiles, one_tile, 0, unroll=2)
        spread = spread_s[...]
        gq = gq_s[:rows, :] * SCALE + mm_wide(spread, gq_s[rows:, :] * query_scale)
        gk = (gk_s[:rows, :] * SCALE + mm_wide(spread, gk_s[rows:, :] * key_scale)) * live
        gv = (gv_s[:rows, :] + mm_wide(spread, gv_s[rows:, :] * value_scale)) * live
        gq, gk, gv = gq.astype(BF16), gk.astype(BF16), gv.astype(BF16)
        b_qv_ref[p, 0:1, :] = jnp.sum(gq.astype(F32), axis=0, keepdims=True)
        b_qv_ref[p, 1:2, :] = jnp.sum(gv.astype(F32), axis=0, keepdims=True)
        grads = jnp.concatenate([gq, gk, gv], axis=1)
        grads_ref[p] = grads
        acc_s[...] += mm_nt(grads, full_weight(weight_ref, p, slice(0, 3 * TILE)))
        return carry

    lax.fori_loop(0, pairs, one_pair, 0)
    unit, inverse = unit_rows(own_ref[...].astype(F32))
    grad_normed = acc_s[...]
    vector_ref[0:1, :] = jnp.sum(grad_normed * unit, axis=0, keepdims=True)
    vector_ref[1:2, :] = jnp.sum(grad_normed, axis=0, keepdims=True)
    grad_tokens_ref[...] = (
        grad_hidden_ref[...] + norm_back(grad_normed, unit, inverse, gain_ref[...])
    ).astype(BF16)


def attend_grads_kernel(normed_ref, grads_ref, grad_hidden_ref, mixed_ref, out_ref):
    pairs = grads_ref.shape[0]
    inner, outer, _, chunk, _ = out_ref.shape
    for z in range(pairs):
        qkv = mm_tn(normed_ref[...], grads_ref[z]).astype(BF16)
        back = mm_tn(grad_hidden_ref[...], mixed_ref[z]).astype(BF16)
        both = jnp.concatenate([qkv, back], axis=1)
        for o in range(outer):
            for c in range(inner):
                at = (o * inner + c) * chunk
                out_ref[c, o, z] = both[at : at + chunk]


VMEM_SPEC = pl.BlockSpec(memory_space=pltpu.VMEM)
SMEM_SPEC = pl.BlockSpec(memory_space=pltpu.SMEM)


def call(kernel, outs, scalars, args, scratch=(), limit=48, flops=0):
    return pl.pallas_call(
        kernel,
        out_shape=[jax.ShapeDtypeStruct(shape, dtype) for shape, dtype in outs],
        in_specs=[SMEM_SPEC] * len(scalars) + [VMEM_SPEC] * len(args),
        out_specs=[VMEM_SPEC] * len(outs),
        scratch_shapes=list(scratch),
        compiler_params=pltpu.CompilerParams(vmem_limit_bytes=limit << 20),
        cost_estimate=pl.CostEstimate(flops=flops, transcendentals=0, bytes_accessed=8 << 20),
    )(*scalars, *args)


def exchange(pieces, axis, groups=None):
    return lax.all_to_all(pieces, axis, 0, 0, tiled=True, axis_index_groups=groups)


def gather(piece, axis, count, groups=None):
    return exchange(jnp.broadcast_to(piece[None], (count,) + piece.shape), axis, groups)


def total_of(pieces):
    return jnp.sum(pieces.astype(F32), axis=0).astype(BF16)


def local(
    tokens,
    cotangent,
    lengths,
    dealing,
    ln1_gain,
    ln1_bias,
    w_query,
    b_query,
    w_key,
    w_value,
    b_value,
    w_out,
    b_out,
    ln2_gain,
    ln2_bias,
    w_up,
    b_up,
    w_down,
    b_down,
):
    seq_dev, length, width = tokens.shape
    dp = lax.axis_size("dp")
    nt = lax.axis_size("tensor")
    d = lax.axis_index("dp")
    t = lax.axis_index("tensor")
    rows = seq_dev * length // nt
    inner = 2
    outer = dp // inner
    pairs = [[inner * i + c for c in range(inner)] for i in range(outer)]
    planes = [[inner * i + c for i in range(outer)] for c in range(inner)]
    chunk = width // dp
    hid = w_up.shape[1]

    def own_rows(weight):
        return lax.dynamic_slice_in_dim(weight, d * chunk, chunk, axis=0)

    out_cols = lax.dynamic_slice_in_dim(w_out, d * chunk, chunk, axis=1).T
    attn_piece = jnp.concatenate(
        [own_rows(w_query), own_rows(w_key), own_rows(w_value), out_cols], axis=1
    )
    ffn_piece = jnp.stack([own_rows(w_up), own_rows(w_down)])
    bias_piece = jnp.concatenate([b_query, b_value, b_up]).reshape(-1, TILE)
    bias_piece = jnp.pad(bias_piece, ((0, -bias_piece.shape[0] % 8), (0, 0)))
    attn_w = gather(attn_piece, "tensor", nt)
    biases = gather(bias_piece, "tensor", nt)
    attn_w = gather(attn_w, "dp", outer, planes)
    ffn_w = gather(ffn_piece, "tensor", nt)
    attn_w = gather(attn_w, "dp", inner, pairs)
    ffn_w = gather(ffn_w, "dp", outer, planes)
    ffn_w = gather(ffn_w, "dp", inner, pairs)
    b_qv = biases[:, 0:2]
    b_ups = biases[:, 2 : 2 + hid // TILE].reshape(nt, 1, hid)

    halves = tokens.reshape(nt, rows, width)
    own = lax.dynamic_index_in_dim(halves, t, 0, keepdims=False)
    other = lax.dynamic_index_in_dim(halves, t ^ 1, 0, keepdims=False)
    dy = lax.dynamic_index_in_dim(cotangent.reshape(nt, rows, width), t, 0, keepdims=False)
    own_length = lengths[d * seq_dev + t // 2]
    own_base = (t % 2) * rows
    info = jnp.stack([own_length, own_base, rows - own_base]).astype(jnp.int32)
    row = lambda v: v.reshape(1, -1)
    top = rows >> level_shifts(rows)[-1]

    normed_one, pooled = call(
        norm_one_kernel,
        [((rows, width), BF16), ((4 * top, width), BF16)],
        [info],
        [own, other, row(ln1_gain), row(ln1_bias)],
        limit=16,
    )
    mixed, mixed_wide, total, q, k, v, prob = call(
        attend_kernel,
        [((nt, rows, TILE), BF16), ((nt, rows, TILE), F32), ((nt, rows, TILE), F32)]
        + [((nt, 2 * rows, TILE), BF16)] * 3
        + [((nt, 2 * rows // TILE, TILE, 2 * TILE), BF16)],
        [info],
        [normed_one, pooled, attn_w, b_qv],
        scratch=[
            pltpu.VMEM((rows, rows), BF16),
            pltpu.VMEM((rows, rows), BF16),
            pltpu.VMEM((2 * rows // TILE, 1, 2 * TILE), F32),
            pltpu.VMEM((2, TILE, 2 * TILE), F32),
            pltpu.VMEM((2 * rows, 2 * TILE), F32),
        ],
        flops=10**10,
    )
    out, hidden, normed_two, act, slope = call(
        feed_kernel,
        [((rows, width), BF16), ((rows, width), F32), ((rows, width), BF16)]
        + [((nt, rows, hid), BF16)] * 2,
        [],
        [own, mixed, attn_w, ffn_w, row(b_out), row(ln2_gain), row(ln2_bias), b_ups, row(b_down)],
        flops=10**10,
    )

    n_all = dp * nt
    piece = rows // n_all
    dealt = exchange(out.reshape(n_all, piece, width), ("dp", "tensor"))
    dealt = jnp.take(dealt.reshape(dp * seq_dev, -1, piece, width), dealing, axis=0)
    dealt = exchange(dealt.reshape(dp, seq_dev, -1, piece, width), "dp")
    dealt = gather(dealt, "tensor", nt)
    output = dealt.transpose(2, 3, 1, 0, 4, 5).reshape(seq_dev, length, width)

    grad_pre, grad_hidden, grad_hidden_low, numer, gtotal, sent, vec_two, vec_up = call(
        feed_back_kernel,
        [
            ((nt, rows, hid), BF16),
            ((rows, width), F32),
            ((rows, width), BF16),
            ((nt, rows, TILE), F32),
            ((nt, rows, TILE), F32),
            ((2 * top, width), F32),
            ((4, width), F32),
            ((nt, 1, hid), F32),
        ],
        [],
        [dy, ffn_w, attn_w, slope, hidden, row(ln2_gain), mixed_wide, total],
        flops=10**10,
    )
    swapped = lax.ppermute(sent, "tensor", [(i, i ^ 1) for i in range(nt)])
    swapped = swapped.reshape(2 * top, nt, TILE).transpose(1, 0, 2)
    (ffn_grads,) = call(
        feed_grads_kernel,
        [((inner, outer, nt, 2, chunk, hid), BF16)],
        [],
        [normed_two, act, grad_pre, dy],
        flops=10**10,
    )
    grad_low, qkv_grads, vec_one, vec_qv = call(
        attend_back_kernel,
        [
            ((rows, width), BF16),
            ((nt, rows, 3 * TILE), BF16),
            ((2, width), F32),
            ((nt, 2, TILE), F32),
        ],
        [info],
        [numer, gtotal, swapped, q, k, v, prob, attn_w, own, row(ln1_gain), grad_hidden],
        scratch=[
            pltpu.VMEM((rows, rows), BF16),
            pltpu.VMEM((rows, rows), BF16),
            pltpu.VMEM((2 * rows, TILE), BF16),
            pltpu.VMEM((2 * rows, TILE), F32),
            pltpu.VMEM((2 * rows, TILE), F32),
            pltpu.VMEM((2 * rows, TILE), F32),
            pltpu.VMEM((2 * rows, TILE), F32),
            pltpu.VMEM((rows, width), F32),
        ],
        flops=10**10,
    )
    grad_tokens = gather(grad_low, "tensor", nt).reshape(seq_dev, length, width)
    (attn_grads,) = call(
        attend_grads_kernel,
        [((inner, outer, nt, chunk, 4 * TILE), BF16)],
        [],
        [normed_one, qkv_grads, grad_hidden_low, mixed],
        flops=10**10,
    )

    def reduced(grads):
        grads = total_of(exchange(grads, "dp", pairs))
        grads = total_of(exchange(grads, "dp", planes))
        grads = total_of(exchange(grads, "tensor"))
        return gather(grads, "dp", dp)

    ffn_grads = reduced(ffn_grads).astype(F32)
    attn_grads = reduced(attn_grads).astype(F32)
    g_up = ffn_grads[:, 0].reshape(width, hid)
    g_down = ffn_grads[:, 1].reshape(hid, width)
    attn_grads = attn_grads.reshape(width, 4 * TILE)
    g_query = attn_grads[:, :TILE]
    g_key = attn_grads[:, TILE : 2 * TILE]
    g_value = attn_grads[:, 2 * TILE : 3 * TILE]
    g_out = attn_grads[:, 3 * TILE :].T

    vectors = jnp.concatenate(
        [vec_two, vec_up.reshape(nt, hid), vec_one, vec_qv.transpose(1, 0, 2).reshape(2, -1)]
    )
    vectors = gather(vectors.astype(BF16), ("dp", "tensor"), n_all)
    vectors = jnp.sum(vectors.astype(F32), axis=0)
    base = 4 + nt
    g_b_up = lax.dynamic_index_in_dim(vectors[4:base], t, 0, keepdims=False)
    g_b_q = lax.dynamic_index_in_dim(vectors[base + 2].reshape(nt, TILE), t, 0, keepdims=False)
    g_b_v = lax.dynamic_index_in_dim(vectors[base + 3].reshape(nt, TILE), t, 0, keepdims=False)
    return (
        output,
        grad_tokens,
        vectors[base],
        vectors[base + 1],
        g_query,
        g_b_q,
        g_key,
        g_value,
        g_b_v,
        g_out,
        vectors[3],
        vectors[0],
        vectors[1],
        g_up,
        g_b_up,
        g_down,
        vectors[2],
    )


def solution(mesh):
    placed = (
        P("dp", None, None),
        P("dp", None, None),
        P(),
        P(),
        P(),
        P(),
        P(None, "tensor"),
        P("tensor"),
        P(None, "tensor"),
        P(None, "tensor"),
        P("tensor"),
        P("tensor", None),
        P(),
        P(),
        P(),
        P(None, "tensor"),
        P("tensor"),
        P("tensor", None),
        P(),
    )
    return jax.shard_map(
        local,
        mesh=mesh,
        in_specs=placed,
        out_specs=(
            P("dp", None, None),
            P("dp", None, None),
            P(),
            P(),
            P(None, "tensor"),
            P("tensor"),
            P(None, "tensor"),
            P(None, "tensor"),
            P("tensor"),
            P("tensor", None),
            P(),
            P(),
            P(),
            P(None, "tensor"),
            P("tensor"),
            P("tensor", None),
            P(),
        ),
        check_vma=False,
    )
```

time: 1040 us -> 446 us (0.43)
  waiting for transfers between devices: 487 us -> 172 us
  local copies, waits for them, and re-layouts: 257 us -> 44 us
  other arithmetic: 146 us -> 14.5 us
  Pallas kernels: 0 us -> 61.1 us
  matrix products: 56.5 us -> 0 us
  blocking collectives: 42.4 us -> 84.2 us
  starting transfers between devices: 21.1 us -> 62.2 us
  between operations: 16.4 us -> 1.18 us
    psum x4 -> x0, waiting for transfers between devices: 401 us -> none  [the longest x1 152 us: local(): lax.psum(jnp.dot(activated_low, w_down, preferred_element_type=jnp.float3...]
    all_to_all x5 -> x13, waiting for transfers between devices: 85.7 us -> 172 us  [exchange(): lax.all_to_all(pieces, axis, 0, 0, tiled=True, axis_index_groups=groups)]
    reshape x31 -> x0, local copies, waits for them, and re-layouts: 77.4 us -> none  [the longest x6 17.3 us: attend_backward(): jnp.repeat(grad_keys[..., 1, offset:offset + level_rows, :] / floors, gro...]
    reduce_sum x39 -> x7, other arithmetic: 77.2 us -> 10.7 us  [the longest x6 9.45 us: total_of(): return jnp.sum(pieces.astype(F32), axis=0).astype(BF16)]
    pallas_call x0 -> x7, Pallas kernels: none -> 61.1 us  [call(): pl.pallas_call(kernel, out_shape=[jax.ShapeDtypeStruct(shape, dtype) for...]
    dot_general x24 -> x0, matrix products: 56.5 us -> none  [the longest x6 11.8 us: rows_product(): lax.dot_general(left, right, (((0,), (0,)), ((), ())), preferred_element_...]
    all_to_all x1 -> x7, blocking collectives: 30.3 us -> 84.2 us  [exchange(): lax.all_to_all(pieces, axis, 0, 0, tiled=True, axis_index_groups=groups)]
    broadcast_in_dim x63 -> x13, local copies, waits for them, and re-layouts: 59.8 us -> 12.6 us  [the longest x12 12.5 us: gather(): jnp.broadcast_to(piece[None], (count,) + piece.shape)]
  transfers between devices with their start and end apart: 9 -> 14, of which waited for: 8 -> 12; matrix products, arithmetic and copies ran while one was open for 7% -> 6% of each run, Pallas kernels for 0% -> 10%
where the time goes in v1:
time: 446 us; the launch traced here: 439 us
  waiting for transfers between devices  172 us (39%)
  blocking collectives  84.2 us (19%)
  starting transfers between devices  62.2 us (14%)
  Pallas kernels  61.1 us (14%)
  local copies, waits for them, and re-layouts  44 us (10%)
  other arithmetic  14.5 us (3%)
    all_to_all x13, waiting for transfers between devices, exchange(): lax.all_to_all(pieces, axis, 0, 0, tiled=True, axis_index_groups=groups)  172 us
    all_to_all x7, blocking collectives, exchange(): lax.all_to_all(pieces, axis, 0, 0, tiled=True, axis_index_groups=groups)  84.2 us
    pallas_call x7, Pallas kernels, call(): pl.pallas_call(kernel, out_shape=[jax.ShapeDtypeStruct(shape, dtype) for...  61.1 us
    all_to_all x13, starting transfers between devices, exchange(): lax.all_to_all(pieces, axis, 0, 0, tiled=True, axis_index_groups=groups)  59.3 us
    unnamed x70, local copies, waits for them, and re-layouts  16.4 us
    broadcast_in_dim x12, local copies, waits for them, and re-layouts, gather(): jnp.broadcast_to(piece[None], (count,) + piece.shape)  12.5 us
    reduce_sum x6, other arithmetic, total_of(): return jnp.sum(pieces.astype(F32), axis=0).astype(BF16)  9.45 us
  transfers between devices with their start and end apart: 14, of which 12 were waited for; matrix products, arithmetic and copies ran while one was open for 6% of the time, Pallas kernels for 10%

profile of v1, /device:TPU:8, one launch (start us, length us, event | category | flops | bytes accessed | tf_op | source)
XLA Modules:
  0.0 438.7 jit_solution(2551521301450125189)
XLA Ops:
  2.1 5.3 %all-to-all-start.3 = ((f32[4,8,128]{2,1,0:T(8,128)}), f32[4,8,128]{2,1,0:T(8,128)S(1)}, u32[]{:S(2)}, u32[]{:S(2)}) async-start(f32[4,8,128]{2,1,0:T(8,128)} %broadcast_in_dim.43), calls=%async_computation.3 | async-start | bytes 32768 | tf_op jit(solution)/shard_map/all_to_all | solution.py:506
  12.4 4.7 %all-to-all-start = ((bf16[4,64,512]{2,1,0:T(8,128)(2,1)}), bf16[4,64,512]{2,1,0:T(8,128)(2,1)S(1)}, u32[]{:S(2)}, u32[]{:S(2)}) async-start(bf16[4,64,512]{2,1,0:T(8,128)(2,1)} %broadcast_in_dim.40), calls=%async_computation | async-start | bytes 524288 | tf_op jit(solution)/shard_map/all_to_all | solution.py:506
  18.9 4.6 %all-to-all-done = bf16[4,64,512]{2,1,0:T(8,128)(2,1)S(1)} async-done(((bf16[4,64,512]{2,1,0:T(8,128)(2,1)}), bf16[4,64,512]{2,1,0:T(8,128)(2,1)S(1)}, u32[]{:S(2)}, u32[]{:S(2)}) %all-to-all-start) | async-done | bytes 262176 | tf_op jit(solution)/shard_map/all_to_all | solution.py:506
  23.5 15.8 %all_to_all.100 = bf16[4,2,64,512]{3,2,1,0:T(8,128)(2,1)S(1)} all-to-all(bf16[4,2,64,512]{3,2,1,0:T(8,128)(2,1)S(1)} %broadcast_in_dim.44), channel_id=1, replica_groups=mesh['dp'=8,'tensor'=4] {'tensor'}, dimensions={0} | all-to-all | bytes 1048576 | tf_op jit(solution)/shard_map/all_to_all | solution.py:506
  39.5 15.4 %all_to_all.101 = bf16[4,4,64,512]{3,2,1,0:T(8,128)(2,1)S(1)} all-to-all(bf16[4,4,64,512]{3,2,1,0:T(8,128)(2,1)S(1)} %broadcast_in_dim.41), channel_id=1, replica_groups={{0,8,16,24},{4,12,20,28},{1,9,17,25},{5,13,21,29},{2,10,18,26},{6,14,22..., dimensions={0} | all-to-all | bytes 2097152 | tf_op jit(solution)/shard_map/all_to_all | solution.py:506
  55.1 6.3 %all_to_all.102.weight_ref = bf16[2,4,4,64,512]{4,3,2,1,0:T(8,128)(2,1)} all-to-all(bf16[2,4,4,64,512]{4,3,2,1,0:T(8,128)(2,1)S(1)} %broadcast_in_dim.42), channel_id=1, replica_groups={{0,4},{8,12},{16,20},{24,28},{1,5},{9,13},{17,21},{25,29},{2,6},{10,14}..., dimensions={0} | all-to-all | bytes 4194304 | tf_op jit(solution)/shard_map/all_to_all | solution.py:506
  61.4 1.6 broadcast_in_dim.45
  63.0 4.6 %all-to-all-start.5 = ((bf16[4,4,2,64,512]{4,3,2,1,0:T(8,128)(2,1)}), bf16[4,4,2,64,512]{4,3,2,1,0:T(8,128)(2,1)}, u32[]{:S(2)}, u32[]{:S(2)}) async-start(bf16[4,4,2,64,512]{4,3,2,1,0:T(8,128)(2,1)} %broadcast_in_dim.45), calls=%async_computation.5 | async-start | bytes 4194304 | tf_op jit(solution)/shard_map/all_to_all | solution.py:506
  72.3 14.1 %shard_map.315 = (bf16[4,512,128]{2,1,0:T(8,128)(2,1)S(1)}, f32[4,512,128]{2,1,0:T(8,128)S(1)}, f32[4,512,128]{2,1,0:T(8,128)S(1)}, bf16[4,1024,128]{2,1,0:T(8,1...) custom-call(s32[3]{0:T(128)S(1)} %pad_add_fusion.info, ...), custom_call_target="tpu_custom_call" | custom-call | flops 10000000000 | bytes 8388608 | tf_op jit(solution)/shard_map/pallas_call | solution.py:494
  89.4 3.6 all-to-all-done.5
  93.1 2.2 broadcast_in_dim.46
  95.4 8.3 %all_to_all.103.ffn_ref = bf16[2,4,4,2,64,512]{5,4,3,2,1,0:T(8,128)(2,1)} all-to-all(bf16[2,4,4,2,64,512]{5,4,3,2,1,0:T(8,128)(2,1)S(1)} %broadcast_in_dim.46), channel_id=1, replica_groups={{0,4},{8,12},{16,20},{24,28},{1,5},{9,13},{17,21},{25,29},{2,6},{10,14}..., dimensions={0} | all-to-all | bytes 8388608 | tf_op jit(solution)/shard_map/all_to_all | solution.py:506
  103.7 8.4 %shard_map.316 = (bf16[512,512]{1,0:T(8,128)(2,1)}, f32[512,512]{1,0:T(8,128)S(1)}, bf16[512,512]{1,0:T(8,128)(2,1)S(1)}, bf16[4,512,512]{2,1,0:T(8,128)(2,1)S(1)}, bf16[4,512,512]{2,1,0:T(8,128)(2,1)}) custom-call(bf16[512,512]{1,0:T(8,128)(2,1)S(1)} %get-tuple-element.189.own_ref, bf16[4,512,128]{2,1,0:T(8,128)(2,1)S(1)} %get-tuple-element.45.mixed_ref, ...), custom_call_target="tpu_custom_call" | custom-call | flops 10000000000 | bytes 8388608 | tf_op jit(solution)/shard_map/pallas_call | solution.py:494
  112.1 9.6 %shard_map.317 = (bf16[4,512,512]{2,1,0:T(8,128)(2,1)}, f32[512,512]{1,0:T(8,128)S(1)}, bf16[512,512]{1,0:T(8,128)(2,1)S(1)}, f32[4,512,128]{2,1,0:T(8,128)S(1)}...) custom-call(bf16[512,512]{1,0:T(8,128)(2,1)S(1)} %dynamic-slice_bitcast_f, ...), custom_call_target="tpu_custom_call" | custom-call | flops 10000000000 | bytes 8388608 | tf_op jit(solution)/shard_map/pallas_call | solution.py:494
  123.7 2.9 collective-permute-start
  126.5 1.6 copy-done.10
  128.1 4.4 %shard_map.320 = bf16[2,4,4,2,64,512]{5,4,3,2,1,0:T(8,128)(2,1)} custom-call(bf16[512,512]{1,0:T(8,128)(2,1)S(1)} %get-tuple-element.66.normed_ref, bf16[4,512,512]{2,1,0:T(8,128)(2,1)S(1)} %get-tuple-element.67.act_ref, bf16[4,512,512]{2,1,0:T(8,128)(2,1)S(1)} %copy-done.10, bf16[512,512]{1,0:T(8,128)(2,1)S(1)} %dynamic-slice_bitcast_fusion.dy_ref), custom_call_target="tpu_custom_call" | custom-call | flops 10000000000 | bytes 8388608 | tf_op jit(solution)/shard_map/pallas_call | solution.py:494
  132.5 5.8 %all-to-all-start.16 = ((bf16[2,4,4,2,64,512]{5,4,3,2,1,0:T(8,128)(2,1)}), bf16[2,4,4,2,64,512]{5,4,3,2,1,0:T(8,128)(2,1)}, u32[]{:S(2)}, u32[]{:S(2)}) async-start(bf16[2,4,4,2,64,512]{5,4,3,2,1,0:T(8,128)(2,1)} %shard_map.320), calls=%async_computation.16 | async-start | bytes 8388608 | tf_op jit(solution)/shard_map/all_to_all | solution.py:506
  142.1 21.4 %shard_map.318 = (bf16[512,512]{1,0:T(8,128)(2,1)S(1)}, bf16[4,512,384]{2,1,0:T(8,128)(2,1)}, f32[2,512]{1,0:T(2,128)S(1)}, f32[4,2,128]{2,1,0:T(2,128)S(1)}) custom-call(s32[3]{0:T(128)S(1)} %pad_add_fusion.info, f32[4,512,128]{2,1,0:T(8,128)S(1)} %get-tuple-element.51.numer_ref, f32[4,512,128]{2,1,0:T(8,128)S(1)} %copy-done.14, ...), custom_call_target="tpu_custom_call" | custom-call | flops 10000000000 | bytes 8388608 | tf_op jit(solution)/shard_map/pallas_call | solution.py:494
  164.9 1.8 shard_map.319
  166.8 6.3 %all_to_all.104 = bf16[2,4,4,64,512]{4,3,2,1,0:T(8,128)(2,1)} all-to-all(bf16[2,4,4,64,512]{4,3,2,1,0:T(8,128)(2,1)S(1)} %shard_map.319), channel_id=1, replica_groups={{0,4},{8,12},{16,20},{24,28},{1,5},{9,13},{17,21},{25,29},{2,6},{10,14}..., dimensions={0} | all-to-all | bytes 4194304 | tf_op jit(solution)/shard_map/all_to_all | solution.py:506
  174.0 3.2 all-to-all-start.11
  177.2 2.1 reduce_sum.82
  179.3 13.0 %all-to-all-done.11 = bf16[32,12,512]{2,1,0:T(8,128)(2,1)S(1)} async-done(((bf16[32,12,512]{2,1,0:T(8,128)(2,1)}), bf16[32,12,512]{2,1,0:T(8,128)(2,1)S(1)}, u32[]{:S(2)}, u32[]{:S(2)}) %all-to-all-start.11) | async-done | bytes 393248 | tf_op jit(solution)/shard_map/all_to_all | solution.py:506
  192.3 16.2 %all_to_all.105 = bf16[4,4,64,512]{3,2,1,0:T(8,128)(2,1)S(1)} all-to-all(bf16[4,4,64,512]{3,2,1,0:T(8,128)(2,1)S(1)} %reduce_sum.82), channel_id=1, replica_groups={{0,8,16,24},{4,12,20,28},{1,9,17,25},{5,13,21,29},{2,10,18,26},{6,14,22..., dimensions={0} | all-to-all | bytes 2097152 | tf_op jit(solution)/shard_map/all_to_all | solution.py:506
  208.6 3.7 all-to-all-start.7
  213.2 14.3 %all-to-all-done.7 = bf16[32,16,512]{2,1,0:T(8,128)(2,1)S(1)} async-done(((bf16[32,16,512]{2,1,0:T(8,128)(2,1)}), bf16[32,16,512]{2,1,0:T(8,128)(2,1)S(1)}, u32[]{:S(2)}, u32[]{:S(2)}) %all-to-all-start.7) | async-done | bytes 524320 | tf_op jit(solution)/shard_map/all_to_all | solution.py:506
  227.5 3.5 all-to-all-start.14
  232.6 6.4 %all-to-all-done.14 = bf16[4,64,512]{2,1,0:T(8,128)(2,1)S(1)} async-done(((bf16[4,64,512]{2,1,0:T(8,128)(2,1)}), bf16[4,64,512]{2,1,0:T(8,128)(2,1)S(1)}, u32[]{:S(2)}, u32[]{:S(2)}) %all-to-all-start.14) | async-done | bytes 262176 | tf_op jit(solution)/shard_map/all_to_all | solution.py:506
  239.0 3.5 all-to-all-start.8
  242.5 5.0 %reduce_sum.85 = bf16[4,4,2,64,512]{4,3,2,1,0:T(8,128)(2,1)} reduce(bf16[2,4,4,2,64,512]{5,4,3,2,1,0:T(8,128)(2,1)} %all-to-all-done.16, bf16[]{:T(256)} %constant.83.clone.1), dimensions={0}, to_apply=%region_4.5 | reduce | flops 1048576 | bytes 6291458 | tf_op jit(solution)/shard_map/reduce_sum | solution.py:514
  247.6 4.6 %all-to-all-done.8 = bf16[8,2,2,16,512]{4,3,2,1,0:T(8,128)(2,1)S(1)} async-done(((bf16[8,2,2,16,512]{4,3,2,1,0:T(8,128)(2,1)}), bf16[8,2,2,16,512]{4,3,2,1,0:T(8,128)(2,1)S(1)}, u32[]{:S(2)}, u32[]{:S(2)}) %all-to-all-start.8) | async-done | bytes 524320 | tf_op jit(solution)/shard_map/all_to_all | solution.py:506
  253.0 3.6 all-to-all-start.17
  256.7 24.1 %all-to-all-done.17 = bf16[4,4,2,64,512]{4,3,2,1,0:T(8,128)(2,1)S(1)} async-done(((bf16[4,4,2,64,512]{4,3,2,1,0:T(8,128)(2,1)}), bf16[4,4,2,64,512]{4,3,2,1,0:T(8,128)(2,1)S(1)}, u32[]{:S(2)}, u32[]{:S(2)}) %all-to-all-start.17) | async-done | bytes 2097184 | tf_op jit(solution)/shard_map/all_to_all | solution.py:506
  281.6 3.5 all-to-all-start.15
  286.4 8.4 %all-to-all-done.15 = bf16[8,64,512]{2,1,0:T(8,128)(2,1)S(1)} async-done(((bf16[8,64,512]{2,1,0:T(8,128)(2,1)}), bf16[8,64,512]{2,1,0:T(8,128)(2,1)S(1)}, u32[]{:S(2)}, u32[]{:S(2)}) %all-to-all-start.15) | async-done | bytes 524320 | tf_op jit(solution)/shard_map/all_to_all | solution.py:506
  294.8 15.9 %all_to_all.106 = bf16[4,2,64,512]{3,2,1,0:T(8,128)(2,1)S(1)} all-to-all(bf16[4,2,64,512]{3,2,1,0:T(8,128)(2,1)} %reduce_sum.86), channel_id=1, replica_groups=mesh['dp'=8,'tensor'=4] {'tensor'}, dimensions={0} | all-to-all | bytes 1048576 | tf_op jit(solution)/shard_map/all_to_all | solution.py:506
  310.6 1.5 broadcast_in_dim.50
  312.1 5.4 %all-to-all-start.10 = ((bf16[4,512,512]{2,1,0:T(8,128)(2,1)}), bf16[4,512,512]{2,1,0:T(8,128)(2,1)S(1)}, u32[]{:S(2)}, u32[]{:S(2)}) async-start(bf16[4,512,512]{2,1,0:T(8,128)(2,1)} %broadcast_in_dim.50), calls=%async_computation.10 | async-start | bytes 4194304 | tf_op jit(solution)/shard_map/all_to_all | solution.py:506
  317.6 43.3 %all-to-all-done.10 = bf16[4,512,512]{2,1,0:T(8,128)(2,1)S(1)} async-done(((bf16[4,512,512]{2,1,0:T(8,128)(2,1)}), bf16[4,512,512]{2,1,0:T(8,128)(2,1)S(1)}, u32[]{:S(2)}, u32[]{:S(2)}) %all-to-all-start.10) | async-done | bytes 2097184 | tf_op jit(solution)/shard_map/all_to_all | solution.py:506
  362.1 5.6 %all-to-all-start.19 = ((bf16[8,2,64,512]{3,2,1,0:T(8,128)(2,1)}), bf16[8,2,64,512]{3,2,1,0:T(8,128)(2,1)S(1)}, u32[]{:S(2)}, u32[]{:S(2)}) async-start(bf16[8,2,64,512]{3,2,1,0:T(8,128)(2,1)} %broadcast_in_dim.53), calls=%async_computation.19 | async-start | bytes 2097152 | tf_op jit(solution)/shard_map/all_to_all | solution.py:506
  367.7 1.9 copy.89
  369.6 13.5 %all-to-all-done.19 = bf16[8,2,64,512]{3,2,1,0:T(8,128)(2,1)S(1)} async-done(((bf16[8,2,64,512]{3,2,1,0:T(8,128)(2,1)}), bf16[8,2,64,512]{3,2,1,0:T(8,128)(2,1)S(1)}, u32[]{:S(2)}, u32[]{:S(2)}) %all-to-all-start.19) | async-done | bytes 1048608 | tf_op jit(solution)/shard_map/all_to_all | solution.py:506
  383.1 2.6 broadcast_in_dim.49
  385.7 6.9 %all-to-all-start.9 = ((bf16[4,8,2,2,16,512]{5,4,1,3,2,0:T(8,128)(2,1)}), bf16[4,8,2,2,16,512]{5,4,1,3,2,0:T(8,128)(2,1)S(1)}, u32[]{:S(2)}, u32[]{:S(2)}) async-start(bf16[4,8,2,2,16,512]{5,4,1,3,2,0:T(8,128)(2,1)} %broadcast_in_dim.49), calls=%async_computation.9 | async-start | bytes 4194304 | tf_op jit(solution)/shard_map/all_to_all | solution.py:506
  398.5 1.6 fusion.2
  400.1 34.9 %all-to-all-done.9 = bf16[4,8,2,2,16,512]{5,4,1,3,2,0:T(8,128)(2,1)S(1)} async-done(((bf16[4,8,2,2,16,512]{5,4,1,3,2,0:T(8,128)(2,1)}), bf16[4,8,2,2,16,512]{5,4,1,3,2,0:T(8,128)(2,1)S(1)}, u32[]{:S(2)}, u32[]{:S(2)}) %all-to-all-start.9) | async-done | bytes 2097184 | tf_op jit(solution)/shard_map/all_to_all | solution.py:506
  435.0 1.6 copy.90
  (121 shorter events, 38.8 us)
Async XLA Ops:
  0.7 70.9 %copy-start = (bf16[2,1024,512]{2,1,0:T(8,128)(2,1)S(1)}, bf16[2,1024,512]{2,1,0:T(8,128)(2,1)}, u32[]{:S(2)}) copy-start(bf16[2,1024,512]{2,1,0:T(8,128)(2,1)} %param.20) | copy-start | bytes 6291460
  2.1 9.6 %all-to-all-start.3 = ((f32[4,8,128]{2,1,0:T(8,128)}), f32[4,8,128]{2,1,0:T(8,128)S(1)}, u32[]{:S(2)}, u32[]{:S(2)}) async-start(f32[4,8,128]{2,1,0:T(8,128)} %broadcast_in_dim.43), calls=%async_computation.3 | async-start | bytes 32768 | tf_op jit(solution)/shard_map/all_to_all | solution.py:506
  12.4 11.1 %all-to-all-start = ((bf16[4,64,512]{2,1,0:T(8,128)(2,1)}), bf16[4,64,512]{2,1,0:T(8,128)(2,1)S(1)}, u32[]{:S(2)}, u32[]{:S(2)}) async-start(bf16[4,64,512]{2,1,0:T(8,128)(2,1)} %broadcast_in_dim.40), calls=%async_computation | async-start | bytes 524288 | tf_op jit(solution)/shard_map/all_to_all | solution.py:506
  63.0 4.7 %copy-start.30 = (s32[16]{0:T(128)S(1)}, s32[16]{0:T(128)}, u32[]{:S(2)}) copy-start(s32[16]{0:T(128)} %param.21) | copy-start | bytes 196
  63.0 30.1 %all-to-all-start.5 = ((bf16[4,4,2,64,512]{4,3,2,1,0:T(8,128)(2,1)}), bf16[4,4,2,64,512]{4,3,2,1,0:T(8,128)(2,1)}, u32[]{:S(2)}, u32[]{:S(2)}) async-start(bf16[4,4,2,64,512]{4,3,2,1,0:T(8,128)(2,1)} %broadcast_in_dim.45), calls=%async_computation.5 | async-start | bytes 4194304 | tf_op jit(solution)/shard_map/all_to_all | solution.py:506
  67.5 2.7 copy-start.2
  67.6 2.7 copy-start.3
  71.5 0.8 copy-start.4
  86.5 1.0 copy-start.15
  87.4 1.0 copy-start.16
  88.4 1.0 copy-start.17
  89.4 5.9 %copy-start.19 = (bf16[4,1024,128]{2,1,0:T(8,128)(2,1)}, bf16[4,1024,128]{2,1,0:T(8,128)(2,1)S(1)}, u32[]{:S(2)}) copy-start(bf16[4,1024,128]{2,1,0:T(8,128)(2,1)S(1)} %get-tuple-element.55.k_ref) | copy-start | bytes 3145732
  89.4 14.3 %copy-start.23 = (bf16[4,512,128]{2,1,0:T(8,128)(2,1)}, bf16[4,512,128]{2,1,0:T(8,128)(2,1)S(1)}, u32[]{:S(2)}) copy-start(bf16[4,512,128]{2,1,0:T(8,128)(2,1)S(1)} %get-tuple-element.45.mixed_ref) | copy-start | bytes 1572868
  95.3 8.3 %copy-start.6 = (f32[512]{0:T(512)S(1)}, f32[512]{0:T(512)}, u32[]{:S(2)}) copy-start(f32[512]{0:T(512)} %param.31) | copy-start | bytes 6148
  95.3 8.3 %copy-start.7 = (f32[512]{0:T(512)S(1)}, f32[512]{0:T(512)}, u32[]{:S(2)}) copy-start(f32[512]{0:T(512)} %param.33) | copy-start | bytes 6148
  95.3 8.3 %copy-start.8 = (f32[512]{0:T(512)S(1)}, f32[512]{0:T(512)}, u32[]{:S(2)}) copy-start(f32[512]{0:T(512)} %param.37) | copy-start | bytes 6148
  95.4 8.3 %copy-start.9 = (f32[512]{0:T(512)S(1)}, f32[512]{0:T(512)}, u32[]{:S(2)}) copy-start(f32[512]{0:T(512)} %param.32) | copy-start | bytes 6148
  121.7 1.0 copy-start.12
  122.7 1.0 copy-start.13
  123.7 8.9 %copy-start.21 = (bf16[512,512]{1,0:T(8,128)(2,1)}, bf16[512,512]{1,0:T(8,128)(2,1)S(1)}, u32[]{:S(2)}) copy-start(bf16[512,512]{1,0:T(8,128)(2,1)S(1)} %get-tuple-element.65.grad_hidden_ref) | copy-start | bytes 1572868
  123.7 14.7 %collective-permute-start = (f32[32,512]{1,0:T(8,128)S(1)}, f32[32,512]{1,0:T(8,128)S(1)}, u32[]{:S(2)}, u32[]{:S(2)}) collective-permute-start(f32[32,512]{1,0:T(8,128)S(1)} %get-tuple-element.53), channel_id=1, source_target_pairs={{0,1},{1,0},{2,3},{3,2},{4,5},{5,4},{6,7},{7,6},{8,9},{9,8},{10,11... | collective-permute-start | bytes 196616 | tf_op jit(solution)/shard_map/ppermute | solution.py:637
  126.5 1.6 copy-start.10
  132.5 34.3 %all-to-all-start.16 = ((bf16[2,4,4,2,64,512]{5,4,3,2,1,0:T(8,128)(2,1)}), bf16[2,4,4,2,64,512]{5,4,3,2,1,0:T(8,128)(2,1)}, u32[]{:S(2)}, u32[]{:S(2)}) async-start(bf16[2,4,4,2,64,512]{5,4,3,2,1,0:T(8,128)(2,1)} %shard_map.320), calls=%async_computation.16 | async-start | bytes 8388608 | tf_op jit(solution)/shard_map/all_to_all | solution.py:506
  138.4 1.2 copy-start.14
  139.7 1.2 copy-start.18
  140.9 1.2 copy-start.20
  142.1 21.4 %copy-start.5 = (bf16[512,512]{1,0:T(8,128)(2,1)S(1)}, bf16[512,512]{1,0:T(8,128)(2,1)}, u32[]{:S(2)}) copy-start(bf16[512,512]{1,0:T(8,128)(2,1)} %copy-done.4) | copy-start | bytes 1572868
  142.1 21.4 %copy-start.22 = (bf16[512,512]{1,0:T(8,128)(2,1)S(1)}, bf16[512,512]{1,0:T(8,128)(2,1)}, u32[]{:S(2)}) copy-start(bf16[512,512]{1,0:T(8,128)(2,1)} %copy-done.21) | copy-start | bytes 1572868
  142.1 21.4 %copy-start.24 = (bf16[4,512,128]{2,1,0:T(8,128)(2,1)S(1)}, bf16[4,512,128]{2,1,0:T(8,128)(2,1)}, u32[]{:S(2)}) copy-start(bf16[4,512,128]{2,1,0:T(8,128)(2,1)} %copy-done.23) | copy-start | bytes 1572868
  163.5 1.4 copy-start.11
  174.0 18.4 %all-to-all-start.11 = ((bf16[32,12,512]{2,1,0:T(8,128)(2,1)}), bf16[32,12,512]{2,1,0:T(8,128)(2,1)S(1)}, u32[]{:S(2)}, u32[]{:S(2)}) async-start(bf16[32,12,512]{2,1,0:T(8,128)(2,1)} %broadcast_in_dim.51), calls=%async_computation.11 | async-start | bytes 1048576 | tf_op jit(solution)/shard_map/all_to_all | solution.py:506
  179.3 33.0 %copy-start.31 = (s32[16]{0:T(128)S(1)}, s32[16]{0:T(128)}, u32[]{:S(2)}) copy-start(s32[16]{0:T(128)} %param.22) | copy-start | bytes 196
  192.3 20.9 %copy-start.28 = (bf16[32,12,512]{2,1,0:T(8,128)(2,1)}, bf16[32,12,512]{2,1,0:T(8,128)(2,1)S(1)}, u32[]{:S(2)}) copy-start(bf16[32,12,512]{2,1,0:T(8,128)(2,1)S(1)} %all-to-all-done.11) | copy-start | bytes 1179652
  208.6 18.9 %all-to-all-start.7 = ((bf16[32,16,512]{2,1,0:T(8,128)(2,1)}), bf16[32,16,512]{2,1,0:T(8,128)(2,1)S(1)}, u32[]{:S(2)}, u32[]{:S(2)}) async-start(bf16[32,16,512]{2,1,0:T(8,128)(2,1)} %bitcast.16), calls=%async_computation.7 | async-start | bytes 1048576 | tf_op jit(solution)/shard_map/all_to_all | solution.py:506
  227.5 11.5 %all-to-all-start.14 = ((bf16[4,64,512]{2,1,0:T(8,128)(2,1)}), bf16[4,64,512]{2,1,0:T(8,128)(2,1)S(1)}, u32[]{:S(2)}, u32[]{:S(2)}) async-start(bf16[4,64,512]{2,1,0:T(8,128)(2,1)} %reduce_sum.83), calls=%async_computation.14 | async-start | bytes 524288 | tf_op jit(solution)/shard_map/all_to_all | solution.py:506
  239.0 13.2 %all-to-all-start.8 = ((bf16[8,2,2,16,512]{4,3,2,1,0:T(8,128)(2,1)}), bf16[8,2,2,16,512]{4,3,2,1,0:T(8,128)(2,1)S(1)}, u32[]{:S(2)}, u32[]{:S(2)}) async-start(bf16[8,2,2,16,512]{4,3,2,1,0:T(8,128)(2,1)} %broadcast_select_fusion), calls=%async_computation.8 | async-start | bytes 1048576 | tf_op jit(solution)/shard_map/all_to_all | solution.py:506
  252.2 0.8 copy-start.29
  253.0 27.8 %all-to-all-start.17 = ((bf16[4,4,2,64,512]{4,3,2,1,0:T(8,128)(2,1)}), bf16[4,4,2,64,512]{4,3,2,1,0:T(8,128)(2,1)S(1)}, u32[]{:S(2)}, u32[]{:S(2)}) async-start(bf16[4,4,2,64,512]{4,3,2,1,0:T(8,128)(2,1)} %reduce_sum.85), calls=%async_computation.17 | async-start | bytes 4194304 | tf_op jit(solution)/shard_map/all_to_all | solution.py:506
  281.6 13.2 %all-to-all-start.15 = ((bf16[8,64,512]{2,1,0:T(8,128)(2,1)}), bf16[8,64,512]{2,1,0:T(8,128)(2,1)S(1)}, u32[]{:S(2)}, u32[]{:S(2)}) async-start(bf16[8,64,512]{2,1,0:T(8,128)(2,1)} %broadcast_in_dim.52), calls=%async_computation.15 | async-start | bytes 1048576 | tf_op jit(solution)/shard_map/all_to_all | solution.py:506
  294.8 17.4 %copy-start.27 = (bf16[8,64,512]{2,1,0:T(8,128)(2,1)}, bf16[8,64,512]{2,1,0:T(8,128)(2,1)S(1)}, u32[]{:S(2)}) copy-start(bf16[8,64,512]{2,1,0:T(8,128)(2,1)S(1)} %all-to-all-done.15) | copy-start | bytes 1572868
  312.1 48.8 %all-to-all-start.10 = ((bf16[4,512,512]{2,1,0:T(8,128)(2,1)}), bf16[4,512,512]{2,1,0:T(8,128)(2,1)S(1)}, u32[]{:S(2)}, u32[]{:S(2)}) async-start(bf16[4,512,512]{2,1,0:T(8,128)(2,1)} %broadcast_in_dim.50), calls=%async_computation.10 | async-start | bytes 4194304 | tf_op jit(solution)/shard_map/all_to_all | solution.py:506
  360.9 8.7 %copy-start.25 = (bf16[4,512,512]{2,1,0:T(8,128)(2,1)}, bf16[4,512,512]{2,1,0:T(8,128)(2,1)S(1)}, u32[]{:S(2)}) copy-start(bf16[4,512,512]{2,1,0:T(8,128)(2,1)S(1)} %all-to-all-done.10) | copy-start | bytes 6291460
  362.1 21.0 %all-to-all-start.19 = ((bf16[8,2,64,512]{3,2,1,0:T(8,128)(2,1)}), bf16[8,2,64,512]{3,2,1,0:T(8,128)(2,1)S(1)}, u32[]{:S(2)}, u32[]{:S(2)}) async-start(bf16[8,2,64,512]{3,2,1,0:T(8,128)(2,1)} %broadcast_in_dim.53), calls=%async_computation.19 | async-start | bytes 2097152 | tf_op jit(solution)/shard_map/all_to_all | solution.py:506
  385.7 49.3 %all-to-all-start.9 = ((bf16[4,8,2,2,16,512]{5,4,1,3,2,0:T(8,128)(2,1)}), bf16[4,8,2,2,16,512]{5,4,1,3,2,0:T(8,128)(2,1)S(1)}, u32[]{:S(2)}, u32[]{:S(2)}) async-start(bf16[4,8,2,2,16,512]{5,4,1,3,2,0:T(8,128)(2,1)} %broadcast_in_dim.49), calls=%async_computation.9 | async-start | bytes 4194304 | tf_op jit(solution)/shard_map/all_to_all | solution.py:506
  435.0 2.3 copy-start.26
  436.6 2.1 copy-start.1

commit v2 on v1

--- a/solution.py
+++ b/solution.py
@@ -119,18 +119,19 @@
     return first.astype(BF16), (1.0 - first).astype(BF16)
 
 
-def full_weight(ref, z, lanes):
-    inner, outer = ref.shape[0], ref.shape[1]
-    return jnp.concatenate(
-        [ref[c, o, z, :, lanes] for o in range(outer) for c in range(inner)], axis=0
-    )
-
-
-def full_weight2(ref, z, which):
-    inner, outer = ref.shape[0], ref.shape[1]
-    return jnp.concatenate(
-        [ref[c, o, z, which, :, :] for o in range(outer) for c in range(inner)], axis=0
-    )
+def assemble(info, near_ref, far_ref, to_ref):
+    core, plane, line = info[3], info[4], info[5]
+    chunk = near_ref.shape[-2]
+    for far, ref in enumerate((near_ref, far_ref)):
+        for o in range(ref.shape[0]):
+            at = ((o ^ plane) * 2 + (far ^ core)) * chunk
+            at = pl.ds(pl.multiple_of(at, chunk), chunk)
+            for z in range(ref.shape[1]):
+                if len(ref.shape) == 5:
+                    for part in range(ref.shape[2]):
+                        to_ref[z ^ line, part, at, :] = ref[o, z, part]
+                else:
+                    to_ref[z ^ line, at, :] = ref[o, z]
 
 
 def norm_one_kernel(info, own_ref, other_ref, gain_ref, bias_ref, normed_ref, pooled_ref):
@@ -161,7 +162,8 @@
     info,
     normed_ref,
     pooled_ref,
-    weight_ref,
+    near_ref,
+    far_ref,
     bias_ref,
     mixed_ref,
     mixed_wide_ref,
@@ -175,12 +177,15 @@
     weight_s,
     mask_s,
     numer_s,
+    full_s,
 ):
     rows = normed_ref.shape[0]
     pairs = q_ref.shape[0]
     tiles = 2 * rows // TILE
     half_tiles = rows // TILE
     length, own, partner = info[0], info[1], info[2]
+    line = info[5]
+    assemble(info, near_ref, far_ref, full_s)
     pool_s[...] = pool_matrix(rows)
     spread_s[...] = spread_matrix(rows)
     lane = iota((1, 2 * TILE), 1) & (TILE - 1)
@@ -206,10 +211,10 @@
     ones_first = (1.0 - head_lane).astype(BF16)
 
     def one_pair(p, carry):
-        weight = full_weight(weight_ref, p, slice(0, 3 * TILE))
+        weight = full_s[p, :, : 3 * TILE]
         wide = mm(normed_ref[...], weight)
-        bq = bias_ref[p, 0:1, :]
-        bv = bias_ref[p, 1:2, :]
+        bq = bias_ref[p ^ line, 0:1, :]
+        bv = bias_ref[p ^ line, 1:2, :]
         query = (wide[:, :TILE] + bq).astype(BF16)
         key = (wide[:, TILE : 2 * TILE].astype(BF16).astype(F32) * live).astype(BF16)
         value = ((wide[:, 2 * TILE :] + bv).astype(BF16).astype(F32) * live).astype(BF16)
@@ -262,10 +267,13 @@
 
 
 def feed_kernel(
+    info,
     own_ref,
     mixed_ref,
-    weight_ref,
-    ffn_ref,
+    near_ref,
+    far_ref,
+    ffn_near_ref,
+    ffn_far_ref,
     b_out_ref,
     gain_ref,
     shift_ref,
@@ -276,30 +284,38 @@
     normed_ref,
     act_ref,
     slope_ref,
+    full_s,
+    ffn_s,
 ):
     pairs = mixed_ref.shape[0]
+    line = info[5]
+    assemble(info, near_ref, far_ref, full_s)
+    assemble(info, ffn_near_ref, ffn_far_ref, ffn_s)
     hidden = own_ref[...].astype(F32) + b_out_ref[...]
     for p in range(pairs):
-        hidden = hidden + mm_nt(mixed_ref[p], full_weight(weight_ref, p, slice(3 * TILE, None)))
+        hidden = hidden + mm_nt(mixed_ref[p], full_s[p, :, 3 * TILE :])
     hidden_ref[...] = hidden
     unit, _ = unit_rows(hidden)
     normed = (unit * gain_ref[...] + shift_ref[...]).astype(BF16)
     normed_ref[...] = normed
     result = hidden + b_down_ref[...]
     for z in range(pairs):
-        pre = mm(normed, full_weight2(ffn_ref, z, 0)) + b_up_ref[z]
+        pre = mm(normed, ffn_s[z, 0]) + b_up_ref[z ^ line]
         half_erf = 0.5 + 0.5 * lax.erf(pre * INV_ROOT_TWO)
         act = (pre * half_erf).astype(BF16)
         act_ref[z] = act
         slope_ref[z] = (half_erf + pre * jnp.exp(-0.5 * pre * pre) * INV_ROOT_TAU).astype(BF16)
-        result = result + mm(act, full_weight2(ffn_ref, z, 1))
+        result = result + mm(act, ffn_s[z, 1])
     out_ref[...] = result.astype(BF16)
 
 
 def feed_back_kernel(
+    info,
     dy_ref,
-    ffn_ref,
-    weight_ref,
+    ffn_near_ref,
+    ffn_far_ref,
+    near_ref,
+    far_ref,
     slope_ref,
     hidden_ref,
     gain_ref,
@@ -313,17 +329,21 @@
     exchange_ref,
     vector_ref,
     b_up_ref,
+    full_s,
+    ffn_s,
 ):
     rows = dy_ref.shape[0]
+    assemble(info, ffn_near_ref, ffn_far_ref, ffn_s)
+    assemble(info, near_ref, far_ref, full_s)
     pairs = slope_ref.shape[0]
     dy = dy_ref[...]
     grad_normed = jnp.zeros((rows, dy.shape[1]), F32)
     for z in range(pairs):
-        grad_act = mm_nt(dy, full_weight2(ffn_ref, z, 1))
+        grad_act = mm_nt(dy, ffn_s[z, 1])
         grad_pre = (grad_act * slope_ref[z].astype(F32)).astype(BF16)
         grad_pre_ref[z] = grad_pre
         b_up_ref[z] = jnp.sum(grad_pre.astype(F32), axis=0, keepdims=True)
-        grad_normed = grad_normed + mm_nt(grad_pre, full_weight2(ffn_ref, z, 0))
+        grad_normed = grad_normed + mm_nt(grad_pre, ffn_s[z, 0])
     unit, inverse = unit_rows(hidden_ref[...])
     dy_wide = dy.astype(F32)
     vector_ref[0:1, :] = jnp.sum(grad_normed * unit, axis=0, keepdims=True)
@@ -338,7 +358,7 @@
     top = pool.shape[0]
     same = ((iota((TILE, TILE), 0) // HEAD_SIZE) == (iota((TILE, TILE), 1) // HEAD_SIZE)).astype(F32).astype(BF16)
     for p in range(pairs):
-        grad_mixed = mm(low, full_weight(weight_ref, p, slice(3 * TILE, None))).astype(BF16).astype(F32)
+        grad_mixed = mm(low, full_s[p, :, 3 * TILE :]).astype(BF16).astype(F32)
         inv = 1.0 / total_ref[p]
         numer = grad_mixed * inv
         high, rest = split_low(grad_mixed * mixed_wide_ref[p])
@@ -349,17 +369,24 @@
         exchange_ref[top:, p * TILE : (p + 1) * TILE] = mm_wide(pool, gtotal)
 
 
-def feed_grads_kernel(normed_ref, act_ref, grad_pre_ref, dy_ref, out_ref):
-    pairs = act_ref.shape[0]
-    inner, outer, _, _, chunk, _ = out_ref.shape
-    for z in range(pairs):
-        up = mm_tn(normed_ref[...], grad_pre_ref[z]).astype(BF16)
-        down = mm_tn(act_ref[z], dy_ref[...]).astype(BF16)
-        for o in range(outer):
-            for c in range(inner):
-                at = (o * inner + c) * chunk
-                out_ref[c, o, z, 0] = up[at : at + chunk]
-                out_ref[c, o, z, 1] = down[at : at + chunk]
+def give_out(info, near_ref, far_ref, z, part, values_s):
+    core, plane = info[3], info[4]
+    chunk = near_ref.shape[-2]
+    for far, ref in enumerate((near_ref, far_ref)):
+        for o in range(ref.shape[0]):
+            at = ((o ^ plane) * 2 + (far ^ core)) * chunk
+            ref[o, z, part] = values_s[pl.ds(pl.multiple_of(at, chunk), chunk), :]
+
+
+def feed_grads_kernel(
+    info, normed_ref, act_ref, grad_pre_ref, dy_ref, near_ref, far_ref, up_s, down_s
+):
+    line = info[5]
+    for z in range(act_ref.shape[0]):
+        up_s[...] = mm_tn(normed_ref[...], grad_pre_ref[z ^ line]).astype(BF16)
+        give_out(info, near_ref, far_ref, z, 0, up_s)
+        down_s[...] = mm_tn(act_ref[z ^ line], dy_ref[...]).astype(BF16)
+        give_out(info, near_ref, far_ref, z, 1, down_s)
 
 
 def attend_back_kernel(
@@ -371,7 +398,8 @@
     k_ref,
     v_ref,
     prob_ref,
-    weight_ref,
+    near_ref,
+    far_ref,
     own_ref,
     gain_ref,
     grad_hidden_ref,
@@ -387,11 +415,13 @@
     gk_s,
     gv_s,
     acc_s,
+    full_s,
 ):
     rows = own_ref.shape[0]
     pairs = q_ref.shape[0]
     tiles = 2 * rows // TILE
     length, own, partner = info[0], info[1], info[2]
+    assemble(info, near_ref, far_ref, full_s)
     pool_s[...] = pool_matrix(rows)
     spread_s[...] = spread_matrix(rows)
     live = (iota((rows, 1), 0) + own < length).astype(F32)
@@ -460,7 +490,7 @@
         b_qv_ref[p, 1:2, :] = jnp.sum(gv.astype(F32), axis=0, keepdims=True)
         grads = jnp.concatenate([gq, gk, gv], axis=1)
         grads_ref[p] = grads
-        acc_s[...] += mm_nt(grads, full_weight(weight_ref, p, slice(0, 3 * TILE)))
+        acc_s[...] += mm_nt(grads, full_s[p, :, : 3 * TILE])
         return carry
 
     lax.fori_loop(0, pairs, one_pair, 0)
@@ -473,17 +503,45 @@
     ).astype(BF16)
 
 
-def attend_grads_kernel(normed_ref, grads_ref, grad_hidden_ref, mixed_ref, out_ref):
-    pairs = grads_ref.shape[0]
-    inner, outer, _, chunk, _ = out_ref.shape
-    for z in range(pairs):
-        qkv = mm_tn(normed_ref[...], grads_ref[z]).astype(BF16)
-        back = mm_tn(grad_hidden_ref[...], mixed_ref[z]).astype(BF16)
-        both = jnp.concatenate([qkv, back], axis=1)
-        for o in range(outer):
-            for c in range(inner):
-                at = (o * inner + c) * chunk
-                out_ref[c, o, z] = both[at : at + chunk]
+def attend_grads_kernel(
+    info, normed_ref, grads_ref, grad_hidden_ref, mixed_ref, near_ref, far_ref, both_s
+):
+    line = info[5]
+    for z in range(grads_ref.shape[0]):
+        both_s[:, : 3 * TILE] = mm_tn(normed_ref[...], grads_ref[z ^ line]).astype(BF16)
+        both_s[:, 3 * TILE :] = mm_tn(grad_hidden_ref[...], mixed_ref[z ^ line]).astype(BF16)
+        give_out(info, near_ref, far_ref, z, 0, both_s)
+
+
+def place_grads_kernel(info, near_ref, far_ref, *outs):
+    core, plane = info[3], info[4]
+    chunk = near_ref.shape[-2]
+    for far, ref in enumerate((near_ref, far_ref)):
+        for o in range(ref.shape[0]):
+            at = ((o ^ plane) * 2 + (far ^ core)) * chunk
+            at = pl.ds(pl.multiple_of(at, chunk), chunk)
+            for part in range(ref.shape[1]):
+                piece = ref[o, part].astype(F32)
+                width = piece.shape[1] * ref.shape[1] // len(outs)
+                for n in range(piece.shape[1] // width):
+                    outs[part + n][at, :] = piece[:, n * width : (n + 1) * width]
+
+
+def place_line_kernel(info, *refs):
+    line = info[5]
+    out_ref = refs[-1]
+    for z, ref in enumerate(refs[:-1]):
+        out_ref[z ^ line] = ref[...]
+
+
+def place_dealt_kernel(info, *refs):
+    line = info[5]
+    out_ref = refs[-1]
+    for z, ref in enumerate(refs[:-1]):
+        for i in range(ref.shape[0]):
+            for a in range(ref.shape[1]):
+                for b in range(ref.shape[2]):
+                    out_ref[a, b, i, z ^ line] = ref[i, a, b]
 
 
 VMEM_SPEC = pl.BlockSpec(memory_space=pltpu.VMEM)
@@ -502,16 +560,17 @@
     )(*scalars, *args)
 
 
-def exchange(pieces, axis, groups=None):
-    return lax.all_to_all(pieces, axis, 0, 0, tiled=True, axis_index_groups=groups)
-
-
-def gather(piece, axis, count, groups=None):
-    return exchange(jnp.broadcast_to(piece[None], (count,) + piece.shape), axis, groups)
+def exchange(pieces, axis):
+    return lax.all_to_all(pieces, axis, 0, 0, tiled=True)
+
+
+def swap(piece, axis, distance):
+    size = lax.axis_size(axis)
+    return lax.ppermute(piece, axis, [(i, i ^ distance) for i in range(size)])
 
 
 def total_of(pieces):
-    return jnp.sum(pieces.astype(F32), axis=0).astype(BF16)
+    return functools.reduce(jnp.add, [piece.astype(F32) for piece in pieces]).astype(BF16)
 
 
 def local(
@@ -541,12 +600,19 @@
     d = lax.axis_index("dp")
     t = lax.axis_index("tensor")
     rows = seq_dev * length // nt
-    inner = 2
-    outer = dp // inner
-    pairs = [[inner * i + c for c in range(inner)] for i in range(outer)]
-    planes = [[inner * i + c for i in range(outer)] for c in range(inner)]
+    outer = dp // 2
     chunk = width // dp
     hid = w_up.shape[1]
+
+    def line_pieces(piece):
+        return [piece] + [swap(piece, "tensor", z) for z in range(1, nt)]
+
+    def plane_pieces(piece):
+        return [piece] + [swap(piece, "dp", 2 * o) for o in range(1, outer)]
+
+    def gathered(piece):
+        near = jnp.stack(plane_pieces(jnp.stack(line_pieces(piece))))
+        return near, swap(near, "dp", 1)
 
     def own_rows(weight):
         return lax.dynamic_slice_in_dim(weight, d * chunk, chunk, axis=0)
@@ -558,13 +624,9 @@
     ffn_piece = jnp.stack([own_rows(w_up), own_rows(w_down)])
     bias_piece = jnp.concatenate([b_query, b_value, b_up]).reshape(-1, TILE)
     bias_piece = jnp.pad(bias_piece, ((0, -bias_piece.shape[0] % 8), (0, 0)))
-    attn_w = gather(attn_piece, "tensor", nt)
-    biases = gather(bias_piece, "tensor", nt)
-    attn_w = gather(attn_w, "dp", outer, planes)
-    ffn_w = gather(ffn_piece, "tensor", nt)
-    attn_w = gather(attn_w, "dp", inner, pairs)
-    ffn_w = gather(ffn_w, "dp", outer, planes)
-    ffn_w = gather(ffn_w, "dp", inner, pairs)
+    attn_w = gathered(attn_piece)
+    biases = jnp.stack(line_pieces(bias_piece))
+    ffn_w = gathered(ffn_piece)
     b_qv = biases[:, 0:2]
     b_ups = biases[:, 2 : 2 + hid // TILE].reshape(nt, 1, hid)
 
@@ -574,9 +636,12 @@
     dy = lax.dynamic_index_in_dim(cotangent.reshape(nt, rows, width), t, 0, keepdims=False)
     own_length = lengths[d * seq_dev + t // 2]
     own_base = (t % 2) * rows
-    info = jnp.stack([own_length, own_base, rows - own_base]).astype(jnp.int32)
+    info = jnp.stack([own_length, own_base, rows - own_base, d % 2, d // 2, t]).astype(jnp.int32)
     row = lambda v: v.reshape(1, -1)
     top = rows >> level_shifts(rows)[-1]
+
+    attn_full = pltpu.VMEM((nt, width, 4 * TILE), BF16)
+    ffn_full = pltpu.VMEM((nt, 2, width, hid), BF16)
 
     normed_one, pooled = call(
         norm_one_kernel,
@@ -591,13 +656,14 @@
         + [((nt, 2 * rows, TILE), BF16)] * 3
         + [((nt, 2 * rows // TILE, TILE, 2 * TILE), BF16)],
         [info],
-        [normed_one, pooled, attn_w, b_qv],
+        [normed_one, pooled, *attn_w, b_qv],
         scratch=[
             pltpu.VMEM((rows, rows), BF16),
             pltpu.VMEM((rows, rows), BF16),
             pltpu.VMEM((2 * rows // TILE, 1, 2 * TILE), F32),
             pltpu.VMEM((2, TILE, 2 * TILE), F32),
             pltpu.VMEM((2 * rows, 2 * TILE), F32),
+            attn_full,
         ],
         flops=10**10,
     )
@@ -605,8 +671,10 @@
         feed_kernel,
         [((rows, width), BF16), ((rows, width), F32), ((rows, width), BF16)]
         + [((nt, rows, hid), BF16)] * 2,
-        [],
-        [own, mixed, attn_w, ffn_w, row(b_out), row(ln2_gain), row(ln2_bias), b_ups, row(b_down)],
+        [info],
+        [own, mixed, *attn_w, *ffn_w]
+        + [row(b_out), row(ln2_gain), row(ln2_bias), b_ups, row(b_down)],
+        scratch=[attn_full, ffn_full],
         flops=10**10,
     )
 
@@ -615,8 +683,14 @@
     dealt = exchange(out.reshape(n_all, piece, width), ("dp", "tensor"))
     dealt = jnp.take(dealt.reshape(dp * seq_dev, -1, piece, width), dealing, axis=0)
     dealt = exchange(dealt.reshape(dp, seq_dev, -1, piece, width), "dp")
-    dealt = gather(dealt, "tensor", nt)
-    output = dealt.transpose(2, 3, 1, 0, 4, 5).reshape(seq_dev, length, width)
+    (output,) = call(
+        place_dealt_kernel,
+        [((seq_dev, dealt.shape[2], dp, nt, piece, width), BF16)],
+        [info],
+        line_pieces(dealt),
+        limit=16,
+    )
+    output = output.reshape(seq_dev, length, width)
 
     grad_pre, grad_hidden, grad_hidden_low, numer, gtotal, sent, vec_two, vec_up = call(
         feed_back_kernel,
@@ -630,17 +704,19 @@
             ((4, width), F32),
             ((nt, 1, hid), F32),
         ],
-        [],
-        [dy, ffn_w, attn_w, slope, hidden, row(ln2_gain), mixed_wide, total],
+        [info],
+        [dy, *ffn_w, *attn_w, slope, hidden, row(ln2_gain), mixed_wide, total],
+        scratch=[attn_full, ffn_full],
         flops=10**10,
     )
-    swapped = lax.ppermute(sent, "tensor", [(i, i ^ 1) for i in range(nt)])
+    swapped = swap(sent, "tensor", 1)
     swapped = swapped.reshape(2 * top, nt, TILE).transpose(1, 0, 2)
-    (ffn_grads,) = call(
+    ffn_grads = call(
         feed_grads_kernel,
-        [((inner, outer, nt, 2, chunk, hid), BF16)],
-        [],
+        [((outer, nt, 2, chunk, hid), BF16)] * 2,
+        [info],
         [normed_two, act, grad_pre, dy],
+        scratch=[pltpu.VMEM((width, hid), BF16)] * 2,
         flops=10**10,
     )
     grad_low, qkv_grads, vec_one, vec_qv = call(
@@ -652,7 +728,7 @@
             ((nt, 2, TILE), F32),
         ],
         [info],
-        [numer, gtotal, swapped, q, k, v, prob, attn_w, own, row(ln1_gain), grad_hidden],
+        [numer, gtotal, swapped, q, k, v, prob, *attn_w, own, row(ln1_gain), grad_hidden],
         scratch=[
             pltpu.VMEM((rows, rows), BF16),
             pltpu.VMEM((rows, rows), BF16),
@@ -662,38 +738,60 @@
             pltpu.VMEM((2 * rows, TILE), F32),
             pltpu.VMEM((2 * rows, TILE), F32),
             pltpu.VMEM((rows, width), F32),
+            attn_full,
         ],
         flops=10**10,
     )
-    grad_tokens = gather(grad_low, "tensor", nt).reshape(seq_dev, length, width)
-    (attn_grads,) = call(
+    (grad_tokens,) = call(
+        place_line_kernel,
+        [((nt, rows, width), BF16)],
+        [info],
+        line_pieces(grad_low),
+        limit=16,
+    )
+    grad_tokens = grad_tokens.reshape(seq_dev, length, width)
+    attn_grads = call(
         attend_grads_kernel,
-        [((inner, outer, nt, chunk, 4 * TILE), BF16)],
-        [],
+        [((outer, nt, 1, chunk, 4 * TILE), BF16)] * 2,
+        [info],
         [normed_one, qkv_grads, grad_hidden_low, mixed],
+        scratch=[pltpu.VMEM((width, 4 * TILE), BF16)],
         flops=10**10,
     )
 
     def reduced(grads):
-        grads = total_of(exchange(grads, "dp", pairs))
-        grads = total_of(exchange(grads, "dp", planes))
-        grads = total_of(exchange(grads, "tensor"))
-        return gather(grads, "dp", dp)
-
-    ffn_grads = reduced(ffn_grads).astype(F32)
-    attn_grads = reduced(attn_grads).astype(F32)
-    g_up = ffn_grads[:, 0].reshape(width, hid)
-    g_down = ffn_grads[:, 1].reshape(hid, width)
-    attn_grads = attn_grads.reshape(width, 4 * TILE)
-    g_query = attn_grads[:, :TILE]
-    g_key = attn_grads[:, TILE : 2 * TILE]
-    g_value = attn_grads[:, 2 * TILE : 3 * TILE]
-    g_out = attn_grads[:, 3 * TILE :].T
+        near, far = grads
+        far = swap(far, "dp", 1)
+        pieces = [total_of([near[o], far[o]]) for o in range(outer)]
+        pieces = [pieces[0]] + [swap(pieces[o], "dp", 2 * o) for o in range(1, outer)]
+        pieces = [total_of([piece[z] for piece in pieces]) for z in range(nt)]
+        pieces = [pieces[0]] + [swap(pieces[z], "tensor", z) for z in range(1, nt)]
+        near = jnp.stack(plane_pieces(total_of(pieces)))
+        return near, swap(near, "dp", 1)
+
+    g_up, g_down = call(
+        place_grads_kernel,
+        [((width, hid), F32), ((hid, width), F32)],
+        [info],
+        reduced(ffn_grads),
+        limit=16,
+    )
+    g_query, g_key, g_value, g_out = call(
+        place_grads_kernel,
+        [((width, TILE), F32)] * 4,
+        [info],
+        reduced(attn_grads),
+        limit=16,
+    )
+    g_out = g_out.T
 
     vectors = jnp.concatenate(
         [vec_two, vec_up.reshape(nt, hid), vec_one, vec_qv.transpose(1, 0, 2).reshape(2, -1)]
     )
-    vectors = gather(vectors.astype(BF16), ("dp", "tensor"), n_all)
+    vectors = vectors.astype(BF16)
+    vectors = exchange(
+        jnp.broadcast_to(vectors[None], (n_all,) + vectors.shape), ("dp", "tensor")
+    )
     vectors = jnp.sum(vectors.astype(F32), axis=0)
     base = 4 + nt
     g_b_up = lax.dynamic_index_in_dim(vectors[4:base], t, 0, keepdims=False)

time: 446 us -> 332 us (0.74); the launches traced: 439 us -> 330 us
  blocking collectives: 84.2 us -> 0 us
  waiting for transfers between devices: 172 us -> 150 us
  local copies, waits for them, and re-layouts: 44 us -> 24.7 us
  Pallas kernels: 61.1 us -> 74.9 us
    all_to_all x13 -> x3, waiting for transfers between devices: 172 us -> 7.03 us  [exchange(): return lax.all_to_all(pieces, axis, 0, 0, tiled=True)]
    ppermute x1 -> x46, waiting for transfers between devices: 0.01 us -> 143 us  [swap(): return lax.ppermute(piece, axis, [(i, i ^ distance) for i in range(size)])]
    all_to_all x7 -> x0, blocking collectives: 84.2 us -> none  [exchange(): lax.all_to_all(pieces, axis, 0, 0, tiled=True, axis_index_groups=groups)]
    ppermute x1 -> x46, starting transfers between devices: 2.86 us -> 51.6 us  [swap(): return lax.ppermute(piece, axis, [(i, i ^ distance) for i in range(size)])]
    all_to_all x13 -> x3, starting transfers between devices: 59.3 us -> 11.6 us  [exchange(): return lax.all_to_all(pieces, axis, 0, 0, tiled=True)]
    pallas_call x7 -> x11, Pallas kernels: 61.1 us -> 74.9 us  [call(): pl.pallas_call(kernel, out_shape=[jax.ShapeDtypeStruct(shape, dtype) for...]
    broadcast_in_dim x12 -> x1, local copies, waits for them, and re-layouts: 12.5 us -> 0.85 us  [local(): jnp.broadcast_to(vectors[None], (n_all,) + vectors.shape)]
    reduce_sum x6 -> x0, other arithmetic: 9.45 us -> none  [total_of(): return jnp.sum(pieces.astype(F32), axis=0).astype(BF16)]
  transfers between devices with their start and end apart: 14 -> 49, of which waited for: 12 -> 22; matrix products, arithmetic and copies ran while one was open for 6% -> 8% of each run, Pallas kernels for 10% -> 16%
where the time goes in v2:
time: 332 us; the launch traced here: 330 us
  waiting for transfers between devices  150 us (45%)
  Pallas kernels  74.9 us (23%)
  starting transfers between devices  63.2 us (19%)
  local copies, waits for them, and re-layouts  24.7 us (7%)
  other arithmetic  16.3 us (5%)
    ppermute x46, waiting for transfers between devices, swap(): return lax.ppermute(piece, axis, [(i, i ^ distance) for i in range(size)])  143 us
    pallas_call x11, Pallas kernels, call(): pl.pallas_call(kernel, out_shape=[jax.ShapeDtypeStruct(shape, dtype) for...  74.9 us
    ppermute x46, starting transfers between devices, swap(): return lax.ppermute(piece, axis, [(i, i ^ distance) for i in range(size)])  51.6 us
    unnamed x61, local copies, waits for them, and re-layouts  12.1 us
    all_to_all x3, starting transfers between devices, exchange(): return lax.all_to_all(pieces, axis, 0, 0, tiled=True)  11.6 us
    convert_element_type x4, other arithmetic, total_of(): functools.reduce(jnp.add, [piece.astype(F32) for piece in pieces])  7.65 us
    all_to_all x3, waiting for transfers between devices, exchange(): return lax.all_to_all(pieces, axis, 0, 0, tiled=True)  7.03 us
  transfers between devices with their start and end apart: 49, of which 22 were waited for; matrix products, arithmetic and copies ran while one was open for 8% of the time, Pallas kernels for 16%

profile of v2, /device:TPU:8, one launch (start us, length us, event | category | flops | bytes accessed | tf_op | source)
XLA Modules:
  0.0 330.4 jit_solution(11668224886129126095)
XLA Ops:
  2.6 3.0 collective-permute-start.11
  8.3 6.7 %collective-permute-done.11 = bf16[2,64,512]{2,1,0:T(8,128)(2,1)S(1)} collective-permute-done((bf16[2,64,512]{2,1,0:T(8,128)(2,1)S(1)}, bf16[2,64,512]{2,1,0:T(8,128)(2,1)S(1)}, u32[]{:S(2)}, u32[]{:S(2)}) %collective-permute-start.11) | collective-permute-done | bytes 131104 | tf_op jit(solution)/shard_map/ppermute | solution.py:569
  15.0 2.5 collective-permute-done.12
  17.6 1.6 collective-permute-start.13
  20.0 1.6 collective-permute-start.14
  22.9 3.0 collective-permute-start.1
  27.1 2.0 collective-permute-start.2
  29.2 2.8 collective-permute-done.2
  32.1 1.6 collective-permute-start.3
  35.7 9.3 %collective-permute-done.14 = bf16[4,2,64,512]{3,2,1,0:T(8,128)(2,1)S(1)} collective-permute-done((bf16[4,2,64,512]{3,2,1,0:T(8,128)(2,1)S(1)}, bf16[4,2,64,512]{3,2,1,0:T(8,128)(2,1)S(1)}, u32[]{:S(2)}, u32[]{:S(2)}) %collective-permute-start.14) | collective-permute-done | bytes 524320 | tf_op jit(solution)/shard_map/ppermute | solution.py:569
  44.9 2.6 pad_maximum_fusion.ffn_near_ref
  47.6 1.8 collective-permute-done.3
  49.4 5.0 %collective-permute-done.4 = bf16[4,64,512]{2,1,0:T(8,128)(2,1)S(1)} collective-permute-done((bf16[4,64,512]{2,1,0:T(8,128)(2,1)S(1)}, bf16[4,64,512]{2,1,0:T(8,128)(2,1)S(1)}, u32[]{:S(2)}, u32[]{:S(2)}) %collective-permute-start.4) | collective-permute-done | bytes 262176 | tf_op jit(solution)/shard_map/ppermute | solution.py:569
  55.7 3.5 %collective-permute-start.8 = (f32[8,128]{1,0:T(8,128)S(1)}, f32[8,128]{1,0:T(8,128)S(1)}, u32[]{:S(2)}, u32[]{:S(2)}) collective-permute-start(f32[8,128]{1,0:T(8,128)S(1)} %get-tuple-element.207), channel_id=1, source_target_pairs={{0,2},{1,3},{2,0},{3,1},{4,6},{5,7},{6,4},{7,5},{8,10},{9,11},{10,... | collective-permute-start | bytes 12296 | tf_op jit(solution)/shard_map/ppermute | solution.py:569
  64.1 14.3 %shard_map.315 = (bf16[4,512,128]{2,1,0:T(8,128)(2,1)S(1)}, f32[4,512,128]{2,1,0:T(8,128)S(1)}, f32[4,512,128]{2,1,0:T(8,128)S(1)}, bf16[4,1024,128]{2,1,0:T(8,1...) custom-call(s32[6]{0:T(128)S(1)} %stack.137.info, ...), custom_call_target="tpu_custom_call" | custom-call | flops 10000000000 | bytes 8388608 | tf_op jit(solution)/shard_map/pallas_call | solution.py:552
  80.5 9.6 %shard_map.316 = (bf16[512,512]{1,0:T(8,128)(2,1)S(1)}, f32[512,512]{1,0:T(8,128)S(1)}, bf16[512,512]{1,0:T(8,128)(2,1)S(1)}, bf16[4,512,512]{2,1,0:T(8,128)(2,1)}, bf16[4,512,512]{2,1,0:T(8,128)(2,1)}) custom-call(s32[6]{0:T(128)S(1)} %stack.137.info, bf16[512,512]{1,0:T(8,128)(2,1)S(1)} %get-tuple-element.186.own_ref, ...), custom_call_target="tpu_custom_call" | custom-call | flops 10000000000 | bytes 8388608 | tf_op jit(solution)/shard_map/pallas_call | solution.py:552
  91.9 9.2 %shard_map.318 = (bf16[4,512,512]{2,1,0:T(8,128)(2,1)}, f32[512,512]{1,0:T(8,128)S(1)}, bf16[512,512]{1,0:T(8,128)(2,1)S(1)}, f32[4,512,128]{2,1,0:T(8,128)S(1)}...) custom-call(s32[6]{0:T(128)S(1)} %stack.137.info, ...), custom_call_target="tpu_custom_call" | custom-call | flops 10000000000 | bytes 8388608 | tf_op jit(solution)/shard_map/pallas_call | solution.py:552
  103.6 6.0 %shard_map.323 = (bf16[4,4,2,64,512]{4,3,2,1,0:T(8,128)(2,1)S(1)}, bf16[4,4,2,64,512]{4,3,2,1,0:T(8,128)(2,1)}) custom-call(s32[6]{0:T(128)S(1)} %stack.137.info, bf16[512,512]{1,0:T(8,128)(2,1)S(1)} %get-tuple-element.82.normed_ref, bf16[4,512,512]{2,1,0:T(8,128)(2,1)} %get-tuple-element.83.act_ref, bf16[4,512,512]{2,1,0:T(8,128)(2,1)} %get-tuple-element.84.grad_pre_ref, ...), custom_call_target="tpu_custom_call" | custom-call | flops 10000000000 | bytes 8388608 | tf_op jit(solution)/shard_map/pallas_call | solution.py:552
  109.6 21.3 %shard_map.319 = (bf16[512,512]{1,0:T(8,128)(2,1)S(1)}, bf16[4,512,384]{2,1,0:T(8,128)(2,1)}, f32[2,512]{1,0:T(2,128)S(1)}, f32[4,2,128]{2,1,0:T(2,128)S(1)}) custom-call(s32[6]{0:T(128)S(1)} %stack.137.info, f32[4,512,128]{2,1,0:T(8,128)S(1)} %get-tuple-element.61.numer_ref, f32[4,512,128]{2,1,0:T(8,128)S(1)} %get-tuple-element.62.gtotal_ref, ...), custom_call_target="tpu_custom_call" | custom-call | flops 10000000000 | bytes 8388608 | tf_op jit(solution)/shard_map/pallas_call | solution.py:552
  132.6 4.7 %all-to-all-start.2 = ((bf16[32,12,512]{2,1,0:T(8,128)(2,1)}), bf16[32,12,512]{2,1,0:T(8,128)(2,1)}, u32[]{:S(2)}, u32[]{:S(2)}) async-start(bf16[32,12,512]{2,1,0:T(8,128)(2,1)} %broadcast_in_dim.24), calls=%async_computation.2 | async-start | bytes 1048576 | tf_op jit(solution)/shard_map/all_to_all | solution.py:564
  141.9 3.5 %shard_map.321 = (bf16[4,4,1,64,512]{4,3,2,1,0:T(8,128)(2,1)S(1)}, bf16[4,4,1,64,512]{4,3,2,1,0:T(8,128)(2,1)}) custom-call(s32[6]{0:T(128)S(1)} %stack.137.info, bf16[512,512]{1,0:T(8,128)(2,1)S(1)} %copy-done.9, bf16[4,512,384]{2,1,0:T(8,128)(2,1)S(1)} %copy-done.14, bf16[512,512]{1,0:T(8,128)(2,1)S(1)} %copy-done.20, bf16[4,512,128]{2,1,0:T(8,128)(2,1)S(1)} %copy-done.22), custom_call_target="tpu_custom_call" | custom-call | flops 10000000000 | bytes 8388608 | tf_op jit(solution)/shard_map/pallas_call | solution.py:552
  145.5 7.0 %all-to-all-done.2 = bf16[32,12,512]{2,1,0:T(8,128)(2,1)} async-done(((bf16[32,12,512]{2,1,0:T(8,128)(2,1)}), bf16[32,12,512]{2,1,0:T(8,128)(2,1)}, u32[]{:S(2)}, u32[]{:S(2)}) %all-to-all-start.2) | async-done | bytes 393248 | tf_op jit(solution)/shard_map/all_to_all | solution.py:564
  152.5 3.4 %all-to-all-start = ((bf16[32,16,512]{2,1,0:T(8,128)(2,1)}), bf16[32,16,512]{2,1,0:T(8,128)(2,1)}, u32[]{:S(2)}, u32[]{:S(2)}) async-start(bf16[32,16,512]{2,1,0:T(8,128)(2,1)} %bitcast.174), calls=%async_computation | async-start | bytes 1048576 | tf_op jit(solution)/shard_map/all_to_all | solution.py:564
  156.3 2.6 collective-permute-start.22
  159.5 3.4 %add_convert_fusion.3 = (bf16[1,4,2,64,512]{4,3,2,1,0:T(8,128)(2,1)}, bf16[4,2,64,512]{3,2,1,0:T(8,128)(2,1)}, bf16[4,2,64,512]{3,2,1,0:T(8,128)(2,1)}, bf16[4,2,64,512]{3,2,1,0:T(8,128)(2,1)}) fusion(bf16[4,4,2,64,512]{4,3,2,1,0:T(8,128)(2,1)} %collective-permute-done.35, bf16[4,4,2,64,512]{4,3,2,1,0:T(8,128)(2,1)S(1)} %get-tuple-element.85), kind=kLoop, calls=%fused_computation.6 | loop fusion | flops 4194304 | bytes 6291456 | tf_op jit(solution)/shard_map/convert_element_type | solution.py:573
  164.4 21.3 %collective-permute-done.21.refs_1_ = bf16[512,512]{1,0:T(8,128)(2,1)} collective-permute-done((bf16[512,512]{1,0:T(8,128)(2,1)}, bf16[512,512]{1,0:T(8,128)(2,1)}, u32[]{:S(2)}, u32[]{:S(2)}) %collective-permute-start.21) | collective-permute-done | bytes 524320 | tf_op jit(solution)/shard_map/ppermute | solution.py:569
  185.7 15.9 %collective-permute-done.22.refs_2_ = bf16[512,512]{1,0:T(8,128)(2,1)} collective-permute-done((bf16[512,512]{1,0:T(8,128)(2,1)}, bf16[512,512]{1,0:T(8,128)(2,1)}, u32[]{:S(2)}, u32[]{:S(2)}) %collective-permute-start.22) | collective-permute-done | bytes 524320 | tf_op jit(solution)/shard_map/ppermute | solution.py:569
  201.7 13.0 %collective-permute-done.23.refs_3_ = bf16[512,512]{1,0:T(8,128)(2,1)} collective-permute-done((bf16[512,512]{1,0:T(8,128)(2,1)}, bf16[512,512]{1,0:T(8,128)(2,1)}, u32[]{:S(2)}, u32[]{:S(2)}) %collective-permute-start.23) | collective-permute-done | bytes 524320 | tf_op jit(solution)/shard_map/ppermute | solution.py:569
  215.7 2.8 shard_map.320
  222.8 1.6 gather_fusion
  224.4 2.3 add_convert_fusion.7
  231.1 3.5 %all-to-all-start.1 = ((bf16[8,2,2,16,512]{4,3,2,1,0:T(8,128)(2,1)}), bf16[8,2,2,16,512]{4,3,2,1,0:T(8,128)(2,1)S(1)}, u32[]{:S(2)}, u32[]{:S(2)}) async-start(bf16[8,2,2,16,512]{4,3,2,1,0:T(8,128)(2,1)} %broadcast_select_fusion), calls=%async_computation.1 | async-start | bytes 1048576 | tf_op jit(solution)/shard_map/all_to_all | solution.py:564
  234.6 18.7 %collective-permute-done.37 = bf16[4,2,64,512]{3,2,1,0:T(8,128)(2,1)S(1)} collective-permute-done((bf16[4,2,64,512]{3,2,1,0:T(8,128)(2,1)}, bf16[4,2,64,512]{3,2,1,0:T(8,128)(2,1)S(1)}, u32[]{:S(2)}, u32[]{:S(2)}) %collective-permute-start.37) | collective-permute-done | bytes 524320 | tf_op jit(solution)/shard_map/ppermute | solution.py:569
  254.8 1.9 collective-permute-start.40
  256.7 1.5 collective-permute-start.41
  260.3 1.6 collective-permute-start.29
  261.9 1.5 collective-permute-start.30
  263.5 2.0 collective-permute-done.40
  265.4 4.6 %collective-permute-done.41 = bf16[2,64,512]{2,1,0:T(8,128)(2,1)S(1)} collective-permute-done((bf16[2,64,512]{2,1,0:T(8,128)(2,1)S(1)}, bf16[2,64,512]{2,1,0:T(8,128)(2,1)S(1)}, u32[]{:S(2)}, u32[]{:S(2)}) %collective-permute-start.41) | collective-permute-done | bytes 131104 | tf_op jit(solution)/shard_map/ppermute | solution.py:569
  271.2 2.1 collective-permute-start.42
  273.3 2.2 collective-permute-start.43
  277.9 2.0 collective-permute-start.32
  281.7 1.8 collective-permute-start.18
  289.4 6.7 %collective-permute-done.17.refs_1_ = bf16[8,2,2,16,512]{4,3,2,1,0:T(8,128)(2,1)} collective-permute-done((bf16[8,2,2,16,512]{4,3,2,1,0:T(8,128)(2,1)S(1)}, bf16[8,2,2,16,512]{4,3,2,1,0:T(8,128)(2,1)}, u32[]{:S(2)}, u32[]{:S(2)}) %collective-permute-start.17) | collective-permute-done | bytes 524320 | tf_op jit(solution)/shard_map/ppermute | solution.py:569
  296.0 21.5 %collective-permute-done.18.refs_2_ = bf16[8,2,2,16,512]{4,3,2,1,0:T(8,128)(2,1)} collective-permute-done((bf16[8,2,2,16,512]{4,3,2,1,0:T(8,128)(2,1)S(1)}, bf16[8,2,2,16,512]{4,3,2,1,0:T(8,128)(2,1)}, u32[]{:S(2)}, u32[]{:S(2)}) %collective-permute-start.18) | collective-permute-done | bytes 524320 | tf_op jit(solution)/shard_map/ppermute | solution.py:569
  317.6 7.5 %collective-permute-done.19.refs_3_ = bf16[8,2,2,16,512]{4,3,2,1,0:T(8,128)(2,1)} collective-permute-done((bf16[8,2,2,16,512]{4,3,2,1,0:T(8,128)(2,1)S(1)}, bf16[8,2,2,16,512]{4,3,2,1,0:T(8,128)(2,1)}, u32[]{:S(2)}, u32[]{:S(2)}) %collective-permute-start.19) | collective-permute-done | bytes 524320 | tf_op jit(solution)/shard_map/ppermute | solution.py:569
  325.0 2.8 shard_map.317
  327.8 2.5 shard_map.324
  (168 shorter events, 55.7 us)
Async XLA Ops:
  2.5 5.8 %collective-permute-start.10 = (bf16[2,64,512]{2,1,0:T(8,128)(2,1)S(1)}, bf16[2,64,512]{2,1,0:T(8,128)(2,1)S(1)}, u32[]{:S(2)}, u32[]{:S(2)}) collective-permute-start(bf16[2,64,512]{2,1,0:T(8,128)(2,1)S(1)} %get-tuple-element.195), channel_id=1, source_target_pairs={{0,1},{1,0},{2,3},{3,2},{4,5},{5,4},{6,7},{7,6},{8,9},{9,8},{10,11... | collective-permute-start | bytes 393224 | tf_op jit(solution)/shard_map/ppermute | solution.py:569
  2.6 12.4 %collective-permute-start.11 = (bf16[2,64,512]{2,1,0:T(8,128)(2,1)S(1)}, bf16[2,64,512]{2,1,0:T(8,128)(2,1)S(1)}, u32[]{:S(2)}, u32[]{:S(2)}) collective-permute-start(bf16[2,64,512]{2,1,0:T(8,128)(2,1)S(1)} %get-tuple-element.195), channel_id=1, source_target_pairs={{0,2},{1,3},{2,0},{3,1},{4,6},{5,7},{6,4},{7,5},{8,10},{9,11},{10,... | collective-permute-start | bytes 393224 | tf_op jit(solution)/shard_map/ppermute | solution.py:569
  5.6 11.9 %collective-permute-start.12 = (bf16[2,64,512]{2,1,0:T(8,128)(2,1)S(1)}, bf16[2,64,512]{2,1,0:T(8,128)(2,1)S(1)}, u32[]{:S(2)}, u32[]{:S(2)}) collective-permute-start(bf16[2,64,512]{2,1,0:T(8,128)(2,1)S(1)} %get-tuple-element.195), channel_id=1, source_target_pairs={{0,3},{1,2},{2,1},{3,0},{4,7},{5,6},{6,5},{7,4},{8,11},{9,10},{10,... | collective-permute-start | bytes 393224 | tf_op jit(solution)/shard_map/ppermute | solution.py:569
  17.6 17.6 %collective-permute-start.13 = (bf16[4,2,64,512]{3,2,1,0:T(8,128)(2,1)S(1)}, bf16[4,2,64,512]{3,2,1,0:T(8,128)(2,1)}, u32[]{:S(2)}, u32[]{:S(2)}) collective-permute-start(bf16[4,2,64,512]{3,2,1,0:T(8,128)(2,1)S(1)} %get-tuple-element.191), channel_id=1, source_target_pairs={{0,8},{4,12},{8,0},{12,4},{16,24},{20,28},{24,16},{28,20},{1,9},{5... | collective-permute-start | bytes 1572872 | tf_op jit(solution)/shard_map/ppermute | solution.py:569
  20.0 25.0 %collective-permute-start.14 = (bf16[4,2,64,512]{3,2,1,0:T(8,128)(2,1)S(1)}, bf16[4,2,64,512]{3,2,1,0:T(8,128)(2,1)S(1)}, u32[]{:S(2)}, u32[]{:S(2)}) collective-permute-start(bf16[4,2,64,512]{3,2,1,0:T(8,128)(2,1)S(1)} %get-tuple-element.191), channel_id=1, source_target_pairs={{0,16},{4,20},{8,24},{12,28},{16,0},{20,4},{24,8},{28,12},{1,17},{... | collective-permute-start | bytes 1572872 | tf_op jit(solution)/shard_map/ppermute | solution.py:569
  21.5 23.4 %collective-permute-start.15 = (bf16[4,2,64,512]{3,2,1,0:T(8,128)(2,1)S(1)}, bf16[4,2,64,512]{3,2,1,0:T(8,128)(2,1)S(1)}, u32[]{:S(2)}, u32[]{:S(2)}) collective-permute-start(bf16[4,2,64,512]{3,2,1,0:T(8,128)(2,1)S(1)} %get-tuple-element.191), channel_id=1, source_target_pairs={{0,24},{4,28},{8,16},{12,20},{16,8},{20,12},{24,0},{28,4},{1,25},{... | collective-permute-start | bytes 1572872 | tf_op jit(solution)/shard_map/ppermute | solution.py:569
  22.8 4.3 %collective-permute-start = (bf16[64,512]{1,0:T(8,128)(2,1)S(1)}, bf16[64,512]{1,0:T(8,128)(2,1)S(1)}, u32[]{:S(2)}, u32[]{:S(2)}) collective-permute-start(bf16[64,512]{1,0:T(8,128)(2,1)S(1)} %get-tuple-element.197), channel_id=1, source_target_pairs={{0,1},{1,0},{2,3},{3,2},{4,5},{5,4},{6,7},{7,6},{8,9},{9,8},{10,11... | collective-permute-start | bytes 196616 | tf_op jit(solution)/shard_map/ppermute | solution.py:569
  22.9 6.3 %collective-permute-start.1 = (bf16[64,512]{1,0:T(8,128)(2,1)S(1)}, bf16[64,512]{1,0:T(8,128)(2,1)S(1)}, u32[]{:S(2)}, u32[]{:S(2)}) collective-permute-start(bf16[64,512]{1,0:T(8,128)(2,1)S(1)} %get-tuple-element.197), channel_id=1, source_target_pairs={{0,2},{1,3},{2,0},{3,1},{4,6},{5,7},{6,4},{7,5},{8,10},{9,11},{10,... | collective-permute-start | bytes 196616 | tf_op jit(solution)/shard_map/ppermute | solution.py:569
  27.1 5.0 %collective-permute-start.2 = (bf16[64,512]{1,0:T(8,128)(2,1)S(1)}, bf16[64,512]{1,0:T(8,128)(2,1)S(1)}, u32[]{:S(2)}, u32[]{:S(2)}) collective-permute-start(bf16[64,512]{1,0:T(8,128)(2,1)S(1)} %get-tuple-element.197), channel_id=1, source_target_pairs={{0,3},{1,2},{2,1},{3,0},{4,7},{5,6},{6,5},{7,4},{8,11},{9,10},{10,... | collective-permute-start | bytes 196616 | tf_op jit(solution)/shard_map/ppermute | solution.py:569
  32.1 17.3 %collective-permute-start.3 = (bf16[4,64,512]{2,1,0:T(8,128)(2,1)S(1)}, bf16[4,64,512]{2,1,0:T(8,128)(2,1)S(1)}, u32[]{:S(2)}, u32[]{:S(2)}) collective-permute-start(bf16[4,64,512]{2,1,0:T(8,128)(2,1)S(1)} %get-tuple-element.193), channel_id=1, source_target_pairs={{0,8},{4,12},{8,0},{12,4},{16,24},{20,28},{24,16},{28,20},{1,9},{5... | collective-permute-start | bytes 786440 | tf_op jit(solution)/shard_map/ppermute | solution.py:569
  33.7 20.8 %collective-permute-start.4 = (bf16[4,64,512]{2,1,0:T(8,128)(2,1)S(1)}, bf16[4,64,512]{2,1,0:T(8,128)(2,1)S(1)}, u32[]{:S(2)}, u32[]{:S(2)}) collective-permute-start(bf16[4,64,512]{2,1,0:T(8,128)(2,1)S(1)} %get-tuple-element.193), channel_id=1, source_target_pairs={{0,16},{4,20},{8,24},{12,28},{16,0},{20,4},{24,8},{28,12},{1,17},{... | collective-permute-start | bytes 786440 | tf_op jit(solution)/shard_map/ppermute | solution.py:569
  35.2 19.3 %collective-permute-start.5 = (bf16[4,64,512]{2,1,0:T(8,128)(2,1)S(1)}, bf16[4,64,512]{2,1,0:T(8,128)(2,1)S(1)}, u32[]{:S(2)}, u32[]{:S(2)}) collective-permute-start(bf16[4,64,512]{2,1,0:T(8,128)(2,1)S(1)} %get-tuple-element.193), channel_id=1, source_target_pairs={{0,24},{4,28},{8,16},{12,20},{16,8},{20,12},{24,0},{28,4},{1,25},{... | collective-permute-start | bytes 786440 | tf_op jit(solution)/shard_map/ppermute | solution.py:569
  47.6 32.9 %collective-permute-start.16 = (bf16[4,4,2,64,512]{4,3,2,1,0:T(8,128)(2,1)}, bf16[4,4,2,64,512]{4,3,2,1,0:T(8,128)(2,1)}, u32[]{:S(2)}, u32[]{:S(2)}) collective-permute-start(bf16[4,4,2,64,512]{4,3,2,1,0:T(8,128)(2,1)} %pad_maximum_fusion.ffn_near_ref), channel_id=1, source_target_pairs={{0,4},{4,0},{8,12},{12,8},{16,20},{20,16},{24,28},{28,24},{1,5},{5... | collective-permute-start | bytes 6291464 | tf_op jit(solution)/shard_map/ppermute | solution.py:569
  55.6 8.5 %collective-permute-start.6 = (bf16[4,4,64,512]{3,2,1,0:T(8,128)(2,1)}, bf16[4,4,64,512]{3,2,1,0:T(8,128)(2,1)}, u32[]{:S(2)}, u32[]{:S(2)}) collective-permute-start(bf16[4,4,64,512]{3,2,1,0:T(8,128)(2,1)} %pad_maximum_fusion.1.near_ref), channel_id=1, source_target_pairs={{0,4},{4,0},{8,12},{12,8},{16,20},{20,16},{24,28},{28,24},{1,5},{5... | collective-permute-start | bytes 3145736 | tf_op jit(solution)/shard_map/ppermute | solution.py:569
  55.6 8.4 %collective-permute-start.7 = (f32[8,128]{1,0:T(8,128)S(1)}, f32[8,128]{1,0:T(8,128)S(1)}, u32[]{:S(2)}, u32[]{:S(2)}) collective-permute-start(f32[8,128]{1,0:T(8,128)S(1)} %get-tuple-element.207), channel_id=1, source_target_pairs={{0,1},{1,0},{2,3},{3,2},{4,5},{5,4},{6,7},{7,6},{8,9},{9,8},{10,11... | collective-permute-start | bytes 12296 | tf_op jit(solution)/shard_map/ppermute | solution.py:569
  55.7 8.3 %collective-permute-start.8 = (f32[8,128]{1,0:T(8,128)S(1)}, f32[8,128]{1,0:T(8,128)S(1)}, u32[]{:S(2)}, u32[]{:S(2)}) collective-permute-start(f32[8,128]{1,0:T(8,128)S(1)} %get-tuple-element.207), channel_id=1, source_target_pairs={{0,2},{1,3},{2,0},{3,1},{4,6},{5,7},{6,4},{7,5},{8,10},{9,11},{10,... | collective-permute-start | bytes 12296 | tf_op jit(solution)/shard_map/ppermute | solution.py:569
  59.2 4.8 %collective-permute-start.9 = (f32[8,128]{1,0:T(8,128)S(1)}, f32[8,128]{1,0:T(8,128)S(1)}, u32[]{:S(2)}, u32[]{:S(2)}) collective-permute-start(f32[8,128]{1,0:T(8,128)S(1)} %get-tuple-element.207), channel_id=1, source_target_pairs={{0,3},{1,2},{2,1},{3,0},{4,7},{5,6},{6,5},{7,4},{8,11},{9,10},{10,... | collective-permute-start | bytes 12296 | tf_op jit(solution)/shard_map/ppermute | solution.py:569
  102.1 7.5 %collective-permute-start.20 = (f32[32,512]{1,0:T(8,128)S(1)}, f32[32,512]{1,0:T(8,128)S(1)}, u32[]{:S(2)}, u32[]{:S(2)}) collective-permute-start(f32[32,512]{1,0:T(8,128)S(1)} %get-tuple-element.63), channel_id=1, source_target_pairs={{0,1},{1,0},{2,3},{3,2},{4,5},{5,4},{6,7},{7,6},{8,9},{9,8},{10,11... | collective-permute-start | bytes 196616 | tf_op jit(solution)/shard_map/ppermute | solution.py:569
  109.5 49.9 %collective-permute-start.35 = (bf16[4,4,2,64,512]{4,3,2,1,0:T(8,128)(2,1)}, bf16[4,4,2,64,512]{4,3,2,1,0:T(8,128)(2,1)}, u32[]{:S(2)}, u32[]{:S(2)}) collective-permute-start(bf16[4,4,2,64,512]{4,3,2,1,0:T(8,128)(2,1)} %get-tuple-element.86), channel_id=1, source_target_pairs={{0,4},{4,0},{8,12},{12,8},{16,20},{20,16},{24,28},{28,24},{1,5},{5... | collective-permute-start | bytes 6291464 | tf_op jit(solution)/shard_map/ppermute | solution.py:569
  132.6 19.9 %all-to-all-start.2 = ((bf16[32,12,512]{2,1,0:T(8,128)(2,1)}), bf16[32,12,512]{2,1,0:T(8,128)(2,1)}, u32[]{:S(2)}, u32[]{:S(2)}) async-start(bf16[32,12,512]{2,1,0:T(8,128)(2,1)} %broadcast_in_dim.24), calls=%async_computation.2 | async-start | bytes 1048576 | tf_op jit(solution)/shard_map/all_to_all | solution.py:564
  145.4 79.1 %collective-permute-start.24 = (bf16[4,4,1,64,512]{4,3,2,1,0:T(8,128)(2,1)}, bf16[4,4,1,64,512]{4,3,2,1,0:T(8,128)(2,1)}, u32[]{:S(2)}, u32[]{:S(2)}) collective-permute-start(bf16[4,4,1,64,512]{4,3,2,1,0:T(8,128)(2,1)} %get-tuple-element.77), channel_id=1, source_target_pairs={{0,4},{4,0},{8,12},{12,8},{16,20},{20,16},{24,28},{28,24},{1,5},{5... | collective-permute-start | bytes 3145736 | tf_op jit(solution)/shard_map/ppermute | solution.py:569
  152.5 70.2 %all-to-all-start = ((bf16[32,16,512]{2,1,0:T(8,128)(2,1)}), bf16[32,16,512]{2,1,0:T(8,128)(2,1)}, u32[]{:S(2)}, u32[]{:S(2)}) async-start(bf16[32,16,512]{2,1,0:T(8,128)(2,1)} %bitcast.174), calls=%async_computation | async-start | bytes 1048576 | tf_op jit(solution)/shard_map/all_to_all | solution.py:564
  155.9 29.8 %collective-permute-start.21 = (bf16[512,512]{1,0:T(8,128)(2,1)}, bf16[512,512]{1,0:T(8,128)(2,1)}, u32[]{:S(2)}, u32[]{:S(2)}) collective-permute-start(bf16[512,512]{1,0:T(8,128)(2,1)} %copy-done.2), channel_id=1, source_target_pairs={{0,1},{1,0},{2,3},{3,2},{4,5},{5,4},{6,7},{7,6},{8,9},{9,8},{10,11... | collective-permute-start | bytes 1572872 | tf_op jit(solution)/shard_map/ppermute | solution.py:569
  156.3 45.4 %collective-permute-start.22 = (bf16[512,512]{1,0:T(8,128)(2,1)}, bf16[512,512]{1,0:T(8,128)(2,1)}, u32[]{:S(2)}, u32[]{:S(2)}) collective-permute-start(bf16[512,512]{1,0:T(8,128)(2,1)} %copy-done.2), channel_id=1, source_target_pairs={{0,2},{1,3},{2,0},{3,1},{4,6},{5,7},{6,4},{7,5},{8,10},{9,11},{10,... | collective-permute-start | bytes 1572872 | tf_op jit(solution)/shard_map/ppermute | solution.py:569
  158.9 55.8 %collective-permute-start.23 = (bf16[512,512]{1,0:T(8,128)(2,1)}, bf16[512,512]{1,0:T(8,128)(2,1)}, u32[]{:S(2)}, u32[]{:S(2)}) collective-permute-start(bf16[512,512]{1,0:T(8,128)(2,1)} %copy-done.2), channel_id=1, source_target_pairs={{0,3},{1,2},{2,1},{3,0},{4,7},{5,6},{6,5},{7,4},{8,11},{9,10},{10,... | collective-permute-start | bytes 1572872 | tf_op jit(solution)/shard_map/ppermute | solution.py:569
  162.9 65.9 %collective-permute-start.36 = (bf16[4,2,64,512]{3,2,1,0:T(8,128)(2,1)}, bf16[4,2,64,512]{3,2,1,0:T(8,128)(2,1)}, u32[]{:S(2)}, u32[]{:S(2)}) collective-permute-start(bf16[4,2,64,512]{3,2,1,0:T(8,128)(2,1)} %get-tuple-element.177), channel_id=1, source_target_pairs={{0,8},{4,12},{8,0},{12,4},{16,24},{20,28},{24,16},{28,20},{1,9},{5... | collective-permute-start | bytes 1572872 | tf_op jit(solution)/shard_map/ppermute | solution.py:569
  218.6 34.7 %collective-permute-start.37 = (bf16[4,2,64,512]{3,2,1,0:T(8,128)(2,1)}, bf16[4,2,64,512]{3,2,1,0:T(8,128)(2,1)S(1)}, u32[]{:S(2)}, u32[]{:S(2)}) collective-permute-start(bf16[4,2,64,512]{3,2,1,0:T(8,128)(2,1)} %get-tuple-element.176), channel_id=1, source_target_pairs={{0,16},{4,20},{8,24},{12,28},{16,0},{20,4},{24,8},{28,12},{1,17},{... | collective-permute-start | bytes 1572872 | tf_op jit(solution)/shard_map/ppermute | solution.py:569
  220.0 33.2 %collective-permute-start.38 = (bf16[4,2,64,512]{3,2,1,0:T(8,128)(2,1)}, bf16[4,2,64,512]{3,2,1,0:T(8,128)(2,1)}, u32[]{:S(2)}, u32[]{:S(2)}) collective-permute-start(bf16[4,2,64,512]{3,2,1,0:T(8,128)(2,1)} %get-tuple-element.175), channel_id=1, source_target_pairs={{0,24},{4,28},{8,16},{12,20},{16,8},{20,12},{24,0},{28,4},{1,25},{... | collective-permute-start | bytes 1572872 | tf_op jit(solution)/shard_map/ppermute | solution.py:569
  226.7 30.0 %collective-permute-start.25 = (bf16[4,1,64,512]{3,2,1,0:T(8,128)(2,1)}, bf16[4,1,64,512]{3,2,1,0:T(8,128)(2,1)S(1)}, u32[]{:S(2)}, u32[]{:S(2)}) collective-permute-start(bf16[4,1,64,512]{3,2,1,0:T(8,128)(2,1)} %get-tuple-element.184), channel_id=1, source_target_pairs={{0,8},{4,12},{8,0},{12,4},{16,24},{20,28},{24,16},{28,20},{1,9},{5... | collective-permute-start | bytes 786440 | tf_op jit(solution)/shard_map/ppermute | solution.py:569
  227.3 31.6 %collective-permute-start.26 = (bf16[4,1,64,512]{3,2,1,0:T(8,128)(2,1)S(1)}, bf16[4,1,64,512]{3,2,1,0:T(8,128)(2,1)S(1)}, u32[]{:S(2)}, u32[]{:S(2)}) collective-permute-start(bf16[4,1,64,512]{3,2,1,0:T(8,128)(2,1)S(1)} %get-tuple-element.183), channel_id=1, source_target_pairs={{0,16},{4,20},{8,24},{12,28},{16,0},{20,4},{24,8},{28,12},{1,17},{... | collective-permute-start | bytes 786440 | tf_op jit(solution)/shard_map/ppermute | solution.py:569
  228.8 30.1 %collective-permute-start.27 = (bf16[4,1,64,512]{3,2,1,0:T(8,128)(2,1)S(1)}, bf16[4,1,64,512]{3,2,1,0:T(8,128)(2,1)}, u32[]{:S(2)}, u32[]{:S(2)}) collective-permute-start(bf16[4,1,64,512]{3,2,1,0:T(8,128)(2,1)S(1)} %get-tuple-element.182), channel_id=1, source_target_pairs={{0,24},{4,28},{8,16},{12,20},{16,8},{20,12},{24,0},{28,4},{1,25},{... | collective-permute-start | bytes 786440 | tf_op jit(solution)/shard_map/ppermute | solution.py:569
  231.1 49.9 %all-to-all-start.1 = ((bf16[8,2,2,16,512]{4,3,2,1,0:T(8,128)(2,1)}), bf16[8,2,2,16,512]{4,3,2,1,0:T(8,128)(2,1)S(1)}, u32[]{:S(2)}, u32[]{:S(2)}) async-start(bf16[8,2,2,16,512]{4,3,2,1,0:T(8,128)(2,1)} %broadcast_select_fusion), calls=%async_computation.1 | async-start | bytes 1048576 | tf_op jit(solution)/shard_map/all_to_all | solution.py:564
  254.7 7.2 %collective-permute-start.39 = (bf16[2,64,512]{2,1,0:T(8,128)(2,1)S(1)}, bf16[2,64,512]{2,1,0:T(8,128)(2,1)S(1)}, u32[]{:S(2)}, u32[]{:S(2)}) collective-permute-start(bf16[2,64,512]{2,1,0:T(8,128)(2,1)S(1)} %get-tuple-element.178), channel_id=1, source_target_pairs={{0,1},{1,0},{2,3},{3,2},{4,5},{5,4},{6,7},{7,6},{8,9},{9,8},{10,11... | collective-permute-start | bytes 393224 | tf_op jit(solution)/shard_map/ppermute | solution.py:569
  254.8 10.7 %collective-permute-start.40 = (bf16[2,64,512]{2,1,0:T(8,128)(2,1)S(1)}, bf16[2,64,512]{2,1,0:T(8,128)(2,1)S(1)}, u32[]{:S(2)}, u32[]{:S(2)}) collective-permute-start(bf16[2,64,512]{2,1,0:T(8,128)(2,1)S(1)} %get-tuple-element.180), channel_id=1, source_target_pairs={{0,2},{1,3},{2,0},{3,1},{4,6},{5,7},{6,4},{7,5},{8,10},{9,11},{10,... | collective-permute-start | bytes 393224 | tf_op jit(solution)/shard_map/ppermute | solution.py:569
  256.7 13.4 %collective-permute-start.41 = (bf16[2,64,512]{2,1,0:T(8,128)(2,1)S(1)}, bf16[2,64,512]{2,1,0:T(8,128)(2,1)S(1)}, u32[]{:S(2)}, u32[]{:S(2)}) collective-permute-start(bf16[2,64,512]{2,1,0:T(8,128)(2,1)S(1)} %get-tuple-element.179), channel_id=1, source_target_pairs={{0,3},{1,2},{2,1},{3,0},{4,7},{5,6},{6,5},{7,4},{8,11},{9,10},{10,... | collective-permute-start | bytes 393224 | tf_op jit(solution)/shard_map/ppermute | solution.py:569
  259.9 15.6 %collective-permute-start.28 = (bf16[1,64,512]{2,1,0:T(8,128)(2,1)S(1)}, bf16[1,64,512]{2,1,0:T(8,128)(2,1)S(1)}, u32[]{:S(2)}, u32[]{:S(2)}) collective-permute-start(bf16[1,64,512]{2,1,0:T(8,128)(2,1)S(1)} %get-tuple-element.187), channel_id=1, source_target_pairs={{0,1},{1,0},{2,3},{3,2},{4,5},{5,4},{6,7},{7,6},{8,9},{9,8},{10,11... | collective-permute-start | bytes 196616 | tf_op jit(solution)/shard_map/ppermute | solution.py:569
  260.3 15.2 %collective-permute-start.29 = (bf16[1,64,512]{2,1,0:T(8,128)(2,1)S(1)}, bf16[1,64,512]{2,1,0:T(8,128)(2,1)S(1)}, u32[]{:S(2)}, u32[]{:S(2)}) collective-permute-start(bf16[1,64,512]{2,1,0:T(8,128)(2,1)S(1)} %get-tuple-element.189), channel_id=1, source_target_pairs={{0,2},{1,3},{2,0},{3,1},{4,6},{5,7},{6,4},{7,5},{8,10},{9,11},{10,... | collective-permute-start | bytes 196616 | tf_op jit(solution)/shard_map/ppermute | solution.py:569
  261.9 13.6 %collective-permute-start.30 = (bf16[1,64,512]{2,1,0:T(8,128)(2,1)S(1)}, bf16[1,64,512]{2,1,0:T(8,128)(2,1)S(1)}, u32[]{:S(2)}, u32[]{:S(2)}) collective-permute-start(bf16[1,64,512]{2,1,0:T(8,128)(2,1)S(1)} %get-tuple-element.188), channel_id=1, source_target_pairs={{0,3},{1,2},{2,1},{3,0},{4,7},{5,6},{6,5},{7,4},{8,11},{9,10},{10,... | collective-permute-start | bytes 196616 | tf_op jit(solution)/shard_map/ppermute | solution.py:569
  271.2 8.8 %collective-permute-start.42 = (bf16[2,64,512]{2,1,0:T(8,128)(2,1)S(1)}, bf16[2,64,512]{2,1,0:T(8,128)(2,1)S(1)}, u32[]{:S(2)}, u32[]{:S(2)}) collective-permute-start(bf16[2,64,512]{2,1,0:T(8,128)(2,1)S(1)} %fusion.17), channel_id=1, source_target_pairs={{0,8},{4,12},{8,0},{12,4},{16,24},{20,28},{24,16},{28,20},{1,9},{5... | collective-permute-start | bytes 393224 | tf_op jit(solution)/shard_map/ppermute | solution.py:569
  273.3 7.8 %collective-permute-start.43 = (bf16[2,64,512]{2,1,0:T(8,128)(2,1)S(1)}, bf16[2,64,512]{2,1,0:T(8,128)(2,1)S(1)}, u32[]{:S(2)}, u32[]{:S(2)}) collective-permute-start(bf16[2,64,512]{2,1,0:T(8,128)(2,1)S(1)} %fusion.17), channel_id=1, source_target_pairs={{0,16},{4,20},{8,24},{12,28},{16,0},{20,4},{24,8},{28,12},{1,17},{... | collective-permute-start | bytes 393224 | tf_op jit(solution)/shard_map/ppermute | solution.py:569
  275.5 6.2 %collective-permute-start.44 = (bf16[2,64,512]{2,1,0:T(8,128)(2,1)S(1)}, bf16[2,64,512]{2,1,0:T(8,128)(2,1)S(1)}, u32[]{:S(2)}, u32[]{:S(2)}) collective-permute-start(bf16[2,64,512]{2,1,0:T(8,128)(2,1)S(1)} %fusion.17), channel_id=1, source_target_pairs={{0,24},{4,28},{8,16},{12,20},{16,8},{20,12},{24,0},{28,4},{1,25},{... | collective-permute-start | bytes 393224 | tf_op jit(solution)/shard_map/ppermute | solution.py:569
  276.4 7.2 %collective-permute-start.31 = (bf16[1,64,512]{2,1,0:T(8,128)(2,1)S(1)}, bf16[1,64,512]{2,1,0:T(8,128)(2,1)S(1)}, u32[]{:S(2)}, u32[]{:S(2)}) collective-permute-start(bf16[1,64,512]{2,1,0:T(8,128)(2,1)S(1)} %fusion.36), channel_id=1, source_target_pairs={{0,8},{4,12},{8,0},{12,4},{16,24},{20,28},{24,16},{28,20},{1,9},{5... | collective-permute-start | bytes 196616 | tf_op jit(solution)/shard_map/ppermute | solution.py:569
  277.9 6.8 %collective-permute-start.32 = (bf16[1,64,512]{2,1,0:T(8,128)(2,1)S(1)}, bf16[1,64,512]{2,1,0:T(8,128)(2,1)S(1)}, u32[]{:S(2)}, u32[]{:S(2)}) collective-permute-start(bf16[1,64,512]{2,1,0:T(8,128)(2,1)S(1)} %fusion.36), channel_id=1, source_target_pairs={{0,16},{4,20},{8,24},{12,28},{16,0},{20,4},{24,8},{28,12},{1,17},{... | collective-permute-start | bytes 196616 | tf_op jit(solution)/shard_map/ppermute | solution.py:569
  280.0 5.2 %collective-permute-start.33 = (bf16[1,64,512]{2,1,0:T(8,128)(2,1)S(1)}, bf16[1,64,512]{2,1,0:T(8,128)(2,1)S(1)}, u32[]{:S(2)}, u32[]{:S(2)}) collective-permute-start(bf16[1,64,512]{2,1,0:T(8,128)(2,1)S(1)} %fusion.36), channel_id=1, source_target_pairs={{0,24},{4,28},{8,16},{12,20},{16,8},{20,12},{24,0},{28,4},{1,25},{... | collective-permute-start | bytes 196616 | tf_op jit(solution)/shard_map/ppermute | solution.py:569
  281.1 15.0 %collective-permute-start.17 = (bf16[8,2,2,16,512]{4,3,2,1,0:T(8,128)(2,1)S(1)}, bf16[8,2,2,16,512]{4,3,2,1,0:T(8,128)(2,1)}, u32[]{:S(2)}, u32[]{:S(2)}) collective-permute-start(bf16[8,2,2,16,512]{4,3,2,1,0:T(8,128)(2,1)S(1)} %all-to-all-done.1.refs_0_), channel_id=1, source_target_pairs={{0,1},{1,0},{2,3},{3,2},{4,5},{5,4},{6,7},{7,6},{8,9},{9,8},{10,11... | collective-permute-start | bytes 1572872 | tf_op jit(solution)/shard_map/ppermute | solution.py:569
  281.7 35.9 %collective-permute-start.18 = (bf16[8,2,2,16,512]{4,3,2,1,0:T(8,128)(2,1)S(1)}, bf16[8,2,2,16,512]{4,3,2,1,0:T(8,128)(2,1)}, u32[]{:S(2)}, u32[]{:S(2)}) collective-permute-start(bf16[8,2,2,16,512]{4,3,2,1,0:T(8,128)(2,1)S(1)} %all-to-all-done.1.refs_0_), channel_id=1, source_target_pairs={{0,2},{1,3},{2,0},{3,1},{4,6},{5,7},{6,4},{7,5},{8,10},{9,11},{10,... | collective-permute-start | bytes 1572872 | tf_op jit(solution)/shard_map/ppermute | solution.py:569
  283.6 41.4 %collective-permute-start.19 = (bf16[8,2,2,16,512]{4,3,2,1,0:T(8,128)(2,1)S(1)}, bf16[8,2,2,16,512]{4,3,2,1,0:T(8,128)(2,1)}, u32[]{:S(2)}, u32[]{:S(2)}) collective-permute-start(bf16[8,2,2,16,512]{4,3,2,1,0:T(8,128)(2,1)S(1)} %all-to-all-done.1.refs_0_), channel_id=1, source_target_pairs={{0,3},{1,2},{2,1},{3,0},{4,7},{5,6},{6,5},{7,4},{8,11},{9,10},{10,... | collective-permute-start | bytes 1572872 | tf_op jit(solution)/shard_map/ppermute | solution.py:569
  284.7 43.1 %collective-permute-start.45 = (bf16[4,2,64,512]{3,2,1,0:T(8,128)(2,1)S(1)}, bf16[4,2,64,512]{3,2,1,0:T(8,128)(2,1)}, u32[]{:S(2)}, u32[]{:S(2)}) collective-permute-start(bf16[4,2,64,512]{3,2,1,0:T(8,128)(2,1)S(1)} %pad_maximum_fusion.3.near_ref), channel_id=1, source_target_pairs={{0,4},{4,0},{8,12},{12,8},{16,20},{20,16},{24,28},{28,24},{1,5},{5... | collective-permute-start | bytes 1572872 | tf_op jit(solution)/shard_map/ppermute | solution.py:569
  (30 other events, 310.1 us)

commit v3 on v2

v3 whole, which is shorter than its diff:
```python
import functools

import jax
import jax.numpy as jnp
from jax import lax
from jax.experimental import pallas as pl
from jax.experimental.pallas import tpu as pltpu
from jax.sharding import PartitionSpec as P

F32 = jnp.float32
BF16 = jnp.bfloat16
HEAD_SIZE = 64
BLOCK = 16
TILE = 128
EPS = 1e-05
INV_ROOT_TWO = 0.7071067811865476
INV_ROOT_TAU = 0.3989422804014327
SCALE = HEAD_SIZE ** (-0.5)


def mm(left, right):
    return lax.dot_general(left, right, (((1,), (0,)), ((), ())), preferred_element_type=F32)


def mm_nt(left, right):
    return lax.dot_general(left, right, (((1,), (1,)), ((), ())), preferred_element_type=F32)


def mm_tn(left, right):
    return lax.dot_general(left, right, (((0,), (0,)), ((), ())), preferred_element_type=F32)


def split_low(values):
    high = values.astype(BF16)
    return high, (values - high.astype(F32)).astype(BF16)


def mm_wide(left, values):
    high, low = split_low(values)
    return mm(left, high) + mm(left, low)


def iota(shape, axis):
    return lax.broadcasted_iota(jnp.int32, shape, axis)


def unit_rows(values):
    centred = values - jnp.mean(values, axis=-1, keepdims=True)
    inverse = lax.rsqrt(jnp.mean(centred * centred, axis=-1, keepdims=True) + EPS)
    return centred * inverse, inverse


def norm_back(grad, unit, inverse, gain):
    scaled = grad * gain
    return inverse * (
        scaled
        - jnp.mean(scaled, axis=-1, keepdims=True)
        - unit * jnp.mean(scaled * unit, axis=-1, keepdims=True)
    )


def level_shifts(rows):
    shifts = []
    shift = 1
    while (2 * rows) >> shift >= 2 * BLOCK:
        shifts.append(shift)
        shift += 1
    return shifts


def coarse_map(index, rows):
    shifts = level_shifts(rows)
    shift = jnp.zeros_like(index)
    start = jnp.zeros_like(index)
    offset = 0
    for s in shifts:
        here = index >= offset
        shift = jnp.where(here, s, shift)
        start = jnp.where(here, offset, start)
        offset += rows >> s
    other = index >= offset
    start = jnp.where(other, offset, start)
    return shift, index - start, other


def coarse_counts(index, rows, length, own, partner):
    shift, place, other = coarse_map(index, rows)
    base = jnp.where(other, partner, own)
    left = length - base - lax.shift_left(place, shift)
    return jnp.clip(left, 0, lax.shift_left(jnp.ones_like(shift), shift)).astype(F32), shift


def tile_map(index):
    shift = jnp.zeros_like(index)
    start = jnp.zeros_like(index)
    offset = 0
    for s in range(1, 6):
        here = index >= offset
        shift = jnp.where(here, s, shift)
        start = jnp.where(here, offset, start)
        offset += TILE >> s
    return shift, index - start, index >= offset - (TILE >> 5)


def pool_tile(odd):
    shift, place, last = tile_map(iota((TILE, TILE), 0))
    place = jnp.where(last, place - odd * (TILE >> 5), place)
    hit = lax.shift_right_logical(iota((TILE, TILE), 1), shift) == place
    return hit.astype(F32).astype(BF16)


def spread_tile(odd):
    shift, place, last = tile_map(iota((TILE, TILE), 1))
    place = jnp.where(last, place - odd * (TILE >> 5), place)
    hit = lax.shift_right_logical(iota((TILE, TILE), 0), shift) == place
    return hit.astype(F32).astype(BF16)


def level_places(rows, tile):
    found = []
    local, offset = 0, 0
    for s in level_shifts(rows):
        count = TILE >> s
        found.append((local, count, offset + tile * count))
        local += count
        offset += rows >> s
    return found[:-1], found[-1]


def put_pooled(to_s, rows, tile, pooled):
    levels, (local, count, at) = level_places(rows, tile)
    for start, number, place in levels:
        to_s[place : place + number, :] = pooled[start : start + number]
    at -= (tile % 2) * count
    if tile % 2:
        to_s[at : at + 2 * count, :] += pooled[local : local + 2 * count]
    else:
        to_s[at : at + 2 * count, :] = pooled[local : local + 2 * count]


def take_local(from_s, base, rows, tile):
    levels, (local, count, at) = level_places(rows, tile)
    at -= (tile % 2) * count
    parts = [from_s[base + place : base + place + number, :] for _, number, place in levels]
    return jnp.concatenate(parts + [from_s[base + at : base + at + 2 * count, :]], axis=0)


def stacked_low(values):
    return jnp.concatenate(split_low(values), axis=0)


def top_pool(rows):
    shift = level_shifts(rows)[-1]
    count = rows >> shift
    hit = lax.shift_right_logical(iota((count, rows), 1), shift) == iota((count, rows), 0)
    return hit.astype(F32).astype(BF16)


def head_ones():
    second = (iota((TILE, TILE), 1) >= HEAD_SIZE).astype(F32)
    return (1.0 - second).astype(BF16), second.astype(BF16)


def two_heads(values, first, second):
    return jnp.concatenate([values * first, values * second], axis=0)


def stand(values):
    return jnp.concatenate([values[:, :TILE], values[:, TILE:]], axis=0)


def assemble(info, near_ref, far_ref, to_ref, by_line=True):
    core, plane = info[3], info[4]
    line = info[5] if by_line else 0
    chunk = near_ref.shape[-2]
    for far, ref in enumerate((near_ref, far_ref)):
        for o in range(ref.shape[0]):
            at = ((o ^ plane) * 2 + (far ^ core)) * chunk
            at = pl.ds(pl.multiple_of(at, chunk), chunk)
            for z in range(ref.shape[1]):
                if len(ref.shape) == 5:
                    for part in range(ref.shape[2]):
                        to_ref[z ^ line, part, at, :] = ref[o, z, part]
                else:
                    to_ref[z ^ line, at, :] = ref[o, z]


def pack_kernel(info, q_ref, k_ref, v_ref, o_ref, up_ref, down_ref, bq_ref, bv_ref, bu_ref, attn_ref, ffn_ref, turn_s):
    chunk = q_ref.shape[0]
    attn_ref[:chunk, 0 * TILE : 1 * TILE] = q_ref[...]
    attn_ref[:chunk, 1 * TILE : 2 * TILE] = k_ref[...]
    attn_ref[:chunk, 2 * TILE : 3 * TILE] = v_ref[...]
    turn_s[...] = o_ref[...].T
    at = pl.ds(pl.multiple_of((info[4] * 2 + info[3]) * chunk, chunk), chunk)
    attn_ref[:chunk, 3 * TILE :] = turn_s[at, :]
    ffn_ref[0] = up_ref[...]
    ffn_ref[1] = down_ref[...]
    lanes = bu_ref.shape[1]
    blank = jnp.zeros((1, lanes - 2 * TILE), F32)
    rest = jnp.concatenate(
        [bu_ref[...], jnp.concatenate([bq_ref[...], bv_ref[...], blank], axis=1)], axis=0
    )
    rows = []
    for _ in range(3):
        part = rest.astype(BF16).astype(F32)
        rows.append(part)
        rest = rest - part
    rows.append(jnp.zeros((10, lanes), F32))
    attn_ref[chunk:, :] = jnp.concatenate(rows, axis=0).astype(BF16)


def bias_row(bias_ref, z, row):
    total = bias_ref[z, row : row + 1, :].astype(F32)
    for part in range(1, 3):
        at = 2 * part + row
        total = total + bias_ref[z, at : at + 1, :].astype(F32)
    return total


def norm_one_kernel(info, lengths, own_ref, other_ref, gain_ref, bias_ref, normed_ref, pooled_ref):
    rows = own_ref.shape[0]
    length, partner = lengths[info[0]], info[2]
    gain, bias = gain_ref[...], bias_ref[...]
    unit, _ = unit_rows(own_ref[...].astype(F32))
    normed_ref[...] = (unit * gain + bias).astype(BF16)
    unit, _ = unit_rows(other_ref[...].astype(F32))
    normed = (unit * gain + bias).astype(BF16)
    pool = top_pool(rows)
    count = pool.shape[0]
    live = (iota((1, rows), 1) + partner < length).astype(F32)
    pool_live = (pool.astype(F32) * live).astype(BF16)
    sums = mm(pool_live, normed)
    counts = jnp.sum(pool_live.astype(F32), axis=-1, keepdims=True)
    mean_live = sums / jnp.maximum(counts, 1.0)
    mean_all = mm(pool, normed) * (count / rows)
    high, low = split_low(mean_all)
    pooled_ref[0 * count : 1 * count, :] = high
    pooled_ref[1 * count : 2 * count, :] = low
    high, low = split_low(mean_live)
    pooled_ref[2 * count : 3 * count, :] = high
    pooled_ref[3 * count : 4 * count, :] = low


def attend_kernel(
    info,
    lengths,
    normed_ref,
    pooled_ref,
    near_ref,
    far_ref,
    bias_ref,
    mixed_ref,
    mixed_wide_ref,
    total_ref,
    q_ref,
    k_ref,
    v_ref,
    prob_ref,
    weight_s,
    mask_s,
    coarse_s,
    numer_s,
    full_s,
):
    rows = normed_ref.shape[0]
    pairs = q_ref.shape[0]
    tiles = 2 * rows // TILE
    half_tiles = rows // TILE
    length, own, partner = lengths[info[0]], info[1], info[2]
    line = info[5]
    assemble(info, near_ref, far_ref, full_s)
    pools = [pool_tile(odd) for odd in range(2)]
    spreads = [jnp.concatenate([spread_tile(odd)] * 2, axis=1) for odd in range(2)]
    lane = iota((1, 2 * TILE), 1) & (TILE - 1)
    for i in range(half_tiles):
        weight_s[i] = (lane + (own + i * TILE) < length).astype(F32)
        counts, _ = coarse_counts(lane + i * TILE, rows, length, own, partner)
        weight_s[half_tiles + i] = counts
    row_at = iota((TILE, 2 * TILE), 0)
    key_at = iota((TILE, 2 * TILE), 1) & (TILE - 1)
    pair_same = (row_at >> 5) == (key_at >> 5)
    apart = (row_at >> 4) != (key_at >> 4)
    mask_s[0] = pair_same.astype(F32)
    mask_s[1] = (pair_same & apart).astype(F32)
    live = (iota((rows, 1), 0) + own < length).astype(F32)
    counts, shift = coarse_counts(iota((rows, 1), 0), rows, length, own, partner)
    key_scale = 1.0 / jnp.maximum(counts, 1.0)
    query_scale = 1.0 / lax.shift_left(jnp.ones_like(shift), shift).astype(F32)
    top = pooled_ref.shape[0] // 4
    counts_other = counts[rows - top :]
    filled = counts_other / jnp.maximum(counts_other, 1.0)
    first, second = head_ones()

    def one_pair(p, carry):
        weight = full_s[p, :, : 3 * TILE]
        wide = mm(normed_ref[...], weight)
        biases = bias_row(bias_ref, p ^ line, 1)
        bq, bv = biases[:, :TILE], biases[:, TILE : 2 * TILE]
        query = (wide[:, :TILE] + bq).astype(BF16)
        key = (wide[:, TILE : 2 * TILE].astype(BF16).astype(F32) * live).astype(BF16)
        value = ((wide[:, 2 * TILE :] + bv).astype(BF16).astype(F32) * live).astype(BF16)
        extra = mm(pooled_ref[...], weight)
        q_other = extra[:top, :TILE] + extra[top : 2 * top, :TILE] + bq
        kv_other = extra[2 * top : 3 * top, TILE:] + extra[3 * top :, TILE:]
        k_other = kv_other[:, :TILE]
        v_other = kv_other[:, TILE:] + bv * filled
        q_ref[p, :rows, :] = query
        k_ref[p, :rows, :] = key
        v_ref[p, :rows, :] = value
        rows_all = jnp.concatenate([query, key, value], axis=1)
        for t in range(half_tiles):
            put_pooled(coarse_s, rows, t, mm(pools[t % 2], rows_all[t * TILE : (t + 1) * TILE]))
        q_ref[p, rows:, :] = (coarse_s[:, :TILE] * query_scale).astype(BF16)
        k_ref[p, rows:, :] = (coarse_s[:, TILE : 2 * TILE] * key_scale).astype(BF16)
        v_ref[p, rows:, :] = (coarse_s[:, 2 * TILE :] * key_scale).astype(BF16)
        q_ref[p, 2 * rows - top :, :] = q_other.astype(BF16)
        k_ref[p, 2 * rows - top :, :] = k_other.astype(BF16)
        v_ref[p, 2 * rows - top :, :] = v_other.astype(BF16)

        def one_tile(i, inner):
            at = pl.ds(pl.multiple_of(i * TILE, TILE), TILE)
            v = v_ref[p, at, :]
            score = mm_nt(q_ref[p, at, :], two_heads(k_ref[p, at, :], first, second)) * SCALE
            mask = mask_s[jnp.where(i >= half_tiles, 1, 0)]
            prob = jnp.where(mask > 0.0, jnp.exp(score) * weight_s[i], 0.0).astype(BF16)
            prob_ref[p, i] = prob
            values = jnp.concatenate(
                [
                    jnp.concatenate([v * first, first], axis=1),
                    jnp.concatenate([v * second, second], axis=1),
                ],
                axis=0,
            )
            numer_s[at, :] = mm(prob, values)
            return inner

        lax.fori_loop(0, tiles, one_tile, 0, unroll=4)
        for t in range(half_tiles):
            at = slice(t * TILE, (t + 1) * TILE)
            both = numer_s[at, :] + mm(
                spreads[t % 2], stacked_low(take_local(numer_s, rows, rows, t))
            )
            total = both[:, TILE:]
            mixed = both[:, :TILE] / total
            total_ref[p, at, :] = total
            mixed_wide_ref[p, at, :] = mixed
            mixed_ref[p, at, :] = mixed.astype(BF16)
        return carry

    lax.fori_loop(0, pairs, one_pair, 0)


def feed_kernel(
    info,
    own_ref,
    mixed_ref,
    near_ref,
    far_ref,
    ffn_near_ref,
    ffn_far_ref,
    b_out_ref,
    gain_ref,
    shift_ref,
    bias_ref,
    b_down_ref,
    hidden_ref,
    normed_ref,
    act_ref,
    slope_ref,
    *refs,
):
    *out_refs, result_s, full_s, ffn_s = refs
    pairs = mixed_ref.shape[0]
    line = info[5]
    assemble(info, near_ref, far_ref, full_s)
    assemble(info, ffn_near_ref, ffn_far_ref, ffn_s, by_line=False)
    hidden = own_ref[...].astype(F32) + b_out_ref[...]
    for p in range(pairs):
        hidden = hidden + mm_nt(mixed_ref[p], full_s[p, :, 3 * TILE :])
    hidden_ref[...] = hidden
    unit, _ = unit_rows(hidden)
    normed = (unit * gain_ref[...] + shift_ref[...]).astype(BF16)
    normed_ref[...] = normed
    result = hidden + b_down_ref[...]
    for z in range(pairs):
        pre = mm(normed, ffn_s[z, 0]) + bias_row(bias_ref, z ^ line, 0)
        half_erf = 0.5 + 0.5 * lax.erf(pre * INV_ROOT_TWO)
        act = (pre * half_erf).astype(BF16)
        act_ref[z] = act
        slope_ref[z] = (half_erf + pre * jnp.exp(-0.5 * pre * pre) * INV_ROOT_TAU).astype(BF16)
        result = result + mm(act, ffn_s[z, 1])
    result_s[...] = result
    chunk = out_refs[0].shape[0]
    for k, out_ref in enumerate(out_refs):
        at = ((info[4] * 2 + info[3]) ^ k) * chunk
        out_ref[...] = result_s[pl.ds(pl.multiple_of(at, chunk), chunk), :].astype(BF16)


def feed_back_kernel(
    info,
    dy_ref,
    ffn_near_ref,
    ffn_far_ref,
    near_ref,
    far_ref,
    slope_ref,
    hidden_ref,
    gain_ref,
    mixed_wide_ref,
    total_ref,
    grad_pre_ref,
    grad_hidden_ref,
    grad_hidden_low_ref,
    numer_ref,
    gtotal_ref,
    exchange_ref,
    vector_ref,
    b_up_ref,
    full_s,
    ffn_s,
):
    rows = dy_ref.shape[0]
    assemble(info, ffn_near_ref, ffn_far_ref, ffn_s, by_line=False)
    assemble(info, near_ref, far_ref, full_s)
    pairs = slope_ref.shape[0]
    dy = dy_ref[...]
    grad_normed = jnp.zeros((rows, dy.shape[1]), F32)
    for z in range(pairs):
        grad_act = mm_nt(dy, ffn_s[z, 1])
        grad_pre = (grad_act * slope_ref[z].astype(F32)).astype(BF16)
        grad_pre_ref[z] = grad_pre
        b_up_ref[z] = jnp.sum(grad_pre.astype(F32), axis=0, keepdims=True)
        grad_normed = grad_normed + mm_nt(grad_pre, ffn_s[z, 0])
    unit, inverse = unit_rows(hidden_ref[...])
    dy_wide = dy.astype(F32)
    vector_ref[0:1, :] = jnp.sum(grad_normed * unit, axis=0, keepdims=True)
    vector_ref[1:2, :] = jnp.sum(grad_normed, axis=0, keepdims=True)
    vector_ref[2:3, :] = jnp.sum(dy_wide, axis=0, keepdims=True)
    grad_hidden = dy_wide + norm_back(grad_normed, unit, inverse, gain_ref[...])
    vector_ref[3:4, :] = jnp.sum(grad_hidden, axis=0, keepdims=True)
    grad_hidden_ref[...] = grad_hidden
    low = grad_hidden.astype(BF16)
    grad_hidden_low_ref[...] = low
    pool = top_pool(rows)
    top = pool.shape[0]
    same = ((iota((TILE, TILE), 0) // HEAD_SIZE) == (iota((TILE, TILE), 1) // HEAD_SIZE)).astype(F32).astype(BF16)
    for p in range(pairs):
        grad_mixed = mm(low, full_s[p, :, 3 * TILE :]).astype(BF16).astype(F32)
        inv = 1.0 / total_ref[p]
        numer = grad_mixed * inv
        high, rest = split_low(grad_mixed * mixed_wide_ref[p])
        gtotal = -(mm(high, same) + mm(rest, same)) * inv
        numer_ref[p] = numer
        gtotal_ref[p] = gtotal
        exchange_ref[p, :top, :] = mm_wide(pool, numer)
        exchange_ref[p, top:, :] = mm_wide(pool, gtotal)


def give_out(info, near_ref, far_ref, z, part, values_s):
    core, plane = info[3], info[4]
    chunk = near_ref.shape[-2]
    for far, ref in enumerate((near_ref, far_ref)):
        for o in range(ref.shape[0]):
            at = ((o ^ plane) * 2 + (far ^ core)) * chunk
            ref[o, z, part] = values_s[pl.ds(pl.multiple_of(at, chunk), chunk), :]


def feed_grads_kernel(
    info, normed_ref, act_ref, grad_pre_ref, dy_ref, near_ref, far_ref, up_s, down_s
):
    line = info[5]
    for z in range(act_ref.shape[0]):
        up_s[...] = mm_tn(normed_ref[...], grad_pre_ref[z]).astype(BF16)
        give_out(info, near_ref, far_ref, z ^ line, 0, up_s)
        down_s[...] = mm_tn(act_ref[z], dy_ref[...]).astype(BF16)
        give_out(info, near_ref, far_ref, z ^ line, 1, down_s)


def attend_back_kernel(first_pair, *refs):
    final = first_pair > 0
    info, lengths, numer_ref, gtotal_ref, exchange_ref = refs[:5]
    q_ref, k_ref, v_ref, prob_ref, near_ref, far_ref = refs[5:11]
    refs = refs[11:]
    if final:
        before_ref, own_ref, gain_ref, grad_hidden_ref, grads_ref, b_qv_ref, grad_tokens_ref, vector_ref = refs[:8]
        refs = refs[8:]
    else:
        grads_ref, b_qv_ref, acc_ref = refs[:3]
        refs = refs[3:]
    coarse_s, left_s, grad_s, full_s = refs[:4]
    acc_s = refs[4] if final else acc_ref
    pairs, rows = numer_ref.shape[0], numer_ref.shape[1]
    tiles = 2 * rows // TILE
    half_tiles = rows // TILE
    length, own, partner = lengths[info[0]], info[1], info[2]
    assemble(info, near_ref, far_ref, full_s)
    pools = [jnp.concatenate([pool_tile(odd)] * 2, axis=1) for odd in range(2)]
    spreads = [jnp.concatenate([spread_tile(odd)] * 2, axis=1) for odd in range(2)]
    live = (iota((rows, 1), 0) + own < length).astype(F32)
    counts, shift = coarse_counts(iota((rows, 1), 0), rows, length, own, partner)
    value_scale = 1.0 / jnp.maximum(counts, 1.0)
    query_scale = 1.0 / lax.shift_left(jnp.ones_like(shift), shift).astype(F32)
    first, second = head_ones()
    at_lane = iota((1, TILE), 1) & (HEAD_SIZE - 1)
    pick = (at_lane < 2).astype(F32)
    pick_first = (pick * first.astype(F32)).astype(BF16)
    pick_second = (pick * second.astype(F32)).astype(BF16)
    is_low = at_lane == 1
    top = exchange_ref.shape[1] // 2

    def two_parts(gtotal):
        high = gtotal.astype(BF16).astype(F32)
        return jnp.where(is_low, gtotal - high, high).astype(BF16)

    def one_pair(p, carry):
        for t in range(half_tiles):
            at = slice(t * TILE, (t + 1) * TILE)
            numer, gtotal = numer_ref[p, at, :], gtotal_ref[p, at, :]
            left_s[at, :TILE] = numer.astype(BF16)
            left_s[at, TILE:] = two_parts(gtotal)
            both = jnp.concatenate([numer, gtotal], axis=1)
            put_pooled(coarse_s, rows, t, mm(pools[t % 2], stacked_low(both)))
        coarse_s[rows - top :, :TILE] = exchange_ref[p, :top, :]
        coarse_s[rows - top :, TILE:] = exchange_ref[p, top:, :]
        left_s[rows:, :TILE] = coarse_s[:, :TILE].astype(BF16)
        left_s[rows:, TILE:] = two_parts(coarse_s[:, TILE:])

        def one_tile(i, inner):
            at = pl.ds(pl.multiple_of(i * TILE, TILE), TILE)
            v = v_ref[p, at, :]
            prob = prob_ref[p, i]
            left = left_s[at, :]
            right = jnp.concatenate(
                [
                    jnp.concatenate([v * first, pick_first], axis=1),
                    jnp.concatenate([v * second, pick_second], axis=1),
                ],
                axis=0,
            )
            grad_score = (mm_nt(left, right) * prob.astype(F32)).astype(BF16)
            grad_s[at, :TILE] = mm(grad_score, two_heads(k_ref[p, at, :], first, second))
            grad_s[at, TILE : 2 * TILE] = mm_tn(
                stand(grad_score), two_heads(q_ref[p, at, :], first, second)
            )
            grad_s[at, 2 * TILE :] = mm_tn(stand(prob), two_heads(left[:, :TILE], first, second))
            return inner

        lax.fori_loop(0, tiles, one_tile, 0, unroll=4)
        grad_s[rows:, :TILE] *= query_scale
        grad_s[rows:, TILE:] *= value_scale
        for t in range(half_tiles):
            at = slice(t * TILE, (t + 1) * TILE)
            fine = grad_s[at, :] + mm(
                spreads[t % 2], stacked_low(take_local(grad_s, rows, rows, t))
            )
            gq = (fine[:, :TILE] * SCALE).astype(BF16)
            gk = (fine[:, TILE : 2 * TILE] * (SCALE * live[at])).astype(BF16)
            gv = (fine[:, 2 * TILE :] * live[at]).astype(BF16)
            grads_ref[p, at, :] = jnp.concatenate([gq, gk, gv], axis=1)
        sums = jnp.sum(grads_ref[p].astype(F32), axis=0, keepdims=True)
        b_qv_ref[p, 0:1, :] = sums[:, :TILE]
        b_qv_ref[p, 1:2, :] = sums[:, 2 * TILE :]
        acc_s[...] += mm_nt(grads_ref[p], full_s[first_pair + p, :, : 3 * TILE])
        return carry

    acc_s[...] = before_ref[...] if final else jnp.zeros_like(acc_s)
    lax.fori_loop(0, pairs, one_pair, 0)
    if final:
        unit, inverse = unit_rows(own_ref[...].astype(F32))
        grad_normed = acc_s[...]
        vector_ref[0:1, :] = jnp.sum(grad_normed * unit, axis=0, keepdims=True)
        vector_ref[1:2, :] = jnp.sum(grad_normed, axis=0, keepdims=True)
        grad_tokens_ref[...] = (
            grad_hidden_ref[...] + norm_back(grad_normed, unit, inverse, gain_ref[...])
        ).astype(BF16)


def attend_grads_kernel(
    info,
    normed_ref,
    low_ref,
    high_ref,
    grad_hidden_ref,
    mixed_ref,
    vec_two_ref,
    vec_up_ref,
    vec_one_ref,
    qv_low_ref,
    qv_high_ref,
    near_ref,
    far_ref,
    both_s,
):
    core, plane, line = info[3], info[4], info[5]
    half, pairs = low_ref.shape[0], mixed_ref.shape[0]
    dp = 2 * near_ref.shape[0]
    chunk = both_s.shape[0] // dp
    for z in range(pairs):
        grads = low_ref[z] if z < half else high_ref[z - half]
        both_s[:, : 3 * TILE] = mm_tn(normed_ref[...], grads).astype(BF16)
        both_s[:, 3 * TILE :] = mm_tn(grad_hidden_ref[...], mixed_ref[z]).astype(BF16)
        for far, ref in enumerate((near_ref, far_ref)):
            for o in range(ref.shape[0]):
                at = ((o ^ plane) * 2 + (far ^ core)) * chunk
                at = pl.ds(pl.multiple_of(at, chunk), chunk)
                to = pl.ds(pl.multiple_of((z ^ line) * chunk, chunk), chunk)
                ref[o, to, :] = both_s[at, :]
    vectors = [vec_two_ref[...]] + [vec_up_ref[z] for z in range(pairs)] + [vec_one_ref[...]]
    for row in range(2):
        parts = [ref[p, row : row + 1, :] for ref in (qv_low_ref, qv_high_ref) for p in range(half)]
        vectors.append(jnp.concatenate(parts, axis=1))
    vectors = jnp.concatenate(vectors, axis=0)
    blank = jnp.zeros((near_ref.shape[1] - pairs * chunk - vectors.shape[0], vectors.shape[1]), F32)
    vectors = jnp.concatenate([vectors, blank], axis=0).astype(BF16)
    for ref in (near_ref, far_ref):
        for o in range(ref.shape[0]):
            ref[o, pairs * chunk :, :] = vectors


def place_grads_kernel(info, near_ref, far_ref, up_ref, down_ref, q_ref, k_ref, v_ref, o_ref, turn_s):
    core, plane = info[3], info[4]
    chunk = near_ref.shape[-2]
    for far, ref in enumerate((near_ref, far_ref)):
        for o in range(ref.shape[0]):
            at = ((o ^ plane) * 2 + (far ^ core)) * chunk
            at = pl.ds(pl.multiple_of(at, chunk), chunk)
            up_ref[at, :] = ref[o, 0].astype(F32)
            down_ref[at, :] = ref[o, 1].astype(F32)
            rest = ref[o, 2].astype(F32)
            q_ref[at, :] = rest[:, :TILE]
            k_ref[at, :] = rest[:, TILE : 2 * TILE]
            v_ref[at, :] = rest[:, 2 * TILE : 3 * TILE]
            turn_s[at, :] = rest[:, 3 * TILE :]
    o_ref[...] = turn_s[...].T


def gather_line(line, refs, to_ref):
    own, one, two, three, passed = refs
    middle = (line == 1) | (line == 2)
    to_ref[line] = own[...]
    to_ref[line ^ 1] = one[...]
    to_ref[line ^ 2] = two[...]

    @pl.when(middle)
    def _():
        to_ref[line ^ 3] = three[...]

    @pl.when(jnp.logical_not(middle))
    def _():
        to_ref[line ^ 3] = passed[...]


def place_rows_kernel(info, *refs):
    gather_line(info[5], refs[:-1], refs[-1])


def deal_kernel(info, dealing, *refs):
    *pieces, out_ref, all_s = refs
    gather_line(info[5], pieces, all_s)
    own = info[4] * 2 + info[3]
    for i in range(out_ref.shape[0]):
        for slot in range(out_ref.shape[1]):
            seq = dealing[i * out_ref.shape[1] + slot]
            for half in range(out_ref.shape[2]):
                out_ref[i, slot, half] = all_s[(seq & 1) * 2 + half, (seq >> 1) ^ own]


def settle_kernel(pieces_ref, out_ref):
    dps, slots, halves = pieces_ref.shape[:3]
    for i in range(dps):
        for slot in range(slots):
            for half in range(halves):
                out_ref[slot, half, i] = pieces_ref[i, slot, half]


VMEM_SPEC = pl.BlockSpec(memory_space=pltpu.VMEM)
SMEM_SPEC = pl.BlockSpec(memory_space=pltpu.SMEM)


def part_of(array, half):
    block = (array.shape[0] // 2,) + array.shape[1:]
    return array, pl.BlockSpec(
        block, lambda i: (half,) + (0,) * (len(block) - 1), pipeline_mode=pl.Buffered(1)
    )


def call(kernel, outs, scalars, args, scratch=(), limit=16, long=False):
    args = [arg if isinstance(arg, tuple) else (arg, VMEM_SPEC) for arg in args]
    grid = (1,) if any(spec is not VMEM_SPEC for _, spec in args) else ()
    return pl.pallas_call(
        kernel,
        out_shape=[jax.ShapeDtypeStruct(shape, dtype) for shape, dtype in outs],
        grid=grid,
        in_specs=[SMEM_SPEC] * len(scalars) + [spec for _, spec in args],
        out_specs=[VMEM_SPEC] * len(outs),
        scratch_shapes=list(scratch),
        compiler_params=pltpu.CompilerParams(vmem_limit_bytes=limit << 20),
        cost_estimate=pl.CostEstimate(
            flops=10**10 if long else 1, transcendentals=0, bytes_accessed=1
        ),
    )(*scalars, *[arg for arg, _ in args])


def exchange(pieces, axis, groups=None):
    return lax.all_to_all(pieces, axis, 0, 0, tiled=True, axis_index_groups=groups)


def gather(piece, axis, count):
    return exchange(jnp.broadcast_to(piece[None], (count,) + piece.shape), axis)


def swap(piece, axis, distance):
    size = lax.axis_size(axis)
    return lax.ppermute(piece, axis, [(i, i ^ distance) for i in range(size)])


def after(value, *others):
    return lax.optimization_barrier((value, *others))[0]


def total_of(pieces):
    return functools.reduce(jnp.add, [piece.astype(F32) for piece in pieces]).astype(BF16)


def local(
    tokens,
    cotangent,
    lengths,
    dealing,
    ln1_gain,
    ln1_bias,
    w_query,
    b_query,
    w_key,
    w_value,
    b_value,
    w_out,
    b_out,
    ln2_gain,
    ln2_bias,
    w_up,
    b_up,
    w_down,
    b_down,
):
    seq_dev, length, width = tokens.shape
    dp = lax.axis_size("dp")
    nt = lax.axis_size("tensor")
    d = lax.axis_index("dp")
    t = lax.axis_index("tensor")
    rows = seq_dev * length // nt
    outer = dp // 2
    planes = [[2 * o + c for o in range(outer)] for c in range(2)]
    chunk = width // dp
    hid = w_up.shape[1]

    def near_line(piece):
        return [piece] + [swap(piece, "tensor", z) for z in range(1, nt)]

    def line_first(piece):
        return [piece, swap(piece, "tensor", 1), swap(piece, "tensor", 2)]

    def line_second(pieces):
        piece, one, two = pieces
        three = lax.ppermute(after(piece, two), "tensor", [(1, 2), (2, 1)])
        passed = lax.ppermute(two, "tensor", [(1, 0), (2, 3)])
        return [piece, one, two, three, passed]

    def plane_pieces(piece):
        return [piece] + [swap(piece, "dp", 2 * o) for o in range(1, outer)]

    own_base = (t % 2) * rows
    info = jnp.stack([d * seq_dev + t // 2, own_base, rows - own_base, d % 2, d // 2, t])
    row = lambda v: v.reshape(1, -1)

    slice_spec = lambda lanes: pl.BlockSpec((chunk, lanes), lambda i, info: (info[4] * 2 + info[3], 0))
    whole_spec = lambda shape: pl.BlockSpec(shape, lambda i, info: (0,) * len(shape))
    attn_piece, ffn_piece = pl.pallas_call(
        pack_kernel,
        out_shape=[
            jax.ShapeDtypeStruct((chunk + 16, 4 * TILE), BF16),
            jax.ShapeDtypeStruct((2, chunk, hid), BF16),
        ],
        grid_spec=pltpu.PrefetchScalarGridSpec(
            num_scalar_prefetch=1,
            grid=(1,),
            in_specs=[slice_spec(TILE)] * 3
            + [whole_spec((TILE, width)), slice_spec(hid), slice_spec(width)]
            + [whole_spec((1, TILE)), whole_spec((1, TILE)), whole_spec((1, hid))],
            out_specs=[whole_spec((chunk + 16, 4 * TILE)), whole_spec((2, chunk, hid))],
            scratch_shapes=[pltpu.VMEM((width, TILE), BF16)],
        ),
    )(info, w_query, w_key, w_value, w_out, w_up, w_down, row(b_query), row(b_value), row(b_up))
    halves = tokens.reshape(nt, rows, width)
    own = lax.dynamic_index_in_dim(halves, t, 0, keepdims=False)
    other = lax.dynamic_index_in_dim(halves, t ^ 1, 0, keepdims=False)
    dy = lax.dynamic_index_in_dim(cotangent.reshape(nt, rows, width), t, 0, keepdims=False)
    top = rows >> level_shifts(rows)[-1]

    attn_full = pltpu.VMEM((nt, width, 4 * TILE), BF16)
    ffn_full = pltpu.VMEM((nt, 2, width, hid), BF16)

    normed_one, pooled = call(
        norm_one_kernel,
        [((rows, width), BF16), ((4 * top, width), BF16)],
        [info, lengths],
        [own, other, row(ln1_gain), row(ln1_bias)],
    )
    attn_line = near_line(attn_piece)
    normed_one, *attn_line = lax.optimization_barrier((normed_one, *attn_line))
    attn_near = jnp.stack(plane_pieces(jnp.stack([piece[:chunk] for piece in attn_line])))
    biases = jnp.stack([piece[chunk:] for piece in attn_line])
    ffn_line = gather(ffn_piece, "tensor", nt)
    attn_w = attn_near, swap(attn_near, "dp", 1)
    ffn_pieces = plane_pieces(after(ffn_line, attn_near))
    normed_one = after(normed_one, ffn_line)

    mixed, mixed_wide, total, q, k, v, prob = call(
        attend_kernel,
        [((nt, rows, TILE), BF16), ((nt, rows, TILE), F32), ((nt, rows, TILE), F32)]
        + [((nt, 2 * rows, TILE), BF16)] * 3
        + [((nt, 2 * rows // TILE, TILE, 2 * TILE), BF16)],
        [info, lengths],
        [normed_one, pooled, *attn_w, biases],
        scratch=[
            pltpu.VMEM((2 * rows // TILE, 1, 2 * TILE), F32),
            pltpu.VMEM((2, TILE, 2 * TILE), F32),
            pltpu.VMEM((rows, 3 * TILE), F32),
            pltpu.VMEM((2 * rows, 2 * TILE), F32),
            attn_full,
        ],
        limit=24,
        long=True,
    )
    ffn_near = jnp.stack([after(each, mixed) for each in ffn_pieces])
    ffn_w = ffn_near, swap(ffn_near, "dp", 1)
    piece = rows // dp
    hidden, normed_two, act, slope, *outs = call(
        feed_kernel,
        [((rows, width), F32), ((rows, width), BF16)]
        + [((nt, rows, hid), BF16)] * 2
        + [((piece, width), BF16)] * dp,
        [info],
        [own, mixed, *attn_w, *ffn_w]
        + [row(b_out), row(ln2_gain), row(ln2_bias), biases, row(b_down)],
        scratch=[pltpu.VMEM((rows, width), F32), attn_full, ffn_full],
        limit=28,
    )
    chunks = [outs[0]] + [swap(outs[k], "dp", k) for k in range(1, dp)]

    grad_pre, grad_hidden, grad_hidden_low, numer, gtotal, sent, vec_two, vec_up = call(
        feed_back_kernel,
        [
            ((nt, rows, hid), BF16),
            ((rows, width), F32),
            ((rows, width), BF16),
            ((nt, rows, TILE), F32),
            ((nt, rows, TILE), F32),
            ((nt, 2 * top, TILE), F32),
            ((4, width), F32),
            ((nt, 1, hid), F32),
        ],
        [info],
        [dy, *ffn_w, *attn_w, slope, hidden, row(ln2_gain), mixed_wide, total],
        scratch=[attn_full, ffn_full],
        limit=28,
    )
    swapped = swap(sent, "tensor", 1)
    ffn_grads = call(
        feed_grads_kernel,
        [((outer, nt, 2, chunk, hid), BF16)] * 2,
        [info],
        [normed_two, act, grad_pre, dy],
        scratch=[pltpu.VMEM((width, hid), BF16)] * 2,
    )
    ffn_far = swap(ffn_grads[1], "dp", 1)

    back_scratch = [
        pltpu.VMEM((rows, 2 * TILE), F32),
        pltpu.VMEM((2 * rows, 2 * TILE), BF16),
        pltpu.VMEM((2 * rows, 3 * TILE), F32),
        attn_full,
    ]

    def back_args(half):
        return [part_of(each, half) for each in (numer, gtotal, swapped, q, k, v, prob)] + [*attn_w]

    def core_sums(near, far):
        return [total_of([near[o], far[o]]) for o in range(outer)]

    def plane_parts(pieces):
        return [pieces[0]] + [swap(pieces[o], "dp", 2 * o) for o in range(1, outer)]

    chunks = line_first(jnp.stack(chunks))
    gtotal, chunks[0] = lax.optimization_barrier((gtotal, chunks[0]))
    grads_low, qv_low, acc = call(
        functools.partial(attend_back_kernel, 0),
        [((nt // 2, rows, 3 * TILE), BF16), ((nt // 2, 2, TILE), F32), ((rows, width), F32)],
        [info, lengths],
        back_args(0),
        scratch=back_scratch,
        limit=20,
        long=True,
    )
    ffn_parts = core_sums(after(ffn_grads[0], acc), ffn_far)
    acc, chunks[1], chunks[2], *ffn_parts = lax.optimization_barrier(
        (acc, chunks[1], chunks[2], *ffn_parts)
    )
    chunks = line_second(chunks)
    ffn_parts = plane_parts(ffn_parts)
    grads_high, qv_high, grad_low, vec_one = call(
        functools.partial(attend_back_kernel, nt // 2),
        [
            ((nt // 2, rows, 3 * TILE), BF16),
            ((nt // 2, 2, TILE), F32),
            ((rows, width), BF16),
            ((2, width), F32),
        ],
        [info, lengths],
        back_args(1) + [acc, own, row(ln1_gain), grad_hidden],
        scratch=back_scratch + [pltpu.VMEM((rows, width), F32)],
        limit=20,
        long=True,
    )
    grad_low, grad_hidden_low = lax.optimization_barrier((grad_low, grad_hidden_low))
    row_pieces = line_first(grad_low)
    attn_near, attn_far = call(
        attend_grads_kernel,
        [((outer, nt * chunk + 16, 4 * TILE), BF16)] * 2,
        [info],
        [normed_one, grads_low, grads_high, grad_hidden_low, mixed]
        + [vec_two, vec_up, vec_one, qv_low, qv_high],
        scratch=[pltpu.VMEM((width, 4 * TILE), BF16)],
    )
    chunks[3], chunks[4], attn_near = lax.optimization_barrier((chunks[3], chunks[4], attn_near))
    (dealt,) = call(
        deal_kernel,
        [((dp, seq_dev, nt // seq_dev, piece, width), BF16)],
        [info, dealing],
        chunks,
        scratch=[pltpu.VMEM((nt, dp, piece, width), BF16)],
    )
    dealt = exchange(dealt, "dp")
    attn_parts = core_sums(attn_near, swap(attn_far, "dp", 1))
    attn_parts = total_of(plane_parts(attn_parts))
    attn_parts, *row_pieces = lax.optimization_barrier((attn_parts, *row_pieces))
    ffn_parts = total_of(ffn_parts)
    grads = [
        jnp.concatenate(
            [ffn_parts[z].reshape(2 * chunk, hid), attn_parts[z * chunk : (z + 1) * chunk]]
            + [attn_parts[nt * chunk :]]
        )
        for z in range(nt)
    ]
    grads = total_of([grads[0]] + [swap(grads[z], "tensor", z) for z in range(1, nt)])
    vectors = grads[3 * chunk :].astype(F32)
    row_pieces = line_second(row_pieces)
    near = jnp.stack(plane_pieces(grads[: 3 * chunk].reshape(3, chunk, width)))
    grads = near, swap(near, "dp", 1)
    g_up, g_down, g_query, g_key, g_value, g_out = call(
        place_grads_kernel,
        [((width, hid), F32), ((hid, width), F32)]
        + [((width, TILE), F32)] * 3
        + [((TILE, width), F32)],
        [info],
        grads,
        scratch=[pltpu.VMEM((width, TILE), F32)],
    )
    (grad_tokens,) = call(
        place_rows_kernel, [((nt, rows, width), BF16)], [info], row_pieces
    )
    grad_tokens = grad_tokens.reshape(seq_dev, length, width)
    (output,) = call(
        settle_kernel, [((seq_dev, nt // seq_dev, dp, piece, width), BF16)], [], [dealt]
    )
    output = output.reshape(seq_dev, length, width)
    base = 4 + nt
    g_b_up = lax.dynamic_index_in_dim(vectors[4:base], t, 0, keepdims=False)
    g_b_q = lax.dynamic_index_in_dim(vectors[base + 2].reshape(nt, TILE), t, 0, keepdims=False)
    g_b_v = lax.dynamic_index_in_dim(vectors[base + 3].reshape(nt, TILE), t, 0, keepdims=False)
    return (
        output,
        grad_tokens,
        vectors[base],
        vectors[base + 1],
        g_query,
        g_b_q,
        g_key,
        g_value,
        g_b_v,
        g_out,
        vectors[3],
        vectors[0],
        vectors[1],
        g_up,
        g_b_up,
        g_down,
        vectors[2],
    )


def solution(mesh):
    placed = (
        P("dp", None, None),
        P("dp", None, None),
        P(),
        P(),
        P(),
        P(),
        P(None, "tensor"),
        P("tensor"),
        P(None, "tensor"),
        P(None, "tensor"),
        P("tensor"),
        P("tensor", None),
        P(),
        P(),
        P(),
        P(None, "tensor"),
        P("tensor"),
        P("tensor", None),
        P(),
    )
    return jax.shard_map(
        local,
        mesh=mesh,
        in_specs=placed,
        out_specs=(
            P("dp", None, None),
            P("dp", None, None),
            P(),
            P(),
            P(None, "tensor"),
            P("tensor"),
            P(None, "tensor"),
            P(None, "tensor"),
            P("tensor"),
            P("tensor", None),
            P(),
            P(),
            P(),
            P(None, "tensor"),
            P("tensor"),
            P("tensor", None),
            P(),
        ),
        check_vma=False,
    )
```

time: 332 us -> 273 us (0.82)
  waiting for transfers between devices: 150 us -> 131 us
  local copies, waits for them, and re-layouts: 24.7 us -> 7.91 us
  Pallas kernels: 74.9 us -> 59 us
  other arithmetic: 16.3 us -> 6.68 us
    ppermute x46 -> x38, waiting for transfers between devices: 143 us -> 99.8 us  [swap(): return lax.ppermute(piece, axis, [(i, i ^ distance) for i in range(size)])]
    ppermute x0 -> x4, waiting for transfers between devices: none -> 20.9 us  [the longest x2 20.9 us: line_second(): three = lax.ppermute(after(piece, two), 'tensor', [(1, 2), (2, 1)])]
    pallas_call x11 -> x12, Pallas kernels: 74.9 us -> 56.5 us  [call(): pl.pallas_call(kernel, out_shape=[jax.ShapeDtypeStruct(shape, dtype) for...]
    unnamed x61 -> x51, local copies, waits for them, and re-layouts: 12.1 us -> 1.18 us
    ppermute x0 -> x4, starting transfers between devices: none -> 9.3 us  [the longest x2 6.66 us: line_second(): three = lax.ppermute(after(piece, two), 'tensor', [(1, 2), (2, 1)])]
    ppermute x46 -> x38, starting transfers between devices: 51.6 us -> 46.1 us  [swap(): return lax.ppermute(piece, axis, [(i, i ^ distance) for i in range(size)])]
    dynamic_slice x5 -> x0, local copies, waits for them, and re-layouts: 3.57 us -> none  [the longest x3 2.16 us: own_rows(): return lax.dynamic_slice_in_dim(weight, d * chunk, chunk, axis=0)]
    all_to_all x3 -> x2, waiting for transfers between devices: 7.03 us -> 10.1 us  [exchange(): lax.all_to_all(pieces, axis, 0, 0, tiled=True, axis_index_groups=groups)]
  transfers between devices with their start and end apart: 49 -> 44, of which waited for: 22 -> 26; matrix products, arithmetic and copies ran while one was open for 8% -> 4% of each run, Pallas kernels for 16% -> 11%
where the time goes in v3:
time: 273 us; the launch traced here: 272 us
  waiting for transfers between devices  131 us (48%)
  starting transfers between devices  66.1 us (24%)
  Pallas kernels  59 us (22%)
  local copies, waits for them, and re-layouts  7.91 us (3%)
  other arithmetic  6.68 us (2%)
    ppermute x38, waiting for transfers between devices, swap(): return lax.ppermute(piece, axis, [(i, i ^ distance) for i in range(size)])  99.8 us
    pallas_call x12, Pallas kernels, call(): pl.pallas_call(kernel, out_shape=[jax.ShapeDtypeStruct(shape, dtype) for...  56.5 us
    ppermute x38, starting transfers between devices, swap(): return lax.ppermute(piece, axis, [(i, i ^ distance) for i in range(size)])  46.1 us
    ppermute x2, waiting for transfers between devices, line_second(): three = lax.ppermute(after(piece, two), 'tensor', [(1, 2), (2, 1)])  20.9 us
    all_to_all x2, starting transfers between devices, exchange(): lax.all_to_all(pieces, axis, 0, 0, tiled=True, axis_index_groups=groups)  10.7 us
    all_to_all x2, waiting for transfers between devices, exchange(): lax.all_to_all(pieces, axis, 0, 0, tiled=True, axis_index_groups=groups)  10.1 us
    ppermute x2, starting transfers between devices, line_second(): three = lax.ppermute(after(piece, two), 'tensor', [(1, 2), (2, 1)])  6.66 us
  transfers between devices with their start and end apart: 44, of which 26 were waited for; matrix products, arithmetic and copies ran while one was open for 4% of the time, Pallas kernels for 11%

profile of v3, /device:TPU:8, one launch (start us, length us, event | category | flops | bytes accessed | tf_op | source)
XLA Modules:
  0.0 271.9 jit_solution(14853992759324000580)
XLA Ops:
  1.3 2.5 shard_map.314
  10.6 2.0 collective-permute-done.2
  14.0 1.6 collective-permute-start.4
  17.5 4.8 %collective-permute-done.4 = bf16[4,64,512]{2,1,0:T(8,128)(2,1)S(1)} collective-permute-done((bf16[4,64,512]{2,1,0:T(8,128)(2,1)S(1)}, bf16[4,64,512]{2,1,0:T(8,128)(2,1)S(1)}, u32[]{:S(2)}, u32[]{:S(2)}) %collective-permute-start.4) | collective-permute-done | bytes 262176 | tf_op jit(solution)/shard_map/ppermute | solution.py:714
  22.4 2.4 collective-permute-done.3
  24.8 3.1 %collective-permute-done.5 = bf16[4,64,512]{2,1,0:T(8,128)(2,1)S(1)} collective-permute-done((bf16[4,64,512]{2,1,0:T(8,128)(2,1)S(1)}, bf16[4,64,512]{2,1,0:T(8,128)(2,1)S(1)}, u32[]{:S(2)}, u32[]{:S(2)}) %collective-permute-start.5) | collective-permute-done | bytes 262176 | tf_op jit(solution)/shard_map/ppermute | solution.py:714
  29.0 6.3 %all-to-all-start = ((bf16[4,2,64,512]{3,2,1,0:T(8,128)(2,1)}), bf16[4,2,64,512]{3,2,1,0:T(8,128)(2,1)}, u32[]{:S(2)}, u32[]{:S(2)}) async-start(bf16[4,2,64,512]{3,2,1,0:T(8,128)(2,1)} %broadcast_in_dim.2), calls=%async_computation | async-start | bytes 1048576 | tf_op jit(solution)/shard_map/all_to_all | solution.py:705
  37.5 10.1 %all-to-all-done = bf16[4,2,64,512]{3,2,1,0:T(8,128)(2,1)} async-done(((bf16[4,2,64,512]{3,2,1,0:T(8,128)(2,1)}), bf16[4,2,64,512]{3,2,1,0:T(8,128)(2,1)}, u32[]{:S(2)}, u32[]{:S(2)}) %all-to-all-start) | async-done | bytes 524320 | tf_op jit(solution)/shard_map/all_to_all | solution.py:705
  47.6 2.5 collective-permute-start.9
  52.2 8.5 %shard_map.316 = (bf16[4,512,128]{2,1,0:T(8,128)(2,1)S(1)}, f32[4,512,128]{2,1,0:T(8,128)S(1)}, f32[4,512,128]{2,1,0:T(8,128)S(1)}, bf16[4,1024,128]{2,1,0:T(8,1...) custom-call(s32[6]{0:T(128)S(1)} %copy-done.7, ...), custom_call_target="tpu_custom_call" | custom-call | flops 10000000000 | bytes 1 | tf_op jit(solution)/shard_map/pallas_call | solution.py:690
  60.6 3.0 %collective-permute-done.9 = bf16[4,2,64,512]{3,2,1,0:T(8,128)(2,1)S(1)} collective-permute-done((bf16[4,2,64,512]{3,2,1,0:T(8,128)(2,1)}, bf16[4,2,64,512]{3,2,1,0:T(8,128)(2,1)S(1)}, u32[]{:S(2)}, u32[]{:S(2)}) %collective-permute-start.9) | collective-permute-done | bytes 524320 | tf_op jit(solution)/shard_map/ppermute | solution.py:714
  63.6 9.8 %collective-permute-done.8 = bf16[4,2,64,512]{3,2,1,0:T(8,128)(2,1)S(1)} collective-permute-done((bf16[4,2,64,512]{3,2,1,0:T(8,128)(2,1)}, bf16[4,2,64,512]{3,2,1,0:T(8,128)(2,1)S(1)}, u32[]{:S(2)}, u32[]{:S(2)}) %collective-permute-start.8) | collective-permute-done | bytes 524320 | tf_op jit(solution)/shard_map/ppermute | solution.py:714
  75.2 4.1 %collective-permute-done.10.ffn_far_ref = bf16[4,4,2,64,512]{4,3,2,1,0:T(8,128)(2,1)S(1)} collective-permute-done((bf16[4,4,2,64,512]{4,3,2,1,0:T(8,128)(2,1)S(1)}, bf16[4,4,2,64,512]{4,3,2,1,0:T(8,128)(2,1)S(1)}, u32[]{:S(2)}, u32[]{:S(2)}) %collective-permute-start.10) | collective-permute-done | bytes 2097184 | tf_op jit(solution)/shard_map/ppermute | solution.py:714
  79.3 6.0 %shard_map.317 = (f32[512,512]{1,0:T(8,128)S(1)}, bf16[512,512]{1,0:T(8,128)(2,1)S(1)}, bf16[4,512,512]{2,1,0:T(8,128)(2,1)S(1)}, bf16[4,512,512]{2,1,0:T(8,128)...) custom-call(s32[6]{0:T(128)S(1)} %copy-done.7, ...), custom_call_target="tpu_custom_call" | custom-call | flops 1 | bytes 1 | tf_op jit(solution)/shard_map/pallas_call | solution.py:690
  85.3 6.2 %shard_map.318 = (bf16[4,512,512]{2,1,0:T(8,128)(2,1)S(1)}, f32[512,512]{1,0:T(8,128)S(1)}, bf16[512,512]{1,0:T(8,128)(2,1)S(1)}, f32[4,512,128]{2,1,0:T(8,128)S...) custom-call(s32[6]{0:T(128)S(1)} %copy-done.7, ...), custom_call_target="tpu_custom_call" | custom-call | flops 1 | bytes 1 | tf_op jit(solution)/shard_map/pallas_call | solution.py:690
  91.5 3.3 %collective-permute-start.18 = (f32[4,32,128]{2,1,0:T(8,128)S(1)}, f32[4,32,128]{2,1,0:T(8,128)S(1)}, u32[]{:S(2)}, u32[]{:S(2)}) collective-permute-start(f32[4,32,128]{2,1,0:T(8,128)S(1)} %get-tuple-element.129), channel_id=1, source_target_pairs={{0,1},{1,0},{2,3},{3,2},{4,5},{5,4},{6,7},{7,6},{8,9},{9,8},{10,11... | collective-permute-start | bytes 196616 | tf_op jit(solution)/shard_map/ppermute | solution.py:714
  98.1 3.0 %shard_map.320 = (bf16[4,4,2,64,512]{4,3,2,1,0:T(8,128)(2,1)S(1)}, bf16[4,4,2,64,512]{4,3,2,1,0:T(8,128)(2,1)S(1)}) custom-call(s32[6]{0:T(128)S(1)} %copy-done.7, bf16[512,512]{1,0:T(8,128)(2,1)S(1)} %get-tuple-element.135.normed_ref, bf16[4,512,512]{2,1,0:T(8,128)(2,1)S(1)} %get-tuple-element.136.act_ref, ...), custom_call_target="tpu_custom_call" | custom-call | flops 1 | bytes 1 | tf_op jit(solution)/shard_map/pallas_call | solution.py:690
  102.0 1.6 collective-permute-start.16
  105.4 1.8 collective-permute-done.16
  107.3 1.7 collective-permute-done.17
  109.0 1.9 collective-permute-start.19
  111.0 7.9 %shard_map.319 = (bf16[2,512,384]{2,1,0:T(8,128)(2,1)S(1)}, f32[2,2,128]{2,1,0:T(2,128)S(1)}, f32[512,512]{1,0:T(8,128)S(1)}) custom-call(s32[6]{0:T(128)S(1)} %copy-done.7, s32[16]{0:T(128)S(1)} %copy-done.14, f32[4,512,128]{2,1,0:T(8,128)S(1)} %get-tuple-element.127.refs_2_, f32[4,512,128]{2,1,0:T(8,128)S(1)} %get-tuple-element.128.refs_3_, ...), custom_call_target="tpu_custom_call" | custom-call | flops 10000000000 | bytes 1 | tf_op jit(solution)/shard_map/pallas_call | solution.py:690
  118.9 1.9 fusion.6
  120.8 11.1 %collective-permute-done.20.refs_2_ = bf16[8,64,512]{2,1,0:T(8,128)(2,1)S(1)} collective-permute-done((bf16[8,64,512]{2,1,0:T(8,128)(2,1)S(1)}, bf16[8,64,512]{2,1,0:T(8,128)(2,1)S(1)}, u32[]{:S(2)}, u32[]{:S(2)}) %collective-permute-start.20) | collective-permute-done | bytes 524320 | tf_op jit(solution)/shard_map/ppermute | solution.py:714
  131.9 2.2 collective-permute-done.19.refs_1_
  134.1 9.3 %shard_map.321 = (bf16[2,512,384]{2,1,0:T(8,128)(2,1)S(1)}, f32[2,2,128]{2,1,0:T(2,128)S(1)}, bf16[512,512]{1,0:T(8,128)(2,1)}, f32[2,512]{1,0:T(2,128)S(1)}) custom-call(s32[6]{0:T(128)S(1)} %copy-done.7, s32[16]{0:T(128)S(1)} %copy-done.14, f32[4,512,128]{2,1,0:T(8,128)S(1)} %get-tuple-element.127.refs_2_, f32[4,512,128]{2,1,0:T(8,128)S(1)} %get-tuple-element.128.refs_3_, ...), custom_call_target="tpu_custom_call" | custom-call | flops 10000000000 | bytes 1 | tf_op jit(solution)/shard_map/pallas_call | solution.py:690
  143.4 3.5 %shard_map.322 = (bf16[4,272,512]{2,1,0:T(8,128)(2,1)S(1)}, bf16[4,272,512]{2,1,0:T(8,128)(2,1)}) custom-call(s32[6]{0:T(128)S(1)} %copy-done.7, bf16[512,512]{1,0:T(8,128)(2,1)S(1)} %copy-done.6, bf16[2,512,384]{2,1,0:T(8,128)(2,1)S(1)} %get-tuple-element.144.low_ref, bf16[2,512,384]{2,1,0:T(8,128)(2,1)S(1)} %get-tuple-element.147.high_ref, ...), custom_call_target="tpu_custom_call" | custom-call | flops 1 | bytes 1 | tf_op jit(solution)/shard_map/pallas_call | solution.py:690
  147.0 3.4 %collective-permute-start.22 = (bf16[8,64,512]{2,1,0:T(8,128)(2,1)S(1)}, bf16[8,64,512]{2,1,0:T(8,128)(2,1)S(1)}, u32[]{:S(2)}, u32[]{:S(2)}) collective-permute-start(bf16[8,64,512]{2,1,0:T(8,128)(2,1)S(1)} %bitcast_dynamic-update-slice_fusion.refs_0_), channel_id=1, source_target_pairs={{1,2},{2,1},{5,6},{6,5},{9,10},{10,9},{13,14},{14,13},{17,18},{18,... | collective-permute-start | bytes 1572872 | tf_op jit(solution)/shard_map/ppermute | solution.py:765
  153.7 9.5 %collective-permute-done.22.refs_3_ = bf16[8,64,512]{2,1,0:T(8,128)(2,1)S(1)} collective-permute-done((bf16[8,64,512]{2,1,0:T(8,128)(2,1)S(1)}, bf16[8,64,512]{2,1,0:T(8,128)(2,1)S(1)}, u32[]{:S(2)}, u32[]{:S(2)}) %collective-permute-start.22) | collective-permute-done | bytes 524320 | tf_op jit(solution)/shard_map/ppermute | solution.py:765
  166.0 2.1 shard_map.323
  168.1 4.3 %all-to-all-start.1 = ((bf16[8,2,2,64,512]{4,3,2,1,0:T(8,128)(2,1)}), bf16[8,2,2,64,512]{4,3,2,1,0:T(8,128)(2,1)}, u32[]{:S(2)}, u32[]{:S(2)}) async-start(bf16[8,2,2,64,512]{4,3,2,1,0:T(8,128)(2,1)} %shard_map.323), calls=%async_computation.1 | async-start | bytes 4194304 | tf_op jit(solution)/shard_map/all_to_all | solution.py:705
  172.5 1.6 collective-permute-start.28
  174.3 1.9 collective-permute-start.25
  177.7 7.4 %collective-permute-start.27 = (bf16[272,512]{1,0:T(8,128)(2,1)S(1)}, bf16[272,512]{1,0:T(8,128)(2,1)S(1)}, u32[]{:S(2)}, u32[]{:S(2)}) collective-permute-start(bf16[272,512]{1,0:T(8,128)(2,1)S(1)} %get-tuple-element.182), channel_id=1, source_target_pairs={{0,24},{4,28},{8,16},{12,20},{16,8},{20,12},{24,0},{28,4},{1,25},{... | collective-permute-start | bytes 835592 | tf_op jit(solution)/shard_map/ppermute | solution.py:714
  185.2 1.6 add_convert_fusion
  186.8 20.8 %collective-permute-done.25 = bf16[272,512]{1,0:T(8,128)(2,1)S(1)} collective-permute-done((bf16[272,512]{1,0:T(8,128)(2,1)S(1)}, bf16[272,512]{1,0:T(8,128)(2,1)S(1)}, u32[]{:S(2)}, u32[]{:S(2)}) %collective-permute-start.25) | collective-permute-done | bytes 278560 | tf_op jit(solution)/shard_map/ppermute | solution.py:714
  207.6 5.1 %collective-permute-done.27 = bf16[272,512]{1,0:T(8,128)(2,1)S(1)} collective-permute-done((bf16[272,512]{1,0:T(8,128)(2,1)S(1)}, bf16[272,512]{1,0:T(8,128)(2,1)S(1)}, u32[]{:S(2)}, u32[]{:S(2)}) %collective-permute-start.27) | collective-permute-done | bytes 278560 | tf_op jit(solution)/shard_map/ppermute | solution.py:714
  214.0 2.7 collective-permute-start.36
  217.6 4.6 %collective-permute-done.35 = bf16[208,512]{1,0:T(8,128)(2,1)S(1)} collective-permute-done((bf16[208,512]{1,0:T(8,128)(2,1)S(1)}, bf16[208,512]{1,0:T(8,128)(2,1)S(1)}, u32[]{:S(2)}, u32[]{:S(2)}) %collective-permute-start.35) | collective-permute-done | bytes 213024 | tf_op jit(solution)/shard_map/ppermute | solution.py:714
  222.2 9.1 %collective-permute-done.36 = bf16[208,512]{1,0:T(8,128)(2,1)S(1)} collective-permute-done((bf16[208,512]{1,0:T(8,128)(2,1)S(1)}, bf16[208,512]{1,0:T(8,128)(2,1)S(1)}, u32[]{:S(2)}, u32[]{:S(2)}) %collective-permute-start.36) | collective-permute-done | bytes 213024 | tf_op jit(solution)/shard_map/ppermute | solution.py:714
  231.3 3.9 %collective-permute-done.37 = bf16[208,512]{1,0:T(8,128)(2,1)S(1)} collective-permute-done((bf16[208,512]{1,0:T(8,128)(2,1)S(1)}, bf16[208,512]{1,0:T(8,128)(2,1)S(1)}, u32[]{:S(2)}, u32[]{:S(2)}) %collective-permute-start.37) | collective-permute-done | bytes 213024 | tf_op jit(solution)/shard_map/ppermute | solution.py:714
  238.8 4.5 %collective-permute-done.40 = bf16[3,64,512]{2,1,0:T(8,128)(2,1)S(1)} collective-permute-done((bf16[3,64,512]{2,1,0:T(8,128)(2,1)S(1)}, bf16[3,64,512]{2,1,0:T(8,128)(2,1)S(1)}, u32[]{:S(2)}, u32[]{:S(2)}) %collective-permute-start.40) | collective-permute-done | bytes 196640 | tf_op jit(solution)/shard_map/ppermute | solution.py:714
  243.3 2.0 collective-permute-done.39
  246.8 3.3 %collective-permute-start.30 = (bf16[512,512]{1,0:T(8,128)(2,1)}, bf16[512,512]{1,0:T(8,128)(2,1)S(1)}, u32[]{:S(2)}, u32[]{:S(2)}) collective-permute-start(bf16[512,512]{1,0:T(8,128)(2,1)} %get-tuple-element.165.refs_0_), channel_id=1, source_target_pairs={{1,2},{2,1},{5,6},{6,5},{9,10},{10,9},{13,14},{14,13},{17,18},{18,... | collective-permute-start | bytes 1572872 | tf_op jit(solution)/shard_map/ppermute | solution.py:765
  251.9 11.4 %collective-permute-done.30.refs_3_ = bf16[512,512]{1,0:T(8,128)(2,1)S(1)} collective-permute-done((bf16[512,512]{1,0:T(8,128)(2,1)}, bf16[512,512]{1,0:T(8,128)(2,1)S(1)}, u32[]{:S(2)}, u32[]{:S(2)}) %collective-permute-start.30) | collective-permute-done | bytes 524320 | tf_op jit(solution)/shard_map/ppermute | solution.py:765
  263.2 2.7 shard_map.325
  265.9 3.0 %shard_map.324 = bf16[2,2,8,64,512]{4,3,2,1,0:T(8,128)(2,1)} custom-call(bf16[8,2,2,64,512]{4,3,2,1,0:T(8,128)(2,1)} %all-to-all-done.1.pieces_ref), custom_call_target="tpu_custom_call" | custom-call | flops 1 | bytes 1 | tf_op jit(solution)/shard_map/pallas_call | solution.py:690
  269.0 2.9 %shard_map.326 = (f32[512,512]{1,0:T(8,128)}, f32[512,512]{1,0:T(8,128)}, f32[512,128]{1,0:T(8,128)}, f32[512,128]{1,0:T(8,128)}, f32[512,128]{1,0:T(8,128)}, /*index=5*/f32[128,512]{1,0:T(8,128)}) custom-call(s32[6]{0:T(128)S(1)} %copy-done.7, bf16[4,3,64,512]{3,2,1,0:T(8,128)(2,1)S(1)} %pad_maximum_fusion.2.near_ref, ...), custom_call_target="tpu_custom_call" | custom-call | flops 1 | bytes 1 | tf_op jit(solution)/shard_map/pallas_call | solution.py:690
  (139 shorter events, 40.3 us)
Async XLA Ops:
  0.7 74.4 %copy-start = (bf16[2,1024,512]{2,1,0:T(8,128)(2,1)S(1)}, bf16[2,1024,512]{2,1,0:T(8,128)(2,1)}, u32[]{:S(2)}) copy-start(bf16[2,1024,512]{2,1,0:T(8,128)(2,1)} %param.20) | copy-start | bytes 6291460
  3.9 8.7 %collective-permute-start.2 = (bf16[80,512]{1,0:T(8,128)(2,1)}, bf16[80,512]{1,0:T(8,128)(2,1)S(1)}, u32[]{:S(2)}, u32[]{:S(2)}) collective-permute-start(bf16[80,512]{1,0:T(8,128)(2,1)} %get-tuple-element.100), channel_id=1, source_target_pairs={{0,3},{1,2},{2,1},{3,0},{4,7},{5,6},{6,5},{7,4},{8,11},{9,10},{10,... | collective-permute-start | bytes 245768 | tf_op jit(solution)/shard_map/ppermute | solution.py:714
  5.4 7.5 %collective-permute-start.1 = (bf16[80,512]{1,0:T(8,128)(2,1)}, bf16[80,512]{1,0:T(8,128)(2,1)S(1)}, u32[]{:S(2)}, u32[]{:S(2)}) collective-permute-start(bf16[80,512]{1,0:T(8,128)(2,1)} %get-tuple-element.100), channel_id=1, source_target_pairs={{0,2},{1,3},{2,0},{3,1},{4,6},{5,7},{6,4},{7,5},{8,10},{9,11},{10,... | collective-permute-start | bytes 245768 | tf_op jit(solution)/shard_map/ppermute | solution.py:714
  6.5 7.3 %collective-permute-start = (bf16[80,512]{1,0:T(8,128)(2,1)}, bf16[80,512]{1,0:T(8,128)(2,1)S(1)}, u32[]{:S(2)}, u32[]{:S(2)}) collective-permute-start(bf16[80,512]{1,0:T(8,128)(2,1)} %get-tuple-element.100), channel_id=1, source_target_pairs={{0,1},{1,0},{2,3},{3,2},{4,5},{5,4},{6,7},{7,6},{8,9},{9,8},{10,11... | collective-permute-start | bytes 245768 | tf_op jit(solution)/shard_map/ppermute | solution.py:714
  9.2 18.9 %copy-start.2 = (bf16[512,512]{1,0:T(8,128)(2,1)}, bf16[512,512]{1,0:T(8,128)(2,1)S(1)}, u32[]{:S(2)}) copy-start(bf16[512,512]{1,0:T(8,128)(2,1)S(1)} %get-tuple-element.185.own_ref.refs_12_) | copy-start | bytes 1572868
  9.3 18.9 %copy-start.18 = (bf16[2,64,512]{2,1,0:T(8,128)(2,1)S(1)}, bf16[2,64,512]{2,1,0:T(8,128)(2,1)}, u32[]{:S(2)}) copy-start(bf16[2,64,512]{2,1,0:T(8,128)(2,1)} %get-tuple-element.97) | copy-start | bytes 393220
  14.0 8.4 %collective-permute-start.4 = (bf16[4,64,512]{2,1,0:T(8,128)(2,1)S(1)}, bf16[4,64,512]{2,1,0:T(8,128)(2,1)S(1)}, u32[]{:S(2)}, u32[]{:S(2)}) collective-permute-start(bf16[4,64,512]{2,1,0:T(8,128)(2,1)S(1)} %get-tuple-element.194), channel_id=1, source_target_pairs={{0,16},{4,20},{8,24},{12,28},{16,0},{20,4},{24,8},{28,12},{1,17},{... | collective-permute-start | bytes 786440 | tf_op jit(solution)/shard_map/ppermute | solution.py:714
  15.6 9.2 %collective-permute-start.3 = (bf16[4,64,512]{2,1,0:T(8,128)(2,1)S(1)}, bf16[4,64,512]{2,1,0:T(8,128)(2,1)S(1)}, u32[]{:S(2)}, u32[]{:S(2)}) collective-permute-start(bf16[4,64,512]{2,1,0:T(8,128)(2,1)S(1)} %get-tuple-element.194), channel_id=1, source_target_pairs={{0,8},{4,12},{8,0},{12,4},{16,24},{20,28},{24,16},{28,20},{1,9},{5... | collective-permute-start | bytes 786440 | tf_op jit(solution)/shard_map/ppermute | solution.py:714
  17.1 10.9 %collective-permute-start.5 = (bf16[4,64,512]{2,1,0:T(8,128)(2,1)S(1)}, bf16[4,64,512]{2,1,0:T(8,128)(2,1)S(1)}, u32[]{:S(2)}, u32[]{:S(2)}) collective-permute-start(bf16[4,64,512]{2,1,0:T(8,128)(2,1)S(1)} %get-tuple-element.194), channel_id=1, source_target_pairs={{0,24},{4,28},{8,16},{12,20},{16,8},{20,12},{24,0},{28,4},{1,25},{... | collective-permute-start | bytes 786440 | tf_op jit(solution)/shard_map/ppermute | solution.py:714
  28.1 23.1 %collective-permute-start.6 = (bf16[4,4,64,512]{3,2,1,0:T(8,128)(2,1)S(1)}, bf16[4,4,64,512]{3,2,1,0:T(8,128)(2,1)}, u32[]{:S(2)}, u32[]{:S(2)}) collective-permute-start(bf16[4,4,64,512]{3,2,1,0:T(8,128)(2,1)S(1)} %pad_maximum_fusion.1.near_ref.refs_9_), channel_id=1, source_target_pairs={{0,4},{4,0},{8,12},{12,8},{16,20},{20,16},{24,28},{28,24},{1,5},{5... | collective-permute-start | bytes 3145736 | tf_op jit(solution)/shard_map/ppermute | solution.py:714
  29.0 18.6 %all-to-all-start = ((bf16[4,2,64,512]{3,2,1,0:T(8,128)(2,1)}), bf16[4,2,64,512]{3,2,1,0:T(8,128)(2,1)}, u32[]{:S(2)}, u32[]{:S(2)}) async-start(bf16[4,2,64,512]{3,2,1,0:T(8,128)(2,1)} %broadcast_in_dim.2), calls=%async_computation | async-start | bytes 1048576 | tf_op jit(solution)/shard_map/all_to_all | solution.py:705
  47.6 16.0 %collective-permute-start.9 = (bf16[4,2,64,512]{3,2,1,0:T(8,128)(2,1)}, bf16[4,2,64,512]{3,2,1,0:T(8,128)(2,1)S(1)}, u32[]{:S(2)}, u32[]{:S(2)}) collective-permute-start(bf16[4,2,64,512]{3,2,1,0:T(8,128)(2,1)} %all-to-all-done), channel_id=1, source_target_pairs={{0,24},{4,28},{8,16},{12,20},{16,8},{20,12},{24,0},{28,4},{1,25},{... | collective-permute-start | bytes 1572872 | tf_op jit(solution)/shard_map/ppermute | solution.py:714
  50.2 23.3 %collective-permute-start.8 = (bf16[4,2,64,512]{3,2,1,0:T(8,128)(2,1)}, bf16[4,2,64,512]{3,2,1,0:T(8,128)(2,1)S(1)}, u32[]{:S(2)}, u32[]{:S(2)}) collective-permute-start(bf16[4,2,64,512]{3,2,1,0:T(8,128)(2,1)} %all-to-all-done), channel_id=1, source_target_pairs={{0,16},{4,20},{8,24},{12,28},{16,0},{20,4},{24,8},{28,12},{1,17},{... | collective-permute-start | bytes 1572872 | tf_op jit(solution)/shard_map/ppermute | solution.py:714
  50.7 23.0 %collective-permute-start.7 = (bf16[4,2,64,512]{3,2,1,0:T(8,128)(2,1)}, bf16[4,2,64,512]{3,2,1,0:T(8,128)(2,1)S(1)}, u32[]{:S(2)}, u32[]{:S(2)}) collective-permute-start(bf16[4,2,64,512]{3,2,1,0:T(8,128)(2,1)} %all-to-all-done), channel_id=1, source_target_pairs={{0,8},{4,12},{8,0},{12,4},{16,24},{20,28},{24,16},{28,20},{1,9},{5... | collective-permute-start | bytes 1572872 | tf_op jit(solution)/shard_map/ppermute | solution.py:714
  75.0 4.2 %collective-permute-start.10 = (bf16[4,4,2,64,512]{4,3,2,1,0:T(8,128)(2,1)S(1)}, bf16[4,4,2,64,512]{4,3,2,1,0:T(8,128)(2,1)S(1)}, u32[]{:S(2)}, u32[]{:S(2)}) collective-permute-start(bf16[4,4,2,64,512]{4,3,2,1,0:T(8,128)(2,1)S(1)} %pad_maximum_fusion.ffn_near_ref), channel_id=1, source_target_pairs={{0,4},{4,0},{8,12},{12,8},{16,20},{20,16},{24,28},{28,24},{1,5},{5... | collective-permute-start | bytes 6291464 | tf_op jit(solution)/shard_map/ppermute | solution.py:714
  91.5 19.5 %collective-permute-start.18 = (f32[4,32,128]{2,1,0:T(8,128)S(1)}, f32[4,32,128]{2,1,0:T(8,128)S(1)}, u32[]{:S(2)}, u32[]{:S(2)}) collective-permute-start(f32[4,32,128]{2,1,0:T(8,128)S(1)} %get-tuple-element.129), channel_id=1, source_target_pairs={{0,1},{1,0},{2,3},{3,2},{4,5},{5,4},{6,7},{7,6},{8,9},{9,8},{10,11... | collective-permute-start | bytes 196616 | tf_op jit(solution)/shard_map/ppermute | solution.py:714
  94.8 6.3 %collective-permute-start.11 = (bf16[64,512]{1,0:T(8,128)(2,1)S(1)}, bf16[64,512]{1,0:T(8,128)(2,1)S(1)}, u32[]{:S(2)}, u32[]{:S(2)}) collective-permute-start(bf16[64,512]{1,0:T(8,128)(2,1)S(1)} %get-tuple-element.119), channel_id=1, source_target_pairs={{0,4},{4,0},{8,12},{12,8},{16,20},{20,16},{24,28},{28,24},{1,5},{5... | collective-permute-start | bytes 196616 | tf_op jit(solution)/shard_map/ppermute | solution.py:714
  94.8 6.6 %collective-permute-start.12 = (bf16[64,512]{1,0:T(8,128)(2,1)S(1)}, bf16[64,512]{1,0:T(8,128)(2,1)S(1)}, u32[]{:S(2)}, u32[]{:S(2)}) collective-permute-start(bf16[64,512]{1,0:T(8,128)(2,1)S(1)} %get-tuple-element.120), channel_id=1, source_target_pairs={{0,8},{4,12},{8,0},{12,4},{16,24},{20,28},{24,16},{28,20},{1,9},{5... | collective-permute-start | bytes 196616 | tf_op jit(solution)/shard_map/ppermute | solution.py:714
  96.3 5.7 %collective-permute-start.13 = (bf16[64,512]{1,0:T(8,128)(2,1)S(1)}, bf16[64,512]{1,0:T(8,128)(2,1)S(1)}, u32[]{:S(2)}, u32[]{:S(2)}) collective-permute-start(bf16[64,512]{1,0:T(8,128)(2,1)S(1)} %get-tuple-element.121), channel_id=1, source_target_pairs={{0,12},{4,8},{8,4},{12,0},{16,28},{20,24},{24,20},{28,16},{1,13},{... | collective-permute-start | bytes 196616 | tf_op jit(solution)/shard_map/ppermute | solution.py:714
  96.7 7.0 %collective-permute-start.14 = (bf16[64,512]{1,0:T(8,128)(2,1)S(1)}, bf16[64,512]{1,0:T(8,128)(2,1)S(1)}, u32[]{:S(2)}, u32[]{:S(2)}) collective-permute-start(bf16[64,512]{1,0:T(8,128)(2,1)S(1)} %get-tuple-element.122), channel_id=1, source_target_pairs={{0,16},{4,20},{8,24},{12,28},{16,0},{20,4},{24,8},{28,12},{1,17},{... | collective-permute-start | bytes 196616 | tf_op jit(solution)/shard_map/ppermute | solution.py:714
  101.2 4.3 %collective-permute-start.15 = (bf16[64,512]{1,0:T(8,128)(2,1)S(1)}, bf16[64,512]{1,0:T(8,128)(2,1)S(1)}, u32[]{:S(2)}, u32[]{:S(2)}) collective-permute-start(bf16[64,512]{1,0:T(8,128)(2,1)S(1)} %get-tuple-element.123), channel_id=1, source_target_pairs={{0,20},{4,16},{8,28},{12,24},{16,4},{20,0},{24,12},{28,8},{1,21},{... | collective-permute-start | bytes 196616 | tf_op jit(solution)/shard_map/ppermute | solution.py:714
  101.4 17.5 %collective-permute-start.21 = (bf16[4,4,2,64,512]{4,3,2,1,0:T(8,128)(2,1)S(1)}, bf16[4,4,2,64,512]{4,3,2,1,0:T(8,128)(2,1)S(1)}, u32[]{:S(2)}, u32[]{:S(2)}) collective-permute-start(bf16[4,4,2,64,512]{4,3,2,1,0:T(8,128)(2,1)S(1)} %get-tuple-element.140), channel_id=1, source_target_pairs={{0,4},{4,0},{8,12},{12,8},{16,20},{20,16},{24,28},{28,24},{1,5},{5... | collective-permute-start | bytes 6291464 | tf_op jit(solution)/shard_map/ppermute | solution.py:714
  102.0 5.2 %collective-permute-start.16 = (bf16[64,512]{1,0:T(8,128)(2,1)S(1)}, bf16[64,512]{1,0:T(8,128)(2,1)S(1)}, u32[]{:S(2)}, u32[]{:S(2)}) collective-permute-start(bf16[64,512]{1,0:T(8,128)(2,1)S(1)} %get-tuple-element.124), channel_id=1, source_target_pairs={{0,24},{4,28},{8,16},{12,20},{16,8},{20,12},{24,0},{28,4},{1,25},{... | collective-permute-start | bytes 196616 | tf_op jit(solution)/shard_map/ppermute | solution.py:714
  103.7 5.3 %collective-permute-start.17 = (bf16[64,512]{1,0:T(8,128)(2,1)S(1)}, bf16[64,512]{1,0:T(8,128)(2,1)S(1)}, u32[]{:S(2)}, u32[]{:S(2)}) collective-permute-start(bf16[64,512]{1,0:T(8,128)(2,1)S(1)} %get-tuple-element.125), channel_id=1, source_target_pairs={{0,28},{4,24},{8,20},{12,16},{16,12},{20,8},{24,4},{28,0},{1,29},{... | collective-permute-start | bytes 196616 | tf_op jit(solution)/shard_map/ppermute | solution.py:714
  109.0 23.0 %collective-permute-start.20 = (bf16[8,64,512]{2,1,0:T(8,128)(2,1)S(1)}, bf16[8,64,512]{2,1,0:T(8,128)(2,1)S(1)}, u32[]{:S(2)}, u32[]{:S(2)}) collective-permute-start(bf16[8,64,512]{2,1,0:T(8,128)(2,1)S(1)} %bitcast_dynamic-update-slice_fusion.refs_0_), channel_id=1, source_target_pairs={{0,2},{1,3},{2,0},{3,1},{4,6},{5,7},{6,4},{7,5},{8,10},{9,11},{10,... | collective-permute-start | bytes 1572872 | tf_op jit(solution)/shard_map/ppermute | solution.py:714
  109.0 25.1 %collective-permute-start.19 = (bf16[8,64,512]{2,1,0:T(8,128)(2,1)S(1)}, bf16[8,64,512]{2,1,0:T(8,128)(2,1)S(1)}, u32[]{:S(2)}, u32[]{:S(2)}) collective-permute-start(bf16[8,64,512]{2,1,0:T(8,128)(2,1)S(1)} %bitcast_dynamic-update-slice_fusion.refs_0_), channel_id=1, source_target_pairs={{0,1},{1,0},{2,3},{3,2},{4,5},{5,4},{6,7},{7,6},{8,9},{9,8},{10,11... | collective-permute-start | bytes 1572872 | tf_op jit(solution)/shard_map/ppermute | solution.py:714
  143.4 22.5 %copy-start.15 = (s32[16]{0:T(128)S(1)}, s32[16]{0:T(128)}, u32[]{:S(2)}) copy-start(s32[16]{0:T(128)} %dealing.1) | copy-start | bytes 196
  147.0 25.5 %collective-permute-start.24 = (bf16[4,272,512]{2,1,0:T(8,128)(2,1)}, bf16[4,272,512]{2,1,0:T(8,128)(2,1)S(1)}, u32[]{:S(2)}, u32[]{:S(2)}) collective-permute-start(bf16[4,272,512]{2,1,0:T(8,128)(2,1)} %get-tuple-element.160), channel_id=1, source_target_pairs={{0,4},{4,0},{8,12},{12,8},{16,20},{20,16},{24,28},{28,24},{1,5},{5... | collective-permute-start | bytes 3342344 | tf_op jit(solution)/shard_map/ppermute | solution.py:714
  147.0 16.2 %collective-permute-start.22 = (bf16[8,64,512]{2,1,0:T(8,128)(2,1)S(1)}, bf16[8,64,512]{2,1,0:T(8,128)(2,1)S(1)}, u32[]{:S(2)}, u32[]{:S(2)}) collective-permute-start(bf16[8,64,512]{2,1,0:T(8,128)(2,1)S(1)} %bitcast_dynamic-update-slice_fusion.refs_0_), channel_id=1, source_target_pairs={{1,2},{2,1},{5,6},{6,5},{9,10},{10,9},{13,14},{14,13},{17,18},{18,... | collective-permute-start | bytes 1572872 | tf_op jit(solution)/shard_map/ppermute | solution.py:765
  150.3 14.2 %collective-permute-start.23 = (bf16[8,64,512]{2,1,0:T(8,128)(2,1)S(1)}, bf16[8,64,512]{2,1,0:T(8,128)(2,1)S(1)}, u32[]{:S(2)}, u32[]{:S(2)}) collective-permute-start(bf16[8,64,512]{2,1,0:T(8,128)(2,1)S(1)} %collective-permute-done.20.refs_2_), channel_id=1, source_target_pairs={{1,0},{2,3},{5,4},{6,7},{9,8},{10,11},{13,12},{14,15},{17,16},{18,... | collective-permute-start | bytes 1572872 | tf_op jit(solution)/shard_map/ppermute | solution.py:766
  151.7 22.6 %collective-permute-start.32 = (bf16[4,2,64,512]{3,2,1,0:T(8,128)(2,1)}, bf16[4,2,64,512]{3,2,1,0:T(8,128)(2,1)}, u32[]{:S(2)}, u32[]{:S(2)}) collective-permute-start(bf16[4,2,64,512]{3,2,1,0:T(8,128)(2,1)} %get-tuple-element.167), channel_id=1, source_target_pairs={{0,8},{4,12},{8,0},{12,4},{16,24},{20,28},{24,16},{28,20},{1,9},{5... | collective-permute-start | bytes 1572872 | tf_op jit(solution)/shard_map/ppermute | solution.py:714
  153.1 24.6 %collective-permute-start.33 = (bf16[4,2,64,512]{3,2,1,0:T(8,128)(2,1)}, bf16[4,2,64,512]{3,2,1,0:T(8,128)(2,1)}, u32[]{:S(2)}, u32[]{:S(2)}) collective-permute-start(bf16[4,2,64,512]{3,2,1,0:T(8,128)(2,1)} %get-tuple-element.168), channel_id=1, source_target_pairs={{0,16},{4,20},{8,24},{12,28},{16,0},{20,4},{24,8},{28,12},{1,17},{... | collective-permute-start | bytes 1572872 | tf_op jit(solution)/shard_map/ppermute | solution.py:714
  163.2 21.9 %collective-permute-start.34 = (bf16[4,2,64,512]{3,2,1,0:T(8,128)(2,1)}, bf16[4,2,64,512]{3,2,1,0:T(8,128)(2,1)}, u32[]{:S(2)}, u32[]{:S(2)}) collective-permute-start(bf16[4,2,64,512]{3,2,1,0:T(8,128)(2,1)} %get-tuple-element.169), channel_id=1, source_target_pairs={{0,24},{4,28},{8,16},{12,20},{16,8},{20,12},{24,0},{28,4},{1,25},{... | collective-permute-start | bytes 1572872 | tf_op jit(solution)/shard_map/ppermute | solution.py:714
  164.5 49.3 %collective-permute-start.29 = (bf16[512,512]{1,0:T(8,128)(2,1)}, bf16[512,512]{1,0:T(8,128)(2,1)S(1)}, u32[]{:S(2)}, u32[]{:S(2)}) collective-permute-start(bf16[512,512]{1,0:T(8,128)(2,1)} %get-tuple-element.165.refs_0_), channel_id=1, source_target_pairs={{0,2},{1,3},{2,0},{3,1},{4,6},{5,7},{6,4},{7,5},{8,10},{9,11},{10,... | collective-permute-start | bytes 1572872 | tf_op jit(solution)/shard_map/ppermute | solution.py:714
  168.1 97.8 %all-to-all-start.1 = ((bf16[8,2,2,64,512]{4,3,2,1,0:T(8,128)(2,1)}), bf16[8,2,2,64,512]{4,3,2,1,0:T(8,128)(2,1)}, u32[]{:S(2)}, u32[]{:S(2)}) async-start(bf16[8,2,2,64,512]{4,3,2,1,0:T(8,128)(2,1)} %shard_map.323), calls=%async_computation.1 | async-start | bytes 4194304 | tf_op jit(solution)/shard_map/all_to_all | solution.py:705
  172.5 41.4 %collective-permute-start.28 = (bf16[512,512]{1,0:T(8,128)(2,1)}, bf16[512,512]{1,0:T(8,128)(2,1)S(1)}, u32[]{:S(2)}, u32[]{:S(2)}) collective-permute-start(bf16[512,512]{1,0:T(8,128)(2,1)} %get-tuple-element.165.refs_0_), channel_id=1, source_target_pairs={{0,1},{1,0},{2,3},{3,2},{4,5},{5,4},{6,7},{7,6},{8,9},{9,8},{10,11... | collective-permute-start | bytes 1572872 | tf_op jit(solution)/shard_map/ppermute | solution.py:714
  174.3 33.3 %collective-permute-start.25 = (bf16[272,512]{1,0:T(8,128)(2,1)S(1)}, bf16[272,512]{1,0:T(8,128)(2,1)S(1)}, u32[]{:S(2)}, u32[]{:S(2)}) collective-permute-start(bf16[272,512]{1,0:T(8,128)(2,1)S(1)} %get-tuple-element.181), channel_id=1, source_target_pairs={{0,8},{4,12},{8,0},{12,4},{16,24},{20,28},{24,16},{28,20},{1,9},{5... | collective-permute-start | bytes 835592 | tf_op jit(solution)/shard_map/ppermute | solution.py:714
  177.7 35.0 %collective-permute-start.27 = (bf16[272,512]{1,0:T(8,128)(2,1)S(1)}, bf16[272,512]{1,0:T(8,128)(2,1)S(1)}, u32[]{:S(2)}, u32[]{:S(2)}) collective-permute-start(bf16[272,512]{1,0:T(8,128)(2,1)S(1)} %get-tuple-element.182), channel_id=1, source_target_pairs={{0,24},{4,28},{8,16},{12,20},{16,8},{20,12},{24,0},{28,4},{1,25},{... | collective-permute-start | bytes 835592 | tf_op jit(solution)/shard_map/ppermute | solution.py:714
  185.1 27.6 %collective-permute-start.26 = (bf16[272,512]{1,0:T(8,128)(2,1)S(1)}, bf16[272,512]{1,0:T(8,128)(2,1)S(1)}, u32[]{:S(2)}, u32[]{:S(2)}) collective-permute-start(bf16[272,512]{1,0:T(8,128)(2,1)S(1)} %get-tuple-element.183), channel_id=1, source_target_pairs={{0,16},{4,20},{8,24},{12,28},{16,0},{20,4},{24,8},{28,12},{1,17},{... | collective-permute-start | bytes 835592 | tf_op jit(solution)/shard_map/ppermute | solution.py:714
  213.9 8.3 %collective-permute-start.35 = (bf16[208,512]{1,0:T(8,128)(2,1)S(1)}, bf16[208,512]{1,0:T(8,128)(2,1)S(1)}, u32[]{:S(2)}, u32[]{:S(2)}) collective-permute-start(bf16[208,512]{1,0:T(8,128)(2,1)S(1)} %get-tuple-element.203), channel_id=1, source_target_pairs={{0,1},{1,0},{2,3},{3,2},{4,5},{5,4},{6,7},{7,6},{8,9},{9,8},{10,11... | collective-permute-start | bytes 638984 | tf_op jit(solution)/shard_map/ppermute | solution.py:714
  214.0 17.2 %collective-permute-start.36 = (bf16[208,512]{1,0:T(8,128)(2,1)S(1)}, bf16[208,512]{1,0:T(8,128)(2,1)S(1)}, u32[]{:S(2)}, u32[]{:S(2)}) collective-permute-start(bf16[208,512]{1,0:T(8,128)(2,1)S(1)} %get-tuple-element.204), channel_id=1, source_target_pairs={{0,2},{1,3},{2,0},{3,1},{4,6},{5,7},{6,4},{7,5},{8,10},{9,11},{10,... | collective-permute-start | bytes 638984 | tf_op jit(solution)/shard_map/ppermute | solution.py:714
  216.7 18.4 %collective-permute-start.37 = (bf16[208,512]{1,0:T(8,128)(2,1)S(1)}, bf16[208,512]{1,0:T(8,128)(2,1)S(1)}, u32[]{:S(2)}, u32[]{:S(2)}) collective-permute-start(bf16[208,512]{1,0:T(8,128)(2,1)S(1)} %pad_maximum_fusion.7), channel_id=1, source_target_pairs={{0,3},{1,2},{2,1},{3,0},{4,7},{5,6},{6,5},{7,4},{8,11},{9,10},{10,... | collective-permute-start | bytes 638984 | tf_op jit(solution)/shard_map/ppermute | solution.py:714
  235.3 8.1 %collective-permute-start.40 = (bf16[3,64,512]{2,1,0:T(8,128)(2,1)S(1)}, bf16[3,64,512]{2,1,0:T(8,128)(2,1)S(1)}, u32[]{:S(2)}, u32[]{:S(2)}) collective-permute-start(bf16[3,64,512]{2,1,0:T(8,128)(2,1)S(1)} %bitcast.118), channel_id=1, source_target_pairs={{0,24},{4,28},{8,16},{12,20},{16,8},{20,12},{24,0},{28,4},{1,25},{... | collective-permute-start | bytes 589832 | tf_op jit(solution)/shard_map/ppermute | solution.py:714
  236.7 8.6 %collective-permute-start.39 = (bf16[3,64,512]{2,1,0:T(8,128)(2,1)S(1)}, bf16[3,64,512]{2,1,0:T(8,128)(2,1)S(1)}, u32[]{:S(2)}, u32[]{:S(2)}) collective-permute-start(bf16[3,64,512]{2,1,0:T(8,128)(2,1)S(1)} %bitcast.119), channel_id=1, source_target_pairs={{0,16},{4,20},{8,24},{12,28},{16,0},{20,4},{24,8},{28,12},{1,17},{... | collective-permute-start | bytes 589832 | tf_op jit(solution)/shard_map/ppermute | solution.py:714
  237.8 7.5 %collective-permute-start.38 = (bf16[3,64,512]{2,1,0:T(8,128)(2,1)S(1)}, bf16[3,64,512]{2,1,0:T(8,128)(2,1)S(1)}, u32[]{:S(2)}, u32[]{:S(2)}) collective-permute-start(bf16[3,64,512]{2,1,0:T(8,128)(2,1)S(1)} %bitcast.120), channel_id=1, source_target_pairs={{0,8},{4,12},{8,0},{12,4},{16,24},{20,28},{24,16},{28,20},{1,9},{5... | collective-permute-start | bytes 589832 | tf_op jit(solution)/shard_map/ppermute | solution.py:714
  245.4 23.5 %collective-permute-start.41 = (bf16[4,3,64,512]{3,2,1,0:T(8,128)(2,1)S(1)}, bf16[4,3,64,512]{3,2,1,0:T(8,128)(2,1)}, u32[]{:S(2)}, u32[]{:S(2)}) collective-permute-start(bf16[4,3,64,512]{3,2,1,0:T(8,128)(2,1)S(1)} %pad_maximum_fusion.2.near_ref), channel_id=1, source_target_pairs={{0,4},{4,0},{8,12},{12,8},{16,20},{20,16},{24,28},{28,24},{1,5},{5... | collective-permute-start | bytes 2359304 | tf_op jit(solution)/shard_map/ppermute | solution.py:714
  245.5 17.8 %collective-permute-start.31 = (bf16[512,512]{1,0:T(8,128)(2,1)S(1)}, bf16[512,512]{1,0:T(8,128)(2,1)S(1)}, u32[]{:S(2)}, u32[]{:S(2)}) collective-permute-start(bf16[512,512]{1,0:T(8,128)(2,1)S(1)} %collective-permute-done.29.refs_2_), channel_id=1, source_target_pairs={{1,0},{2,3},{5,4},{6,7},{9,8},{10,11},{13,12},{14,15},{17,16},{18,... | collective-permute-start | bytes 1572872 | tf_op jit(solution)/shard_map/ppermute | solution.py:766
  246.8 16.4 %collective-permute-start.30 = (bf16[512,512]{1,0:T(8,128)(2,1)}, bf16[512,512]{1,0:T(8,128)(2,1)S(1)}, u32[]{:S(2)}, u32[]{:S(2)}) collective-permute-start(bf16[512,512]{1,0:T(8,128)(2,1)} %get-tuple-element.165.refs_0_), channel_id=1, source_target_pairs={{1,2},{2,1},{5,6},{6,5},{9,10},{10,9},{13,14},{14,13},{17,18},{18,... | collective-permute-start | bytes 1572872 | tf_op jit(solution)/shard_map/ppermute | solution.py:765
  (18 other events, 148.5 us)

commit v4 on v3

--- a/solution.py
+++ b/solution.py
@@ -476,19 +476,31 @@
         give_out(info, near_ref, far_ref, z ^ line, 1, down_s)
 
 
-def attend_back_kernel(first_pair, *refs):
-    final = first_pair > 0
-    info, lengths, numer_ref, gtotal_ref, exchange_ref = refs[:5]
-    q_ref, k_ref, v_ref, prob_ref, near_ref, far_ref = refs[5:11]
-    refs = refs[11:]
-    if final:
-        before_ref, own_ref, gain_ref, grad_hidden_ref, grads_ref, b_qv_ref, grad_tokens_ref, vector_ref = refs[:8]
-        refs = refs[8:]
-    else:
-        grads_ref, b_qv_ref, acc_ref = refs[:3]
-        refs = refs[3:]
-    coarse_s, left_s, grad_s, full_s = refs[:4]
-    acc_s = refs[4] if final else acc_ref
+def attend_back_kernel(
+    info,
+    lengths,
+    numer_ref,
+    gtotal_ref,
+    exchange_ref,
+    q_ref,
+    k_ref,
+    v_ref,
+    prob_ref,
+    near_ref,
+    far_ref,
+    own_ref,
+    gain_ref,
+    grad_hidden_ref,
+    grads_ref,
+    b_qv_ref,
+    grad_tokens_ref,
+    vector_ref,
+    coarse_s,
+    left_s,
+    grad_s,
+    full_s,
+    acc_s,
+):
     pairs, rows = numer_ref.shape[0], numer_ref.shape[1]
     tiles = 2 * rows // TILE
     half_tiles = rows // TILE
@@ -560,54 +572,51 @@
         sums = jnp.sum(grads_ref[p].astype(F32), axis=0, keepdims=True)
         b_qv_ref[p, 0:1, :] = sums[:, :TILE]
         b_qv_ref[p, 1:2, :] = sums[:, 2 * TILE :]
-        acc_s[...] += mm_nt(grads_ref[p], full_s[first_pair + p, :, : 3 * TILE])
+        acc_s[...] += mm_nt(grads_ref[p], full_s[p, :, : 3 * TILE])
         return carry
 
-    acc_s[...] = before_ref[...] if final else jnp.zeros_like(acc_s)
+    acc_s[...] = jnp.zeros_like(acc_s)
     lax.fori_loop(0, pairs, one_pair, 0)
-    if final:
-        unit, inverse = unit_rows(own_ref[...].astype(F32))
-        grad_normed = acc_s[...]
-        vector_ref[0:1, :] = jnp.sum(grad_normed * unit, axis=0, keepdims=True)
-        vector_ref[1:2, :] = jnp.sum(grad_normed, axis=0, keepdims=True)
-        grad_tokens_ref[...] = (
-            grad_hidden_ref[...] + norm_back(grad_normed, unit, inverse, gain_ref[...])
-        ).astype(BF16)
+    unit, inverse = unit_rows(own_ref[...].astype(F32))
+    grad_normed = acc_s[...]
+    vector_ref[0:1, :] = jnp.sum(grad_normed * unit, axis=0, keepdims=True)
+    vector_ref[1:2, :] = jnp.sum(grad_normed, axis=0, keepdims=True)
+    grad_tokens_ref[...] = (
+        grad_hidden_ref[...] + norm_back(grad_normed, unit, inverse, gain_ref[...])
+    ).astype(BF16)
 
 
 def attend_grads_kernel(
     info,
     normed_ref,
-    low_ref,
-    high_ref,
+    grads_ref,
     grad_hidden_ref,
     mixed_ref,
     vec_two_ref,
     vec_up_ref,
     vec_one_ref,
-    qv_low_ref,
-    qv_high_ref,
+    b_qv_ref,
     near_ref,
     far_ref,
     both_s,
 ):
-    core, plane, line = info[3], info[4], info[5]
-    half, pairs = low_ref.shape[0], mixed_ref.shape[0]
+    core, line = info[3], info[5]
+    pairs = mixed_ref.shape[0]
     dp = 2 * near_ref.shape[0]
     chunk = both_s.shape[0] // dp
     for z in range(pairs):
-        grads = low_ref[z] if z < half else high_ref[z - half]
+        grads = grads_ref[z]
         both_s[:, : 3 * TILE] = mm_tn(normed_ref[...], grads).astype(BF16)
         both_s[:, 3 * TILE :] = mm_tn(grad_hidden_ref[...], mixed_ref[z]).astype(BF16)
         for far, ref in enumerate((near_ref, far_ref)):
             for o in range(ref.shape[0]):
-                at = ((o ^ plane) * 2 + (far ^ core)) * chunk
+                at = (o * 2 + (far ^ core)) * chunk
                 at = pl.ds(pl.multiple_of(at, chunk), chunk)
                 to = pl.ds(pl.multiple_of((z ^ line) * chunk, chunk), chunk)
                 ref[o, to, :] = both_s[at, :]
     vectors = [vec_two_ref[...]] + [vec_up_ref[z] for z in range(pairs)] + [vec_one_ref[...]]
     for row in range(2):
-        parts = [ref[p, row : row + 1, :] for ref in (qv_low_ref, qv_high_ref) for p in range(half)]
+        parts = [b_qv_ref[p, row : row + 1, :] for p in range(pairs)]
         vectors.append(jnp.concatenate(parts, axis=1))
     vectors = jnp.concatenate(vectors, axis=0)
     blank = jnp.zeros((near_ref.shape[1] - pairs * chunk - vectors.shape[0], vectors.shape[1]), F32)
@@ -677,28 +686,18 @@
 SMEM_SPEC = pl.BlockSpec(memory_space=pltpu.SMEM)
 
 
-def part_of(array, half):
-    block = (array.shape[0] // 2,) + array.shape[1:]
-    return array, pl.BlockSpec(
-        block, lambda i: (half,) + (0,) * (len(block) - 1), pipeline_mode=pl.Buffered(1)
-    )
-
-
 def call(kernel, outs, scalars, args, scratch=(), limit=16, long=False):
-    args = [arg if isinstance(arg, tuple) else (arg, VMEM_SPEC) for arg in args]
-    grid = (1,) if any(spec is not VMEM_SPEC for _, spec in args) else ()
     return pl.pallas_call(
         kernel,
         out_shape=[jax.ShapeDtypeStruct(shape, dtype) for shape, dtype in outs],
-        grid=grid,
-        in_specs=[SMEM_SPEC] * len(scalars) + [spec for _, spec in args],
+        in_specs=[SMEM_SPEC] * len(scalars) + [VMEM_SPEC] * len(args),
         out_specs=[VMEM_SPEC] * len(outs),
         scratch_shapes=list(scratch),
         compiler_params=pltpu.CompilerParams(vmem_limit_bytes=limit << 20),
         cost_estimate=pl.CostEstimate(
             flops=10**10 if long else 1, transcendentals=0, bytes_accessed=1
         ),
-    )(*scalars, *[arg for arg, _ in args])
+    )(*scalars, *args)
 
 
 def exchange(pieces, axis, groups=None):
@@ -715,7 +714,7 @@
 
 
 def after(value, *others):
-    return lax.optimization_barrier((value, *others))[0]
+    return lax.optimization_barrier((value, others))[0]
 
 
 def total_of(pieces):
@@ -808,11 +807,12 @@
     )
     attn_line = near_line(attn_piece)
     normed_one, *attn_line = lax.optimization_barrier((normed_one, *attn_line))
-    attn_near = jnp.stack(plane_pieces(jnp.stack([piece[:chunk] for piece in attn_line])))
     biases = jnp.stack([piece[chunk:] for piece in attn_line])
     ffn_line = gather(ffn_piece, "tensor", nt)
+    attn_pieces = plane_pieces(jnp.stack([piece[:chunk] for piece in attn_line]))
+    attn_near = jnp.stack(after(tuple(attn_pieces), ffn_line))
     attn_w = attn_near, swap(attn_near, "dp", 1)
-    ffn_pieces = plane_pieces(after(ffn_line, attn_near))
+    ffn_pieces = plane_pieces(after(ffn_line, attn_pieces[1]))
     normed_one = after(normed_one, ffn_line)
 
     mixed, mixed_wide, total, q, k, v, prob = call(
@@ -875,75 +875,60 @@
     )
     ffn_far = swap(ffn_grads[1], "dp", 1)
 
-    back_scratch = [
-        pltpu.VMEM((rows, 2 * TILE), F32),
-        pltpu.VMEM((2 * rows, 2 * TILE), BF16),
-        pltpu.VMEM((2 * rows, 3 * TILE), F32),
-        attn_full,
-    ]
-
-    def back_args(half):
-        return [part_of(each, half) for each in (numer, gtotal, swapped, q, k, v, prob)] + [*attn_w]
-
     def core_sums(near, far):
         return [total_of([near[o], far[o]]) for o in range(outer)]
 
     def plane_parts(pieces):
         return [pieces[0]] + [swap(pieces[o], "dp", 2 * o) for o in range(1, outer)]
 
-    chunks = line_first(jnp.stack(chunks))
-    gtotal, chunks[0] = lax.optimization_barrier((gtotal, chunks[0]))
-    grads_low, qv_low, acc = call(
-        functools.partial(attend_back_kernel, 0),
-        [((nt // 2, rows, 3 * TILE), BF16), ((nt // 2, 2, TILE), F32), ((rows, width), F32)],
-        [info, lengths],
-        back_args(0),
-        scratch=back_scratch,
-        limit=20,
-        long=True,
-    )
-    ffn_parts = core_sums(after(ffn_grads[0], acc), ffn_far)
-    acc, chunks[1], chunks[2], *ffn_parts = lax.optimization_barrier(
-        (acc, chunks[1], chunks[2], *ffn_parts)
-    )
-    chunks = line_second(chunks)
+    ffn_parts = core_sums(ffn_grads[0], ffn_far)
+    gtotal, chunks, ffn_parts, swapped = lax.optimization_barrier(
+        (gtotal, jnp.stack(chunks), ffn_parts, swapped)
+    )
+    chunks = line_first(chunks)
     ffn_parts = plane_parts(ffn_parts)
-    grads_high, qv_high, grad_low, vec_one = call(
-        functools.partial(attend_back_kernel, nt // 2),
+    qkv_grads, vec_qv, grad_low, vec_one = call(
+        attend_back_kernel,
         [
-            ((nt // 2, rows, 3 * TILE), BF16),
-            ((nt // 2, 2, TILE), F32),
+            ((nt, rows, 3 * TILE), BF16),
+            ((nt, 2, TILE), F32),
             ((rows, width), BF16),
             ((2, width), F32),
         ],
         [info, lengths],
-        back_args(1) + [acc, own, row(ln1_gain), grad_hidden],
-        scratch=back_scratch + [pltpu.VMEM((rows, width), F32)],
+        [numer, gtotal, swapped, q, k, v, prob, *attn_w]
+        + [own, row(ln1_gain), grad_hidden],
+        scratch=[
+            pltpu.VMEM((rows, 2 * TILE), F32),
+            pltpu.VMEM((2 * rows, 2 * TILE), BF16),
+            pltpu.VMEM((2 * rows, 3 * TILE), F32),
+            attn_full,
+            pltpu.VMEM((rows, width), F32),
+        ],
         limit=20,
         long=True,
     )
-    grad_low, grad_hidden_low = lax.optimization_barrier((grad_low, grad_hidden_low))
     row_pieces = line_first(grad_low)
     attn_near, attn_far = call(
         attend_grads_kernel,
         [((outer, nt * chunk + 16, 4 * TILE), BF16)] * 2,
         [info],
-        [normed_one, grads_low, grads_high, grad_hidden_low, mixed]
-        + [vec_two, vec_up, vec_one, qv_low, qv_high],
+        [normed_one, qkv_grads, grad_hidden_low, mixed, vec_two, vec_up, vec_one, vec_qv],
         scratch=[pltpu.VMEM((width, 4 * TILE), BF16)],
     )
-    chunks[3], chunks[4], attn_near = lax.optimization_barrier((chunks[3], chunks[4], attn_near))
+    attn_far, chunks, ffn_parts = lax.optimization_barrier((attn_far, chunks, ffn_parts))
+    attn_far = swap(attn_far, "dp", 1)
     (dealt,) = call(
         deal_kernel,
         [((dp, seq_dev, nt // seq_dev, piece, width), BF16)],
         [info, dealing],
-        chunks,
+        line_second(chunks),
         scratch=[pltpu.VMEM((nt, dp, piece, width), BF16)],
     )
     dealt = exchange(dealt, "dp")
-    attn_parts = core_sums(attn_near, swap(attn_far, "dp", 1))
-    attn_parts = total_of(plane_parts(attn_parts))
-    attn_parts, *row_pieces = lax.optimization_barrier((attn_parts, *row_pieces))
+    attn_parts = exchange(total_of([attn_near, attn_far]), "dp", planes)
+    attn_parts = total_of(list(attn_parts))
+    attn_parts, row_pieces = lax.optimization_barrier((attn_parts, row_pieces))
     ffn_parts = total_of(ffn_parts)
     grads = [
         jnp.concatenate(
@@ -956,6 +941,7 @@
     vectors = grads[3 * chunk :].astype(F32)
     row_pieces = line_second(row_pieces)
     near = jnp.stack(plane_pieces(grads[: 3 * chunk].reshape(3, chunk, width)))
+    near = after(near, dealt)
     grads = near, swap(near, "dp", 1)
     g_up, g_down, g_query, g_key, g_value, g_out = call(
         place_grads_kernel,

time: 273 us -> 233 us (0.85)
  waiting for transfers between devices: 131 us -> 99.6 us
  Pallas kernels: 59 us -> 50.4 us
  starting transfers between devices: 66.1 us -> 57.6 us
  local copies, waits for them, and re-layouts: 7.91 us -> 12.4 us
  other arithmetic: 6.68 us -> 10.7 us
    ppermute x38 -> x35, waiting for transfers between devices: 99.8 us -> 70.7 us  [swap(): return lax.ppermute(piece, axis, [(i, i ^ distance) for i in range(size)])]
    ppermute x38 -> x35, starting transfers between devices: 46.1 us -> 35.8 us  [swap(): return lax.ppermute(piece, axis, [(i, i ^ distance) for i in range(size)])]
    all_to_all x2 -> x3, waiting for transfers between devices: 10.1 us -> 0.01 us  [exchange(): lax.all_to_all(pieces, axis, 0, 0, tiled=True, axis_index_groups=groups)]
    pallas_call x12 -> x11, Pallas kernels: 56.5 us -> 48 us  [call(): pl.pallas_call(kernel, out_shape=[jax.ShapeDtypeStruct(shape, dtype) for...]
    ppermute x2, waiting for transfers between devices: 20.9 us -> 28.9 us  [line_second(): three = lax.ppermute(after(piece, two), 'tensor', [(1, 2), (2, 1)])]
    all_to_all x2 -> x3, starting transfers between devices: 10.7 us -> 14.2 us  [exchange(): lax.all_to_all(pieces, axis, 0, 0, tiled=True, axis_index_groups=groups)]
  transfers between devices with their start and end apart: 44 -> 42, of which waited for: 26 -> 22; matrix products, arithmetic and copies ran while one was open for 4% -> 7% of each run, Pallas kernels for 11% -> 14%
where the time goes in v4:
time: 233 us; the launch traced here: 232 us
  waiting for transfers between devices  99.6 us (43%)
  starting transfers between devices  57.6 us (25%)
  Pallas kernels  50.4 us (22%)
  local copies, waits for them, and re-layouts  12.4 us (5%)
  other arithmetic  10.7 us (5%)
    ppermute x35, waiting for transfers between devices, swap(): return lax.ppermute(piece, axis, [(i, i ^ distance) for i in range(size)])  70.7 us
    pallas_call x11, Pallas kernels, call(): pl.pallas_call(kernel, out_shape=[jax.ShapeDtypeStruct(shape, dtype) for...  48 us
    ppermute x35, starting transfers between devices, swap(): return lax.ppermute(piece, axis, [(i, i ^ distance) for i in range(size)])  35.8 us
    ppermute x2, waiting for transfers between devices, line_second(): three = lax.ppermute(after(piece, two), 'tensor', [(1, 2), (2, 1)])  28.9 us
    all_to_all x3, starting transfers between devices, exchange(): lax.all_to_all(pieces, axis, 0, 0, tiled=True, axis_index_groups=groups)  14.2 us
    convert_element_type x4, other arithmetic, total_of(): functools.reduce(jnp.add, [piece.astype(F32) for piece in pieces])  5.02 us
    ppermute x2, starting transfers between devices, line_second(): three = lax.ppermute(after(piece, two), 'tensor', [(1, 2), (2, 1)])  4.87 us
  transfers between devices with their start and end apart: 42, of which 22 were waited for; matrix products, arithmetic and copies ran while one was open for 7% of the time, Pallas kernels for 14%

profile of v4, /device:TPU:8, one launch (start us, length us, event | category | flops | bytes accessed | tf_op | source)
XLA Modules:
  0.0 231.9 jit_solution(8657745916789825055)
XLA Ops:
  1.3 2.4 %shard_map.315 = (bf16[80,512]{1,0:T(8,128)(2,1)}, bf16[2,64,512]{2,1,0:T(8,128)(2,1)}) custom-call(s32[6]{0:T(128)} %stack.126.info, bf16[512,128]{1,0:T(8,128)(2,1)} %q_ref.1, bf16[512,128]{1,0:T(8,128)(2,1)} %k_ref.1, bf16[512,128]{1,0:T(8,128)(2,1)} %v_ref.1, bf16[128,512]{1,0:T(8,128)(2,1)} %o_ref.1, bf16[512,512]{1,0:T(8,128)(2,1)} %up_ref.1, ...), custom_call_target="tpu_custom_call" | custom-call | tf_op jit(solution)/shard_map/pallas_call | solution.py:777
  3.7 1.6 collective-permute-start.2
  6.5 1.4 collective-permute-start
  7.9 1.7 broadcast_in_dim.2
  9.6 5.8 %all-to-all-start = ((bf16[4,2,64,512]{3,2,1,0:T(8,128)(2,1)}), bf16[4,2,64,512]{3,2,1,0:T(8,128)(2,1)}, u32[]{:S(2)}, u32[]{:S(2)}) async-start(bf16[4,2,64,512]{3,2,1,0:T(8,128)(2,1)} %broadcast_in_dim.2), calls=%async_computation | async-start | bytes 1048576 | tf_op jit(solution)/shard_map/all_to_all | solution.py:704
  20.6 2.4 %collective-permute-start.5 = (bf16[4,64,512]{2,1,0:T(8,128)(2,1)}, bf16[4,64,512]{2,1,0:T(8,128)(2,1)}, u32[]{:S(2)}, u32[]{:S(2)}) collective-permute-start(bf16[4,64,512]{2,1,0:T(8,128)(2,1)} %pad_maximum_fusion.6), channel_id=1, source_target_pairs={{0,24},{4,28},{8,16},{12,20},{16,8},{20,12},{24,0},{28,4},{1,25},{... | collective-permute-start | bytes 786440 | tf_op jit(solution)/shard_map/ppermute | solution.py:713
  24.1 7.0 %collective-permute-done.5 = bf16[4,64,512]{2,1,0:T(8,128)(2,1)} collective-permute-done((bf16[4,64,512]{2,1,0:T(8,128)(2,1)}, bf16[4,64,512]{2,1,0:T(8,128)(2,1)}, u32[]{:S(2)}, u32[]{:S(2)}) %collective-permute-start.5) | collective-permute-done | bytes 262176 | tf_op jit(solution)/shard_map/ppermute | solution.py:713
  31.1 3.0 %collective-permute-done.4 = bf16[4,64,512]{2,1,0:T(8,128)(2,1)} collective-permute-done((bf16[4,64,512]{2,1,0:T(8,128)(2,1)}, bf16[4,64,512]{2,1,0:T(8,128)(2,1)}, u32[]{:S(2)}, u32[]{:S(2)}) %collective-permute-start.4) | collective-permute-done | bytes 262176 | tf_op jit(solution)/shard_map/ppermute | solution.py:713
  37.8 1.7 collective-permute-start.9
  41.3 7.8 %shard_map.316 = (bf16[4,512,128]{2,1,0:T(8,128)(2,1)S(1)}, f32[4,512,128]{2,1,0:T(8,128)S(1)}, f32[4,512,128]{2,1,0:T(8,128)S(1)}, bf16[4,1024,128]{2,1,0:T(8,1...) custom-call(s32[6]{0:T(128)S(1)} %copy-done.8, ...), custom_call_target="tpu_custom_call" | custom-call | flops 10000000000 | bytes 1 | tf_op jit(solution)/shard_map/pallas_call | solution.py:690
  49.1 4.6 %collective-permute-done.9 = bf16[4,2,64,512]{3,2,1,0:T(8,128)(2,1)S(1)} collective-permute-done((bf16[4,2,64,512]{3,2,1,0:T(8,128)(2,1)}, bf16[4,2,64,512]{3,2,1,0:T(8,128)(2,1)S(1)}, u32[]{:S(2)}, u32[]{:S(2)}) %collective-permute-start.9) | collective-permute-done | bytes 524320 | tf_op jit(solution)/shard_map/ppermute | solution.py:713
  53.7 10.8 %collective-permute-done.8 = bf16[4,2,64,512]{3,2,1,0:T(8,128)(2,1)S(1)} collective-permute-done((bf16[4,2,64,512]{3,2,1,0:T(8,128)(2,1)}, bf16[4,2,64,512]{3,2,1,0:T(8,128)(2,1)S(1)}, u32[]{:S(2)}, u32[]{:S(2)}) %collective-permute-start.8) | collective-permute-done | bytes 524320 | tf_op jit(solution)/shard_map/ppermute | solution.py:713
  66.0 4.1 %collective-permute-done.10.ffn_far_ref = bf16[4,4,2,64,512]{4,3,2,1,0:T(8,128)(2,1)S(1)} collective-permute-done((bf16[4,4,2,64,512]{4,3,2,1,0:T(8,128)(2,1)S(1)}, bf16[4,4,2,64,512]{4,3,2,1,0:T(8,128)(2,1)S(1)}, u32[]{:S(2)}, u32[]{:S(2)}) %collective-permute-start.10) | collective-permute-done | bytes 2097184 | tf_op jit(solution)/shard_map/ppermute | solution.py:713
  70.1 5.3 %shard_map.317 = (f32[512,512]{1,0:T(8,128)S(1)}, bf16[512,512]{1,0:T(8,128)(2,1)S(1)}, bf16[4,512,512]{2,1,0:T(8,128)(2,1)S(1)}, bf16[4,512,512]{2,1,0:T(8,128)...) custom-call(s32[6]{0:T(128)S(1)} %copy-done.8, ...), custom_call_target="tpu_custom_call" | custom-call | flops 1 | bytes 1 | tf_op jit(solution)/shard_map/pallas_call | solution.py:690
  75.4 5.6 %shard_map.318 = (bf16[4,512,512]{2,1,0:T(8,128)(2,1)S(1)}, f32[512,512]{1,0:T(8,128)S(1)}, bf16[512,512]{1,0:T(8,128)(2,1)S(1)}, f32[4,512,128]{2,1,0:T(8,128)S...) custom-call(s32[6]{0:T(128)S(1)} %copy-done.8, ...), custom_call_target="tpu_custom_call" | custom-call | flops 1 | bytes 1 | tf_op jit(solution)/shard_map/pallas_call | solution.py:690
  81.0 3.1 %shard_map.319 = (bf16[4,4,2,64,512]{4,3,2,1,0:T(8,128)(2,1)S(1)}, bf16[4,4,2,64,512]{4,3,2,1,0:T(8,128)(2,1)S(1)}) custom-call(s32[6]{0:T(128)S(1)} %copy-done.8, bf16[512,512]{1,0:T(8,128)(2,1)S(1)} %get-tuple-element.133.normed_ref, bf16[4,512,512]{2,1,0:T(8,128)(2,1)S(1)} %get-tuple-element.134.act_ref, ...), custom_call_target="tpu_custom_call" | custom-call | flops 1 | bytes 1 | tf_op jit(solution)/shard_map/pallas_call | solution.py:690
  84.6 1.5 collective-permute-start.12
  86.4 1.9 collective-permute-done.11
  88.4 1.4 collective-permute-start.14
  90.2 1.7 collective-permute-start.16
  94.2 1.8 collective-permute-done.16
  96.0 1.9 collective-permute-done.17
  97.9 1.8 fusion.3
  99.7 2.1 collective-permute-start.21
  106.2 14.0 %shard_map.320 = (bf16[4,512,384]{2,1,0:T(8,128)(2,1)S(1)}, f32[4,2,128]{2,1,0:T(2,128)S(1)}, bf16[512,512]{1,0:T(8,128)(2,1)S(1)}, f32[2,512]{1,0:T(2,128)S(1)}) custom-call(s32[6]{0:T(128)S(1)} %copy-done.8, s32[16]{0:T(128)S(1)} %copy-done.15, f32[4,512,128]{2,1,0:T(8,128)S(1)} %get-tuple-element.123.numer_ref, ...), custom_call_target="tpu_custom_call" | custom-call | flops 10000000000 | bytes 1 | tf_op jit(solution)/shard_map/pallas_call | solution.py:690
  120.2 2.5 %shard_map.321 = (bf16[4,272,512]{2,1,0:T(8,128)(2,1)S(1)}, bf16[4,272,512]{2,1,0:T(8,128)(2,1)S(1)}) custom-call(s32[6]{0:T(128)S(1)} %copy-done.8, bf16[512,512]{1,0:T(8,128)(2,1)S(1)} %copy-done.7, bf16[4,512,384]{2,1,0:T(8,128)(2,1)S(1)} %get-tuple-element.146.grads_ref, bf16[512,512]{1,0:T(8,128)(2,1)S(1)} %get-tuple-element.147.grad_hidden_ref, ...), custom_call_target="tpu_custom_call" | custom-call | flops 1 | bytes 1 | tf_op jit(solution)/shard_map/pallas_call | solution.py:690
  122.8 5.6 %collective-permute-done.23 = bf16[4,2,64,512]{3,2,1,0:T(8,128)(2,1)S(1)} collective-permute-done((bf16[4,2,64,512]{3,2,1,0:T(8,128)(2,1)S(1)}, bf16[4,2,64,512]{3,2,1,0:T(8,128)(2,1)S(1)}, u32[]{:S(2)}, u32[]{:S(2)}) %collective-permute-start.23) | collective-permute-done | bytes 524320 | tf_op jit(solution)/shard_map/ppermute | solution.py:713
  128.5 2.7 %collective-permute-done.27 = bf16[4,272,512]{2,1,0:T(8,128)(2,1)S(1)} collective-permute-done((bf16[4,272,512]{2,1,0:T(8,128)(2,1)S(1)}, bf16[4,272,512]{2,1,0:T(8,128)(2,1)S(1)}, u32[]{:S(2)}, u32[]{:S(2)}) %collective-permute-start.27) | collective-permute-done | bytes 1114144 | tf_op jit(solution)/shard_map/ppermute | solution.py:713
  132.5 4.3 %all-to-all-start.2 = ((bf16[4,272,512]{2,1,0:T(8,128)(2,1)}), bf16[4,272,512]{2,1,0:T(8,128)(2,1)}, u32[]{:S(2)}, u32[]{:S(2)}) async-start(bf16[4,272,512]{2,1,0:T(8,128)(2,1)} %add_convert_fusion), calls=%async_computation.2 | async-start | bytes 2228224 | tf_op jit(solution)/shard_map/all_to_all | solution.py:704
  136.8 1.9 collective-permute-start.25
  140.1 3.5 %collective-permute-start.28 = (bf16[512,512]{1,0:T(8,128)(2,1)S(1)}, bf16[512,512]{1,0:T(8,128)(2,1)}, u32[]{:S(2)}, u32[]{:S(2)}) collective-permute-start(bf16[512,512]{1,0:T(8,128)(2,1)S(1)} %get-tuple-element.168.refs_0_), channel_id=1, source_target_pairs={{0,1},{1,0},{2,3},{3,2},{4,5},{5,4},{6,7},{7,6},{8,9},{9,8},{10,11... | collective-permute-start | bytes 1572872 | tf_op jit(solution)/shard_map/ppermute | solution.py:713
  143.6 21.1 %collective-permute-done.25.refs_3_ = bf16[8,64,512]{2,1,0:T(8,128)(2,1)S(1)} collective-permute-done((bf16[8,64,512]{2,1,0:T(8,128)(2,1)S(1)}, bf16[8,64,512]{2,1,0:T(8,128)(2,1)S(1)}, u32[]{:S(2)}, u32[]{:S(2)}) %collective-permute-start.25) | collective-permute-done | bytes 524320 | tf_op jit(solution)/shard_map/ppermute | solution.py:764
  164.7 2.1 shard_map.322
  166.9 4.2 %all-to-all-start.1 = ((bf16[8,2,2,64,512]{4,3,2,1,0:T(8,128)(2,1)}), bf16[8,2,2,64,512]{4,3,2,1,0:T(8,128)(2,1)S(1)}, u32[]{:S(2)}, u32[]{:S(2)}) async-start(bf16[8,2,2,64,512]{4,3,2,1,0:T(8,128)(2,1)} %shard_map.322), calls=%async_computation.1 | async-start | bytes 4194304 | tf_op jit(solution)/shard_map/all_to_all | solution.py:704
  171.0 1.8 add_convert_fusion.1
  174.4 2.6 %collective-permute-start.32 = (bf16[208,512]{1,0:T(8,128)(2,1)S(1)}, bf16[208,512]{1,0:T(8,128)(2,1)S(1)}, u32[]{:S(2)}, u32[]{:S(2)}) collective-permute-start(bf16[208,512]{1,0:T(8,128)(2,1)S(1)} %get-tuple-element.202), channel_id=1, source_target_pairs={{0,1},{1,0},{2,3},{3,2},{4,5},{5,4},{6,7},{7,6},{8,9},{9,8},{10,11... | collective-permute-start | bytes 638984 | tf_op jit(solution)/shard_map/ppermute | solution.py:713
  178.8 5.6 %collective-permute-done.32 = bf16[208,512]{1,0:T(8,128)(2,1)S(1)} collective-permute-done((bf16[208,512]{1,0:T(8,128)(2,1)S(1)}, bf16[208,512]{1,0:T(8,128)(2,1)S(1)}, u32[]{:S(2)}, u32[]{:S(2)}) %collective-permute-start.32) | collective-permute-done | bytes 213024 | tf_op jit(solution)/shard_map/ppermute | solution.py:713
  184.4 8.7 %collective-permute-done.33 = bf16[208,512]{1,0:T(8,128)(2,1)S(1)} collective-permute-done((bf16[208,512]{1,0:T(8,128)(2,1)S(1)}, bf16[208,512]{1,0:T(8,128)(2,1)S(1)}, u32[]{:S(2)}, u32[]{:S(2)}) %collective-permute-start.33) | collective-permute-done | bytes 213024 | tf_op jit(solution)/shard_map/ppermute | solution.py:713
  193.1 4.0 %collective-permute-done.34 = bf16[208,512]{1,0:T(8,128)(2,1)S(1)} collective-permute-done((bf16[208,512]{1,0:T(8,128)(2,1)S(1)}, bf16[208,512]{1,0:T(8,128)(2,1)S(1)}, u32[]{:S(2)}, u32[]{:S(2)}) %collective-permute-start.34) | collective-permute-done | bytes 213024 | tf_op jit(solution)/shard_map/ppermute | solution.py:713
  197.2 2.6 %collective-permute-start.37 = (bf16[3,64,512]{2,1,0:T(8,128)(2,1)S(1)}, bf16[3,64,512]{2,1,0:T(8,128)(2,1)S(1)}, u32[]{:S(2)}, u32[]{:S(2)}) collective-permute-start(bf16[3,64,512]{2,1,0:T(8,128)(2,1)S(1)} %bitcast.108), channel_id=1, source_target_pairs={{0,24},{4,28},{8,16},{12,20},{16,8},{20,12},{24,0},{28,4},{1,25},{... | collective-permute-start | bytes 589832 | tf_op jit(solution)/shard_map/ppermute | solution.py:713
  200.7 5.0 %collective-permute-done.37 = bf16[3,64,512]{2,1,0:T(8,128)(2,1)S(1)} collective-permute-done((bf16[3,64,512]{2,1,0:T(8,128)(2,1)S(1)}, bf16[3,64,512]{2,1,0:T(8,128)(2,1)S(1)}, u32[]{:S(2)}, u32[]{:S(2)}) %collective-permute-start.37) | collective-permute-done | bytes 196640 | tf_op jit(solution)/shard_map/ppermute | solution.py:713
  205.8 2.0 collective-permute-done.36
  210.7 2.9 %collective-permute-start.30 = (bf16[512,512]{1,0:T(8,128)(2,1)S(1)}, bf16[512,512]{1,0:T(8,128)(2,1)S(1)}, u32[]{:S(2)}, u32[]{:S(2)}) collective-permute-start(bf16[512,512]{1,0:T(8,128)(2,1)S(1)} %get-tuple-element.168.refs_0_), channel_id=1, source_target_pairs={{1,2},{2,1},{5,6},{6,5},{9,10},{10,9},{13,14},{14,13},{17,18},{18,... | collective-permute-start | bytes 1572872 | tf_op jit(solution)/shard_map/ppermute | solution.py:764
  216.1 1.6 copy-done.3
  217.7 1.5 shard_map.323
  219.2 7.8 %collective-permute-done.30.refs_3_ = bf16[512,512]{1,0:T(8,128)(2,1)S(1)} collective-permute-done((bf16[512,512]{1,0:T(8,128)(2,1)S(1)}, bf16[512,512]{1,0:T(8,128)(2,1)S(1)}, u32[]{:S(2)}, u32[]{:S(2)}) %collective-permute-start.30) | collective-permute-done | bytes 524320 | tf_op jit(solution)/shard_map/ppermute | solution.py:764
  227.0 2.5 %shard_map.324 = bf16[4,512,512]{2,1,0:T(8,128)(2,1)} custom-call(s32[6]{0:T(128)S(1)} %copy-done.8, bf16[512,512]{1,0:T(8,128)(2,1)S(1)} %get-tuple-element.168.refs_0_, bf16[512,512]{1,0:T(8,128)(2,1)} %collective-permute-done.28.refs_1_, bf16[512,512]{1,0:T(8,128)(2,1)S(1)} %copy-done.5, bf16[512,512]{1,0:T(8,128)(2,1)S(1)} %collective-permute-done.30.refs_3_, ...), custom_call_target="tpu_custom_call" | custom-call | flops 1 | bytes 1 | tf_op jit(solution)/shard_map/pallas_call | solution.py:690
  229.5 2.4 %shard_map.325 = (f32[512,512]{1,0:T(8,128)}, f32[512,512]{1,0:T(8,128)}, f32[512,128]{1,0:T(8,128)}, f32[512,128]{1,0:T(8,128)}, f32[512,128]{1,0:T(8,128)}, /*index=5*/f32[128,512]{1,0:T(8,128)}) custom-call(s32[6]{0:T(128)S(1)} %copy-done.8, bf16[4,3,64,512]{3,2,1,0:T(8,128)(2,1)S(1)} %pad_maximum_fusion.2.near_ref, ...), custom_call_target="tpu_custom_call" | custom-call | flops 1 | bytes 1 | tf_op jit(solution)/shard_map/pallas_call | solution.py:690
  (134 shorter events, 35.5 us)
Async XLA Ops:
  0.7 65.3 %copy-start = (bf16[2,1024,512]{2,1,0:T(8,128)(2,1)S(1)}, bf16[2,1024,512]{2,1,0:T(8,128)(2,1)}, u32[]{:S(2)}) copy-start(bf16[2,1024,512]{2,1,0:T(8,128)(2,1)} %param.20) | copy-start | bytes 6291460
  3.7 14.3 %collective-permute-start.2 = (bf16[80,512]{1,0:T(8,128)(2,1)}, bf16[80,512]{1,0:T(8,128)(2,1)S(1)}, u32[]{:S(2)}, u32[]{:S(2)}) collective-permute-start(bf16[80,512]{1,0:T(8,128)(2,1)} %get-tuple-element.104), channel_id=1, source_target_pairs={{0,3},{1,2},{2,1},{3,0},{4,7},{5,6},{6,5},{7,4},{8,11},{9,10},{10,... | collective-permute-start | bytes 245768 | tf_op jit(solution)/shard_map/ppermute | solution.py:713
  5.4 12.7 %collective-permute-start.1 = (bf16[80,512]{1,0:T(8,128)(2,1)}, bf16[80,512]{1,0:T(8,128)(2,1)}, u32[]{:S(2)}, u32[]{:S(2)}) collective-permute-start(bf16[80,512]{1,0:T(8,128)(2,1)} %get-tuple-element.104), channel_id=1, source_target_pairs={{0,2},{1,3},{2,0},{3,1},{4,6},{5,7},{6,4},{7,5},{8,10},{9,11},{10,... | collective-permute-start | bytes 245768 | tf_op jit(solution)/shard_map/ppermute | solution.py:713
  6.5 11.6 %collective-permute-start = (bf16[80,512]{1,0:T(8,128)(2,1)}, bf16[80,512]{1,0:T(8,128)(2,1)}, u32[]{:S(2)}, u32[]{:S(2)}) collective-permute-start(bf16[80,512]{1,0:T(8,128)(2,1)} %get-tuple-element.104), channel_id=1, source_target_pairs={{0,1},{1,0},{2,3},{3,2},{4,5},{5,4},{6,7},{7,6},{8,9},{9,8},{10,11... | collective-permute-start | bytes 245768 | tf_op jit(solution)/shard_map/ppermute | solution.py:713
  9.6 24.6 %all-to-all-start = ((bf16[4,2,64,512]{3,2,1,0:T(8,128)(2,1)}), bf16[4,2,64,512]{3,2,1,0:T(8,128)(2,1)}, u32[]{:S(2)}, u32[]{:S(2)}) async-start(bf16[4,2,64,512]{3,2,1,0:T(8,128)(2,1)} %broadcast_in_dim.2), calls=%async_computation | async-start | bytes 1048576 | tf_op jit(solution)/shard_map/all_to_all | solution.py:704
  18.0 31.1 %copy-start.6 = (bf16[512,512]{1,0:T(8,128)(2,1)}, bf16[512,512]{1,0:T(8,128)(2,1)S(1)}, u32[]{:S(2)}) copy-start(bf16[512,512]{1,0:T(8,128)(2,1)S(1)} %get-tuple-element.103.normed_ref) | copy-start | bytes 1572868
  20.6 10.5 %collective-permute-start.5 = (bf16[4,64,512]{2,1,0:T(8,128)(2,1)}, bf16[4,64,512]{2,1,0:T(8,128)(2,1)}, u32[]{:S(2)}, u32[]{:S(2)}) collective-permute-start(bf16[4,64,512]{2,1,0:T(8,128)(2,1)} %pad_maximum_fusion.6), channel_id=1, source_target_pairs={{0,24},{4,28},{8,16},{12,20},{16,8},{20,12},{24,0},{28,4},{1,25},{... | collective-permute-start | bytes 786440 | tf_op jit(solution)/shard_map/ppermute | solution.py:713
  23.1 11.0 %collective-permute-start.4 = (bf16[4,64,512]{2,1,0:T(8,128)(2,1)}, bf16[4,64,512]{2,1,0:T(8,128)(2,1)}, u32[]{:S(2)}, u32[]{:S(2)}) collective-permute-start(bf16[4,64,512]{2,1,0:T(8,128)(2,1)} %pad_maximum_fusion.6), channel_id=1, source_target_pairs={{0,16},{4,20},{8,24},{12,28},{16,0},{20,4},{24,8},{28,12},{1,17},{... | collective-permute-start | bytes 786440 | tf_op jit(solution)/shard_map/ppermute | solution.py:713
  23.6 10.6 %collective-permute-start.3 = (bf16[4,64,512]{2,1,0:T(8,128)(2,1)}, bf16[4,64,512]{2,1,0:T(8,128)(2,1)}, u32[]{:S(2)}, u32[]{:S(2)}) collective-permute-start(bf16[4,64,512]{2,1,0:T(8,128)(2,1)} %pad_maximum_fusion.6), channel_id=1, source_target_pairs={{0,8},{4,12},{8,0},{12,4},{16,24},{20,28},{24,16},{28,20},{1,9},{5... | collective-permute-start | bytes 786440 | tf_op jit(solution)/shard_map/ppermute | solution.py:713
  35.5 5.8 %collective-permute-start.6 = (bf16[4,4,64,512]{3,2,1,0:T(8,128)(2,1)S(1)}, bf16[4,4,64,512]{3,2,1,0:T(8,128)(2,1)S(1)}, u32[]{:S(2)}, u32[]{:S(2)}) collective-permute-start(bf16[4,4,64,512]{3,2,1,0:T(8,128)(2,1)S(1)} %pad_maximum_fusion.1.near_ref), channel_id=1, source_target_pairs={{0,4},{4,0},{8,12},{12,8},{16,20},{20,16},{24,28},{28,24},{1,5},{5... | collective-permute-start | bytes 3145736 | tf_op jit(solution)/shard_map/ppermute | solution.py:713
  37.8 15.9 %collective-permute-start.9 = (bf16[4,2,64,512]{3,2,1,0:T(8,128)(2,1)}, bf16[4,2,64,512]{3,2,1,0:T(8,128)(2,1)S(1)}, u32[]{:S(2)}, u32[]{:S(2)}) collective-permute-start(bf16[4,2,64,512]{3,2,1,0:T(8,128)(2,1)} %all-to-all-done), channel_id=1, source_target_pairs={{0,24},{4,28},{8,16},{12,20},{16,8},{20,12},{24,0},{28,4},{1,25},{... | collective-permute-start | bytes 1572872 | tf_op jit(solution)/shard_map/ppermute | solution.py:713
  39.5 25.0 %collective-permute-start.8 = (bf16[4,2,64,512]{3,2,1,0:T(8,128)(2,1)}, bf16[4,2,64,512]{3,2,1,0:T(8,128)(2,1)S(1)}, u32[]{:S(2)}, u32[]{:S(2)}) collective-permute-start(bf16[4,2,64,512]{3,2,1,0:T(8,128)(2,1)} %all-to-all-done), channel_id=1, source_target_pairs={{0,16},{4,20},{8,24},{12,28},{16,0},{20,4},{24,8},{28,12},{1,17},{... | collective-permute-start | bytes 1572872 | tf_op jit(solution)/shard_map/ppermute | solution.py:713
  40.8 23.7 %collective-permute-start.7 = (bf16[4,2,64,512]{3,2,1,0:T(8,128)(2,1)}, bf16[4,2,64,512]{3,2,1,0:T(8,128)(2,1)S(1)}, u32[]{:S(2)}, u32[]{:S(2)}) collective-permute-start(bf16[4,2,64,512]{3,2,1,0:T(8,128)(2,1)} %all-to-all-done), channel_id=1, source_target_pairs={{0,8},{4,12},{8,0},{12,4},{16,24},{20,28},{24,16},{28,20},{1,9},{5... | collective-permute-start | bytes 1572872 | tf_op jit(solution)/shard_map/ppermute | solution.py:713
  65.9 4.2 %collective-permute-start.10 = (bf16[4,4,2,64,512]{4,3,2,1,0:T(8,128)(2,1)S(1)}, bf16[4,4,2,64,512]{4,3,2,1,0:T(8,128)(2,1)S(1)}, u32[]{:S(2)}, u32[]{:S(2)}) collective-permute-start(bf16[4,4,2,64,512]{4,3,2,1,0:T(8,128)(2,1)S(1)} %pad_maximum_fusion.ffn_near_ref), channel_id=1, source_target_pairs={{0,4},{4,0},{8,12},{12,8},{16,20},{20,16},{24,28},{28,24},{1,5},{5... | collective-permute-start | bytes 6291464 | tf_op jit(solution)/shard_map/ppermute | solution.py:713
  84.0 13.9 %collective-permute-start.18 = (bf16[4,4,2,64,512]{4,3,2,1,0:T(8,128)(2,1)S(1)}, bf16[4,4,2,64,512]{4,3,2,1,0:T(8,128)(2,1)S(1)}, u32[]{:S(2)}, u32[]{:S(2)}) collective-permute-start(bf16[4,4,2,64,512]{4,3,2,1,0:T(8,128)(2,1)S(1)} %get-tuple-element.137), channel_id=1, source_target_pairs={{0,4},{4,0},{8,12},{12,8},{16,20},{20,16},{24,28},{28,24},{1,5},{5... | collective-permute-start | bytes 6291464 | tf_op jit(solution)/shard_map/ppermute | solution.py:713
  84.2 15.5 %collective-permute-start.19 = (f32[4,32,128]{2,1,0:T(8,128)S(1)}, f32[4,32,128]{2,1,0:T(8,128)S(1)}, u32[]{:S(2)}, u32[]{:S(2)}) collective-permute-start(f32[4,32,128]{2,1,0:T(8,128)S(1)} %get-tuple-element.138), channel_id=1, source_target_pairs={{0,1},{1,0},{2,3},{3,2},{4,5},{5,4},{6,7},{7,6},{8,9},{9,8},{10,11... | collective-permute-start | bytes 196616 | tf_op jit(solution)/shard_map/ppermute | solution.py:713
  84.5 3.8 %collective-permute-start.11 = (bf16[64,512]{1,0:T(8,128)(2,1)S(1)}, bf16[64,512]{1,0:T(8,128)(2,1)S(1)}, u32[]{:S(2)}, u32[]{:S(2)}) collective-permute-start(bf16[64,512]{1,0:T(8,128)(2,1)S(1)} %get-tuple-element.126), channel_id=1, source_target_pairs={{0,4},{4,0},{8,12},{12,8},{16,20},{20,16},{24,28},{28,24},{1,5},{5... | collective-permute-start | bytes 196616 | tf_op jit(solution)/shard_map/ppermute | solution.py:713
  84.6 5.2 %collective-permute-start.12 = (bf16[64,512]{1,0:T(8,128)(2,1)S(1)}, bf16[64,512]{1,0:T(8,128)(2,1)S(1)}, u32[]{:S(2)}, u32[]{:S(2)}) collective-permute-start(bf16[64,512]{1,0:T(8,128)(2,1)S(1)} %get-tuple-element.127), channel_id=1, source_target_pairs={{0,8},{4,12},{8,0},{12,4},{16,24},{20,28},{24,16},{28,20},{1,9},{5... | collective-permute-start | bytes 196616 | tf_op jit(solution)/shard_map/ppermute | solution.py:713
  86.1 4.0 %collective-permute-start.13 = (bf16[64,512]{1,0:T(8,128)(2,1)S(1)}, bf16[64,512]{1,0:T(8,128)(2,1)S(1)}, u32[]{:S(2)}, u32[]{:S(2)}) collective-permute-start(bf16[64,512]{1,0:T(8,128)(2,1)S(1)} %get-tuple-element.128), channel_id=1, source_target_pairs={{0,12},{4,8},{8,4},{12,0},{16,28},{20,24},{24,20},{28,16},{1,13},{... | collective-permute-start | bytes 196616 | tf_op jit(solution)/shard_map/ppermute | solution.py:713
  88.4 4.3 %collective-permute-start.14 = (bf16[64,512]{1,0:T(8,128)(2,1)S(1)}, bf16[64,512]{1,0:T(8,128)(2,1)S(1)}, u32[]{:S(2)}, u32[]{:S(2)}) collective-permute-start(bf16[64,512]{1,0:T(8,128)(2,1)S(1)} %get-tuple-element.129), channel_id=1, source_target_pairs={{0,16},{4,20},{8,24},{12,28},{16,0},{20,4},{24,8},{28,12},{1,17},{... | collective-permute-start | bytes 196616 | tf_op jit(solution)/shard_map/ppermute | solution.py:713
  89.8 4.4 %collective-permute-start.15 = (bf16[64,512]{1,0:T(8,128)(2,1)S(1)}, bf16[64,512]{1,0:T(8,128)(2,1)S(1)}, u32[]{:S(2)}, u32[]{:S(2)}) collective-permute-start(bf16[64,512]{1,0:T(8,128)(2,1)S(1)} %get-tuple-element.130), channel_id=1, source_target_pairs={{0,20},{4,16},{8,28},{12,24},{16,4},{20,0},{24,12},{28,8},{1,21},{... | collective-permute-start | bytes 196616 | tf_op jit(solution)/shard_map/ppermute | solution.py:713
  90.2 5.9 %collective-permute-start.16 = (bf16[64,512]{1,0:T(8,128)(2,1)S(1)}, bf16[64,512]{1,0:T(8,128)(2,1)S(1)}, u32[]{:S(2)}, u32[]{:S(2)}) collective-permute-start(bf16[64,512]{1,0:T(8,128)(2,1)S(1)} %get-tuple-element.131), channel_id=1, source_target_pairs={{0,24},{4,28},{8,16},{12,20},{16,8},{20,12},{24,0},{28,4},{1,25},{... | collective-permute-start | bytes 196616 | tf_op jit(solution)/shard_map/ppermute | solution.py:713
  92.6 5.3 %collective-permute-start.17 = (bf16[64,512]{1,0:T(8,128)(2,1)S(1)}, bf16[64,512]{1,0:T(8,128)(2,1)S(1)}, u32[]{:S(2)}, u32[]{:S(2)}) collective-permute-start(bf16[64,512]{1,0:T(8,128)(2,1)S(1)} %get-tuple-element.132), channel_id=1, source_target_pairs={{0,28},{4,24},{8,20},{12,16},{16,12},{20,8},{24,4},{28,0},{1,29},{... | collective-permute-start | bytes 196616 | tf_op jit(solution)/shard_map/ppermute | solution.py:713
  99.7 28.7 %collective-permute-start.21 = (bf16[8,64,512]{2,1,0:T(8,128)(2,1)S(1)}, bf16[8,64,512]{2,1,0:T(8,128)(2,1)S(1)}, u32[]{:S(2)}, u32[]{:S(2)}) collective-permute-start(bf16[8,64,512]{2,1,0:T(8,128)(2,1)S(1)} %bitcast_dynamic-update-slice_fusion.refs_0_), channel_id=1, source_target_pairs={{0,2},{1,3},{2,0},{3,1},{4,6},{5,7},{6,4},{7,5},{8,10},{9,11},{10,... | collective-permute-start | bytes 1572872 | tf_op jit(solution)/shard_map/ppermute | solution.py:713
  101.8 26.6 %collective-permute-start.20 = (bf16[8,64,512]{2,1,0:T(8,128)(2,1)S(1)}, bf16[8,64,512]{2,1,0:T(8,128)(2,1)S(1)}, u32[]{:S(2)}, u32[]{:S(2)}) collective-permute-start(bf16[8,64,512]{2,1,0:T(8,128)(2,1)S(1)} %bitcast_dynamic-update-slice_fusion.refs_0_), channel_id=1, source_target_pairs={{0,1},{1,0},{2,3},{3,2},{4,5},{5,4},{6,7},{7,6},{8,9},{9,8},{10,11... | collective-permute-start | bytes 1572872 | tf_op jit(solution)/shard_map/ppermute | solution.py:713
  102.7 20.0 %collective-permute-start.22 = (bf16[4,2,64,512]{3,2,1,0:T(8,128)(2,1)S(1)}, bf16[4,2,64,512]{3,2,1,0:T(8,128)(2,1)S(1)}, u32[]{:S(2)}, u32[]{:S(2)}) collective-permute-start(bf16[4,2,64,512]{3,2,1,0:T(8,128)(2,1)S(1)} %get-tuple-element.155), channel_id=1, source_target_pairs={{0,8},{4,12},{8,0},{12,4},{16,24},{20,28},{24,16},{28,20},{1,9},{5... | collective-permute-start | bytes 1572872 | tf_op jit(solution)/shard_map/ppermute | solution.py:713
  104.0 24.3 %collective-permute-start.23 = (bf16[4,2,64,512]{3,2,1,0:T(8,128)(2,1)S(1)}, bf16[4,2,64,512]{3,2,1,0:T(8,128)(2,1)S(1)}, u32[]{:S(2)}, u32[]{:S(2)}) collective-permute-start(bf16[4,2,64,512]{3,2,1,0:T(8,128)(2,1)S(1)} %get-tuple-element.156), channel_id=1, source_target_pairs={{0,16},{4,20},{8,24},{12,28},{16,0},{20,4},{24,8},{28,12},{1,17},{... | collective-permute-start | bytes 1572872 | tf_op jit(solution)/shard_map/ppermute | solution.py:713
  105.2 23.2 %collective-permute-start.24 = (bf16[4,2,64,512]{3,2,1,0:T(8,128)(2,1)S(1)}, bf16[4,2,64,512]{3,2,1,0:T(8,128)(2,1)S(1)}, u32[]{:S(2)}, u32[]{:S(2)}) collective-permute-start(bf16[4,2,64,512]{3,2,1,0:T(8,128)(2,1)S(1)} %get-tuple-element.157), channel_id=1, source_target_pairs={{0,24},{4,28},{8,16},{12,20},{16,8},{20,12},{24,0},{28,4},{1,25},{... | collective-permute-start | bytes 1572872 | tf_op jit(solution)/shard_map/ppermute | solution.py:713
  106.2 14.0 %copy-start.7 = (bf16[512,512]{1,0:T(8,128)(2,1)S(1)}, bf16[512,512]{1,0:T(8,128)(2,1)}, u32[]{:S(2)}) copy-start(bf16[512,512]{1,0:T(8,128)(2,1)} %copy-done.6) | copy-start | bytes 1572868
  128.4 2.8 %collective-permute-start.27 = (bf16[4,272,512]{2,1,0:T(8,128)(2,1)S(1)}, bf16[4,272,512]{2,1,0:T(8,128)(2,1)S(1)}, u32[]{:S(2)}, u32[]{:S(2)}) collective-permute-start(bf16[4,272,512]{2,1,0:T(8,128)(2,1)S(1)} %get-tuple-element.163), channel_id=1, source_target_pairs={{0,4},{4,0},{8,12},{12,8},{16,20},{20,16},{24,28},{28,24},{1,5},{5... | collective-permute-start | bytes 3342344 | tf_op jit(solution)/shard_map/ppermute | solution.py:713
  131.2 33.5 %copy-start.16 = (s32[16]{0:T(128)S(1)}, s32[16]{0:T(128)}, u32[]{:S(2)}) copy-start(s32[16]{0:T(128)} %dealing.1) | copy-start | bytes 196
  132.5 34.3 %all-to-all-start.2 = ((bf16[4,272,512]{2,1,0:T(8,128)(2,1)}), bf16[4,272,512]{2,1,0:T(8,128)(2,1)}, u32[]{:S(2)}, u32[]{:S(2)}) async-start(bf16[4,272,512]{2,1,0:T(8,128)(2,1)} %add_convert_fusion), calls=%async_computation.2 | async-start | bytes 2228224 | tf_op jit(solution)/shard_map/all_to_all | solution.py:704
  136.8 27.9 %collective-permute-start.25 = (bf16[8,64,512]{2,1,0:T(8,128)(2,1)S(1)}, bf16[8,64,512]{2,1,0:T(8,128)(2,1)S(1)}, u32[]{:S(2)}, u32[]{:S(2)}) collective-permute-start(bf16[8,64,512]{2,1,0:T(8,128)(2,1)S(1)} %bitcast_dynamic-update-slice_fusion.refs_0_), channel_id=1, source_target_pairs={{1,2},{2,1},{5,6},{6,5},{9,10},{10,9},{13,14},{14,13},{17,18},{18,... | collective-permute-start | bytes 1572872 | tf_op jit(solution)/shard_map/ppermute | solution.py:764
  138.7 26.0 %collective-permute-start.26 = (bf16[8,64,512]{2,1,0:T(8,128)(2,1)S(1)}, bf16[8,64,512]{2,1,0:T(8,128)(2,1)S(1)}, u32[]{:S(2)}, u32[]{:S(2)}) collective-permute-start(bf16[8,64,512]{2,1,0:T(8,128)(2,1)S(1)} %collective-permute-done.21.refs_2_), channel_id=1, source_target_pairs={{1,0},{2,3},{5,4},{6,7},{9,8},{10,11},{13,12},{14,15},{17,16},{18,... | collective-permute-start | bytes 1572872 | tf_op jit(solution)/shard_map/ppermute | solution.py:765
  140.1 34.2 %collective-permute-start.29 = (bf16[512,512]{1,0:T(8,128)(2,1)S(1)}, bf16[512,512]{1,0:T(8,128)(2,1)S(1)}, u32[]{:S(2)}, u32[]{:S(2)}) collective-permute-start(bf16[512,512]{1,0:T(8,128)(2,1)S(1)} %get-tuple-element.168.refs_0_), channel_id=1, source_target_pairs={{0,2},{1,3},{2,0},{3,1},{4,6},{5,7},{6,4},{7,5},{8,10},{9,11},{10,... | collective-permute-start | bytes 1572872 | tf_op jit(solution)/shard_map/ppermute | solution.py:713
  140.1 34.1 %collective-permute-start.28 = (bf16[512,512]{1,0:T(8,128)(2,1)S(1)}, bf16[512,512]{1,0:T(8,128)(2,1)}, u32[]{:S(2)}, u32[]{:S(2)}) collective-permute-start(bf16[512,512]{1,0:T(8,128)(2,1)S(1)} %get-tuple-element.168.refs_0_), channel_id=1, source_target_pairs={{0,1},{1,0},{2,3},{3,2},{4,5},{5,4},{6,7},{7,6},{8,9},{9,8},{10,11... | collective-permute-start | bytes 1572872 | tf_op jit(solution)/shard_map/ppermute | solution.py:713
  166.9 41.2 %all-to-all-start.1 = ((bf16[8,2,2,64,512]{4,3,2,1,0:T(8,128)(2,1)}), bf16[8,2,2,64,512]{4,3,2,1,0:T(8,128)(2,1)S(1)}, u32[]{:S(2)}, u32[]{:S(2)}) async-start(bf16[8,2,2,64,512]{4,3,2,1,0:T(8,128)(2,1)} %shard_map.322), calls=%async_computation.1 | async-start | bytes 4194304 | tf_op jit(solution)/shard_map/all_to_all | solution.py:704
  174.3 33.7 %copy-start.4 = (bf16[512,512]{1,0:T(8,128)(2,1)}, bf16[512,512]{1,0:T(8,128)(2,1)S(1)}, u32[]{:S(2)}) copy-start(bf16[512,512]{1,0:T(8,128)(2,1)S(1)} %collective-permute-done.29.refs_2_) | copy-start | bytes 1572868
  174.4 10.0 %collective-permute-start.32 = (bf16[208,512]{1,0:T(8,128)(2,1)S(1)}, bf16[208,512]{1,0:T(8,128)(2,1)S(1)}, u32[]{:S(2)}, u32[]{:S(2)}) collective-permute-start(bf16[208,512]{1,0:T(8,128)(2,1)S(1)} %get-tuple-element.202), channel_id=1, source_target_pairs={{0,1},{1,0},{2,3},{3,2},{4,5},{5,4},{6,7},{7,6},{8,9},{9,8},{10,11... | collective-permute-start | bytes 638984 | tf_op jit(solution)/shard_map/ppermute | solution.py:713
  177.0 16.1 %collective-permute-start.33 = (bf16[208,512]{1,0:T(8,128)(2,1)S(1)}, bf16[208,512]{1,0:T(8,128)(2,1)S(1)}, u32[]{:S(2)}, u32[]{:S(2)}) collective-permute-start(bf16[208,512]{1,0:T(8,128)(2,1)S(1)} %get-tuple-element.203), channel_id=1, source_target_pairs={{0,2},{1,3},{2,0},{3,1},{4,6},{5,7},{6,4},{7,5},{8,10},{9,11},{10,... | collective-permute-start | bytes 638984 | tf_op jit(solution)/shard_map/ppermute | solution.py:713
  178.2 18.8 %collective-permute-start.34 = (bf16[208,512]{1,0:T(8,128)(2,1)S(1)}, bf16[208,512]{1,0:T(8,128)(2,1)S(1)}, u32[]{:S(2)}, u32[]{:S(2)}) collective-permute-start(bf16[208,512]{1,0:T(8,128)(2,1)S(1)} %pad_maximum_fusion.7), channel_id=1, source_target_pairs={{0,3},{1,2},{2,1},{3,0},{4,7},{5,6},{6,5},{7,4},{8,11},{9,10},{10,... | collective-permute-start | bytes 638984 | tf_op jit(solution)/shard_map/ppermute | solution.py:713
  197.2 8.6 %collective-permute-start.37 = (bf16[3,64,512]{2,1,0:T(8,128)(2,1)S(1)}, bf16[3,64,512]{2,1,0:T(8,128)(2,1)S(1)}, u32[]{:S(2)}, u32[]{:S(2)}) collective-permute-start(bf16[3,64,512]{2,1,0:T(8,128)(2,1)S(1)} %bitcast.108), channel_id=1, source_target_pairs={{0,24},{4,28},{8,16},{12,20},{16,8},{20,12},{24,0},{28,4},{1,25},{... | collective-permute-start | bytes 589832 | tf_op jit(solution)/shard_map/ppermute | solution.py:713
  199.8 7.9 %collective-permute-start.36 = (bf16[3,64,512]{2,1,0:T(8,128)(2,1)S(1)}, bf16[3,64,512]{2,1,0:T(8,128)(2,1)S(1)}, u32[]{:S(2)}, u32[]{:S(2)}) collective-permute-start(bf16[3,64,512]{2,1,0:T(8,128)(2,1)S(1)} %bitcast.109), channel_id=1, source_target_pairs={{0,16},{4,20},{8,24},{12,28},{16,0},{20,4},{24,8},{28,12},{1,17},{... | collective-permute-start | bytes 589832 | tf_op jit(solution)/shard_map/ppermute | solution.py:713
  200.4 7.6 %collective-permute-start.35 = (bf16[3,64,512]{2,1,0:T(8,128)(2,1)S(1)}, bf16[3,64,512]{2,1,0:T(8,128)(2,1)S(1)}, u32[]{:S(2)}, u32[]{:S(2)}) collective-permute-start(bf16[3,64,512]{2,1,0:T(8,128)(2,1)S(1)} %bitcast.110), channel_id=1, source_target_pairs={{0,8},{4,12},{8,0},{12,4},{16,24},{20,28},{24,16},{28,20},{1,9},{5... | collective-permute-start | bytes 589832 | tf_op jit(solution)/shard_map/ppermute | solution.py:713
  209.4 20.1 %collective-permute-start.38 = (bf16[4,3,64,512]{3,2,1,0:T(8,128)(2,1)S(1)}, bf16[4,3,64,512]{3,2,1,0:T(8,128)(2,1)S(1)}, u32[]{:S(2)}, u32[]{:S(2)}) collective-permute-start(bf16[4,3,64,512]{3,2,1,0:T(8,128)(2,1)S(1)} %pad_maximum_fusion.2.near_ref), channel_id=1, source_target_pairs={{0,4},{4,0},{8,12},{12,8},{16,20},{20,16},{24,28},{28,24},{1,5},{5... | collective-permute-start | bytes 2359304 | tf_op jit(solution)/shard_map/ppermute | solution.py:713
  209.4 17.6 %collective-permute-start.31 = (bf16[512,512]{1,0:T(8,128)(2,1)}, bf16[512,512]{1,0:T(8,128)(2,1)S(1)}, u32[]{:S(2)}, u32[]{:S(2)}) collective-permute-start(bf16[512,512]{1,0:T(8,128)(2,1)} %copy-done.4), channel_id=1, source_target_pairs={{1,0},{2,3},{5,4},{6,7},{9,8},{10,11},{13,12},{14,15},{17,16},{18,... | collective-permute-start | bytes 1572872 | tf_op jit(solution)/shard_map/ppermute | solution.py:765
  210.7 16.2 %collective-permute-start.30 = (bf16[512,512]{1,0:T(8,128)(2,1)S(1)}, bf16[512,512]{1,0:T(8,128)(2,1)S(1)}, u32[]{:S(2)}, u32[]{:S(2)}) collective-permute-start(bf16[512,512]{1,0:T(8,128)(2,1)S(1)} %get-tuple-element.168.refs_0_), channel_id=1, source_target_pairs={{1,2},{2,1},{5,6},{6,5},{9,10},{10,9},{13,14},{14,13},{17,18},{18,... | collective-permute-start | bytes 1572872 | tf_op jit(solution)/shard_map/ppermute | solution.py:764
  217.7 14.1 %copy-start.1 = (bf16[2,1024,512]{2,1,0:T(8,128)(2,1)S(1)}, bf16[2,1024,512]{2,1,0:T(8,128)(2,1)}, u32[]{:S(2)}) copy-start(bf16[2,1024,512]{2,1,0:T(8,128)(2,1)} %param.20) | copy-start | bytes 6291460
  (16 other events, 121.1 us)

commit v5 on v4

--- a/solution.py
+++ b/solution.py
@@ -169,20 +169,26 @@
     return jnp.concatenate([values[:, :TILE], values[:, TILE:]], axis=0)
 
 
-def assemble(info, near_ref, far_ref, to_ref, by_line=True):
-    core, plane = info[3], info[4]
-    line = info[5] if by_line else 0
+def assemble(info, near_ref, far_ref, to_ref):
+    core, plane, line = info[3], info[4], info[5]
     chunk = near_ref.shape[-2]
     for far, ref in enumerate((near_ref, far_ref)):
         for o in range(ref.shape[0]):
             at = ((o ^ plane) * 2 + (far ^ core)) * chunk
             at = pl.ds(pl.multiple_of(at, chunk), chunk)
             for z in range(ref.shape[1]):
-                if len(ref.shape) == 5:
-                    for part in range(ref.shape[2]):
-                        to_ref[z ^ line, part, at, :] = ref[o, z, part]
-                else:
-                    to_ref[z ^ line, at, :] = ref[o, z]
+                to_ref[z ^ line, at, :] = ref[o, z]
+
+
+def assemble_feed(info, plan, refs, to_ref):
+    core, plane = info[3], info[4]
+    for (part, far, chips), ref in zip(plan, refs):
+        chunk = ref.shape[-2]
+        for i, o in enumerate(chips):
+            at = ((o ^ plane) * 2 + (far ^ core)) * chunk
+            at = pl.ds(pl.multiple_of(at, chunk), chunk)
+            for z in range(ref.shape[1]):
+                to_ref[z, part, at, :] = ref[i, z]
 
 
 def pack_kernel(info, q_ref, k_ref, v_ref, o_ref, up_ref, down_ref, bq_ref, bv_ref, bu_ref, attn_ref, ffn_ref, turn_s):
@@ -207,6 +213,31 @@
         rest = rest - part
     rows.append(jnp.zeros((10, lanes), F32))
     attn_ref[chunk:, :] = jnp.concatenate(rows, axis=0).astype(BF16)
+
+
+def stack_kernel(*refs):
+    *pieces, weight_ref, bias_ref = refs
+    chunk = weight_ref.shape[1]
+    for z, ref in enumerate(pieces):
+        weight_ref[z] = ref[:chunk, :]
+        bias_ref[z] = ref[chunk:, :]
+
+
+def part_kernel(info, *refs):
+    *pieces, up_ref, down_ref = refs
+    for where, z, ref in line_sources(info[5], pieces):
+
+        def put(z=z, ref=ref):
+            up_ref[z] = ref[0]
+            down_ref[z] = ref[1]
+
+        put() if where is None else pl.when(where)(put)
+
+
+def pair_kernel(near_ref, far_ref, *out_refs):
+    for o, ref in enumerate(out_refs):
+        ref[0] = near_ref[o]
+        ref[1] = far_ref[o]
 
 
 def bias_row(bias_ref, z, row):
@@ -350,30 +381,14 @@
     lax.fori_loop(0, pairs, one_pair, 0)
 
 
-def feed_kernel(
-    info,
-    own_ref,
-    mixed_ref,
-    near_ref,
-    far_ref,
-    ffn_near_ref,
-    ffn_far_ref,
-    b_out_ref,
-    gain_ref,
-    shift_ref,
-    bias_ref,
-    b_down_ref,
-    hidden_ref,
-    normed_ref,
-    act_ref,
-    slope_ref,
-    *refs,
-):
-    *out_refs, result_s, full_s, ffn_s = refs
+def feed_kernel(plan, info, own_ref, mixed_ref, near_ref, far_ref, *refs):
+    ffn_refs, refs = refs[: len(plan)], refs[len(plan) :]
+    b_out_ref, gain_ref, shift_ref, bias_ref, b_down_ref, hidden_ref, normed_ref = refs[:7]
+    act_ref, slope_ref, *out_refs, result_s, full_s, ffn_s = refs[7:]
     pairs = mixed_ref.shape[0]
     line = info[5]
     assemble(info, near_ref, far_ref, full_s)
-    assemble(info, ffn_near_ref, ffn_far_ref, ffn_s, by_line=False)
+    assemble_feed(info, plan, ffn_refs, ffn_s)
     hidden = own_ref[...].astype(F32) + b_out_ref[...]
     for p in range(pairs):
         hidden = hidden + mm_nt(mixed_ref[p], full_s[p, :, 3 * TILE :])
@@ -390,37 +405,20 @@
         slope_ref[z] = (half_erf + pre * jnp.exp(-0.5 * pre * pre) * INV_ROOT_TAU).astype(BF16)
         result = result + mm(act, ffn_s[z, 1])
     result_s[...] = result
-    chunk = out_refs[0].shape[0]
-    for k, out_ref in enumerate(out_refs):
-        at = ((info[4] * 2 + info[3]) ^ k) * chunk
-        out_ref[...] = result_s[pl.ds(pl.multiple_of(at, chunk), chunk), :].astype(BF16)
-
-
-def feed_back_kernel(
-    info,
-    dy_ref,
-    ffn_near_ref,
-    ffn_far_ref,
-    near_ref,
-    far_ref,
-    slope_ref,
-    hidden_ref,
-    gain_ref,
-    mixed_wide_ref,
-    total_ref,
-    grad_pre_ref,
-    grad_hidden_ref,
-    grad_hidden_low_ref,
-    numer_ref,
-    gtotal_ref,
-    exchange_ref,
-    vector_ref,
-    b_up_ref,
-    full_s,
-    ffn_s,
-):
+    chunk = out_refs[0].shape[1]
+    for far, out_ref in enumerate(out_refs):
+        for o in range(out_ref.shape[0]):
+            at = ((o ^ info[4]) * 2 + (far ^ info[3])) * chunk
+            out_ref[o] = result_s[pl.ds(pl.multiple_of(at, chunk), chunk), :].astype(BF16)
+
+
+def feed_back_kernel(plan, info, dy_ref, near_ref, far_ref, *refs):
+    ffn_refs, refs = refs[: len(plan)], refs[len(plan) :]
+    slope_ref, hidden_ref, gain_ref, mixed_wide_ref, total_ref, grad_pre_ref, grad_hidden_ref = refs[:7]
+    grad_hidden_low_ref, numer_ref, gtotal_ref, exchange_ref, vector_ref, b_up_ref = refs[7:13]
+    full_s, ffn_s = refs[13:]
     rows = dy_ref.shape[0]
-    assemble(info, ffn_near_ref, ffn_far_ref, ffn_s, by_line=False)
+    assemble_feed(info, plan, ffn_refs, ffn_s)
     assemble(info, near_ref, far_ref, full_s)
     pairs = slope_ref.shape[0]
     dy = dy_ref[...]
@@ -600,7 +598,7 @@
     far_ref,
     both_s,
 ):
-    core, line = info[3], info[5]
+    core, plane, line = info[3], info[4], info[5]
     pairs = mixed_ref.shape[0]
     dp = 2 * near_ref.shape[0]
     chunk = both_s.shape[0] // dp
@@ -610,7 +608,7 @@
         both_s[:, 3 * TILE :] = mm_tn(grad_hidden_ref[...], mixed_ref[z]).astype(BF16)
         for far, ref in enumerate((near_ref, far_ref)):
             for o in range(ref.shape[0]):
-                at = (o * 2 + (far ^ core)) * chunk
+                at = ((o ^ plane) * 2 + (far ^ core)) * chunk
                 at = pl.ds(pl.multiple_of(at, chunk), chunk)
                 to = pl.ds(pl.multiple_of((z ^ line) * chunk, chunk), chunk)
                 ref[o, to, :] = both_s[at, :]
@@ -643,20 +641,25 @@
     o_ref[...] = turn_s[...].T
 
 
-def gather_line(line, refs, to_ref):
+def line_sources(line, refs):
     own, one, two, three, passed = refs
     middle = (line == 1) | (line == 2)
-    to_ref[line] = own[...]
-    to_ref[line ^ 1] = one[...]
-    to_ref[line ^ 2] = two[...]
-
-    @pl.when(middle)
-    def _():
-        to_ref[line ^ 3] = three[...]
-
-    @pl.when(jnp.logical_not(middle))
-    def _():
-        to_ref[line ^ 3] = passed[...]
+    return [
+        (None, line, own),
+        (None, line ^ 1, one),
+        (None, line ^ 2, two),
+        (middle, line ^ 3, three),
+        (jnp.logical_not(middle), line ^ 3, passed),
+    ]
+
+
+def gather_line(line, refs, to_ref):
+    for where, z, ref in line_sources(line, refs):
+
+        def put(z=z, ref=ref):
+            to_ref[z] = ref[...]
+
+        put() if where is None else pl.when(where)(put)
 
 
 def place_rows_kernel(info, *refs):
@@ -765,8 +768,8 @@
         passed = lax.ppermute(two, "tensor", [(1, 0), (2, 3)])
         return [piece, one, two, three, passed]
 
-    def plane_pieces(piece):
-        return [piece] + [swap(piece, "dp", 2 * o) for o in range(1, outer)]
+    def plane_pieces(piece, others=None):
+        return [piece] + [swap(others[o] if others else piece, "dp", 2 * o) for o in range(1, outer)]
 
     own_base = (t % 2) * rows
     info = jnp.stack([d * seq_dev + t // 2, own_base, rows - own_base, d % 2, d // 2, t])
@@ -808,12 +811,27 @@
     attn_line = near_line(attn_piece)
     normed_one, *attn_line = lax.optimization_barrier((normed_one, *attn_line))
     biases = jnp.stack([piece[chunk:] for piece in attn_line])
-    ffn_line = gather(ffn_piece, "tensor", nt)
-    attn_pieces = plane_pieces(jnp.stack([piece[:chunk] for piece in attn_line]))
-    attn_near = jnp.stack(after(tuple(attn_pieces), ffn_line))
+    ffn_line = line_first(after(ffn_piece, attn_line[1]))
+    attn_line, biases = call(
+        stack_kernel,
+        [((nt, chunk, 4 * TILE), BF16), ((nt, 16, 4 * TILE), BF16)],
+        [],
+        attn_line,
+    )
+    attn_pieces = plane_pieces(attn_line)
+    up_line, down_line = call(
+        part_kernel, [((nt, chunk, hid), BF16)] * 2, [info], line_second(ffn_line)
+    )
+    attn_pieces, up_line, down_line = lax.optimization_barrier((attn_pieces, up_line, down_line))
+    attn_near = jnp.stack(attn_pieces)
     attn_w = attn_near, swap(attn_near, "dp", 1)
-    ffn_pieces = plane_pieces(after(ffn_line, attn_pieces[1]))
-    normed_one = after(normed_one, ffn_line)
+    ups = [jnp.stack([up_line, swap(up_line, "dp", 2)])]
+    downs = [jnp.stack([down_line] + [swap(down_line, "dp", 4 * o) for o in range(1, outer // 2)])]
+    ups += [swap(ups[0], "dp", 4 * o) for o in range(1, outer // 2)]
+    downs += [swap(downs[0], "dp", 2)]
+    plan = [(0, 0, (2 * o, 2 * o + 1)) for o in range(outer // 2)]
+    plan += [(1, 0, tuple(range(first, outer, 2))) for first in range(2)]
+    plan += [(part, 1, chips) for part, _, chips in plan]
 
     mixed, mixed_wide, total, q, k, v, prob = call(
         attend_kernel,
@@ -832,24 +850,28 @@
         limit=24,
         long=True,
     )
-    ffn_near = jnp.stack([after(each, mixed) for each in ffn_pieces])
-    ffn_w = ffn_near, swap(ffn_near, "dp", 1)
+    ups, downs, mixed = lax.optimization_barrier((ups, downs, mixed))
+    ffn_w = ups + downs
+    ffn_w += [swap(each, "dp", 1) for each in ffn_w]
     piece = rows // dp
-    hidden, normed_two, act, slope, *outs = call(
-        feed_kernel,
+    hidden, normed_two, act, slope, out_near, out_far = call(
+        functools.partial(feed_kernel, plan),
         [((rows, width), F32), ((rows, width), BF16)]
         + [((nt, rows, hid), BF16)] * 2
-        + [((piece, width), BF16)] * dp,
+        + [((outer, piece, width), BF16)] * 2,
         [info],
         [own, mixed, *attn_w, *ffn_w]
         + [row(b_out), row(ln2_gain), row(ln2_bias), biases, row(b_down)],
         scratch=[pltpu.VMEM((rows, width), F32), attn_full, ffn_full],
         limit=28,
     )
-    chunks = [outs[0]] + [swap(outs[k], "dp", k) for k in range(1, dp)]
+    chunks = call(
+        pair_kernel, [((2, piece, width), BF16)] * outer, [], [out_near, swap(out_far, "dp", 1)]
+    )
+    dy, chunks = lax.optimization_barrier((dy, chunks))
 
     grad_pre, grad_hidden, grad_hidden_low, numer, gtotal, sent, vec_two, vec_up = call(
-        feed_back_kernel,
+        functools.partial(feed_back_kernel, plan),
         [
             ((nt, rows, hid), BF16),
             ((rows, width), F32),
@@ -861,11 +883,15 @@
             ((nt, 1, hid), F32),
         ],
         [info],
-        [dy, *ffn_w, *attn_w, slope, hidden, row(ln2_gain), mixed_wide, total],
+        [dy, *attn_w, *ffn_w, slope, hidden, row(ln2_gain), mixed_wide, total],
         scratch=[attn_full, ffn_full],
         limit=28,
     )
     swapped = swap(sent, "tensor", 1)
+    chunks, grad_pre = lax.optimization_barrier(
+        (jnp.concatenate(plane_pieces(chunks[0], chunks)), grad_pre)
+    )
+    chunks = line_first(chunks)
     ffn_grads = call(
         feed_grads_kernel,
         [((outer, nt, 2, chunk, hid), BF16)] * 2,
@@ -882,10 +908,7 @@
         return [pieces[0]] + [swap(pieces[o], "dp", 2 * o) for o in range(1, outer)]
 
     ffn_parts = core_sums(ffn_grads[0], ffn_far)
-    gtotal, chunks, ffn_parts, swapped = lax.optimization_barrier(
-        (gtotal, jnp.stack(chunks), ffn_parts, swapped)
-    )
-    chunks = line_first(chunks)
+    gtotal, ffn_parts, swapped = lax.optimization_barrier((gtotal, ffn_parts, swapped))
     ffn_parts = plane_parts(ffn_parts)
     qkv_grads, vec_qv, grad_low, vec_one = call(
         attend_back_kernel,
@@ -908,7 +931,9 @@
         limit=20,
         long=True,
     )
-    row_pieces = line_first(grad_low)
+    chunks, grad_low, grad_hidden_low = lax.optimization_barrier(
+        (chunks, grad_low, grad_hidden_low)
+    )
     attn_near, attn_far = call(
         attend_grads_kernel,
         [((outer, nt * chunk + 16, 4 * TILE), BF16)] * 2,
@@ -916,19 +941,24 @@
         [normed_one, qkv_grads, grad_hidden_low, mixed, vec_two, vec_up, vec_one, vec_qv],
         scratch=[pltpu.VMEM((width, 4 * TILE), BF16)],
     )
-    attn_far, chunks, ffn_parts = lax.optimization_barrier((attn_far, chunks, ffn_parts))
+    row_pieces = line_first(grad_low)
+    chunks = line_second(chunks)
+    attn_far, ffn_parts = lax.optimization_barrier((attn_far, ffn_parts))
     attn_far = swap(attn_far, "dp", 1)
+    attn_parts = plane_parts(core_sums(attn_near, attn_far))
+    attn_parts, chunks, row_pieces[1] = lax.optimization_barrier(
+        (attn_parts, chunks, row_pieces[1])
+    )
     (dealt,) = call(
         deal_kernel,
         [((dp, seq_dev, nt // seq_dev, piece, width), BF16)],
         [info, dealing],
-        line_second(chunks),
+        chunks,
         scratch=[pltpu.VMEM((nt, dp, piece, width), BF16)],
     )
     dealt = exchange(dealt, "dp")
-    attn_parts = exchange(total_of([attn_near, attn_far]), "dp", planes)
-    attn_parts = total_of(list(attn_parts))
-    attn_parts, row_pieces = lax.optimization_barrier((attn_parts, row_pieces))
+    attn_parts = total_of(attn_parts)
+    attn_parts, row_pieces[2] = lax.optimization_barrier((attn_parts, row_pieces[2]))
     ffn_parts = total_of(ffn_parts)
     grads = [
         jnp.concatenate(
@@ -939,9 +969,8 @@
     ]
     grads = total_of([grads[0]] + [swap(grads[z], "tensor", z) for z in range(1, nt)])
     vectors = grads[3 * chunk :].astype(F32)
-    row_pieces = line_second(row_pieces)
+    grads, row_pieces = lax.optimization_barrier((grads, line_second(row_pieces)))
     near = jnp.stack(plane_pieces(grads[: 3 * chunk].reshape(3, chunk, width)))
-    near = after(near, dealt)
     grads = near, swap(near, "dp", 1)
     g_up, g_down, g_query, g_key, g_value, g_out = call(
         place_grads_kernel,

time: 233 us -> 213 us (0.914)
  waiting for transfers between devices: 99.6 us -> 90.3 us
  local copies, waits for them, and re-layouts: 12.4 us -> 3.76 us
  other arithmetic: 10.7 us -> 2.31 us
  starting transfers between devices: 57.6 us -> 62.4 us
    all_to_all x3 -> x1, starting transfers between devices: 14.2 us -> 4.37 us  [exchange(): lax.all_to_all(pieces, axis, 0, 0, tiled=True, axis_index_groups=groups)]
    ppermute x2 -> x3, waiting for transfers between devices: 28.9 us -> 20.2 us  [line_second(): three = lax.ppermute(after(piece, two), 'tensor', [(1, 2), (2, 1)])]
    ppermute x2 -> x3, starting transfers between devices: 2.63 us -> 8.52 us  [line_second(): passed = lax.ppermute(two, 'tensor', [(1, 0), (2, 3)])]
    ppermute x35 -> x41, starting transfers between devices: 35.8 us -> 40.5 us  [swap(): return lax.ppermute(piece, axis, [(i, i ^ distance) for i in range(size)])]
    ppermute x2 -> x3, starting transfers between devices: 4.87 us -> 9.02 us  [line_second(): three = lax.ppermute(after(piece, two), 'tensor', [(1, 2), (2, 1)])]
    another operation x9 -> x0, local copies, waits for them, and re-layouts: 3.96 us -> none  [the longest x4 2.16 us: local(): biases = jnp.stack([piece[chunk:] for piece in attn_line])]
    another operation x4 -> x3, other arithmetic: 3.41 us -> 0.23 us  [the longest x1 0.13 us: local(): attn_near = jnp.stack(attn_pieces)]
    convert_element_type x4 -> x5, other arithmetic: 5.02 us -> 1.86 us  [total_of(): functools.reduce(jnp.add, [piece.astype(F32) for piece in pieces])]
  transfers between devices with their start and end apart: 42 -> 48, of which waited for: 22 -> 26; matrix products, arithmetic and copies ran while one was open for 7% -> 2% of each run, Pallas kernels for 14% -> 18%
where the time goes in v5:
time: 213 us; the launch traced here: 212 us
  waiting for transfers between devices  90.3 us (42%)
  starting transfers between devices  62.4 us (29%)
  Pallas kernels  52.2 us (25%)
  local copies, waits for them, and re-layouts  3.76 us (2%)
  other arithmetic  2.31 us (1%)
    ppermute x41, waiting for transfers between devices, swap(): return lax.ppermute(piece, axis, [(i, i ^ distance) for i in range(size)])  69 us
    pallas_call x14, Pallas kernels, call(): pl.pallas_call(kernel, out_shape=[jax.ShapeDtypeStruct(shape, dtype) for...  49.7 us
    ppermute x41, starting transfers between devices, swap(): return lax.ppermute(piece, axis, [(i, i ^ distance) for i in range(size)])  40.5 us
    ppermute x3, waiting for transfers between devices, line_second(): three = lax.ppermute(after(piece, two), 'tensor', [(1, 2), (2, 1)])  20.2 us
    ppermute x3, starting transfers between devices, line_second(): three = lax.ppermute(after(piece, two), 'tensor', [(1, 2), (2, 1)])  9.02 us
    ppermute x3, starting transfers between devices, line_second(): passed = lax.ppermute(two, 'tensor', [(1, 0), (2, 3)])  8.52 us
    all_to_all x1, starting transfers between devices, exchange(): lax.all_to_all(pieces, axis, 0, 0, tiled=True, axis_index_groups=groups)  4.37 us
  transfers between devices with their start and end apart: 48, of which 26 were waited for; matrix products, arithmetic and copies ran while one was open for 2% of the time, Pallas kernels for 18%

profile of v5, /device:TPU:8, one launch (start us, length us, event | category | flops | bytes accessed | tf_op | source)
XLA Modules:
  0.0 212.2 jit_solution(16594410153073799465)
XLA Ops:
  1.3 2.5 %shard_map.315 = (bf16[80,512]{1,0:T(8,128)(2,1)}, bf16[2,64,512]{2,1,0:T(8,128)(2,1)}) custom-call(s32[6]{0:T(128)} %stack.72.info, bf16[512,128]{1,0:T(8,128)(2,1)} %q_ref.1, bf16[512,128]{1,0:T(8,128)(2,1)} %k_ref.1, bf16[512,128]{1,0:T(8,128)(2,1)} %v_ref.1, bf16[128,512]{1,0:T(8,128)(2,1)} %o_ref.1, bf16[512,512]{1,0:T(8,128)(2,1)} %up_ref.1, ...), custom_call_target="tpu_custom_call" | custom-call | tf_op jit(solution)/shard_map/pallas_call | solution.py:780
  3.9 1.6 collective-permute-start.2
  6.6 1.4 collective-permute-start
  9.3 1.3 shard_map.314
  10.6 2.0 collective-permute-done.2.refs_3_
  13.9 2.4 %collective-permute-start.7 = (bf16[2,64,512]{2,1,0:T(8,128)(2,1)S(1)}, bf16[2,64,512]{2,1,0:T(8,128)(2,1)S(1)}, u32[]{:S(2)}, u32[]{:S(2)}) collective-permute-start(bf16[2,64,512]{2,1,0:T(8,128)(2,1)S(1)} %copy-done.2), channel_id=1, source_target_pairs={{0,2},{1,3},{2,0},{3,1},{4,6},{5,7},{6,4},{7,5},{8,10},{9,11},{10,... | collective-permute-start | bytes 393224 | tf_op jit(solution)/shard_map/ppermute | solution.py:716
  16.3 2.5 %collective-permute-start.5 = (bf16[4,64,512]{2,1,0:T(8,128)(2,1)S(1)}, bf16[4,64,512]{2,1,0:T(8,128)(2,1)S(1)}, u32[]{:S(2)}, u32[]{:S(2)}) collective-permute-start(bf16[4,64,512]{2,1,0:T(8,128)(2,1)S(1)} %get-tuple-element.141), channel_id=1, source_target_pairs={{0,24},{4,28},{8,16},{12,20},{16,8},{20,12},{24,0},{28,4},{1,25},{... | collective-permute-start | bytes 786440 | tf_op jit(solution)/shard_map/ppermute | solution.py:716
  20.6 2.9 %collective-permute-start.8 = (bf16[2,64,512]{2,1,0:T(8,128)(2,1)S(1)}, bf16[2,64,512]{2,1,0:T(8,128)(2,1)S(1)}, u32[]{:S(2)}, u32[]{:S(2)}) collective-permute-start(bf16[2,64,512]{2,1,0:T(8,128)(2,1)S(1)} %copy-done.2), channel_id=1, source_target_pairs={{1,2},{2,1},{5,6},{6,5},{9,10},{10,9},{13,14},{14,13},{17,18},{18,... | collective-permute-start | bytes 393224 | tf_op jit(solution)/shard_map/ppermute | solution.py:767
  23.5 2.4 %collective-permute-start.9 = (bf16[2,64,512]{2,1,0:T(8,128)(2,1)S(1)}, bf16[2,64,512]{2,1,0:T(8,128)(2,1)S(1)}, u32[]{:S(2)}, u32[]{:S(2)}) collective-permute-start(bf16[2,64,512]{2,1,0:T(8,128)(2,1)S(1)} %collective-permute-done.7.refs_2_), channel_id=1, source_target_pairs={{1,0},{2,3},{5,4},{6,7},{9,8},{10,11},{13,12},{14,15},{17,16},{18,... | collective-permute-start | bytes 393224 | tf_op jit(solution)/shard_map/ppermute | solution.py:768
  25.9 1.5 collective-permute-done.8.refs_3_
  29.8 1.5 collective-permute-start.12
  32.2 6.3 %collective-permute-done.12 = bf16[4,64,512]{2,1,0:T(8,128)(2,1)S(1)} collective-permute-done((bf16[4,64,512]{2,1,0:T(8,128)(2,1)S(1)}, bf16[4,64,512]{2,1,0:T(8,128)(2,1)S(1)}, u32[]{:S(2)}, u32[]{:S(2)}) %collective-permute-start.12) | collective-permute-done | bytes 262176 | tf_op jit(solution)/shard_map/ppermute | solution.py:716
  38.6 1.6 collective-permute-start.13
  41.2 7.8 %shard_map.318 = (bf16[4,512,128]{2,1,0:T(8,128)(2,1)S(1)}, f32[4,512,128]{2,1,0:T(8,128)S(1)}, f32[4,512,128]{2,1,0:T(8,128)S(1)}, bf16[4,1024,128]{2,1,0:T(8,1...) custom-call(s32[6]{0:T(128)S(1)} %copy-done.4, ...), custom_call_target="tpu_custom_call" | custom-call | flops 10000000000 | bytes 1 | tf_op jit(solution)/shard_map/pallas_call | solution.py:693
  48.9 3.2 %collective-permute-done.13.refs_3_ = bf16[2,4,64,512]{3,2,1,0:T(8,128)(2,1)S(1)} collective-permute-done((bf16[2,4,64,512]{3,2,1,0:T(8,128)(2,1)S(1)}, bf16[2,4,64,512]{3,2,1,0:T(8,128)(2,1)S(1)}, u32[]{:S(2)}, u32[]{:S(2)}) %collective-permute-start.13) | collective-permute-done | bytes 524320 | tf_op jit(solution)/shard_map/ppermute | solution.py:716
  52.1 1.3 collective-permute-done.11.refs_1_
  57.6 5.3 %shard_map.319 = (f32[512,512]{1,0:T(8,128)S(1)}, bf16[512,512]{1,0:T(8,128)(2,1)S(1)}, bf16[4,512,512]{2,1,0:T(8,128)(2,1)S(1)}, bf16[4,512,512]{2,1,0:T(8,128)...) custom-call(s32[6]{0:T(128)S(1)} %copy-done.4, ...), custom_call_target="tpu_custom_call" | custom-call | flops 1 | bytes 1 | tf_op jit(solution)/shard_map/pallas_call | solution.py:693
  63.2 1.4 collective-permute-done.19.far_ref
  65.2 1.4 collective-permute-start.21
  66.6 1.5 collective-permute-start.22
  68.1 5.5 %shard_map.321 = (bf16[4,512,512]{2,1,0:T(8,128)(2,1)S(1)}, f32[512,512]{1,0:T(8,128)S(1)}, bf16[512,512]{1,0:T(8,128)(2,1)S(1)}, f32[4,512,128]{2,1,0:T(8,128)S...) custom-call(s32[6]{0:T(128)S(1)} %copy-done.4, ...), custom_call_target="tpu_custom_call" | custom-call | flops 1 | bytes 1 | tf_op jit(solution)/shard_map/pallas_call | solution.py:693
  73.8 3.0 %shard_map.322 = (bf16[4,4,2,64,512]{4,3,2,1,0:T(8,128)(2,1)S(1)}, bf16[4,4,2,64,512]{4,3,2,1,0:T(8,128)(2,1)S(1)}) custom-call(s32[6]{0:T(128)S(1)} %copy-done.4, bf16[512,512]{1,0:T(8,128)(2,1)S(1)} %get-tuple-element.165.normed_ref, bf16[4,512,512]{2,1,0:T(8,128)(2,1)S(1)} %get-tuple-element.166.act_ref, ...), custom_call_target="tpu_custom_call" | custom-call | flops 1 | bytes 1 | tf_op jit(solution)/shard_map/pallas_call | solution.py:693
  76.9 2.1 collective-permute-start.24
  79.5 1.7 collective-permute-start.25
  83.5 1.5 collective-permute-start.28
  86.1 14.0 %shard_map.323 = (bf16[4,512,384]{2,1,0:T(8,128)(2,1)S(1)}, f32[4,2,128]{2,1,0:T(2,128)S(1)}, bf16[512,512]{1,0:T(8,128)(2,1)S(1)}, f32[2,512]{1,0:T(2,128)S(1)}) custom-call(s32[6]{0:T(128)S(1)} %copy-done.4, s32[16]{0:T(128)S(1)} %copy-done.11, f32[4,512,128]{2,1,0:T(8,128)S(1)} %get-tuple-element.163.numer_ref, ...), custom_call_target="tpu_custom_call" | custom-call | flops 10000000000 | bytes 1 | tf_op jit(solution)/shard_map/pallas_call | solution.py:693
  100.1 2.2 %collective-permute-done.26.refs_2_ = bf16[8,64,512]{2,1,0:T(8,128)(2,1)S(1)} collective-permute-done((bf16[8,64,512]{2,1,0:T(8,128)(2,1)S(1)}, bf16[8,64,512]{2,1,0:T(8,128)(2,1)S(1)}, u32[]{:S(2)}, u32[]{:S(2)}) %collective-permute-start.26) | collective-permute-done | bytes 524320 | tf_op jit(solution)/shard_map/ppermute | solution.py:716
  102.3 2.2 %collective-permute-done.25.refs_1_ = bf16[8,64,512]{2,1,0:T(8,128)(2,1)S(1)} collective-permute-done((bf16[8,64,512]{2,1,0:T(8,128)(2,1)S(1)}, bf16[8,64,512]{2,1,0:T(8,128)(2,1)S(1)}, u32[]{:S(2)}, u32[]{:S(2)}) %collective-permute-start.25) | collective-permute-done | bytes 524320 | tf_op jit(solution)/shard_map/ppermute | solution.py:716
  104.5 2.5 %shard_map.324 = (bf16[4,272,512]{2,1,0:T(8,128)(2,1)S(1)}, bf16[4,272,512]{2,1,0:T(8,128)(2,1)S(1)}) custom-call(s32[6]{0:T(128)S(1)} %copy-done.4, bf16[512,512]{1,0:T(8,128)(2,1)S(1)} %get-tuple-element.127.normed_ref, bf16[4,512,384]{2,1,0:T(8,128)(2,1)S(1)} %get-tuple-element.183.grads_ref, bf16[512,512]{1,0:T(8,128)(2,1)S(1)} %get-tuple-element.187.grad_hidden_ref, ...), custom_call_target="tpu_custom_call" | custom-call | flops 1 | bytes 1 | tf_op jit(solution)/shard_map/pallas_call | solution.py:693
  108.1 2.9 %collective-permute-start.34 = (bf16[8,64,512]{2,1,0:T(8,128)(2,1)S(1)}, bf16[8,64,512]{2,1,0:T(8,128)(2,1)S(1)}, u32[]{:S(2)}, u32[]{:S(2)}) collective-permute-start(bf16[8,64,512]{2,1,0:T(8,128)(2,1)S(1)} %pad_maximum_fusion.4.refs_0_), channel_id=1, source_target_pairs={{1,2},{2,1},{5,6},{6,5},{9,10},{10,9},{13,14},{14,13},{17,18},{18,... | collective-permute-start | bytes 1572872 | tf_op jit(solution)/shard_map/ppermute | solution.py:767
  111.0 1.7 collective-permute-start.35
  112.8 2.2 %collective-permute-start.36 = (bf16[512,512]{1,0:T(8,128)(2,1)S(1)}, bf16[512,512]{1,0:T(8,128)(2,1)S(1)}, u32[]{:S(2)}, u32[]{:S(2)}) collective-permute-start(bf16[512,512]{1,0:T(8,128)(2,1)S(1)} %get-tuple-element.221.refs_0_), channel_id=1, source_target_pairs={{0,1},{1,0},{2,3},{3,2},{4,5},{5,4},{6,7},{7,6},{8,9},{9,8},{10,11... | collective-permute-start | bytes 1572872 | tf_op jit(solution)/shard_map/ppermute | solution.py:716
  115.4 1.8 collective-permute-start.33
  117.2 18.8 %collective-permute-done.34.refs_3_ = bf16[8,64,512]{2,1,0:T(8,128)(2,1)S(1)} collective-permute-done((bf16[8,64,512]{2,1,0:T(8,128)(2,1)S(1)}, bf16[8,64,512]{2,1,0:T(8,128)(2,1)S(1)}, u32[]{:S(2)}, u32[]{:S(2)}) %collective-permute-start.34) | collective-permute-done | bytes 524320 | tf_op jit(solution)/shard_map/ppermute | solution.py:767
  138.2 8.8 %collective-permute-done.36.refs_1_ = bf16[512,512]{1,0:T(8,128)(2,1)S(1)} collective-permute-done((bf16[512,512]{1,0:T(8,128)(2,1)S(1)}, bf16[512,512]{1,0:T(8,128)(2,1)S(1)}, u32[]{:S(2)}, u32[]{:S(2)}) %collective-permute-start.36) | collective-permute-done | bytes 524320 | tf_op jit(solution)/shard_map/ppermute | solution.py:716
  147.0 2.1 %shard_map.325 = bf16[8,2,2,64,512]{4,3,2,1,0:T(8,128)(2,1)} custom-call(s32[6]{0:T(128)S(1)} %copy-done.4, s32[16]{0:T(128)S(1)} %copy-done.12, bf16[8,64,512]{2,1,0:T(8,128)(2,1)S(1)} %pad_maximum_fusion.4.refs_0_, bf16[8,64,512]{2,1,0:T(8,128)(2,1)S(1)} %collective-permute-done.25.refs_1_, bf16[8,64,512]{2,1,0:T(8,128)(2,1)S(1)} %collective-permute-done.26.refs_2_, ...), custom_call_target="tpu_custom_call" | custom-call | flops 1 | bytes 1 | tf_op jit(solution)/shard_map/pallas_call | solution.py:693
  149.2 4.4 %all-to-all-start = ((bf16[8,2,2,64,512]{4,3,2,1,0:T(8,128)(2,1)}), bf16[8,2,2,64,512]{4,3,2,1,0:T(8,128)(2,1)}, u32[]{:S(2)}, u32[]{:S(2)}) async-start(bf16[8,2,2,64,512]{4,3,2,1,0:T(8,128)(2,1)} %shard_map.325), calls=%async_computation | async-start | bytes 4194304 | tf_op jit(solution)/shard_map/all_to_all | solution.py:707
  153.8 4.4 %collective-permute-start.42 = (bf16[512,512]{1,0:T(8,128)(2,1)S(1)}, bf16[512,512]{1,0:T(8,128)(2,1)S(1)}, u32[]{:S(2)}, u32[]{:S(2)}) collective-permute-start(bf16[512,512]{1,0:T(8,128)(2,1)S(1)} %collective-permute-done.37.refs_2_), channel_id=1, source_target_pairs={{1,0},{2,3},{5,4},{6,7},{9,8},{10,11},{13,12},{14,15},{17,16},{18,... | collective-permute-start | bytes 1572872 | tf_op jit(solution)/shard_map/ppermute | solution.py:768
  158.3 2.2 %collective-permute-start.39 = (bf16[208,512]{1,0:T(8,128)(2,1)S(1)}, bf16[208,512]{1,0:T(8,128)(2,1)S(1)}, u32[]{:S(2)}, u32[]{:S(2)}) collective-permute-start(bf16[208,512]{1,0:T(8,128)(2,1)S(1)} %get-tuple-element.259), channel_id=1, source_target_pairs={{0,2},{1,3},{2,0},{3,1},{4,6},{5,7},{6,4},{7,5},{8,10},{9,11},{10,... | collective-permute-start | bytes 638984 | tf_op jit(solution)/shard_map/ppermute | solution.py:716
  160.5 3.1 %collective-permute-start.41 = (bf16[512,512]{1,0:T(8,128)(2,1)S(1)}, bf16[512,512]{1,0:T(8,128)(2,1)S(1)}, u32[]{:S(2)}, u32[]{:S(2)}) collective-permute-start(bf16[512,512]{1,0:T(8,128)(2,1)S(1)} %get-tuple-element.221.refs_0_), channel_id=1, source_target_pairs={{1,2},{2,1},{5,6},{6,5},{9,10},{10,9},{13,14},{14,13},{17,18},{18,... | collective-permute-start | bytes 1572872 | tf_op jit(solution)/shard_map/ppermute | solution.py:767
  164.6 19.0 %collective-permute-done.38 = bf16[208,512]{1,0:T(8,128)(2,1)S(1)} collective-permute-done((bf16[208,512]{1,0:T(8,128)(2,1)S(1)}, bf16[208,512]{1,0:T(8,128)(2,1)S(1)}, u32[]{:S(2)}, u32[]{:S(2)}) %collective-permute-start.38) | collective-permute-done | bytes 213024 | tf_op jit(solution)/shard_map/ppermute | solution.py:716
  183.5 8.2 %collective-permute-done.40 = bf16[208,512]{1,0:T(8,128)(2,1)S(1)} collective-permute-done((bf16[208,512]{1,0:T(8,128)(2,1)S(1)}, bf16[208,512]{1,0:T(8,128)(2,1)S(1)}, u32[]{:S(2)}, u32[]{:S(2)}) %collective-permute-start.40) | collective-permute-done | bytes 213024 | tf_op jit(solution)/shard_map/ppermute | solution.py:716
  191.9 2.7 %collective-permute-start.45 = (bf16[3,64,512]{2,1,0:T(8,128)(2,1)S(1)}, bf16[3,64,512]{2,1,0:T(8,128)(2,1)S(1)}, u32[]{:S(2)}, u32[]{:S(2)}) collective-permute-start(bf16[3,64,512]{2,1,0:T(8,128)(2,1)S(1)} %bitcast.85), channel_id=1, source_target_pairs={{0,24},{4,28},{8,16},{12,20},{16,8},{20,12},{24,0},{28,4},{1,25},{... | collective-permute-start | bytes 589832 | tf_op jit(solution)/shard_map/ppermute | solution.py:716
  195.4 5.0 %collective-permute-done.45 = bf16[3,64,512]{2,1,0:T(8,128)(2,1)S(1)} collective-permute-done((bf16[3,64,512]{2,1,0:T(8,128)(2,1)S(1)}, bf16[3,64,512]{2,1,0:T(8,128)(2,1)S(1)}, u32[]{:S(2)}, u32[]{:S(2)}) %collective-permute-start.45) | collective-permute-done | bytes 196640 | tf_op jit(solution)/shard_map/ppermute | solution.py:716
  200.5 2.4 %collective-permute-done.44 = bf16[3,64,512]{2,1,0:T(8,128)(2,1)S(1)} collective-permute-done((bf16[3,64,512]{2,1,0:T(8,128)(2,1)S(1)}, bf16[3,64,512]{2,1,0:T(8,128)(2,1)S(1)}, u32[]{:S(2)}, u32[]{:S(2)}) %collective-permute-start.44) | collective-permute-done | bytes 196640 | tf_op jit(solution)/shard_map/ppermute | solution.py:716
  204.8 2.0 shard_map.327
  206.8 2.4 %shard_map.328 = (f32[512,512]{1,0:T(8,128)}, f32[512,512]{1,0:T(8,128)}, f32[512,128]{1,0:T(8,128)}, f32[512,128]{1,0:T(8,128)}, f32[512,128]{1,0:T(8,128)}, /*index=5*/f32[128,512]{1,0:T(8,128)}) custom-call(s32[6]{0:T(128)S(1)} %copy-done.4, bf16[4,3,64,512]{3,2,1,0:T(8,128)(2,1)S(1)} %pad_maximum_fusion.1.near_ref, ...), custom_call_target="tpu_custom_call" | custom-call | flops 1 | bytes 1 | tf_op jit(solution)/shard_map/pallas_call | solution.py:693
  209.2 3.0 %shard_map.326 = bf16[2,2,8,64,512]{4,3,2,1,0:T(8,128)(2,1)} custom-call(bf16[8,2,2,64,512]{4,3,2,1,0:T(8,128)(2,1)} %all-to-all-done.pieces_ref), custom_call_target="tpu_custom_call" | custom-call | flops 1 | bytes 1 | tf_op jit(solution)/shard_map/pallas_call | solution.py:693
  (114 shorter events, 27.3 us)
Async XLA Ops:
  3.9 8.8 %collective-permute-start.2 = (bf16[80,512]{1,0:T(8,128)(2,1)}, bf16[80,512]{1,0:T(8,128)(2,1)S(1)}, u32[]{:S(2)}, u32[]{:S(2)}) collective-permute-start(bf16[80,512]{1,0:T(8,128)(2,1)} %get-tuple-element.128.refs_0_), channel_id=1, source_target_pairs={{0,3},{1,2},{2,1},{3,0},{4,7},{5,6},{6,5},{7,4},{8,11},{9,10},{10,... | collective-permute-start | bytes 245768 | tf_op jit(solution)/shard_map/ppermute | solution.py:716
  5.5 7.5 %collective-permute-start.1 = (bf16[80,512]{1,0:T(8,128)(2,1)}, bf16[80,512]{1,0:T(8,128)(2,1)S(1)}, u32[]{:S(2)}, u32[]{:S(2)}) collective-permute-start(bf16[80,512]{1,0:T(8,128)(2,1)} %get-tuple-element.128.refs_0_), channel_id=1, source_target_pairs={{0,2},{1,3},{2,0},{3,1},{4,6},{5,7},{6,4},{7,5},{8,10},{9,11},{10,... | collective-permute-start | bytes 245768 | tf_op jit(solution)/shard_map/ppermute | solution.py:716
  6.6 7.3 %collective-permute-start = (bf16[80,512]{1,0:T(8,128)(2,1)}, bf16[80,512]{1,0:T(8,128)(2,1)S(1)}, u32[]{:S(2)}, u32[]{:S(2)}) collective-permute-start(bf16[80,512]{1,0:T(8,128)(2,1)} %get-tuple-element.128.refs_0_), channel_id=1, source_target_pairs={{0,1},{1,0},{2,3},{3,2},{4,5},{5,4},{6,7},{7,6},{8,9},{9,8},{10,11... | collective-permute-start | bytes 245768 | tf_op jit(solution)/shard_map/ppermute | solution.py:716
  13.9 6.7 %collective-permute-start.7 = (bf16[2,64,512]{2,1,0:T(8,128)(2,1)S(1)}, bf16[2,64,512]{2,1,0:T(8,128)(2,1)S(1)}, u32[]{:S(2)}, u32[]{:S(2)}) collective-permute-start(bf16[2,64,512]{2,1,0:T(8,128)(2,1)S(1)} %copy-done.2), channel_id=1, source_target_pairs={{0,2},{1,3},{2,0},{3,1},{4,6},{5,7},{6,4},{7,5},{8,10},{9,11},{10,... | collective-permute-start | bytes 393224 | tf_op jit(solution)/shard_map/ppermute | solution.py:716
  16.3 7.2 %collective-permute-start.6 = (bf16[2,64,512]{2,1,0:T(8,128)(2,1)S(1)}, bf16[2,64,512]{2,1,0:T(8,128)(2,1)S(1)}, u32[]{:S(2)}, u32[]{:S(2)}) collective-permute-start(bf16[2,64,512]{2,1,0:T(8,128)(2,1)S(1)} %copy-done.2), channel_id=1, source_target_pairs={{0,1},{1,0},{2,3},{3,2},{4,5},{5,4},{6,7},{7,6},{8,9},{9,8},{10,11... | collective-permute-start | bytes 393224 | tf_op jit(solution)/shard_map/ppermute | solution.py:716
  16.3 12.7 %collective-permute-start.5 = (bf16[4,64,512]{2,1,0:T(8,128)(2,1)S(1)}, bf16[4,64,512]{2,1,0:T(8,128)(2,1)S(1)}, u32[]{:S(2)}, u32[]{:S(2)}) collective-permute-start(bf16[4,64,512]{2,1,0:T(8,128)(2,1)S(1)} %get-tuple-element.141), channel_id=1, source_target_pairs={{0,24},{4,28},{8,16},{12,20},{16,8},{20,12},{24,0},{28,4},{1,25},{... | collective-permute-start | bytes 786440 | tf_op jit(solution)/shard_map/ppermute | solution.py:716
  18.8 10.6 %collective-permute-start.4 = (bf16[4,64,512]{2,1,0:T(8,128)(2,1)S(1)}, bf16[4,64,512]{2,1,0:T(8,128)(2,1)S(1)}, u32[]{:S(2)}, u32[]{:S(2)}) collective-permute-start(bf16[4,64,512]{2,1,0:T(8,128)(2,1)S(1)} %get-tuple-element.141), channel_id=1, source_target_pairs={{0,16},{4,20},{8,24},{12,28},{16,0},{20,4},{24,8},{28,12},{1,17},{... | collective-permute-start | bytes 786440 | tf_op jit(solution)/shard_map/ppermute | solution.py:716
  19.4 10.2 %collective-permute-start.3 = (bf16[4,64,512]{2,1,0:T(8,128)(2,1)S(1)}, bf16[4,64,512]{2,1,0:T(8,128)(2,1)S(1)}, u32[]{:S(2)}, u32[]{:S(2)}) collective-permute-start(bf16[4,64,512]{2,1,0:T(8,128)(2,1)S(1)} %get-tuple-element.141), channel_id=1, source_target_pairs={{0,8},{4,12},{8,0},{12,4},{16,24},{20,28},{24,16},{28,20},{1,9},{5... | collective-permute-start | bytes 786440 | tf_op jit(solution)/shard_map/ppermute | solution.py:716
  20.6 6.8 %collective-permute-start.8 = (bf16[2,64,512]{2,1,0:T(8,128)(2,1)S(1)}, bf16[2,64,512]{2,1,0:T(8,128)(2,1)S(1)}, u32[]{:S(2)}, u32[]{:S(2)}) collective-permute-start(bf16[2,64,512]{2,1,0:T(8,128)(2,1)S(1)} %copy-done.2), channel_id=1, source_target_pairs={{1,2},{2,1},{5,6},{6,5},{9,10},{10,9},{13,14},{14,13},{17,18},{18,... | collective-permute-start | bytes 393224 | tf_op jit(solution)/shard_map/ppermute | solution.py:767
  23.5 5.0 %collective-permute-start.9 = (bf16[2,64,512]{2,1,0:T(8,128)(2,1)S(1)}, bf16[2,64,512]{2,1,0:T(8,128)(2,1)S(1)}, u32[]{:S(2)}, u32[]{:S(2)}) collective-permute-start(bf16[2,64,512]{2,1,0:T(8,128)(2,1)S(1)} %collective-permute-done.7.refs_2_), channel_id=1, source_target_pairs={{1,0},{2,3},{5,4},{6,7},{9,8},{10,11},{13,12},{14,15},{17,16},{18,... | collective-permute-start | bytes 393224 | tf_op jit(solution)/shard_map/ppermute | solution.py:768
  29.7 11.4 %collective-permute-start.14 = (bf16[4,4,64,512]{3,2,1,0:T(8,128)(2,1)S(1)}, bf16[4,4,64,512]{3,2,1,0:T(8,128)(2,1)S(1)}, u32[]{:S(2)}, u32[]{:S(2)}) collective-permute-start(bf16[4,4,64,512]{3,2,1,0:T(8,128)(2,1)S(1)} %pad_maximum_fusion.near_ref), channel_id=1, source_target_pairs={{0,4},{4,0},{8,12},{12,8},{16,20},{20,16},{24,28},{28,24},{1,5},{5... | collective-permute-start | bytes 3145736 | tf_op jit(solution)/shard_map/ppermute | solution.py:716
  29.8 8.7 %collective-permute-start.12 = (bf16[4,64,512]{2,1,0:T(8,128)(2,1)S(1)}, bf16[4,64,512]{2,1,0:T(8,128)(2,1)S(1)}, u32[]{:S(2)}, u32[]{:S(2)}) collective-permute-start(bf16[4,64,512]{2,1,0:T(8,128)(2,1)S(1)} %get-tuple-element.139), channel_id=1, source_target_pairs={{0,16},{4,20},{8,24},{12,28},{16,0},{20,4},{24,8},{28,12},{1,17},{... | collective-permute-start | bytes 786440 | tf_op jit(solution)/shard_map/ppermute | solution.py:716
  31.3 8.8 %collective-permute-start.10 = (bf16[4,64,512]{2,1,0:T(8,128)(2,1)S(1)}, bf16[4,64,512]{2,1,0:T(8,128)(2,1)S(1)}, u32[]{:S(2)}, u32[]{:S(2)}) collective-permute-start(bf16[4,64,512]{2,1,0:T(8,128)(2,1)S(1)} %get-tuple-element.138), channel_id=1, source_target_pairs={{0,8},{4,12},{8,0},{12,4},{16,24},{20,28},{24,16},{28,20},{1,9},{5... | collective-permute-start | bytes 786440 | tf_op jit(solution)/shard_map/ppermute | solution.py:716
  38.6 13.6 %collective-permute-start.13 = (bf16[2,4,64,512]{3,2,1,0:T(8,128)(2,1)S(1)}, bf16[2,4,64,512]{3,2,1,0:T(8,128)(2,1)S(1)}, u32[]{:S(2)}, u32[]{:S(2)}) collective-permute-start(bf16[2,4,64,512]{3,2,1,0:T(8,128)(2,1)S(1)} %pad_maximum_fusion.3.refs_2_), channel_id=1, source_target_pairs={{0,8},{4,12},{8,0},{12,4},{16,24},{20,28},{24,16},{28,20},{1,9},{5... | collective-permute-start | bytes 1572872 | tf_op jit(solution)/shard_map/ppermute | solution.py:716
  40.2 13.3 %collective-permute-start.11 = (bf16[2,4,64,512]{3,2,1,0:T(8,128)(2,1)S(1)}, bf16[2,4,64,512]{3,2,1,0:T(8,128)(2,1)S(1)}, u32[]{:S(2)}, u32[]{:S(2)}) collective-permute-start(bf16[2,4,64,512]{3,2,1,0:T(8,128)(2,1)S(1)} %pad_maximum_fusion.2.refs_0_), channel_id=1, source_target_pairs={{0,16},{4,20},{8,24},{12,28},{16,0},{20,4},{24,8},{28,12},{1,17},{... | collective-permute-start | bytes 1572872 | tf_op jit(solution)/shard_map/ppermute | solution.py:716
  53.5 1.9 collective-permute-start.15
  53.5 2.7 %collective-permute-start.16 = (bf16[2,4,64,512]{3,2,1,0:T(8,128)(2,1)S(1)}, bf16[2,4,64,512]{3,2,1,0:T(8,128)(2,1)S(1)}, u32[]{:S(2)}, u32[]{:S(2)}) collective-permute-start(bf16[2,4,64,512]{3,2,1,0:T(8,128)(2,1)S(1)} %collective-permute-done.11.refs_1_), channel_id=1, source_target_pairs={{0,4},{4,0},{8,12},{12,8},{16,20},{20,16},{24,28},{28,24},{1,5},{5... | collective-permute-start | bytes 1572872 | tf_op jit(solution)/shard_map/ppermute | solution.py:716
  54.0 2.9 %collective-permute-start.17 = (bf16[2,4,64,512]{3,2,1,0:T(8,128)(2,1)S(1)}, bf16[2,4,64,512]{3,2,1,0:T(8,128)(2,1)S(1)}, u32[]{:S(2)}, u32[]{:S(2)}) collective-permute-start(bf16[2,4,64,512]{3,2,1,0:T(8,128)(2,1)S(1)} %pad_maximum_fusion.3.refs_2_), channel_id=1, source_target_pairs={{0,4},{4,0},{8,12},{12,8},{16,20},{20,16},{24,28},{28,24},{1,5},{5... | collective-permute-start | bytes 1572872 | tf_op jit(solution)/shard_map/ppermute | solution.py:716
  54.0 3.6 %collective-permute-start.18 = (bf16[2,4,64,512]{3,2,1,0:T(8,128)(2,1)S(1)}, bf16[2,4,64,512]{3,2,1,0:T(8,128)(2,1)S(1)}, u32[]{:S(2)}, u32[]{:S(2)}) collective-permute-start(bf16[2,4,64,512]{3,2,1,0:T(8,128)(2,1)S(1)} %collective-permute-done.13.refs_3_), channel_id=1, source_target_pairs={{0,4},{4,0},{8,12},{12,8},{16,20},{20,16},{24,28},{28,24},{1,5},{5... | collective-permute-start | bytes 1572872 | tf_op jit(solution)/shard_map/ppermute | solution.py:716
  62.9 1.6 collective-permute-start.19
  64.6 9.1 %collective-permute-start.20 = (bf16[2,64,512]{2,1,0:T(8,128)(2,1)S(1)}, bf16[2,64,512]{2,1,0:T(8,128)(2,1)S(1)}, u32[]{:S(2)}, u32[]{:S(2)}) collective-permute-start(bf16[2,64,512]{2,1,0:T(8,128)(2,1)S(1)} %get-tuple-element.168), channel_id=1, source_target_pairs={{0,8},{4,12},{8,0},{12,4},{16,24},{20,28},{24,16},{28,20},{1,9},{5... | collective-permute-start | bytes 393224 | tf_op jit(solution)/shard_map/ppermute | solution.py:716
  65.2 8.5 %collective-permute-start.21 = (bf16[2,64,512]{2,1,0:T(8,128)(2,1)S(1)}, bf16[2,64,512]{2,1,0:T(8,128)(2,1)S(1)}, u32[]{:S(2)}, u32[]{:S(2)}) collective-permute-start(bf16[2,64,512]{2,1,0:T(8,128)(2,1)S(1)} %get-tuple-element.169), channel_id=1, source_target_pairs={{0,16},{4,20},{8,24},{12,28},{16,0},{20,4},{24,8},{28,12},{1,17},{... | collective-permute-start | bytes 393224 | tf_op jit(solution)/shard_map/ppermute | solution.py:716
  66.6 7.1 %collective-permute-start.22 = (bf16[2,64,512]{2,1,0:T(8,128)(2,1)S(1)}, bf16[2,64,512]{2,1,0:T(8,128)(2,1)S(1)}, u32[]{:S(2)}, u32[]{:S(2)}) collective-permute-start(bf16[2,64,512]{2,1,0:T(8,128)(2,1)S(1)} %get-tuple-element.170), channel_id=1, source_target_pairs={{0,24},{4,28},{8,16},{12,20},{16,8},{20,12},{24,0},{28,4},{1,25},{... | collective-permute-start | bytes 393224 | tf_op jit(solution)/shard_map/ppermute | solution.py:716
  76.9 4.4 %collective-permute-start.23 = (bf16[4,4,2,64,512]{4,3,2,1,0:T(8,128)(2,1)S(1)}, bf16[4,4,2,64,512]{4,3,2,1,0:T(8,128)(2,1)S(1)}, u32[]{:S(2)}, u32[]{:S(2)}) collective-permute-start(bf16[4,4,2,64,512]{4,3,2,1,0:T(8,128)(2,1)S(1)} %get-tuple-element.174), channel_id=1, source_target_pairs={{0,4},{4,0},{8,12},{12,8},{16,20},{20,16},{24,28},{28,24},{1,5},{5... | collective-permute-start | bytes 6291464 | tf_op jit(solution)/shard_map/ppermute | solution.py:716
  76.9 5.7 %collective-permute-start.24 = (f32[4,32,128]{2,1,0:T(8,128)S(1)}, f32[4,32,128]{2,1,0:T(8,128)S(1)}, u32[]{:S(2)}, u32[]{:S(2)}) collective-permute-start(f32[4,32,128]{2,1,0:T(8,128)S(1)} %get-tuple-element.175), channel_id=1, source_target_pairs={{0,1},{1,0},{2,3},{3,2},{4,5},{5,4},{6,7},{7,6},{8,9},{9,8},{10,11... | collective-permute-start | bytes 196616 | tf_op jit(solution)/shard_map/ppermute | solution.py:716
  79.0 23.3 %collective-permute-start.26 = (bf16[8,64,512]{2,1,0:T(8,128)(2,1)S(1)}, bf16[8,64,512]{2,1,0:T(8,128)(2,1)S(1)}, u32[]{:S(2)}, u32[]{:S(2)}) collective-permute-start(bf16[8,64,512]{2,1,0:T(8,128)(2,1)S(1)} %pad_maximum_fusion.4.refs_0_), channel_id=1, source_target_pairs={{0,2},{1,3},{2,0},{3,1},{4,6},{5,7},{6,4},{7,5},{8,10},{9,11},{10,... | collective-permute-start | bytes 1572872 | tf_op jit(solution)/shard_map/ppermute | solution.py:716
  79.5 25.0 %collective-permute-start.25 = (bf16[8,64,512]{2,1,0:T(8,128)(2,1)S(1)}, bf16[8,64,512]{2,1,0:T(8,128)(2,1)S(1)}, u32[]{:S(2)}, u32[]{:S(2)}) collective-permute-start(bf16[8,64,512]{2,1,0:T(8,128)(2,1)S(1)} %pad_maximum_fusion.4.refs_0_), channel_id=1, source_target_pairs={{0,1},{1,0},{2,3},{3,2},{4,5},{5,4},{6,7},{7,6},{8,9},{9,8},{10,11... | collective-permute-start | bytes 1572872 | tf_op jit(solution)/shard_map/ppermute | solution.py:716
  82.6 24.4 %collective-permute-start.27 = (bf16[4,2,64,512]{3,2,1,0:T(8,128)(2,1)S(1)}, bf16[4,2,64,512]{3,2,1,0:T(8,128)(2,1)S(1)}, u32[]{:S(2)}, u32[]{:S(2)}) collective-permute-start(bf16[4,2,64,512]{3,2,1,0:T(8,128)(2,1)S(1)} %get-tuple-element.195), channel_id=1, source_target_pairs={{0,8},{4,12},{8,0},{12,4},{16,24},{20,28},{24,16},{28,20},{1,9},{5... | collective-permute-start | bytes 1572872 | tf_op jit(solution)/shard_map/ppermute | solution.py:716
  83.5 24.6 %collective-permute-start.28 = (bf16[4,2,64,512]{3,2,1,0:T(8,128)(2,1)S(1)}, bf16[4,2,64,512]{3,2,1,0:T(8,128)(2,1)S(1)}, u32[]{:S(2)}, u32[]{:S(2)}) collective-permute-start(bf16[4,2,64,512]{3,2,1,0:T(8,128)(2,1)S(1)} %get-tuple-element.196), channel_id=1, source_target_pairs={{0,16},{4,20},{8,24},{12,28},{16,0},{20,4},{24,8},{28,12},{1,17},{... | collective-permute-start | bytes 1572872 | tf_op jit(solution)/shard_map/ppermute | solution.py:716
  85.0 23.1 %collective-permute-start.29 = (bf16[4,2,64,512]{3,2,1,0:T(8,128)(2,1)S(1)}, bf16[4,2,64,512]{3,2,1,0:T(8,128)(2,1)S(1)}, u32[]{:S(2)}, u32[]{:S(2)}) collective-permute-start(bf16[4,2,64,512]{3,2,1,0:T(8,128)(2,1)S(1)} %get-tuple-element.197), channel_id=1, source_target_pairs={{0,24},{4,28},{8,16},{12,20},{16,8},{20,12},{24,0},{28,4},{1,25},{... | collective-permute-start | bytes 1572872 | tf_op jit(solution)/shard_map/ppermute | solution.py:716
  108.1 7.0 %collective-permute-start.30 = (bf16[4,272,512]{2,1,0:T(8,128)(2,1)S(1)}, bf16[4,272,512]{2,1,0:T(8,128)(2,1)S(1)}, u32[]{:S(2)}, u32[]{:S(2)}) collective-permute-start(bf16[4,272,512]{2,1,0:T(8,128)(2,1)S(1)} %get-tuple-element.198), channel_id=1, source_target_pairs={{0,4},{4,0},{8,12},{12,8},{16,20},{20,16},{24,28},{28,24},{1,5},{5... | collective-permute-start | bytes 3342344 | tf_op jit(solution)/shard_map/ppermute | solution.py:716
  108.1 27.8 %collective-permute-start.34 = (bf16[8,64,512]{2,1,0:T(8,128)(2,1)S(1)}, bf16[8,64,512]{2,1,0:T(8,128)(2,1)S(1)}, u32[]{:S(2)}, u32[]{:S(2)}) collective-permute-start(bf16[8,64,512]{2,1,0:T(8,128)(2,1)S(1)} %pad_maximum_fusion.4.refs_0_), channel_id=1, source_target_pairs={{1,2},{2,1},{5,6},{6,5},{9,10},{10,9},{13,14},{14,13},{17,18},{18,... | collective-permute-start | bytes 1572872 | tf_op jit(solution)/shard_map/ppermute | solution.py:767
  111.0 25.8 %collective-permute-start.35 = (bf16[8,64,512]{2,1,0:T(8,128)(2,1)S(1)}, bf16[8,64,512]{2,1,0:T(8,128)(2,1)S(1)}, u32[]{:S(2)}, u32[]{:S(2)}) collective-permute-start(bf16[8,64,512]{2,1,0:T(8,128)(2,1)S(1)} %collective-permute-done.26.refs_2_), channel_id=1, source_target_pairs={{1,0},{2,3},{5,4},{6,7},{9,8},{10,11},{13,12},{14,15},{17,16},{18,... | collective-permute-start | bytes 1572872 | tf_op jit(solution)/shard_map/ppermute | solution.py:768
  112.7 41.0 %collective-permute-start.37 = (bf16[512,512]{1,0:T(8,128)(2,1)S(1)}, bf16[512,512]{1,0:T(8,128)(2,1)S(1)}, u32[]{:S(2)}, u32[]{:S(2)}) collective-permute-start(bf16[512,512]{1,0:T(8,128)(2,1)S(1)} %get-tuple-element.221.refs_0_), channel_id=1, source_target_pairs={{0,2},{1,3},{2,0},{3,1},{4,6},{5,7},{6,4},{7,5},{8,10},{9,11},{10,... | collective-permute-start | bytes 1572872 | tf_op jit(solution)/shard_map/ppermute | solution.py:716
  112.8 34.2 %collective-permute-start.36 = (bf16[512,512]{1,0:T(8,128)(2,1)S(1)}, bf16[512,512]{1,0:T(8,128)(2,1)S(1)}, u32[]{:S(2)}, u32[]{:S(2)}) collective-permute-start(bf16[512,512]{1,0:T(8,128)(2,1)S(1)} %get-tuple-element.221.refs_0_), channel_id=1, source_target_pairs={{0,1},{1,0},{2,3},{3,2},{4,5},{5,4},{6,7},{7,6},{8,9},{9,8},{10,11... | collective-permute-start | bytes 1572872 | tf_op jit(solution)/shard_map/ppermute | solution.py:716
  115.4 31.6 %collective-permute-start.33 = (bf16[272,512]{1,0:T(8,128)(2,1)S(1)}, bf16[272,512]{1,0:T(8,128)(2,1)S(1)}, u32[]{:S(2)}, u32[]{:S(2)}) collective-permute-start(bf16[272,512]{1,0:T(8,128)(2,1)S(1)} %get-tuple-element.237), channel_id=1, source_target_pairs={{0,24},{4,28},{8,16},{12,20},{16,8},{20,12},{24,0},{28,4},{1,25},{... | collective-permute-start | bytes 835592 | tf_op jit(solution)/shard_map/ppermute | solution.py:716
  135.9 11.1 %collective-permute-start.32 = (bf16[272,512]{1,0:T(8,128)(2,1)S(1)}, bf16[272,512]{1,0:T(8,128)(2,1)S(1)}, u32[]{:S(2)}, u32[]{:S(2)}) collective-permute-start(bf16[272,512]{1,0:T(8,128)(2,1)S(1)} %get-tuple-element.238), channel_id=1, source_target_pairs={{0,16},{4,20},{8,24},{12,28},{16,0},{20,4},{24,8},{28,12},{1,17},{... | collective-permute-start | bytes 835592 | tf_op jit(solution)/shard_map/ppermute | solution.py:716
  136.9 10.1 %collective-permute-start.31 = (bf16[272,512]{1,0:T(8,128)(2,1)S(1)}, bf16[272,512]{1,0:T(8,128)(2,1)S(1)}, u32[]{:S(2)}, u32[]{:S(2)}) collective-permute-start(bf16[272,512]{1,0:T(8,128)(2,1)S(1)} %get-tuple-element.239), channel_id=1, source_target_pairs={{0,8},{4,12},{8,0},{12,4},{16,24},{20,28},{24,16},{28,20},{1,9},{5... | collective-permute-start | bytes 835592 | tf_op jit(solution)/shard_map/ppermute | solution.py:716
  149.2 60.0 %all-to-all-start = ((bf16[8,2,2,64,512]{4,3,2,1,0:T(8,128)(2,1)}), bf16[8,2,2,64,512]{4,3,2,1,0:T(8,128)(2,1)}, u32[]{:S(2)}, u32[]{:S(2)}) async-start(bf16[8,2,2,64,512]{4,3,2,1,0:T(8,128)(2,1)} %shard_map.325), calls=%async_computation | async-start | bytes 4194304 | tf_op jit(solution)/shard_map/all_to_all | solution.py:707
  153.8 38.1 %collective-permute-start.42 = (bf16[512,512]{1,0:T(8,128)(2,1)S(1)}, bf16[512,512]{1,0:T(8,128)(2,1)S(1)}, u32[]{:S(2)}, u32[]{:S(2)}) collective-permute-start(bf16[512,512]{1,0:T(8,128)(2,1)S(1)} %collective-permute-done.37.refs_2_), channel_id=1, source_target_pairs={{1,0},{2,3},{5,4},{6,7},{9,8},{10,11},{13,12},{14,15},{17,16},{18,... | collective-permute-start | bytes 1572872 | tf_op jit(solution)/shard_map/ppermute | solution.py:768
  158.2 25.3 %collective-permute-start.38 = (bf16[208,512]{1,0:T(8,128)(2,1)S(1)}, bf16[208,512]{1,0:T(8,128)(2,1)S(1)}, u32[]{:S(2)}, u32[]{:S(2)}) collective-permute-start(bf16[208,512]{1,0:T(8,128)(2,1)S(1)} %get-tuple-element.258), channel_id=1, source_target_pairs={{0,1},{1,0},{2,3},{3,2},{4,5},{5,4},{6,7},{7,6},{8,9},{9,8},{10,11... | collective-permute-start | bytes 638984 | tf_op jit(solution)/shard_map/ppermute | solution.py:716
  158.3 25.2 %collective-permute-start.39 = (bf16[208,512]{1,0:T(8,128)(2,1)S(1)}, bf16[208,512]{1,0:T(8,128)(2,1)S(1)}, u32[]{:S(2)}, u32[]{:S(2)}) collective-permute-start(bf16[208,512]{1,0:T(8,128)(2,1)S(1)} %get-tuple-element.259), channel_id=1, source_target_pairs={{0,2},{1,3},{2,0},{3,1},{4,6},{5,7},{6,4},{7,5},{8,10},{9,11},{10,... | collective-permute-start | bytes 638984 | tf_op jit(solution)/shard_map/ppermute | solution.py:716
  160.5 31.3 %collective-permute-start.41 = (bf16[512,512]{1,0:T(8,128)(2,1)S(1)}, bf16[512,512]{1,0:T(8,128)(2,1)S(1)}, u32[]{:S(2)}, u32[]{:S(2)}) collective-permute-start(bf16[512,512]{1,0:T(8,128)(2,1)S(1)} %get-tuple-element.221.refs_0_), channel_id=1, source_target_pairs={{1,2},{2,1},{5,6},{6,5},{9,10},{10,9},{13,14},{14,13},{17,18},{18,... | collective-permute-start | bytes 1572872 | tf_op jit(solution)/shard_map/ppermute | solution.py:767
  163.7 28.0 %collective-permute-start.40 = (bf16[208,512]{1,0:T(8,128)(2,1)S(1)}, bf16[208,512]{1,0:T(8,128)(2,1)S(1)}, u32[]{:S(2)}, u32[]{:S(2)}) collective-permute-start(bf16[208,512]{1,0:T(8,128)(2,1)S(1)} %pad_maximum_fusion.8), channel_id=1, source_target_pairs={{0,3},{1,2},{2,1},{3,0},{4,7},{5,6},{6,5},{7,4},{8,11},{9,10},{10,... | collective-permute-start | bytes 638984 | tf_op jit(solution)/shard_map/ppermute | solution.py:716
  191.9 8.6 %collective-permute-start.45 = (bf16[3,64,512]{2,1,0:T(8,128)(2,1)S(1)}, bf16[3,64,512]{2,1,0:T(8,128)(2,1)S(1)}, u32[]{:S(2)}, u32[]{:S(2)}) collective-permute-start(bf16[3,64,512]{2,1,0:T(8,128)(2,1)S(1)} %bitcast.85), channel_id=1, source_target_pairs={{0,24},{4,28},{8,16},{12,20},{16,8},{20,12},{24,0},{28,4},{1,25},{... | collective-permute-start | bytes 589832 | tf_op jit(solution)/shard_map/ppermute | solution.py:716
  194.5 8.3 %collective-permute-start.44 = (bf16[3,64,512]{2,1,0:T(8,128)(2,1)S(1)}, bf16[3,64,512]{2,1,0:T(8,128)(2,1)S(1)}, u32[]{:S(2)}, u32[]{:S(2)}) collective-permute-start(bf16[3,64,512]{2,1,0:T(8,128)(2,1)S(1)} %bitcast.86), channel_id=1, source_target_pairs={{0,16},{4,20},{8,24},{12,28},{16,0},{20,4},{24,8},{28,12},{1,17},{... | collective-permute-start | bytes 589832 | tf_op jit(solution)/shard_map/ppermute | solution.py:716
  195.1 7.8 %collective-permute-start.43 = (bf16[3,64,512]{2,1,0:T(8,128)(2,1)S(1)}, bf16[3,64,512]{2,1,0:T(8,128)(2,1)S(1)}, u32[]{:S(2)}, u32[]{:S(2)}) collective-permute-start(bf16[3,64,512]{2,1,0:T(8,128)(2,1)S(1)} %bitcast.87), channel_id=1, source_target_pairs={{0,8},{4,12},{8,0},{12,4},{16,24},{20,28},{24,16},{28,20},{1,9},{5... | collective-permute-start | bytes 589832 | tf_op jit(solution)/shard_map/ppermute | solution.py:716
  203.0 3.8 %collective-permute-start.46 = (bf16[4,3,64,512]{3,2,1,0:T(8,128)(2,1)S(1)}, bf16[4,3,64,512]{3,2,1,0:T(8,128)(2,1)S(1)}, u32[]{:S(2)}, u32[]{:S(2)}) collective-permute-start(bf16[4,3,64,512]{3,2,1,0:T(8,128)(2,1)S(1)} %pad_maximum_fusion.1.near_ref), channel_id=1, source_target_pairs={{0,4},{4,0},{8,12},{12,8},{16,20},{20,16},{24,28},{28,24},{1,5},{5... | collective-permute-start | bytes 2359304 | tf_op jit(solution)/shard_map/ppermute | solution.py:716
  (13 other events, 221.8 us)

commit v6 on v5

--- a/solution.py
+++ b/solution.py
@@ -969,8 +969,19 @@
     ]
     grads = total_of([grads[0]] + [swap(grads[z], "tensor", z) for z in range(1, nt)])
     vectors = grads[3 * chunk :].astype(F32)
-    grads, row_pieces = lax.optimization_barrier((grads, line_second(row_pieces)))
+    row_pieces = line_second(row_pieces)
     near = jnp.stack(plane_pieces(grads[: 3 * chunk].reshape(3, chunk, width)))
+    (grad_tokens,) = call(
+        place_rows_kernel, [((nt, rows, width), BF16)], [info], row_pieces
+    )
+    grad_tokens = grad_tokens.reshape(seq_dev, length, width)
+    (output,) = call(
+        settle_kernel, [((seq_dev, nt // seq_dev, dp, piece, width), BF16)], [], [dealt]
+    )
+    output = output.reshape(seq_dev, length, width)
+    near, output, grad_tokens, vectors = lax.optimization_barrier(
+        (near, output, grad_tokens, vectors)
+    )
     grads = near, swap(near, "dp", 1)
     g_up, g_down, g_query, g_key, g_value, g_out = call(
         place_grads_kernel,
@@ -981,14 +992,6 @@
         grads,
         scratch=[pltpu.VMEM((width, TILE), F32)],
     )
-    (grad_tokens,) = call(
-        place_rows_kernel, [((nt, rows, width), BF16)], [info], row_pieces
-    )
-    grad_tokens = grad_tokens.reshape(seq_dev, length, width)
-    (output,) = call(
-        settle_kernel, [((seq_dev, nt // seq_dev, dp, piece, width), BF16)], [], [dealt]
-    )
-    output = output.reshape(seq_dev, length, width)
     base = 4 + nt
     g_b_up = lax.dynamic_index_in_dim(vectors[4:base], t, 0, keepdims=False)
     g_b_q = lax.dynamic_index_in_dim(vectors[base + 2].reshape(nt, TILE), t, 0, keepdims=False)

time: 213 us -> 196 us (0.920)
  waiting for transfers between devices: 90.3 us -> 67.3 us
  local copies, waits for them, and re-layouts: 3.76 us -> 6.99 us
    ppermute x41, waiting for transfers between devices: 69 us -> 56.1 us  [swap(): return lax.ppermute(piece, axis, [(i, i ^ distance) for i in range(size)])]
    ppermute x3, waiting for transfers between devices: 20.2 us -> 10.1 us  [line_second(): three = lax.ppermute(after(piece, two), 'tensor', [(1, 2), (2, 1)])]
    unnamed x26 -> x50, local copies, waits for them, and re-layouts: 0.06 us -> 3.3 us
  transfers between devices with their start and end apart: 48 -> 48, of which waited for: 26 -> 28; matrix products, arithmetic and copies ran while one was open for 2% -> 3% of each run, Pallas kernels for 18% -> 18%
where the time goes in v6:
time: 196 us; the launch traced here: 195 us
  waiting for transfers between devices  67.3 us (34%)
  starting transfers between devices  63.7 us (32%)
  Pallas kernels  52.2 us (27%)
  local copies, waits for them, and re-layouts  6.99 us (4%)
  other arithmetic  3.6 us (2%)
    ppermute x41, waiting for transfers between devices, swap(): return lax.ppermute(piece, axis, [(i, i ^ distance) for i in range(size)])  56.1 us
    pallas_call x14, Pallas kernels, call(): pl.pallas_call(kernel, out_shape=[jax.ShapeDtypeStruct(shape, dtype) for...  49.7 us
    ppermute x41, starting transfers between devices, swap(): return lax.ppermute(piece, axis, [(i, i ^ distance) for i in range(size)])  41.7 us
    ppermute x3, waiting for transfers between devices, line_second(): three = lax.ppermute(after(piece, two), 'tensor', [(1, 2), (2, 1)])  10.1 us
    ppermute x3, starting transfers between devices, line_second(): three = lax.ppermute(after(piece, two), 'tensor', [(1, 2), (2, 1)])  8.83 us
    ppermute x3, starting transfers between devices, line_second(): passed = lax.ppermute(two, 'tensor', [(1, 0), (2, 3)])  8.79 us
    all_to_all x1, starting transfers between devices, exchange(): lax.all_to_all(pieces, axis, 0, 0, tiled=True, axis_index_groups=groups)  4.35 us
  transfers between devices with their start and end apart: 48, of which 28 were waited for; matrix products, arithmetic and copies ran while one was open for 3% of the time, Pallas kernels for 18%

profile of v6, /device:TPU:8, one launch (start us, length us, event | category | flops | bytes accessed | tf_op | source)
XLA Modules:
  0.0 195.1 jit_solution(18103733485039246804)
XLA Ops:
  1.3 2.5 %shard_map.315 = (bf16[80,512]{1,0:T(8,128)(2,1)}, bf16[2,64,512]{2,1,0:T(8,128)(2,1)}) custom-call(s32[6]{0:T(128)} %stack.72.info, bf16[512,128]{1,0:T(8,128)(2,1)} %q_ref.1, bf16[512,128]{1,0:T(8,128)(2,1)} %k_ref.1, bf16[512,128]{1,0:T(8,128)(2,1)} %v_ref.1, bf16[128,512]{1,0:T(8,128)(2,1)} %o_ref.1, bf16[512,512]{1,0:T(8,128)(2,1)} %up_ref.1, ...), custom_call_target="tpu_custom_call" | custom-call | tf_op jit(solution)/shard_map/pallas_call | solution.py:780
  3.9 1.6 collective-permute-start.2
  6.6 1.4 collective-permute-start
  10.6 2.0 %collective-permute-done.2.refs_3_ = bf16[80,512]{1,0:T(8,128)(2,1)S(1)} collective-permute-done((bf16[80,512]{1,0:T(8,128)(2,1)}, bf16[80,512]{1,0:T(8,128)(2,1)S(1)}, u32[]{:S(2)}, u32[]{:S(2)}) %collective-permute-start.2) | collective-permute-done | bytes 81952 | tf_op jit(solution)/shard_map/ppermute | solution.py:716
  13.9 2.4 %collective-permute-start.7 = (bf16[2,64,512]{2,1,0:T(8,128)(2,1)S(1)}, bf16[2,64,512]{2,1,0:T(8,128)(2,1)S(1)}, u32[]{:S(2)}, u32[]{:S(2)}) collective-permute-start(bf16[2,64,512]{2,1,0:T(8,128)(2,1)S(1)} %copy-done.6), channel_id=1, source_target_pairs={{0,2},{1,3},{2,0},{3,1},{4,6},{5,7},{6,4},{7,5},{8,10},{9,11},{10,... | collective-permute-start | bytes 393224 | tf_op jit(solution)/shard_map/ppermute | solution.py:716
  16.3 2.5 %collective-permute-start.5 = (bf16[4,64,512]{2,1,0:T(8,128)(2,1)S(1)}, bf16[4,64,512]{2,1,0:T(8,128)(2,1)S(1)}, u32[]{:S(2)}, u32[]{:S(2)}) collective-permute-start(bf16[4,64,512]{2,1,0:T(8,128)(2,1)S(1)} %get-tuple-element.139), channel_id=1, source_target_pairs={{0,24},{4,28},{8,16},{12,20},{16,8},{20,12},{24,0},{28,4},{1,25},{... | collective-permute-start | bytes 786440 | tf_op jit(solution)/shard_map/ppermute | solution.py:716
  20.6 2.9 %collective-permute-start.8 = (bf16[2,64,512]{2,1,0:T(8,128)(2,1)S(1)}, bf16[2,64,512]{2,1,0:T(8,128)(2,1)S(1)}, u32[]{:S(2)}, u32[]{:S(2)}) collective-permute-start(bf16[2,64,512]{2,1,0:T(8,128)(2,1)S(1)} %copy-done.6), channel_id=1, source_target_pairs={{1,2},{2,1},{5,6},{6,5},{9,10},{10,9},{13,14},{14,13},{17,18},{18,... | collective-permute-start | bytes 393224 | tf_op jit(solution)/shard_map/ppermute | solution.py:767
  23.5 2.4 %collective-permute-start.9 = (bf16[2,64,512]{2,1,0:T(8,128)(2,1)S(1)}, bf16[2,64,512]{2,1,0:T(8,128)(2,1)S(1)}, u32[]{:S(2)}, u32[]{:S(2)}) collective-permute-start(bf16[2,64,512]{2,1,0:T(8,128)(2,1)S(1)} %collective-permute-done.7.refs_2_), channel_id=1, source_target_pairs={{1,0},{2,3},{5,4},{6,7},{9,8},{10,11},{13,12},{14,15},{17,16},{18,... | collective-permute-start | bytes 393224 | tf_op jit(solution)/shard_map/ppermute | solution.py:768
  25.9 1.5 collective-permute-done.8.refs_3_
  29.8 1.5 collective-permute-start.12
  32.2 6.3 %collective-permute-done.12 = bf16[4,64,512]{2,1,0:T(8,128)(2,1)S(1)} collective-permute-done((bf16[4,64,512]{2,1,0:T(8,128)(2,1)S(1)}, bf16[4,64,512]{2,1,0:T(8,128)(2,1)S(1)}, u32[]{:S(2)}, u32[]{:S(2)}) %collective-permute-start.12) | collective-permute-done | bytes 262176 | tf_op jit(solution)/shard_map/ppermute | solution.py:716
  38.6 1.6 collective-permute-start.13
  41.2 7.8 %shard_map.318 = (bf16[4,512,128]{2,1,0:T(8,128)(2,1)S(1)}, f32[4,512,128]{2,1,0:T(8,128)S(1)}, f32[4,512,128]{2,1,0:T(8,128)S(1)}, bf16[4,1024,128]{2,1,0:T(8,1...) custom-call(s32[6]{0:T(128)S(1)} %copy-done.8, ...), custom_call_target="tpu_custom_call" | custom-call | flops 10000000000 | bytes 1 | tf_op jit(solution)/shard_map/pallas_call | solution.py:693
  48.9 3.2 %collective-permute-done.13.refs_3_ = bf16[2,4,64,512]{3,2,1,0:T(8,128)(2,1)S(1)} collective-permute-done((bf16[2,4,64,512]{3,2,1,0:T(8,128)(2,1)S(1)}, bf16[2,4,64,512]{3,2,1,0:T(8,128)(2,1)S(1)}, u32[]{:S(2)}, u32[]{:S(2)}) %collective-permute-start.13) | collective-permute-done | bytes 524320 | tf_op jit(solution)/shard_map/ppermute | solution.py:716
  57.6 5.3 %shard_map.319 = (f32[512,512]{1,0:T(8,128)S(1)}, bf16[512,512]{1,0:T(8,128)(2,1)S(1)}, bf16[4,512,512]{2,1,0:T(8,128)(2,1)S(1)}, bf16[4,512,512]{2,1,0:T(8,128)...) custom-call(s32[6]{0:T(128)S(1)} %copy-done.8, ...), custom_call_target="tpu_custom_call" | custom-call | flops 1 | bytes 1 | tf_op jit(solution)/shard_map/pallas_call | solution.py:693
  63.2 1.4 collective-permute-done.19.far_ref
  65.2 1.4 collective-permute-start.21
  66.6 1.5 collective-permute-start.22
  68.1 5.6 %shard_map.321 = (bf16[4,512,512]{2,1,0:T(8,128)(2,1)S(1)}, f32[512,512]{1,0:T(8,128)S(1)}, bf16[512,512]{1,0:T(8,128)(2,1)S(1)}, f32[4,512,128]{2,1,0:T(8,128)S...) custom-call(s32[6]{0:T(128)S(1)} %copy-done.8, ...), custom_call_target="tpu_custom_call" | custom-call | flops 1 | bytes 1 | tf_op jit(solution)/shard_map/pallas_call | solution.py:693
  73.8 3.0 %shard_map.322 = (bf16[4,4,2,64,512]{4,3,2,1,0:T(8,128)(2,1)S(1)}, bf16[4,4,2,64,512]{4,3,2,1,0:T(8,128)(2,1)S(1)}) custom-call(s32[6]{0:T(128)S(1)} %copy-done.8, bf16[512,512]{1,0:T(8,128)(2,1)S(1)} %get-tuple-element.163.normed_ref, bf16[4,512,512]{2,1,0:T(8,128)(2,1)S(1)} %get-tuple-element.164.act_ref, ...), custom_call_target="tpu_custom_call" | custom-call | flops 1 | bytes 1 | tf_op jit(solution)/shard_map/pallas_call | solution.py:693
  76.9 2.1 %collective-permute-start.24 = (f32[4,32,128]{2,1,0:T(8,128)S(1)}, f32[4,32,128]{2,1,0:T(8,128)S(1)}, u32[]{:S(2)}, u32[]{:S(2)}) collective-permute-start(f32[4,32,128]{2,1,0:T(8,128)S(1)} %get-tuple-element.173), channel_id=1, source_target_pairs={{0,1},{1,0},{2,3},{3,2},{4,5},{5,4},{6,7},{7,6},{8,9},{9,8},{10,11... | collective-permute-start | bytes 196616 | tf_op jit(solution)/shard_map/ppermute | solution.py:716
  79.5 1.7 collective-permute-start.25
  83.5 1.5 collective-permute-start.28
  86.1 14.0 %shard_map.323 = (bf16[4,512,384]{2,1,0:T(8,128)(2,1)S(1)}, f32[4,2,128]{2,1,0:T(2,128)S(1)}, bf16[512,512]{1,0:T(8,128)(2,1)S(1)}, f32[2,512]{1,0:T(2,128)S(1)}) custom-call(s32[6]{0:T(128)S(1)} %copy-done.8, s32[16]{0:T(128)S(1)} %copy-done.15, f32[4,512,128]{2,1,0:T(8,128)S(1)} %get-tuple-element.161.numer_ref, ...), custom_call_target="tpu_custom_call" | custom-call | flops 10000000000 | bytes 1 | tf_op jit(solution)/shard_map/pallas_call | solution.py:693
  100.1 2.2 %collective-permute-done.26.refs_2_ = bf16[8,64,512]{2,1,0:T(8,128)(2,1)S(1)} collective-permute-done((bf16[8,64,512]{2,1,0:T(8,128)(2,1)S(1)}, bf16[8,64,512]{2,1,0:T(8,128)(2,1)S(1)}, u32[]{:S(2)}, u32[]{:S(2)}) %collective-permute-start.26) | collective-permute-done | bytes 524320 | tf_op jit(solution)/shard_map/ppermute | solution.py:716
  102.4 2.2 %collective-permute-done.25.refs_1_ = bf16[8,64,512]{2,1,0:T(8,128)(2,1)S(1)} collective-permute-done((bf16[8,64,512]{2,1,0:T(8,128)(2,1)S(1)}, bf16[8,64,512]{2,1,0:T(8,128)(2,1)S(1)}, u32[]{:S(2)}, u32[]{:S(2)}) %collective-permute-start.25) | collective-permute-done | bytes 524320 | tf_op jit(solution)/shard_map/ppermute | solution.py:716
  104.5 2.5 %shard_map.324 = (bf16[4,272,512]{2,1,0:T(8,128)(2,1)S(1)}, bf16[4,272,512]{2,1,0:T(8,128)(2,1)S(1)}) custom-call(s32[6]{0:T(128)S(1)} %copy-done.8, bf16[512,512]{1,0:T(8,128)(2,1)S(1)} %get-tuple-element.125.normed_ref, bf16[4,512,384]{2,1,0:T(8,128)(2,1)S(1)} %get-tuple-element.181.grads_ref, bf16[512,512]{1,0:T(8,128)(2,1)S(1)} %get-tuple-element.185.grad_hidden_ref, ...), custom_call_target="tpu_custom_call" | custom-call | flops 1 | bytes 1 | tf_op jit(solution)/shard_map/pallas_call | solution.py:693
  108.2 2.9 %collective-permute-start.34 = (bf16[8,64,512]{2,1,0:T(8,128)(2,1)S(1)}, bf16[8,64,512]{2,1,0:T(8,128)(2,1)S(1)}, u32[]{:S(2)}, u32[]{:S(2)}) collective-permute-start(bf16[8,64,512]{2,1,0:T(8,128)(2,1)S(1)} %pad_maximum_fusion.4.refs_0_), channel_id=1, source_target_pairs={{1,2},{2,1},{5,6},{6,5},{9,10},{10,9},{13,14},{14,13},{17,18},{18,... | collective-permute-start | bytes 1572872 | tf_op jit(solution)/shard_map/ppermute | solution.py:767
  111.1 1.6 collective-permute-start.35
  113.2 1.9 collective-permute-start.33
  115.7 8.6 %collective-permute-done.34.refs_3_ = bf16[8,64,512]{2,1,0:T(8,128)(2,1)S(1)} collective-permute-done((bf16[8,64,512]{2,1,0:T(8,128)(2,1)S(1)}, bf16[8,64,512]{2,1,0:T(8,128)(2,1)S(1)}, u32[]{:S(2)}, u32[]{:S(2)}) %collective-permute-start.34) | collective-permute-done | bytes 524320 | tf_op jit(solution)/shard_map/ppermute | solution.py:767
  125.4 2.2 %collective-permute-start.37 = (bf16[512,512]{1,0:T(8,128)(2,1)S(1)}, bf16[512,512]{1,0:T(8,128)(2,1)S(1)}, u32[]{:S(2)}, u32[]{:S(2)}) collective-permute-start(bf16[512,512]{1,0:T(8,128)(2,1)S(1)} %get-tuple-element.218.refs_0_), channel_id=1, source_target_pairs={{0,2},{1,3},{2,0},{3,1},{4,6},{5,7},{6,4},{7,5},{8,10},{9,11},{10,... | collective-permute-start | bytes 1572872 | tf_op jit(solution)/shard_map/ppermute | solution.py:716
  127.6 8.3 %collective-permute-done.36.refs_1_ = bf16[512,512]{1,0:T(8,128)(2,1)S(1)} collective-permute-done((bf16[512,512]{1,0:T(8,128)(2,1)S(1)}, bf16[512,512]{1,0:T(8,128)(2,1)S(1)}, u32[]{:S(2)}, u32[]{:S(2)}) %collective-permute-start.36) | collective-permute-done | bytes 524320 | tf_op jit(solution)/shard_map/ppermute | solution.py:716
  138.1 2.1 %shard_map.325 = bf16[8,2,2,64,512]{4,3,2,1,0:T(8,128)(2,1)} custom-call(s32[6]{0:T(128)S(1)} %copy-done.8, s32[16]{0:T(128)S(1)} %copy-done.16, bf16[8,64,512]{2,1,0:T(8,128)(2,1)S(1)} %pad_maximum_fusion.4.refs_0_, bf16[8,64,512]{2,1,0:T(8,128)(2,1)S(1)} %collective-permute-done.25.refs_1_, bf16[8,64,512]{2,1,0:T(8,128)(2,1)S(1)} %collective-permute-done.26.refs_2_, ...), custom_call_target="tpu_custom_call" | custom-call | flops 1 | bytes 1 | tf_op jit(solution)/shard_map/pallas_call | solution.py:693
  140.3 4.3 %all-to-all-start = ((bf16[8,2,2,64,512]{4,3,2,1,0:T(8,128)(2,1)}), bf16[8,2,2,64,512]{4,3,2,1,0:T(8,128)(2,1)}, u32[]{:S(2)}, u32[]{:S(2)}) async-start(bf16[8,2,2,64,512]{4,3,2,1,0:T(8,128)(2,1)} %shard_map.325), calls=%async_computation | async-start | bytes 4194304 | tf_op jit(solution)/shard_map/all_to_all | solution.py:707
  144.6 1.6 add_convert_fusion
  146.4 2.9 %collective-permute-done.37.refs_2_ = bf16[512,512]{1,0:T(8,128)(2,1)S(1)} collective-permute-done((bf16[512,512]{1,0:T(8,128)(2,1)S(1)}, bf16[512,512]{1,0:T(8,128)(2,1)S(1)}, u32[]{:S(2)}, u32[]{:S(2)}) %collective-permute-start.37) | collective-permute-done | bytes 524320 | tf_op jit(solution)/shard_map/ppermute | solution.py:716
  149.4 3.0 %collective-permute-start.38 = (bf16[208,512]{1,0:T(8,128)(2,1)S(1)}, bf16[208,512]{1,0:T(8,128)(2,1)S(1)}, u32[]{:S(2)}, u32[]{:S(2)}) collective-permute-start(bf16[208,512]{1,0:T(8,128)(2,1)S(1)} %get-tuple-element.254), channel_id=1, source_target_pairs={{0,1},{1,0},{2,3},{3,2},{4,5},{5,4},{6,7},{7,6},{8,9},{9,8},{10,11... | collective-permute-start | bytes 638984 | tf_op jit(solution)/shard_map/ppermute | solution.py:716
  154.0 4.8 %collective-permute-start.45 = (bf16[512,512]{1,0:T(8,128)(2,1)S(1)}, bf16[512,512]{1,0:T(8,128)(2,1)S(1)}, u32[]{:S(2)}, u32[]{:S(2)}) collective-permute-start(bf16[512,512]{1,0:T(8,128)(2,1)S(1)} %collective-permute-done.37.refs_2_), channel_id=1, source_target_pairs={{1,0},{2,3},{5,4},{6,7},{9,8},{10,11},{13,12},{14,15},{17,16},{18,... | collective-permute-start | bytes 1572872 | tf_op jit(solution)/shard_map/ppermute | solution.py:768
  158.8 3.0 %collective-permute-start.44 = (bf16[512,512]{1,0:T(8,128)(2,1)S(1)}, bf16[512,512]{1,0:T(8,128)(2,1)S(1)}, u32[]{:S(2)}, u32[]{:S(2)}) collective-permute-start(bf16[512,512]{1,0:T(8,128)(2,1)S(1)} %get-tuple-element.218.refs_0_), channel_id=1, source_target_pairs={{1,2},{2,1},{5,6},{6,5},{9,10},{10,9},{13,14},{14,13},{17,18},{18,... | collective-permute-start | bytes 1572872 | tf_op jit(solution)/shard_map/ppermute | solution.py:767
  161.8 6.0 %collective-permute-done.39 = bf16[208,512]{1,0:T(8,128)(2,1)S(1)} collective-permute-done((bf16[208,512]{1,0:T(8,128)(2,1)S(1)}, bf16[208,512]{1,0:T(8,128)(2,1)S(1)}, u32[]{:S(2)}, u32[]{:S(2)}) %collective-permute-start.39) | collective-permute-done | bytes 213024 | tf_op jit(solution)/shard_map/ppermute | solution.py:716
  167.8 6.0 %collective-permute-done.40 = bf16[208,512]{1,0:T(8,128)(2,1)S(1)} collective-permute-done((bf16[208,512]{1,0:T(8,128)(2,1)S(1)}, bf16[208,512]{1,0:T(8,128)(2,1)S(1)}, u32[]{:S(2)}, u32[]{:S(2)}) %collective-permute-start.40) | collective-permute-done | bytes 213024 | tf_op jit(solution)/shard_map/ppermute | solution.py:716
  174.0 1.5 collective-permute-start.43
  177.5 4.7 %collective-permute-done.43 = bf16[3,64,512]{2,1,0:T(8,128)(2,1)S(1)} collective-permute-done((bf16[3,64,512]{2,1,0:T(8,128)(2,1)S(1)}, bf16[3,64,512]{2,1,0:T(8,128)(2,1)S(1)}, u32[]{:S(2)}, u32[]{:S(2)}) %collective-permute-start.43) | collective-permute-done | bytes 196640 | tf_op jit(solution)/shard_map/ppermute | solution.py:716
  182.2 2.0 %collective-permute-done.42 = bf16[3,64,512]{2,1,0:T(8,128)(2,1)S(1)} collective-permute-done((bf16[3,64,512]{2,1,0:T(8,128)(2,1)S(1)}, bf16[3,64,512]{2,1,0:T(8,128)(2,1)S(1)}, u32[]{:S(2)}, u32[]{:S(2)}) %collective-permute-start.42) | collective-permute-done | bytes 196640 | tf_op jit(solution)/shard_map/ppermute | solution.py:716
  185.4 2.0 %shard_map.327 = bf16[4,512,512]{2,1,0:T(8,128)(2,1)} custom-call(s32[6]{0:T(128)S(1)} %copy-done.8, bf16[512,512]{1,0:T(8,128)(2,1)S(1)} %get-tuple-element.218.refs_0_, bf16[512,512]{1,0:T(8,128)(2,1)S(1)} %copy-done.3, bf16[512,512]{1,0:T(8,128)(2,1)S(1)} %copy-done.5, bf16[512,512]{1,0:T(8,128)(2,1)S(1)} %collective-permute-done.44.refs_3_, ...), custom_call_target="tpu_custom_call" | custom-call | flops 1 | bytes 1 | tf_op jit(solution)/shard_map/pallas_call | solution.py:693
  187.4 3.0 %shard_map.326 = bf16[2,2,8,64,512]{4,3,2,1,0:T(8,128)(2,1)} custom-call(bf16[8,2,2,64,512]{4,3,2,1,0:T(8,128)(2,1)} %all-to-all-done.pieces_ref), custom_call_target="tpu_custom_call" | custom-call | flops 1 | bytes 1 | tf_op jit(solution)/shard_map/pallas_call | solution.py:693
  192.7 2.4 %shard_map.328 = (f32[512,512]{1,0:T(8,128)}, f32[512,512]{1,0:T(8,128)}, f32[512,128]{1,0:T(8,128)}, f32[512,128]{1,0:T(8,128)}, f32[512,128]{1,0:T(8,128)}, /*index=5*/f32[128,512]{1,0:T(8,128)}) custom-call(s32[6]{0:T(128)S(1)} %copy-done.8, bf16[4,3,64,512]{3,2,1,0:T(8,128)(2,1)S(1)} %pad_maximum_fusion.1.near_ref, ...), custom_call_target="tpu_custom_call" | custom-call | flops 1 | bytes 1 | tf_op jit(solution)/shard_map/pallas_call | solution.py:693
  (138 shorter events, 35.0 us)
Async XLA Ops:
  3.9 8.8 %collective-permute-start.2 = (bf16[80,512]{1,0:T(8,128)(2,1)}, bf16[80,512]{1,0:T(8,128)(2,1)S(1)}, u32[]{:S(2)}, u32[]{:S(2)}) collective-permute-start(bf16[80,512]{1,0:T(8,128)(2,1)} %get-tuple-element.126.refs_0_), channel_id=1, source_target_pairs={{0,3},{1,2},{2,1},{3,0},{4,7},{5,6},{6,5},{7,4},{8,11},{9,10},{10,... | collective-permute-start | bytes 245768 | tf_op jit(solution)/shard_map/ppermute | solution.py:716
  5.5 7.5 %collective-permute-start.1 = (bf16[80,512]{1,0:T(8,128)(2,1)}, bf16[80,512]{1,0:T(8,128)(2,1)S(1)}, u32[]{:S(2)}, u32[]{:S(2)}) collective-permute-start(bf16[80,512]{1,0:T(8,128)(2,1)} %get-tuple-element.126.refs_0_), channel_id=1, source_target_pairs={{0,2},{1,3},{2,0},{3,1},{4,6},{5,7},{6,4},{7,5},{8,10},{9,11},{10,... | collective-permute-start | bytes 245768 | tf_op jit(solution)/shard_map/ppermute | solution.py:716
  6.6 7.3 %collective-permute-start = (bf16[80,512]{1,0:T(8,128)(2,1)}, bf16[80,512]{1,0:T(8,128)(2,1)S(1)}, u32[]{:S(2)}, u32[]{:S(2)}) collective-permute-start(bf16[80,512]{1,0:T(8,128)(2,1)} %get-tuple-element.126.refs_0_), channel_id=1, source_target_pairs={{0,1},{1,0},{2,3},{3,2},{4,5},{5,4},{6,7},{7,6},{8,9},{9,8},{10,11... | collective-permute-start | bytes 245768 | tf_op jit(solution)/shard_map/ppermute | solution.py:716
  13.9 6.7 %collective-permute-start.7 = (bf16[2,64,512]{2,1,0:T(8,128)(2,1)S(1)}, bf16[2,64,512]{2,1,0:T(8,128)(2,1)S(1)}, u32[]{:S(2)}, u32[]{:S(2)}) collective-permute-start(bf16[2,64,512]{2,1,0:T(8,128)(2,1)S(1)} %copy-done.6), channel_id=1, source_target_pairs={{0,2},{1,3},{2,0},{3,1},{4,6},{5,7},{6,4},{7,5},{8,10},{9,11},{10,... | collective-permute-start | bytes 393224 | tf_op jit(solution)/shard_map/ppermute | solution.py:716
  16.3 7.2 %collective-permute-start.6 = (bf16[2,64,512]{2,1,0:T(8,128)(2,1)S(1)}, bf16[2,64,512]{2,1,0:T(8,128)(2,1)S(1)}, u32[]{:S(2)}, u32[]{:S(2)}) collective-permute-start(bf16[2,64,512]{2,1,0:T(8,128)(2,1)S(1)} %copy-done.6), channel_id=1, source_target_pairs={{0,1},{1,0},{2,3},{3,2},{4,5},{5,4},{6,7},{7,6},{8,9},{9,8},{10,11... | collective-permute-start | bytes 393224 | tf_op jit(solution)/shard_map/ppermute | solution.py:716
  16.3 12.7 %collective-permute-start.5 = (bf16[4,64,512]{2,1,0:T(8,128)(2,1)S(1)}, bf16[4,64,512]{2,1,0:T(8,128)(2,1)S(1)}, u32[]{:S(2)}, u32[]{:S(2)}) collective-permute-start(bf16[4,64,512]{2,1,0:T(8,128)(2,1)S(1)} %get-tuple-element.139), channel_id=1, source_target_pairs={{0,24},{4,28},{8,16},{12,20},{16,8},{20,12},{24,0},{28,4},{1,25},{... | collective-permute-start | bytes 786440 | tf_op jit(solution)/shard_map/ppermute | solution.py:716
  18.8 10.6 %collective-permute-start.4 = (bf16[4,64,512]{2,1,0:T(8,128)(2,1)S(1)}, bf16[4,64,512]{2,1,0:T(8,128)(2,1)S(1)}, u32[]{:S(2)}, u32[]{:S(2)}) collective-permute-start(bf16[4,64,512]{2,1,0:T(8,128)(2,1)S(1)} %get-tuple-element.139), channel_id=1, source_target_pairs={{0,16},{4,20},{8,24},{12,28},{16,0},{20,4},{24,8},{28,12},{1,17},{... | collective-permute-start | bytes 786440 | tf_op jit(solution)/shard_map/ppermute | solution.py:716
  19.4 10.2 %collective-permute-start.3 = (bf16[4,64,512]{2,1,0:T(8,128)(2,1)S(1)}, bf16[4,64,512]{2,1,0:T(8,128)(2,1)S(1)}, u32[]{:S(2)}, u32[]{:S(2)}) collective-permute-start(bf16[4,64,512]{2,1,0:T(8,128)(2,1)S(1)} %get-tuple-element.139), channel_id=1, source_target_pairs={{0,8},{4,12},{8,0},{12,4},{16,24},{20,28},{24,16},{28,20},{1,9},{5... | collective-permute-start | bytes 786440 | tf_op jit(solution)/shard_map/ppermute | solution.py:716
  20.6 6.8 %collective-permute-start.8 = (bf16[2,64,512]{2,1,0:T(8,128)(2,1)S(1)}, bf16[2,64,512]{2,1,0:T(8,128)(2,1)S(1)}, u32[]{:S(2)}, u32[]{:S(2)}) collective-permute-start(bf16[2,64,512]{2,1,0:T(8,128)(2,1)S(1)} %copy-done.6), channel_id=1, source_target_pairs={{1,2},{2,1},{5,6},{6,5},{9,10},{10,9},{13,14},{14,13},{17,18},{18,... | collective-permute-start | bytes 393224 | tf_op jit(solution)/shard_map/ppermute | solution.py:767
  23.5 5.0 %collective-permute-start.9 = (bf16[2,64,512]{2,1,0:T(8,128)(2,1)S(1)}, bf16[2,64,512]{2,1,0:T(8,128)(2,1)S(1)}, u32[]{:S(2)}, u32[]{:S(2)}) collective-permute-start(bf16[2,64,512]{2,1,0:T(8,128)(2,1)S(1)} %collective-permute-done.7.refs_2_), channel_id=1, source_target_pairs={{1,0},{2,3},{5,4},{6,7},{9,8},{10,11},{13,12},{14,15},{17,16},{18,... | collective-permute-start | bytes 393224 | tf_op jit(solution)/shard_map/ppermute | solution.py:768
  29.7 11.4 %collective-permute-start.14 = (bf16[4,4,64,512]{3,2,1,0:T(8,128)(2,1)S(1)}, bf16[4,4,64,512]{3,2,1,0:T(8,128)(2,1)S(1)}, u32[]{:S(2)}, u32[]{:S(2)}) collective-permute-start(bf16[4,4,64,512]{3,2,1,0:T(8,128)(2,1)S(1)} %pad_maximum_fusion.near_ref), channel_id=1, source_target_pairs={{0,4},{4,0},{8,12},{12,8},{16,20},{20,16},{24,28},{28,24},{1,5},{5... | collective-permute-start | bytes 3145736 | tf_op jit(solution)/shard_map/ppermute | solution.py:716
  29.8 8.7 %collective-permute-start.12 = (bf16[4,64,512]{2,1,0:T(8,128)(2,1)S(1)}, bf16[4,64,512]{2,1,0:T(8,128)(2,1)S(1)}, u32[]{:S(2)}, u32[]{:S(2)}) collective-permute-start(bf16[4,64,512]{2,1,0:T(8,128)(2,1)S(1)} %get-tuple-element.137), channel_id=1, source_target_pairs={{0,16},{4,20},{8,24},{12,28},{16,0},{20,4},{24,8},{28,12},{1,17},{... | collective-permute-start | bytes 786440 | tf_op jit(solution)/shard_map/ppermute | solution.py:716
  31.3 8.8 %collective-permute-start.10 = (bf16[4,64,512]{2,1,0:T(8,128)(2,1)S(1)}, bf16[4,64,512]{2,1,0:T(8,128)(2,1)S(1)}, u32[]{:S(2)}, u32[]{:S(2)}) collective-permute-start(bf16[4,64,512]{2,1,0:T(8,128)(2,1)S(1)} %get-tuple-element.136), channel_id=1, source_target_pairs={{0,8},{4,12},{8,0},{12,4},{16,24},{20,28},{24,16},{28,20},{1,9},{5... | collective-permute-start | bytes 786440 | tf_op jit(solution)/shard_map/ppermute | solution.py:716
  38.6 13.6 %collective-permute-start.13 = (bf16[2,4,64,512]{3,2,1,0:T(8,128)(2,1)S(1)}, bf16[2,4,64,512]{3,2,1,0:T(8,128)(2,1)S(1)}, u32[]{:S(2)}, u32[]{:S(2)}) collective-permute-start(bf16[2,4,64,512]{3,2,1,0:T(8,128)(2,1)S(1)} %pad_maximum_fusion.3.refs_2_), channel_id=1, source_target_pairs={{0,8},{4,12},{8,0},{12,4},{16,24},{20,28},{24,16},{28,20},{1,9},{5... | collective-permute-start | bytes 1572872 | tf_op jit(solution)/shard_map/ppermute | solution.py:716
  40.2 13.3 %collective-permute-start.11 = (bf16[2,4,64,512]{3,2,1,0:T(8,128)(2,1)S(1)}, bf16[2,4,64,512]{3,2,1,0:T(8,128)(2,1)S(1)}, u32[]{:S(2)}, u32[]{:S(2)}) collective-permute-start(bf16[2,4,64,512]{3,2,1,0:T(8,128)(2,1)S(1)} %pad_maximum_fusion.2.refs_0_), channel_id=1, source_target_pairs={{0,16},{4,20},{8,24},{12,28},{16,0},{20,4},{24,8},{28,12},{1,17},{... | collective-permute-start | bytes 1572872 | tf_op jit(solution)/shard_map/ppermute | solution.py:716
  53.5 1.9 collective-permute-start.15
  53.5 2.7 %collective-permute-start.16 = (bf16[2,4,64,512]{3,2,1,0:T(8,128)(2,1)S(1)}, bf16[2,4,64,512]{3,2,1,0:T(8,128)(2,1)S(1)}, u32[]{:S(2)}, u32[]{:S(2)}) collective-permute-start(bf16[2,4,64,512]{3,2,1,0:T(8,128)(2,1)S(1)} %collective-permute-done.11.refs_1_), channel_id=1, source_target_pairs={{0,4},{4,0},{8,12},{12,8},{16,20},{20,16},{24,28},{28,24},{1,5},{5... | collective-permute-start | bytes 1572872 | tf_op jit(solution)/shard_map/ppermute | solution.py:716
  54.0 2.9 %collective-permute-start.17 = (bf16[2,4,64,512]{3,2,1,0:T(8,128)(2,1)S(1)}, bf16[2,4,64,512]{3,2,1,0:T(8,128)(2,1)S(1)}, u32[]{:S(2)}, u32[]{:S(2)}) collective-permute-start(bf16[2,4,64,512]{3,2,1,0:T(8,128)(2,1)S(1)} %pad_maximum_fusion.3.refs_2_), channel_id=1, source_target_pairs={{0,4},{4,0},{8,12},{12,8},{16,20},{20,16},{24,28},{28,24},{1,5},{5... | collective-permute-start | bytes 1572872 | tf_op jit(solution)/shard_map/ppermute | solution.py:716
  54.0 3.6 %collective-permute-start.18 = (bf16[2,4,64,512]{3,2,1,0:T(8,128)(2,1)S(1)}, bf16[2,4,64,512]{3,2,1,0:T(8,128)(2,1)S(1)}, u32[]{:S(2)}, u32[]{:S(2)}) collective-permute-start(bf16[2,4,64,512]{3,2,1,0:T(8,128)(2,1)S(1)} %collective-permute-done.13.refs_3_), channel_id=1, source_target_pairs={{0,4},{4,0},{8,12},{12,8},{16,20},{20,16},{24,28},{28,24},{1,5},{5... | collective-permute-start | bytes 1572872 | tf_op jit(solution)/shard_map/ppermute | solution.py:716
  62.9 1.6 collective-permute-start.19
  64.6 9.1 %collective-permute-start.20 = (bf16[2,64,512]{2,1,0:T(8,128)(2,1)S(1)}, bf16[2,64,512]{2,1,0:T(8,128)(2,1)S(1)}, u32[]{:S(2)}, u32[]{:S(2)}) collective-permute-start(bf16[2,64,512]{2,1,0:T(8,128)(2,1)S(1)} %get-tuple-element.166), channel_id=1, source_target_pairs={{0,8},{4,12},{8,0},{12,4},{16,24},{20,28},{24,16},{28,20},{1,9},{5... | collective-permute-start | bytes 393224 | tf_op jit(solution)/shard_map/ppermute | solution.py:716
  65.2 8.5 %collective-permute-start.21 = (bf16[2,64,512]{2,1,0:T(8,128)(2,1)S(1)}, bf16[2,64,512]{2,1,0:T(8,128)(2,1)S(1)}, u32[]{:S(2)}, u32[]{:S(2)}) collective-permute-start(bf16[2,64,512]{2,1,0:T(8,128)(2,1)S(1)} %get-tuple-element.167), channel_id=1, source_target_pairs={{0,16},{4,20},{8,24},{12,28},{16,0},{20,4},{24,8},{28,12},{1,17},{... | collective-permute-start | bytes 393224 | tf_op jit(solution)/shard_map/ppermute | solution.py:716
  66.6 7.1 %collective-permute-start.22 = (bf16[2,64,512]{2,1,0:T(8,128)(2,1)S(1)}, bf16[2,64,512]{2,1,0:T(8,128)(2,1)S(1)}, u32[]{:S(2)}, u32[]{:S(2)}) collective-permute-start(bf16[2,64,512]{2,1,0:T(8,128)(2,1)S(1)} %get-tuple-element.168), channel_id=1, source_target_pairs={{0,24},{4,28},{8,16},{12,20},{16,8},{20,12},{24,0},{28,4},{1,25},{... | collective-permute-start | bytes 393224 | tf_op jit(solution)/shard_map/ppermute | solution.py:716
  76.9 4.4 %collective-permute-start.23 = (bf16[4,4,2,64,512]{4,3,2,1,0:T(8,128)(2,1)S(1)}, bf16[4,4,2,64,512]{4,3,2,1,0:T(8,128)(2,1)S(1)}, u32[]{:S(2)}, u32[]{:S(2)}) collective-permute-start(bf16[4,4,2,64,512]{4,3,2,1,0:T(8,128)(2,1)S(1)} %get-tuple-element.172), channel_id=1, source_target_pairs={{0,4},{4,0},{8,12},{12,8},{16,20},{20,16},{24,28},{28,24},{1,5},{5... | collective-permute-start | bytes 6291464 | tf_op jit(solution)/shard_map/ppermute | solution.py:716
  76.9 5.7 %collective-permute-start.24 = (f32[4,32,128]{2,1,0:T(8,128)S(1)}, f32[4,32,128]{2,1,0:T(8,128)S(1)}, u32[]{:S(2)}, u32[]{:S(2)}) collective-permute-start(f32[4,32,128]{2,1,0:T(8,128)S(1)} %get-tuple-element.173), channel_id=1, source_target_pairs={{0,1},{1,0},{2,3},{3,2},{4,5},{5,4},{6,7},{7,6},{8,9},{9,8},{10,11... | collective-permute-start | bytes 196616 | tf_op jit(solution)/shard_map/ppermute | solution.py:716
  79.0 23.3 %collective-permute-start.26 = (bf16[8,64,512]{2,1,0:T(8,128)(2,1)S(1)}, bf16[8,64,512]{2,1,0:T(8,128)(2,1)S(1)}, u32[]{:S(2)}, u32[]{:S(2)}) collective-permute-start(bf16[8,64,512]{2,1,0:T(8,128)(2,1)S(1)} %pad_maximum_fusion.4.refs_0_), channel_id=1, source_target_pairs={{0,2},{1,3},{2,0},{3,1},{4,6},{5,7},{6,4},{7,5},{8,10},{9,11},{10,... | collective-permute-start | bytes 1572872 | tf_op jit(solution)/shard_map/ppermute | solution.py:716
  79.5 25.0 %collective-permute-start.25 = (bf16[8,64,512]{2,1,0:T(8,128)(2,1)S(1)}, bf16[8,64,512]{2,1,0:T(8,128)(2,1)S(1)}, u32[]{:S(2)}, u32[]{:S(2)}) collective-permute-start(bf16[8,64,512]{2,1,0:T(8,128)(2,1)S(1)} %pad_maximum_fusion.4.refs_0_), channel_id=1, source_target_pairs={{0,1},{1,0},{2,3},{3,2},{4,5},{5,4},{6,7},{7,6},{8,9},{9,8},{10,11... | collective-permute-start | bytes 1572872 | tf_op jit(solution)/shard_map/ppermute | solution.py:716
  82.6 24.4 %collective-permute-start.27 = (bf16[4,2,64,512]{3,2,1,0:T(8,128)(2,1)S(1)}, bf16[4,2,64,512]{3,2,1,0:T(8,128)(2,1)S(1)}, u32[]{:S(2)}, u32[]{:S(2)}) collective-permute-start(bf16[4,2,64,512]{3,2,1,0:T(8,128)(2,1)S(1)} %get-tuple-element.192), channel_id=1, source_target_pairs={{0,8},{4,12},{8,0},{12,4},{16,24},{20,28},{24,16},{28,20},{1,9},{5... | collective-permute-start | bytes 1572872 | tf_op jit(solution)/shard_map/ppermute | solution.py:716
  83.5 24.6 %collective-permute-start.28 = (bf16[4,2,64,512]{3,2,1,0:T(8,128)(2,1)S(1)}, bf16[4,2,64,512]{3,2,1,0:T(8,128)(2,1)S(1)}, u32[]{:S(2)}, u32[]{:S(2)}) collective-permute-start(bf16[4,2,64,512]{3,2,1,0:T(8,128)(2,1)S(1)} %get-tuple-element.193), channel_id=1, source_target_pairs={{0,16},{4,20},{8,24},{12,28},{16,0},{20,4},{24,8},{28,12},{1,17},{... | collective-permute-start | bytes 1572872 | tf_op jit(solution)/shard_map/ppermute | solution.py:716
  85.0 23.1 %collective-permute-start.29 = (bf16[4,2,64,512]{3,2,1,0:T(8,128)(2,1)S(1)}, bf16[4,2,64,512]{3,2,1,0:T(8,128)(2,1)S(1)}, u32[]{:S(2)}, u32[]{:S(2)}) collective-permute-start(bf16[4,2,64,512]{3,2,1,0:T(8,128)(2,1)S(1)} %get-tuple-element.194), channel_id=1, source_target_pairs={{0,24},{4,28},{8,16},{12,20},{16,8},{20,12},{24,0},{28,4},{1,25},{... | collective-permute-start | bytes 1572872 | tf_op jit(solution)/shard_map/ppermute | solution.py:716
  108.1 4.7 %collective-permute-start.30 = (bf16[4,272,512]{2,1,0:T(8,128)(2,1)S(1)}, bf16[4,272,512]{2,1,0:T(8,128)(2,1)S(1)}, u32[]{:S(2)}, u32[]{:S(2)}) collective-permute-start(bf16[4,272,512]{2,1,0:T(8,128)(2,1)S(1)} %get-tuple-element.200), channel_id=1, source_target_pairs={{0,4},{4,0},{8,12},{12,8},{16,20},{20,16},{24,28},{28,24},{1,5},{5... | collective-permute-start | bytes 3342344 | tf_op jit(solution)/shard_map/ppermute | solution.py:716
  108.2 16.2 %collective-permute-start.34 = (bf16[8,64,512]{2,1,0:T(8,128)(2,1)S(1)}, bf16[8,64,512]{2,1,0:T(8,128)(2,1)S(1)}, u32[]{:S(2)}, u32[]{:S(2)}) collective-permute-start(bf16[8,64,512]{2,1,0:T(8,128)(2,1)S(1)} %pad_maximum_fusion.4.refs_0_), channel_id=1, source_target_pairs={{1,2},{2,1},{5,6},{6,5},{9,10},{10,9},{13,14},{14,13},{17,18},{18,... | collective-permute-start | bytes 1572872 | tf_op jit(solution)/shard_map/ppermute | solution.py:767
  111.1 14.3 %collective-permute-start.35 = (bf16[8,64,512]{2,1,0:T(8,128)(2,1)S(1)}, bf16[8,64,512]{2,1,0:T(8,128)(2,1)S(1)}, u32[]{:S(2)}, u32[]{:S(2)}) collective-permute-start(bf16[8,64,512]{2,1,0:T(8,128)(2,1)S(1)} %collective-permute-done.26.refs_2_), channel_id=1, source_target_pairs={{1,0},{2,3},{5,4},{6,7},{9,8},{10,11},{13,12},{14,15},{17,16},{18,... | collective-permute-start | bytes 1572872 | tf_op jit(solution)/shard_map/ppermute | solution.py:768
  112.7 23.2 %collective-permute-start.36 = (bf16[512,512]{1,0:T(8,128)(2,1)S(1)}, bf16[512,512]{1,0:T(8,128)(2,1)S(1)}, u32[]{:S(2)}, u32[]{:S(2)}) collective-permute-start(bf16[512,512]{1,0:T(8,128)(2,1)S(1)} %get-tuple-element.218.refs_0_), channel_id=1, source_target_pairs={{0,1},{1,0},{2,3},{3,2},{4,5},{5,4},{6,7},{7,6},{8,9},{9,8},{10,11... | collective-permute-start | bytes 1572872 | tf_op jit(solution)/shard_map/ppermute | solution.py:716
  113.2 23.5 %collective-permute-start.33 = (bf16[272,512]{1,0:T(8,128)(2,1)S(1)}, bf16[272,512]{1,0:T(8,128)(2,1)S(1)}, u32[]{:S(2)}, u32[]{:S(2)}) collective-permute-start(bf16[272,512]{1,0:T(8,128)(2,1)S(1)} %get-tuple-element.233), channel_id=1, source_target_pairs={{0,24},{4,28},{8,16},{12,20},{16,8},{20,12},{24,0},{28,4},{1,25},{... | collective-permute-start | bytes 835592 | tf_op jit(solution)/shard_map/ppermute | solution.py:716
  115.1 21.6 %collective-permute-start.32 = (bf16[272,512]{1,0:T(8,128)(2,1)S(1)}, bf16[272,512]{1,0:T(8,128)(2,1)S(1)}, u32[]{:S(2)}, u32[]{:S(2)}) collective-permute-start(bf16[272,512]{1,0:T(8,128)(2,1)S(1)} %get-tuple-element.234), channel_id=1, source_target_pairs={{0,16},{4,20},{8,24},{12,28},{16,0},{20,4},{24,8},{28,12},{1,17},{... | collective-permute-start | bytes 835592 | tf_op jit(solution)/shard_map/ppermute | solution.py:716
  124.4 12.3 %collective-permute-start.31 = (bf16[272,512]{1,0:T(8,128)(2,1)S(1)}, bf16[272,512]{1,0:T(8,128)(2,1)S(1)}, u32[]{:S(2)}, u32[]{:S(2)}) collective-permute-start(bf16[272,512]{1,0:T(8,128)(2,1)S(1)} %get-tuple-element.235), channel_id=1, source_target_pairs={{0,8},{4,12},{8,0},{12,4},{16,24},{20,28},{24,16},{28,20},{1,9},{5... | collective-permute-start | bytes 835592 | tf_op jit(solution)/shard_map/ppermute | solution.py:716
  125.4 24.0 %collective-permute-start.37 = (bf16[512,512]{1,0:T(8,128)(2,1)S(1)}, bf16[512,512]{1,0:T(8,128)(2,1)S(1)}, u32[]{:S(2)}, u32[]{:S(2)}) collective-permute-start(bf16[512,512]{1,0:T(8,128)(2,1)S(1)} %get-tuple-element.218.refs_0_), channel_id=1, source_target_pairs={{0,2},{1,3},{2,0},{3,1},{4,6},{5,7},{6,4},{7,5},{8,10},{9,11},{10,... | collective-permute-start | bytes 1572872 | tf_op jit(solution)/shard_map/ppermute | solution.py:716
  140.3 47.1 %all-to-all-start = ((bf16[8,2,2,64,512]{4,3,2,1,0:T(8,128)(2,1)}), bf16[8,2,2,64,512]{4,3,2,1,0:T(8,128)(2,1)}, u32[]{:S(2)}, u32[]{:S(2)}) async-start(bf16[8,2,2,64,512]{4,3,2,1,0:T(8,128)(2,1)} %shard_map.325), calls=%async_computation | async-start | bytes 4194304 | tf_op jit(solution)/shard_map/all_to_all | solution.py:707
  149.4 12.3 %collective-permute-start.38 = (bf16[208,512]{1,0:T(8,128)(2,1)S(1)}, bf16[208,512]{1,0:T(8,128)(2,1)S(1)}, u32[]{:S(2)}, u32[]{:S(2)}) collective-permute-start(bf16[208,512]{1,0:T(8,128)(2,1)S(1)} %get-tuple-element.254), channel_id=1, source_target_pairs={{0,1},{1,0},{2,3},{3,2},{4,5},{5,4},{6,7},{7,6},{8,9},{9,8},{10,11... | collective-permute-start | bytes 638984 | tf_op jit(solution)/shard_map/ppermute | solution.py:716
  152.4 15.4 %collective-permute-start.39 = (bf16[208,512]{1,0:T(8,128)(2,1)S(1)}, bf16[208,512]{1,0:T(8,128)(2,1)S(1)}, u32[]{:S(2)}, u32[]{:S(2)}) collective-permute-start(bf16[208,512]{1,0:T(8,128)(2,1)S(1)} %get-tuple-element.255), channel_id=1, source_target_pairs={{0,2},{1,3},{2,0},{3,1},{4,6},{5,7},{6,4},{7,5},{8,10},{9,11},{10,... | collective-permute-start | bytes 638984 | tf_op jit(solution)/shard_map/ppermute | solution.py:716
  153.0 20.8 %collective-permute-start.40 = (bf16[208,512]{1,0:T(8,128)(2,1)S(1)}, bf16[208,512]{1,0:T(8,128)(2,1)S(1)}, u32[]{:S(2)}, u32[]{:S(2)}) collective-permute-start(bf16[208,512]{1,0:T(8,128)(2,1)S(1)} %pad_maximum_fusion.8), channel_id=1, source_target_pairs={{0,3},{1,2},{2,1},{3,0},{4,7},{5,6},{6,5},{7,4},{8,11},{9,10},{10,... | collective-permute-start | bytes 638984 | tf_op jit(solution)/shard_map/ppermute | solution.py:716
  154.0 30.3 %collective-permute-start.45 = (bf16[512,512]{1,0:T(8,128)(2,1)S(1)}, bf16[512,512]{1,0:T(8,128)(2,1)S(1)}, u32[]{:S(2)}, u32[]{:S(2)}) collective-permute-start(bf16[512,512]{1,0:T(8,128)(2,1)S(1)} %collective-permute-done.37.refs_2_), channel_id=1, source_target_pairs={{1,0},{2,3},{5,4},{6,7},{9,8},{10,11},{13,12},{14,15},{17,16},{18,... | collective-permute-start | bytes 1572872 | tf_op jit(solution)/shard_map/ppermute | solution.py:768
  158.8 25.5 %collective-permute-start.44 = (bf16[512,512]{1,0:T(8,128)(2,1)S(1)}, bf16[512,512]{1,0:T(8,128)(2,1)S(1)}, u32[]{:S(2)}, u32[]{:S(2)}) collective-permute-start(bf16[512,512]{1,0:T(8,128)(2,1)S(1)} %get-tuple-element.218.refs_0_), channel_id=1, source_target_pairs={{1,2},{2,1},{5,6},{6,5},{9,10},{10,9},{13,14},{14,13},{17,18},{18,... | collective-permute-start | bytes 1572872 | tf_op jit(solution)/shard_map/ppermute | solution.py:767
  174.0 8.3 %collective-permute-start.43 = (bf16[3,64,512]{2,1,0:T(8,128)(2,1)S(1)}, bf16[3,64,512]{2,1,0:T(8,128)(2,1)S(1)}, u32[]{:S(2)}, u32[]{:S(2)}) collective-permute-start(bf16[3,64,512]{2,1,0:T(8,128)(2,1)S(1)} %bitcast.85), channel_id=1, source_target_pairs={{0,24},{4,28},{8,16},{12,20},{16,8},{20,12},{24,0},{28,4},{1,25},{... | collective-permute-start | bytes 589832 | tf_op jit(solution)/shard_map/ppermute | solution.py:716
  175.4 8.8 %collective-permute-start.42 = (bf16[3,64,512]{2,1,0:T(8,128)(2,1)S(1)}, bf16[3,64,512]{2,1,0:T(8,128)(2,1)S(1)}, u32[]{:S(2)}, u32[]{:S(2)}) collective-permute-start(bf16[3,64,512]{2,1,0:T(8,128)(2,1)S(1)} %bitcast.86), channel_id=1, source_target_pairs={{0,16},{4,20},{8,24},{12,28},{16,0},{20,4},{24,8},{28,12},{1,17},{... | collective-permute-start | bytes 589832 | tf_op jit(solution)/shard_map/ppermute | solution.py:716
  176.5 7.7 %collective-permute-start.41 = (bf16[3,64,512]{2,1,0:T(8,128)(2,1)S(1)}, bf16[3,64,512]{2,1,0:T(8,128)(2,1)S(1)}, u32[]{:S(2)}, u32[]{:S(2)}) collective-permute-start(bf16[3,64,512]{2,1,0:T(8,128)(2,1)S(1)} %bitcast.87), channel_id=1, source_target_pairs={{0,8},{4,12},{8,0},{12,4},{16,24},{20,28},{24,16},{28,20},{1,9},{5... | collective-permute-start | bytes 589832 | tf_op jit(solution)/shard_map/ppermute | solution.py:716
  190.4 2.3 %collective-permute-start.46 = (bf16[4,3,64,512]{3,2,1,0:T(8,128)(2,1)S(1)}, bf16[4,3,64,512]{3,2,1,0:T(8,128)(2,1)S(1)}, u32[]{:S(2)}, u32[]{:S(2)}) collective-permute-start(bf16[4,3,64,512]{3,2,1,0:T(8,128)(2,1)S(1)} %pad_maximum_fusion.1.near_ref), channel_id=1, source_target_pairs={{0,4},{4,0},{8,12},{12,8},{16,20},{20,16},{24,28},{28,24},{1,5},{5... | collective-permute-start | bytes 2359304 | tf_op jit(solution)/shard_map/ppermute | solution.py:716
  (25 other events, 360.7 us)

commit v7 on v5

--- a/solution.py
+++ b/solution.py
@@ -287,11 +287,11 @@
     k_ref,
     v_ref,
     prob_ref,
+    full_s,
     weight_s,
     mask_s,
     coarse_s,
     numer_s,
-    full_s,
 ):
     rows = normed_ref.shape[0]
     pairs = q_ref.shape[0]
@@ -381,13 +381,12 @@
     lax.fori_loop(0, pairs, one_pair, 0)
 
 
-def feed_kernel(plan, info, own_ref, mixed_ref, near_ref, far_ref, *refs):
+def feed_kernel(plan, info, own_ref, mixed_ref, full_s, *refs):
     ffn_refs, refs = refs[: len(plan)], refs[len(plan) :]
     b_out_ref, gain_ref, shift_ref, bias_ref, b_down_ref, hidden_ref, normed_ref = refs[:7]
-    act_ref, slope_ref, *out_refs, result_s, full_s, ffn_s = refs[7:]
+    act_ref, slope_ref, ffn_s, *out_refs, result_s = refs[7:]
     pairs = mixed_ref.shape[0]
     line = info[5]
-    assemble(info, near_ref, far_ref, full_s)
     assemble_feed(info, plan, ffn_refs, ffn_s)
     hidden = own_ref[...].astype(F32) + b_out_ref[...]
     for p in range(pairs):
@@ -412,14 +411,10 @@
             out_ref[o] = result_s[pl.ds(pl.multiple_of(at, chunk), chunk), :].astype(BF16)
 
 
-def feed_back_kernel(plan, info, dy_ref, near_ref, far_ref, *refs):
-    ffn_refs, refs = refs[: len(plan)], refs[len(plan) :]
+def feed_back_kernel(dy_ref, full_s, ffn_s, *refs):
     slope_ref, hidden_ref, gain_ref, mixed_wide_ref, total_ref, grad_pre_ref, grad_hidden_ref = refs[:7]
     grad_hidden_low_ref, numer_ref, gtotal_ref, exchange_ref, vector_ref, b_up_ref = refs[7:13]
-    full_s, ffn_s = refs[13:]
     rows = dy_ref.shape[0]
-    assemble_feed(info, plan, ffn_refs, ffn_s)
-    assemble(info, near_ref, far_ref, full_s)
     pairs = slope_ref.shape[0]
     dy = dy_ref[...]
     grad_normed = jnp.zeros((rows, dy.shape[1]), F32)
@@ -484,8 +479,7 @@
     k_ref,
     v_ref,
     prob_ref,
-    near_ref,
-    far_ref,
+    full_s,
     own_ref,
     gain_ref,
     grad_hidden_ref,
@@ -496,14 +490,12 @@
     coarse_s,
     left_s,
     grad_s,
-    full_s,
     acc_s,
 ):
     pairs, rows = numer_ref.shape[0], numer_ref.shape[1]
     tiles = 2 * rows // TILE
     half_tiles = rows // TILE
     length, own, partner = lengths[info[0]], info[1], info[2]
-    assemble(info, near_ref, far_ref, full_s)
     pools = [jnp.concatenate([pool_tile(odd)] * 2, axis=1) for odd in range(2)]
     spreads = [jnp.concatenate([spread_tile(odd)] * 2, axis=1) for odd in range(2)]
     live = (iota((rows, 1), 0) + own < length).astype(F32)
@@ -663,7 +655,15 @@
 
 
 def place_rows_kernel(info, *refs):
-    gather_line(info[5], refs[:-1], refs[-1])
+    *pieces, out_ref, sems = refs
+    for step in range(2):
+        for n, (where, z, ref) in enumerate(line_sources(info[5], pieces)):
+
+            def move(n=n, z=z, ref=ref):
+                copy = pltpu.make_async_copy(ref, out_ref.at[z], sems.at[n])
+                copy.wait() if step else copy.start()
+
+            move() if where is None else pl.when(where)(move)
 
 
 def deal_kernel(info, dealing, *refs):
@@ -689,16 +689,19 @@
 SMEM_SPEC = pl.BlockSpec(memory_space=pltpu.SMEM)
 
 
-def call(kernel, outs, scalars, args, scratch=(), limit=16, long=False):
+def call(kernel, outs, scalars, args, scratch=(), limit=16, long=False, flops=1, off_chip=False):
+    spec = VMEM_SPEC
+    if off_chip:
+        spec = pl.BlockSpec(memory_space=pl.ANY)
     return pl.pallas_call(
         kernel,
         out_shape=[jax.ShapeDtypeStruct(shape, dtype) for shape, dtype in outs],
-        in_specs=[SMEM_SPEC] * len(scalars) + [VMEM_SPEC] * len(args),
-        out_specs=[VMEM_SPEC] * len(outs),
+        in_specs=[SMEM_SPEC] * len(scalars) + [spec] * len(args),
+        out_specs=[spec] * len(outs),
         scratch_shapes=list(scratch),
         compiler_params=pltpu.CompilerParams(vmem_limit_bytes=limit << 20),
         cost_estimate=pl.CostEstimate(
-            flops=10**10 if long else 1, transcendentals=0, bytes_accessed=1
+            flops=10**10 if long else flops, transcendentals=0, bytes_accessed=1
         ),
     )(*scalars, *args)
 
@@ -799,8 +802,6 @@
     dy = lax.dynamic_index_in_dim(cotangent.reshape(nt, rows, width), t, 0, keepdims=False)
     top = rows >> level_shifts(rows)[-1]
 
-    attn_full = pltpu.VMEM((nt, width, 4 * TILE), BF16)
-    ffn_full = pltpu.VMEM((nt, 2, width, hid), BF16)
 
     normed_one, pooled = call(
         norm_one_kernel,
@@ -811,7 +812,7 @@
     attn_line = near_line(attn_piece)
     normed_one, *attn_line = lax.optimization_barrier((normed_one, *attn_line))
     biases = jnp.stack([piece[chunk:] for piece in attn_line])
-    ffn_line = line_first(after(ffn_piece, attn_line[1]))
+    ffn_line = line_first(ffn_piece)
     attn_line, biases = call(
         stack_kernel,
         [((nt, chunk, 4 * TILE), BF16), ((nt, 16, 4 * TILE), BF16)],
@@ -833,11 +834,12 @@
     plan += [(1, 0, tuple(range(first, outer, 2))) for first in range(2)]
     plan += [(part, 1, chips) for part, _, chips in plan]
 
-    mixed, mixed_wide, total, q, k, v, prob = call(
+    mixed, mixed_wide, total, q, k, v, prob, attn_full = call(
         attend_kernel,
         [((nt, rows, TILE), BF16), ((nt, rows, TILE), F32), ((nt, rows, TILE), F32)]
         + [((nt, 2 * rows, TILE), BF16)] * 3
-        + [((nt, 2 * rows // TILE, TILE, 2 * TILE), BF16)],
+        + [((nt, 2 * rows // TILE, TILE, 2 * TILE), BF16)]
+        + [((nt, width, 4 * TILE), BF16)],
         [info, lengths],
         [normed_one, pooled, *attn_w, biases],
         scratch=[
@@ -845,7 +847,6 @@
             pltpu.VMEM((2, TILE, 2 * TILE), F32),
             pltpu.VMEM((rows, 3 * TILE), F32),
             pltpu.VMEM((2 * rows, 2 * TILE), F32),
-            attn_full,
         ],
         limit=24,
         long=True,
@@ -854,15 +855,16 @@
     ffn_w = ups + downs
     ffn_w += [swap(each, "dp", 1) for each in ffn_w]
     piece = rows // dp
-    hidden, normed_two, act, slope, out_near, out_far = call(
+    hidden, normed_two, act, slope, ffn_full, out_near, out_far = call(
         functools.partial(feed_kernel, plan),
         [((rows, width), F32), ((rows, width), BF16)]
         + [((nt, rows, hid), BF16)] * 2
+        + [((nt, 2, width, hid), BF16)]
         + [((outer, piece, width), BF16)] * 2,
         [info],
-        [own, mixed, *attn_w, *ffn_w]
+        [own, mixed, attn_full, *ffn_w]
         + [row(b_out), row(ln2_gain), row(ln2_bias), biases, row(b_down)],
-        scratch=[pltpu.VMEM((rows, width), F32), attn_full, ffn_full],
+        scratch=[pltpu.VMEM((rows, width), F32)],
         limit=28,
     )
     chunks = call(
@@ -871,7 +873,7 @@
     dy, chunks = lax.optimization_barrier((dy, chunks))
 
     grad_pre, grad_hidden, grad_hidden_low, numer, gtotal, sent, vec_two, vec_up = call(
-        functools.partial(feed_back_kernel, plan),
+        feed_back_kernel,
         [
             ((nt, rows, hid), BF16),
             ((rows, width), F32),
@@ -882,9 +884,8 @@
             ((4, width), F32),
             ((nt, 1, hid), F32),
         ],
-        [info],
-        [dy, *attn_w, *ffn_w, slope, hidden, row(ln2_gain), mixed_wide, total],
-        scratch=[attn_full, ffn_full],
+        [],
+        [dy, attn_full, ffn_full, slope, hidden, row(ln2_gain), mixed_wide, total],
         limit=28,
     )
     swapped = swap(sent, "tensor", 1)
@@ -919,13 +920,12 @@
             ((2, width), F32),
         ],
         [info, lengths],
-        [numer, gtotal, swapped, q, k, v, prob, *attn_w]
+        [numer, gtotal, swapped, q, k, v, prob, attn_full]
         + [own, row(ln1_gain), grad_hidden],
         scratch=[
             pltpu.VMEM((rows, 2 * TILE), F32),
             pltpu.VMEM((2 * rows, 2 * TILE), BF16),
             pltpu.VMEM((2 * rows, 3 * TILE), F32),
-            attn_full,
             pltpu.VMEM((rows, width), F32),
         ],
         limit=20,
@@ -969,8 +969,18 @@
     ]
     grads = total_of([grads[0]] + [swap(grads[z], "tensor", z) for z in range(1, nt)])
     vectors = grads[3 * chunk :].astype(F32)
-    grads, row_pieces = lax.optimization_barrier((grads, line_second(row_pieces)))
+    row_pieces = line_second(row_pieces)
     near = jnp.stack(plane_pieces(grads[: 3 * chunk].reshape(3, chunk, width)))
+    (grad_tokens,) = call(
+        place_rows_kernel,
+        [((nt, rows, width), BF16)],
+        [info],
+        row_pieces,
+        scratch=[pltpu.SemaphoreType.DMA((5,))],
+        off_chip=True,
+    )
+    grad_tokens = grad_tokens.reshape(seq_dev, length, width)
+    near, grad_tokens, dealt = lax.optimization_barrier((near, grad_tokens, dealt))
     grads = near, swap(near, "dp", 1)
     g_up, g_down, g_query, g_key, g_value, g_out = call(
         place_grads_kernel,
@@ -981,12 +991,11 @@
         grads,
         scratch=[pltpu.VMEM((width, TILE), F32)],
     )
-    (grad_tokens,) = call(
-        place_rows_kernel, [((nt, rows, width), BF16)], [info], row_pieces
-    )
-    grad_tokens = grad_tokens.reshape(seq_dev, length, width)
     (output,) = call(
-        settle_kernel, [((seq_dev, nt // seq_dev, dp, piece, width), BF16)], [], [dealt]
+        settle_kernel,
+        [((seq_dev, nt // seq_dev, dp, piece, width), BF16)],
+        [],
+        [pltpu.with_memory_space_constraint(dealt, pltpu.HBM)],
     )
     output = output.reshape(seq_dev, length, width)
     base = 4 + nt

time: 213 us -> 194 us (0.911)
  waiting for transfers between devices: 90.3 us -> 64.9 us
  starting transfers between devices: 62.4 us -> 66.5 us
    ppermute x41, waiting for transfers between devices: 69 us -> 53.3 us  [swap(): return lax.ppermute(piece, axis, [(i, i ^ distance) for i in range(size)])]
    ppermute x3, waiting for transfers between devices: 20.2 us -> 10.8 us  [line_second(): three = lax.ppermute(after(piece, two), 'tensor', [(1, 2), (2, 1)])]
    ppermute x41, starting transfers between devices: 40.5 us -> 45.1 us  [swap(): return lax.ppermute(piece, axis, [(i, i ^ distance) for i in range(size)])]
  transfers between devices with their start and end apart: 48 -> 48, of which waited for: 26 -> 24; matrix products, arithmetic and copies ran while one was open for 2% -> 3% of each run, Pallas kernels for 18% -> 20%
where the time goes in v7:
time: 194 us; the launch traced here: 193 us
  starting transfers between devices  66.5 us (34%)
  waiting for transfers between devices  64.9 us (33%)
  Pallas kernels  51.3 us (26%)
  local copies, waits for them, and re-layouts  5.19 us (3%)
  other arithmetic  3.52 us (2%)
    ppermute x41, waiting for transfers between devices, swap(): return lax.ppermute(piece, axis, [(i, i ^ distance) for i in range(size)])  53.3 us
    pallas_call x14, Pallas kernels, call(): pl.pallas_call(kernel, out_shape=[jax.ShapeDtypeStruct(shape, dtype) for...  48.7 us
    ppermute x41, starting transfers between devices, swap(): return lax.ppermute(piece, axis, [(i, i ^ distance) for i in range(size)])  45.1 us
    ppermute x3, waiting for transfers between devices, line_second(): three = lax.ppermute(after(piece, two), 'tensor', [(1, 2), (2, 1)])  10.8 us
    ppermute x3, starting transfers between devices, line_second(): passed = lax.ppermute(two, 'tensor', [(1, 0), (2, 3)])  9.68 us
    ppermute x3, starting transfers between devices, line_second(): three = lax.ppermute(after(piece, two), 'tensor', [(1, 2), (2, 1)])  7.34 us
    all_to_all x1, starting transfers between devices, exchange(): lax.all_to_all(pieces, axis, 0, 0, tiled=True, axis_index_groups=groups)  4.35 us
  transfers between devices with their start and end apart: 48, of which 24 were waited for; matrix products, arithmetic and copies ran while one was open for 3% of the time, Pallas kernels for 20%

profile of v7, /device:TPU:8, one launch (start us, length us, event | category | flops | bytes accessed | tf_op | source)
XLA Modules:
  0.0 192.6 jit_solution(16594943511862755902)
XLA Ops:
  1.3 2.5 %shard_map.315 = (bf16[80,512]{1,0:T(8,128)(2,1)}, bf16[2,64,512]{2,1,0:T(8,128)(2,1)}) custom-call(s32[6]{0:T(128)} %stack.72.info, bf16[512,128]{1,0:T(8,128)(2,1)} %q_ref.1, bf16[512,128]{1,0:T(8,128)(2,1)} %k_ref.1, bf16[512,128]{1,0:T(8,128)(2,1)} %v_ref.1, bf16[128,512]{1,0:T(8,128)(2,1)} %o_ref.1, bf16[512,512]{1,0:T(8,128)(2,1)} %up_ref.1, ...), custom_call_target="tpu_custom_call" | custom-call | tf_op jit(solution)/shard_map/pallas_call | solution.py:783
  3.9 1.6 collective-permute-start.2
  6.6 1.4 collective-permute-start
  8.0 2.9 %collective-permute-start.7 = (bf16[2,64,512]{2,1,0:T(8,128)(2,1)}, bf16[2,64,512]{2,1,0:T(8,128)(2,1)S(1)}, u32[]{:S(2)}, u32[]{:S(2)}) collective-permute-start(bf16[2,64,512]{2,1,0:T(8,128)(2,1)} %get-tuple-element.132.refs_0_), channel_id=1, source_target_pairs={{0,2},{1,3},{2,0},{3,1},{4,6},{5,7},{6,4},{7,5},{8,10},{9,11},{10,... | collective-permute-start | bytes 393224 | tf_op jit(solution)/shard_map/ppermute | solution.py:719
  14.1 2.0 %collective-permute-done.1.refs_2_ = bf16[80,512]{1,0:T(8,128)(2,1)S(1)} collective-permute-done((bf16[80,512]{1,0:T(8,128)(2,1)}, bf16[80,512]{1,0:T(8,128)(2,1)S(1)}, u32[]{:S(2)}, u32[]{:S(2)}) %collective-permute-start.1) | collective-permute-done | bytes 81952 | tf_op jit(solution)/shard_map/ppermute | solution.py:719
  16.1 2.5 %collective-permute-start.5 = (bf16[4,64,512]{2,1,0:T(8,128)(2,1)S(1)}, bf16[4,64,512]{2,1,0:T(8,128)(2,1)S(1)}, u32[]{:S(2)}, u32[]{:S(2)}) collective-permute-start(bf16[4,64,512]{2,1,0:T(8,128)(2,1)S(1)} %get-tuple-element.138), channel_id=1, source_target_pairs={{0,24},{4,28},{8,16},{12,20},{16,8},{20,12},{24,0},{28,4},{1,25},{... | collective-permute-start | bytes 786440 | tf_op jit(solution)/shard_map/ppermute | solution.py:719
  19.7 2.1 %collective-permute-start.8 = (bf16[2,64,512]{2,1,0:T(8,128)(2,1)S(1)}, bf16[2,64,512]{2,1,0:T(8,128)(2,1)S(1)}, u32[]{:S(2)}, u32[]{:S(2)}) collective-permute-start(bf16[2,64,512]{2,1,0:T(8,128)(2,1)S(1)} %copy-done.2), channel_id=1, source_target_pairs={{1,2},{2,1},{5,6},{6,5},{9,10},{10,9},{13,14},{14,13},{17,18},{18,... | collective-permute-start | bytes 393224 | tf_op jit(solution)/shard_map/ppermute | solution.py:770
  21.8 3.1 %collective-permute-start.9 = (bf16[2,64,512]{2,1,0:T(8,128)(2,1)S(1)}, bf16[2,64,512]{2,1,0:T(8,128)(2,1)S(1)}, u32[]{:S(2)}, u32[]{:S(2)}) collective-permute-start(bf16[2,64,512]{2,1,0:T(8,128)(2,1)S(1)} %collective-permute-done.7.refs_2_), channel_id=1, source_target_pairs={{1,0},{2,3},{5,4},{6,7},{9,8},{10,11},{13,12},{14,15},{17,16},{18,... | collective-permute-start | bytes 393224 | tf_op jit(solution)/shard_map/ppermute | solution.py:771
  24.9 1.7 collective-permute-done.8.refs_3_
  30.9 6.0 %collective-permute-done.12 = bf16[4,64,512]{2,1,0:T(8,128)(2,1)S(1)} collective-permute-done((bf16[4,64,512]{2,1,0:T(8,128)(2,1)S(1)}, bf16[4,64,512]{2,1,0:T(8,128)(2,1)S(1)}, u32[]{:S(2)}, u32[]{:S(2)}) %collective-permute-start.12) | collective-permute-done | bytes 262176 | tf_op jit(solution)/shard_map/ppermute | solution.py:719
  37.0 1.5 collective-permute-start.13
  39.8 7.8 %shard_map.318 = (bf16[4,512,128]{2,1,0:T(8,128)(2,1)S(1)}, f32[4,512,128]{2,1,0:T(8,128)S(1)}, f32[4,512,128]{2,1,0:T(8,128)S(1)}, bf16[4,1024,128]{2,1,0:T(8,1...) custom-call(s32[6]{0:T(128)S(1)} %copy-done.4, ...), custom_call_target="tpu_custom_call" | custom-call | flops 10000000000 | bytes 1 | tf_op jit(solution)/shard_map/pallas_call | solution.py:696
  47.6 2.9 %collective-permute-done.13.refs_3_ = bf16[2,4,64,512]{3,2,1,0:T(8,128)(2,1)S(1)} collective-permute-done((bf16[2,4,64,512]{3,2,1,0:T(8,128)(2,1)S(1)}, bf16[2,4,64,512]{3,2,1,0:T(8,128)(2,1)S(1)}, u32[]{:S(2)}, u32[]{:S(2)}) %collective-permute-start.13) | collective-permute-done | bytes 524320 | tf_op jit(solution)/shard_map/ppermute | solution.py:719
  56.0 5.2 %shard_map.319 = (f32[512,512]{1,0:T(8,128)S(1)}, bf16[512,512]{1,0:T(8,128)(2,1)S(1)}, bf16[4,512,512]{2,1,0:T(8,128)(2,1)S(1)}, bf16[4,512,512]{2,1,0:T(8,128)...) custom-call(s32[6]{0:T(128)S(1)} %copy-done.4, ...), custom_call_target="tpu_custom_call" | custom-call | flops 1 | bytes 1 | tf_op jit(solution)/shard_map/pallas_call | solution.py:696
  61.4 1.4 collective-permute-done.19.far_ref
  64.8 1.6 collective-permute-start.22
  66.4 4.7 %shard_map.321 = (bf16[4,512,512]{2,1,0:T(8,128)(2,1)S(1)}, f32[512,512]{1,0:T(8,128)S(1)}, bf16[512,512]{1,0:T(8,128)(2,1)S(1)}, f32[4,512,128]{2,1,0:T(8,128)S...) custom-call(bf16[512,512]{1,0:T(8,128)(2,1)S(1)} %dynamic-slice_bitc, ...), custom_call_target="tpu_custom_call" | custom-call | flops 1 | bytes 1 | tf_op jit(solution)/shard_map/pallas_call | solution.py:696
  72.0 3.0 %shard_map.322 = (bf16[4,4,2,64,512]{4,3,2,1,0:T(8,128)(2,1)S(1)}, bf16[4,4,2,64,512]{4,3,2,1,0:T(8,128)(2,1)S(1)}) custom-call(s32[6]{0:T(128)S(1)} %copy-done.4, bf16[512,512]{1,0:T(8,128)(2,1)S(1)} %get-tuple-element.164.normed_ref, bf16[4,512,512]{2,1,0:T(8,128)(2,1)S(1)} %get-tuple-element.165.act_ref, ...), custom_call_target="tpu_custom_call" | custom-call | flops 1 | bytes 1 | tf_op jit(solution)/shard_map/pallas_call | solution.py:696
  75.1 2.6 %collective-permute-start.24 = (f32[4,32,128]{2,1,0:T(8,128)S(1)}, f32[4,32,128]{2,1,0:T(8,128)S(1)}, u32[]{:S(2)}, u32[]{:S(2)}) collective-permute-start(f32[4,32,128]{2,1,0:T(8,128)S(1)} %get-tuple-element.174), channel_id=1, source_target_pairs={{0,1},{1,0},{2,3},{3,2},{4,5},{5,4},{6,7},{7,6},{8,9},{9,8},{10,11... | collective-permute-start | bytes 196616 | tf_op jit(solution)/shard_map/ppermute | solution.py:719
  77.6 1.5 collective-permute-start.26
  79.2 1.9 %collective-permute-start.25 = (bf16[8,64,512]{2,1,0:T(8,128)(2,1)S(1)}, bf16[8,64,512]{2,1,0:T(8,128)(2,1)S(1)}, u32[]{:S(2)}, u32[]{:S(2)}) collective-permute-start(bf16[8,64,512]{2,1,0:T(8,128)(2,1)S(1)} %pad_maximum_fusion.4.refs_0_), channel_id=1, source_target_pairs={{0,1},{1,0},{2,3},{3,2},{4,5},{5,4},{6,7},{7,6},{8,9},{9,8},{10,11... | collective-permute-start | bytes 1572872 | tf_op jit(solution)/shard_map/ppermute | solution.py:719
  82.8 1.5 collective-permute-start.28
  85.5 14.1 %shard_map.323 = (bf16[4,512,384]{2,1,0:T(8,128)(2,1)S(1)}, f32[4,2,128]{2,1,0:T(2,128)S(1)}, bf16[512,512]{1,0:T(8,128)(2,1)S(1)}, f32[2,512]{1,0:T(2,128)S(1)}) custom-call(s32[6]{0:T(128)S(1)} %copy-done.4, s32[16]{0:T(128)S(1)} %copy-done.11, f32[4,512,128]{2,1,0:T(8,128)S(1)} %get-tuple-element.162.numer_ref, ...), custom_call_target="tpu_custom_call" | custom-call | flops 10000000000 | bytes 1 | tf_op jit(solution)/shard_map/pallas_call | solution.py:696
  99.6 2.6 %collective-permute-done.26.refs_2_ = bf16[8,64,512]{2,1,0:T(8,128)(2,1)S(1)} collective-permute-done((bf16[8,64,512]{2,1,0:T(8,128)(2,1)S(1)}, bf16[8,64,512]{2,1,0:T(8,128)(2,1)S(1)}, u32[]{:S(2)}, u32[]{:S(2)}) %collective-permute-start.26) | collective-permute-done | bytes 524320 | tf_op jit(solution)/shard_map/ppermute | solution.py:719
  102.2 2.2 %collective-permute-done.25.refs_1_ = bf16[8,64,512]{2,1,0:T(8,128)(2,1)S(1)} collective-permute-done((bf16[8,64,512]{2,1,0:T(8,128)(2,1)S(1)}, bf16[8,64,512]{2,1,0:T(8,128)(2,1)S(1)}, u32[]{:S(2)}, u32[]{:S(2)}) %collective-permute-start.25) | collective-permute-done | bytes 524320 | tf_op jit(solution)/shard_map/ppermute | solution.py:719
  104.4 2.5 %shard_map.324 = (bf16[4,272,512]{2,1,0:T(8,128)(2,1)S(1)}, bf16[4,272,512]{2,1,0:T(8,128)(2,1)S(1)}) custom-call(s32[6]{0:T(128)S(1)} %copy-done.4, bf16[512,512]{1,0:T(8,128)(2,1)S(1)} %get-tuple-element.125.normed_ref, bf16[4,512,384]{2,1,0:T(8,128)(2,1)S(1)} %get-tuple-element.182.grads_ref, bf16[512,512]{1,0:T(8,128)(2,1)S(1)} %get-tuple-element.186.grad_hidden_ref, ...), custom_call_target="tpu_custom_call" | custom-call | flops 1 | bytes 1 | tf_op jit(solution)/shard_map/pallas_call | solution.py:696
  107.3 2.6 %collective-permute-start.34 = (bf16[8,64,512]{2,1,0:T(8,128)(2,1)S(1)}, bf16[8,64,512]{2,1,0:T(8,128)(2,1)S(1)}, u32[]{:S(2)}, u32[]{:S(2)}) collective-permute-start(bf16[8,64,512]{2,1,0:T(8,128)(2,1)S(1)} %pad_maximum_fusion.4.refs_0_), channel_id=1, source_target_pairs={{1,2},{2,1},{5,6},{6,5},{9,10},{10,9},{13,14},{14,13},{17,18},{18,... | collective-permute-start | bytes 1572872 | tf_op jit(solution)/shard_map/ppermute | solution.py:770
  109.9 1.8 collective-permute-start.35
  112.2 1.5 collective-permute-start.33
  114.3 9.1 %collective-permute-done.34.refs_3_ = bf16[8,64,512]{2,1,0:T(8,128)(2,1)S(1)} collective-permute-done((bf16[8,64,512]{2,1,0:T(8,128)(2,1)S(1)}, bf16[8,64,512]{2,1,0:T(8,128)(2,1)S(1)}, u32[]{:S(2)}, u32[]{:S(2)}) %collective-permute-start.34) | collective-permute-done | bytes 524320 | tf_op jit(solution)/shard_map/ppermute | solution.py:770
  124.6 2.5 %collective-permute-start.37 = (bf16[512,512]{1,0:T(8,128)(2,1)S(1)}, bf16[512,512]{1,0:T(8,128)(2,1)S(1)}, u32[]{:S(2)}, u32[]{:S(2)}) collective-permute-start(bf16[512,512]{1,0:T(8,128)(2,1)S(1)} %get-tuple-element.214.refs_0_), channel_id=1, source_target_pairs={{0,2},{1,3},{2,0},{3,1},{4,6},{5,7},{6,4},{7,5},{8,10},{9,11},{10,... | collective-permute-start | bytes 1572872 | tf_op jit(solution)/shard_map/ppermute | solution.py:719
  127.1 7.7 %collective-permute-done.36.refs_1_ = bf16[512,512]{1,0:T(8,128)(2,1)S(1)} collective-permute-done((bf16[512,512]{1,0:T(8,128)(2,1)S(1)}, bf16[512,512]{1,0:T(8,128)(2,1)S(1)}, u32[]{:S(2)}, u32[]{:S(2)}) %collective-permute-start.36) | collective-permute-done | bytes 524320 | tf_op jit(solution)/shard_map/ppermute | solution.py:719
  136.3 2.1 %shard_map.326 = bf16[8,2,2,64,512]{4,3,2,1,0:T(8,128)(2,1)} custom-call(s32[6]{0:T(128)S(1)} %copy-done.4, s32[16]{0:T(128)S(1)} %copy-done.12, bf16[8,64,512]{2,1,0:T(8,128)(2,1)S(1)} %pad_maximum_fusion.4.refs_0_, bf16[8,64,512]{2,1,0:T(8,128)(2,1)S(1)} %collective-permute-done.25.refs_1_, bf16[8,64,512]{2,1,0:T(8,128)(2,1)S(1)} %collective-permute-done.26.refs_2_, ...), custom_call_target="tpu_custom_call" | custom-call | flops 1 | bytes 1 | tf_op jit(solution)/shard_map/pallas_call | solution.py:696
  138.4 4.4 %all-to-all-start = ((bf16[8,2,2,64,512]{4,3,2,1,0:T(8,128)(2,1)}), bf16[8,2,2,64,512]{4,3,2,1,0:T(8,128)(2,1)}, u32[]{:S(2)}, u32[]{:S(2)}) async-start(bf16[8,2,2,64,512]{4,3,2,1,0:T(8,128)(2,1)} %shard_map.326), calls=%async_computation | async-start | bytes 4194304 | tf_op jit(solution)/shard_map/all_to_all | solution.py:710
  142.8 1.7 add_convert_fusion
  144.7 3.5 %collective-permute-done.37.refs_2_ = bf16[512,512]{1,0:T(8,128)(2,1)S(1)} collective-permute-done((bf16[512,512]{1,0:T(8,128)(2,1)S(1)}, bf16[512,512]{1,0:T(8,128)(2,1)S(1)}, u32[]{:S(2)}, u32[]{:S(2)}) %collective-permute-start.37) | collective-permute-done | bytes 524320 | tf_op jit(solution)/shard_map/ppermute | solution.py:719
  148.3 3.3 %collective-permute-start.38 = (bf16[208,512]{1,0:T(8,128)(2,1)S(1)}, bf16[208,512]{1,0:T(8,128)(2,1)S(1)}, u32[]{:S(2)}, u32[]{:S(2)}) collective-permute-start(bf16[208,512]{1,0:T(8,128)(2,1)S(1)} %get-tuple-element.254), channel_id=1, source_target_pairs={{0,1},{1,0},{2,3},{3,2},{4,5},{5,4},{6,7},{7,6},{8,9},{9,8},{10,11... | collective-permute-start | bytes 638984 | tf_op jit(solution)/shard_map/ppermute | solution.py:719
  151.9 1.4 collective-permute-start.40
  153.3 4.8 %collective-permute-start.45 = (bf16[512,512]{1,0:T(8,128)(2,1)S(1)}, bf16[512,512]{1,0:T(8,128)(2,1)S(1)}, u32[]{:S(2)}, u32[]{:S(2)}) collective-permute-start(bf16[512,512]{1,0:T(8,128)(2,1)S(1)} %collective-permute-done.37.refs_2_), channel_id=1, source_target_pairs={{1,0},{2,3},{5,4},{6,7},{9,8},{10,11},{13,12},{14,15},{17,16},{18,... | collective-permute-start | bytes 1572872 | tf_op jit(solution)/shard_map/ppermute | solution.py:771
  158.0 2.6 %collective-permute-start.44 = (bf16[512,512]{1,0:T(8,128)(2,1)S(1)}, bf16[512,512]{1,0:T(8,128)(2,1)S(1)}, u32[]{:S(2)}, u32[]{:S(2)}) collective-permute-start(bf16[512,512]{1,0:T(8,128)(2,1)S(1)} %get-tuple-element.214.refs_0_), channel_id=1, source_target_pairs={{1,2},{2,1},{5,6},{6,5},{9,10},{10,9},{13,14},{14,13},{17,18},{18,... | collective-permute-start | bytes 1572872 | tf_op jit(solution)/shard_map/ppermute | solution.py:770
  160.8 5.9 %collective-permute-done.39 = bf16[208,512]{1,0:T(8,128)(2,1)S(1)} collective-permute-done((bf16[208,512]{1,0:T(8,128)(2,1)S(1)}, bf16[208,512]{1,0:T(8,128)(2,1)S(1)}, u32[]{:S(2)}, u32[]{:S(2)}) %collective-permute-start.39) | collective-permute-done | bytes 213024 | tf_op jit(solution)/shard_map/ppermute | solution.py:719
  166.7 6.3 %collective-permute-done.40 = bf16[208,512]{1,0:T(8,128)(2,1)S(1)} collective-permute-done((bf16[208,512]{1,0:T(8,128)(2,1)S(1)}, bf16[208,512]{1,0:T(8,128)(2,1)S(1)}, u32[]{:S(2)}, u32[]{:S(2)}) %collective-permute-start.40) | collective-permute-done | bytes 213024 | tf_op jit(solution)/shard_map/ppermute | solution.py:719
  173.2 1.6 collective-permute-start.43
  176.7 4.7 %collective-permute-done.43 = bf16[3,64,512]{2,1,0:T(8,128)(2,1)S(1)} collective-permute-done((bf16[3,64,512]{2,1,0:T(8,128)(2,1)S(1)}, bf16[3,64,512]{2,1,0:T(8,128)(2,1)S(1)}, u32[]{:S(2)}, u32[]{:S(2)}) %collective-permute-start.43) | collective-permute-done | bytes 196640 | tf_op jit(solution)/shard_map/ppermute | solution.py:719
  181.4 1.8 collective-permute-done.42
  183.4 1.9 shard_map.325
  187.2 3.1 %shard_map.327 = bf16[2,2,8,64,512]{4,3,2,1,0:T(8,128)(2,1)} custom-call(bf16[8,2,2,64,512]{4,3,2,1,0:T(8,128)(2,1)} %all-to-all-done.pieces_ref), custom_call_target="tpu_custom_call" | custom-call | flops 1 | bytes 1 | tf_op jit(solution)/shard_map/pallas_call | solution.py:696
  190.3 2.4 %shard_map.328 = (f32[512,512]{1,0:T(8,128)}, f32[512,512]{1,0:T(8,128)}, f32[512,128]{1,0:T(8,128)}, f32[512,128]{1,0:T(8,128)}, f32[512,128]{1,0:T(8,128)}, /*index=5*/f32[128,512]{1,0:T(8,128)}) custom-call(s32[6]{0:T(128)S(1)} %copy-done.4, bf16[4,3,64,512]{3,2,1,0:T(8,128)(2,1)S(1)} %pad_maximum_fusion.1.near_ref, ...), custom_call_target="tpu_custom_call" | custom-call | flops 1 | bytes 1 | tf_op jit(solution)/shard_map/pallas_call | solution.py:696
  (128 shorter events, 31.8 us)
Async XLA Ops:
  3.9 10.2 %collective-permute-start.2 = (bf16[80,512]{1,0:T(8,128)(2,1)}, bf16[80,512]{1,0:T(8,128)(2,1)S(1)}, u32[]{:S(2)}, u32[]{:S(2)}) collective-permute-start(bf16[80,512]{1,0:T(8,128)(2,1)} %get-tuple-element.126.refs_0_), channel_id=1, source_target_pairs={{0,3},{1,2},{2,1},{3,0},{4,7},{5,6},{6,5},{7,4},{8,11},{9,10},{10,... | collective-permute-start | bytes 245768 | tf_op jit(solution)/shard_map/ppermute | solution.py:719
  5.5 10.6 %collective-permute-start.1 = (bf16[80,512]{1,0:T(8,128)(2,1)}, bf16[80,512]{1,0:T(8,128)(2,1)S(1)}, u32[]{:S(2)}, u32[]{:S(2)}) collective-permute-start(bf16[80,512]{1,0:T(8,128)(2,1)} %get-tuple-element.126.refs_0_), channel_id=1, source_target_pairs={{0,2},{1,3},{2,0},{3,1},{4,6},{5,7},{6,4},{7,5},{8,10},{9,11},{10,... | collective-permute-start | bytes 245768 | tf_op jit(solution)/shard_map/ppermute | solution.py:719
  6.6 9.5 %collective-permute-start = (bf16[80,512]{1,0:T(8,128)(2,1)}, bf16[80,512]{1,0:T(8,128)(2,1)S(1)}, u32[]{:S(2)}, u32[]{:S(2)}) collective-permute-start(bf16[80,512]{1,0:T(8,128)(2,1)} %get-tuple-element.126.refs_0_), channel_id=1, source_target_pairs={{0,1},{1,0},{2,3},{3,2},{4,5},{5,4},{6,7},{7,6},{8,9},{9,8},{10,11... | collective-permute-start | bytes 245768 | tf_op jit(solution)/shard_map/ppermute | solution.py:719
  8.0 11.7 %collective-permute-start.7 = (bf16[2,64,512]{2,1,0:T(8,128)(2,1)}, bf16[2,64,512]{2,1,0:T(8,128)(2,1)S(1)}, u32[]{:S(2)}, u32[]{:S(2)}) collective-permute-start(bf16[2,64,512]{2,1,0:T(8,128)(2,1)} %get-tuple-element.132.refs_0_), channel_id=1, source_target_pairs={{0,2},{1,3},{2,0},{3,1},{4,6},{5,7},{6,4},{7,5},{8,10},{9,11},{10,... | collective-permute-start | bytes 393224 | tf_op jit(solution)/shard_map/ppermute | solution.py:719
  10.9 10.9 %collective-permute-start.6 = (bf16[2,64,512]{2,1,0:T(8,128)(2,1)}, bf16[2,64,512]{2,1,0:T(8,128)(2,1)S(1)}, u32[]{:S(2)}, u32[]{:S(2)}) collective-permute-start(bf16[2,64,512]{2,1,0:T(8,128)(2,1)} %get-tuple-element.132.refs_0_), channel_id=1, source_target_pairs={{0,1},{1,0},{2,3},{3,2},{4,5},{5,4},{6,7},{7,6},{8,9},{9,8},{10,11... | collective-permute-start | bytes 393224 | tf_op jit(solution)/shard_map/ppermute | solution.py:719
  16.1 11.8 %collective-permute-start.5 = (bf16[4,64,512]{2,1,0:T(8,128)(2,1)S(1)}, bf16[4,64,512]{2,1,0:T(8,128)(2,1)S(1)}, u32[]{:S(2)}, u32[]{:S(2)}) collective-permute-start(bf16[4,64,512]{2,1,0:T(8,128)(2,1)S(1)} %get-tuple-element.138), channel_id=1, source_target_pairs={{0,24},{4,28},{8,16},{12,20},{16,8},{20,12},{24,0},{28,4},{1,25},{... | collective-permute-start | bytes 786440 | tf_op jit(solution)/shard_map/ppermute | solution.py:719
  18.6 9.4 %collective-permute-start.4 = (bf16[4,64,512]{2,1,0:T(8,128)(2,1)S(1)}, bf16[4,64,512]{2,1,0:T(8,128)(2,1)S(1)}, u32[]{:S(2)}, u32[]{:S(2)}) collective-permute-start(bf16[4,64,512]{2,1,0:T(8,128)(2,1)S(1)} %get-tuple-element.138), channel_id=1, source_target_pairs={{0,16},{4,20},{8,24},{12,28},{16,0},{20,4},{24,8},{28,12},{1,17},{... | collective-permute-start | bytes 786440 | tf_op jit(solution)/shard_map/ppermute | solution.py:719
  19.1 8.9 %collective-permute-start.3 = (bf16[4,64,512]{2,1,0:T(8,128)(2,1)S(1)}, bf16[4,64,512]{2,1,0:T(8,128)(2,1)S(1)}, u32[]{:S(2)}, u32[]{:S(2)}) collective-permute-start(bf16[4,64,512]{2,1,0:T(8,128)(2,1)S(1)} %get-tuple-element.138), channel_id=1, source_target_pairs={{0,8},{4,12},{8,0},{12,4},{16,24},{20,28},{24,16},{28,20},{1,9},{5... | collective-permute-start | bytes 786440 | tf_op jit(solution)/shard_map/ppermute | solution.py:719
  19.7 6.9 %collective-permute-start.8 = (bf16[2,64,512]{2,1,0:T(8,128)(2,1)S(1)}, bf16[2,64,512]{2,1,0:T(8,128)(2,1)S(1)}, u32[]{:S(2)}, u32[]{:S(2)}) collective-permute-start(bf16[2,64,512]{2,1,0:T(8,128)(2,1)S(1)} %copy-done.2), channel_id=1, source_target_pairs={{1,2},{2,1},{5,6},{6,5},{9,10},{10,9},{13,14},{14,13},{17,18},{18,... | collective-permute-start | bytes 393224 | tf_op jit(solution)/shard_map/ppermute | solution.py:770
  21.8 5.6 %collective-permute-start.9 = (bf16[2,64,512]{2,1,0:T(8,128)(2,1)S(1)}, bf16[2,64,512]{2,1,0:T(8,128)(2,1)S(1)}, u32[]{:S(2)}, u32[]{:S(2)}) collective-permute-start(bf16[2,64,512]{2,1,0:T(8,128)(2,1)S(1)} %collective-permute-done.7.refs_2_), channel_id=1, source_target_pairs={{1,0},{2,3},{5,4},{6,7},{9,8},{10,11},{13,12},{14,15},{17,16},{18,... | collective-permute-start | bytes 393224 | tf_op jit(solution)/shard_map/ppermute | solution.py:771
  28.1 11.7 %collective-permute-start.14 = (bf16[4,4,64,512]{3,2,1,0:T(8,128)(2,1)S(1)}, bf16[4,4,64,512]{3,2,1,0:T(8,128)(2,1)S(1)}, u32[]{:S(2)}, u32[]{:S(2)}) collective-permute-start(bf16[4,4,64,512]{3,2,1,0:T(8,128)(2,1)S(1)} %pad_maximum_fusion.near_ref), channel_id=1, source_target_pairs={{0,4},{4,0},{8,12},{12,8},{16,20},{20,16},{24,28},{28,24},{1,5},{5... | collective-permute-start | bytes 3145736 | tf_op jit(solution)/shard_map/ppermute | solution.py:719
  28.2 8.7 %collective-permute-start.12 = (bf16[4,64,512]{2,1,0:T(8,128)(2,1)S(1)}, bf16[4,64,512]{2,1,0:T(8,128)(2,1)S(1)}, u32[]{:S(2)}, u32[]{:S(2)}) collective-permute-start(bf16[4,64,512]{2,1,0:T(8,128)(2,1)S(1)} %get-tuple-element.136), channel_id=1, source_target_pairs={{0,16},{4,20},{8,24},{12,28},{16,0},{20,4},{24,8},{28,12},{1,17},{... | collective-permute-start | bytes 786440 | tf_op jit(solution)/shard_map/ppermute | solution.py:719
  29.6 8.9 %collective-permute-start.10 = (bf16[4,64,512]{2,1,0:T(8,128)(2,1)S(1)}, bf16[4,64,512]{2,1,0:T(8,128)(2,1)S(1)}, u32[]{:S(2)}, u32[]{:S(2)}) collective-permute-start(bf16[4,64,512]{2,1,0:T(8,128)(2,1)S(1)} %get-tuple-element.135), channel_id=1, source_target_pairs={{0,8},{4,12},{8,0},{12,4},{16,24},{20,28},{24,16},{28,20},{1,9},{5... | collective-permute-start | bytes 786440 | tf_op jit(solution)/shard_map/ppermute | solution.py:719
  37.0 13.6 %collective-permute-start.13 = (bf16[2,4,64,512]{3,2,1,0:T(8,128)(2,1)S(1)}, bf16[2,4,64,512]{3,2,1,0:T(8,128)(2,1)S(1)}, u32[]{:S(2)}, u32[]{:S(2)}) collective-permute-start(bf16[2,4,64,512]{3,2,1,0:T(8,128)(2,1)S(1)} %pad_maximum_fusion.3.refs_2_), channel_id=1, source_target_pairs={{0,8},{4,12},{8,0},{12,4},{16,24},{20,28},{24,16},{28,20},{1,9},{5... | collective-permute-start | bytes 1572872 | tf_op jit(solution)/shard_map/ppermute | solution.py:719
  38.5 13.3 %collective-permute-start.11 = (bf16[2,4,64,512]{3,2,1,0:T(8,128)(2,1)S(1)}, bf16[2,4,64,512]{3,2,1,0:T(8,128)(2,1)S(1)}, u32[]{:S(2)}, u32[]{:S(2)}) collective-permute-start(bf16[2,4,64,512]{3,2,1,0:T(8,128)(2,1)S(1)} %pad_maximum_fusion.2.refs_0_), channel_id=1, source_target_pairs={{0,16},{4,20},{8,24},{12,28},{16,0},{20,4},{24,8},{28,12},{1,17},{... | collective-permute-start | bytes 1572872 | tf_op jit(solution)/shard_map/ppermute | solution.py:719
  51.8 1.9 collective-permute-start.15
  51.8 2.7 %collective-permute-start.16 = (bf16[2,4,64,512]{3,2,1,0:T(8,128)(2,1)S(1)}, bf16[2,4,64,512]{3,2,1,0:T(8,128)(2,1)S(1)}, u32[]{:S(2)}, u32[]{:S(2)}) collective-permute-start(bf16[2,4,64,512]{3,2,1,0:T(8,128)(2,1)S(1)} %collective-permute-done.11.refs_1_), channel_id=1, source_target_pairs={{0,4},{4,0},{8,12},{12,8},{16,20},{20,16},{24,28},{28,24},{1,5},{5... | collective-permute-start | bytes 1572872 | tf_op jit(solution)/shard_map/ppermute | solution.py:719
  52.3 2.9 %collective-permute-start.17 = (bf16[2,4,64,512]{3,2,1,0:T(8,128)(2,1)S(1)}, bf16[2,4,64,512]{3,2,1,0:T(8,128)(2,1)S(1)}, u32[]{:S(2)}, u32[]{:S(2)}) collective-permute-start(bf16[2,4,64,512]{3,2,1,0:T(8,128)(2,1)S(1)} %pad_maximum_fusion.3.refs_2_), channel_id=1, source_target_pairs={{0,4},{4,0},{8,12},{12,8},{16,20},{20,16},{24,28},{28,24},{1,5},{5... | collective-permute-start | bytes 1572872 | tf_op jit(solution)/shard_map/ppermute | solution.py:719
  52.3 3.6 %collective-permute-start.18 = (bf16[2,4,64,512]{3,2,1,0:T(8,128)(2,1)S(1)}, bf16[2,4,64,512]{3,2,1,0:T(8,128)(2,1)S(1)}, u32[]{:S(2)}, u32[]{:S(2)}) collective-permute-start(bf16[2,4,64,512]{3,2,1,0:T(8,128)(2,1)S(1)} %collective-permute-done.13.refs_3_), channel_id=1, source_target_pairs={{0,4},{4,0},{8,12},{12,8},{16,20},{20,16},{24,28},{28,24},{1,5},{5... | collective-permute-start | bytes 1572872 | tf_op jit(solution)/shard_map/ppermute | solution.py:719
  61.2 1.6 collective-permute-start.19
  62.8 8.2 %collective-permute-start.20 = (bf16[2,64,512]{2,1,0:T(8,128)(2,1)S(1)}, bf16[2,64,512]{2,1,0:T(8,128)(2,1)S(1)}, u32[]{:S(2)}, u32[]{:S(2)}) collective-permute-start(bf16[2,64,512]{2,1,0:T(8,128)(2,1)S(1)} %get-tuple-element.167), channel_id=1, source_target_pairs={{0,8},{4,12},{8,0},{12,4},{16,24},{20,28},{24,16},{28,20},{1,9},{5... | collective-permute-start | bytes 393224 | tf_op jit(solution)/shard_map/ppermute | solution.py:719
  63.7 7.4 %collective-permute-start.21 = (bf16[2,64,512]{2,1,0:T(8,128)(2,1)S(1)}, bf16[2,64,512]{2,1,0:T(8,128)(2,1)S(1)}, u32[]{:S(2)}, u32[]{:S(2)}) collective-permute-start(bf16[2,64,512]{2,1,0:T(8,128)(2,1)S(1)} %get-tuple-element.168), channel_id=1, source_target_pairs={{0,16},{4,20},{8,24},{12,28},{16,0},{20,4},{24,8},{28,12},{1,17},{... | collective-permute-start | bytes 393224 | tf_op jit(solution)/shard_map/ppermute | solution.py:719
  64.8 7.1 %collective-permute-start.22 = (bf16[2,64,512]{2,1,0:T(8,128)(2,1)S(1)}, bf16[2,64,512]{2,1,0:T(8,128)(2,1)S(1)}, u32[]{:S(2)}, u32[]{:S(2)}) collective-permute-start(bf16[2,64,512]{2,1,0:T(8,128)(2,1)S(1)} %get-tuple-element.169), channel_id=1, source_target_pairs={{0,24},{4,28},{8,16},{12,20},{16,8},{20,12},{24,0},{28,4},{1,25},{... | collective-permute-start | bytes 393224 | tf_op jit(solution)/shard_map/ppermute | solution.py:719
  75.0 6.1 %collective-permute-start.23 = (bf16[4,4,2,64,512]{4,3,2,1,0:T(8,128)(2,1)S(1)}, bf16[4,4,2,64,512]{4,3,2,1,0:T(8,128)(2,1)S(1)}, u32[]{:S(2)}, u32[]{:S(2)}) collective-permute-start(bf16[4,4,2,64,512]{4,3,2,1,0:T(8,128)(2,1)S(1)} %get-tuple-element.173), channel_id=1, source_target_pairs={{0,4},{4,0},{8,12},{12,8},{16,20},{20,16},{24,28},{28,24},{1,5},{5... | collective-permute-start | bytes 6291464 | tf_op jit(solution)/shard_map/ppermute | solution.py:719
  75.1 6.8 %collective-permute-start.24 = (f32[4,32,128]{2,1,0:T(8,128)S(1)}, f32[4,32,128]{2,1,0:T(8,128)S(1)}, u32[]{:S(2)}, u32[]{:S(2)}) collective-permute-start(f32[4,32,128]{2,1,0:T(8,128)S(1)} %get-tuple-element.174), channel_id=1, source_target_pairs={{0,1},{1,0},{2,3},{3,2},{4,5},{5,4},{6,7},{7,6},{8,9},{9,8},{10,11... | collective-permute-start | bytes 196616 | tf_op jit(solution)/shard_map/ppermute | solution.py:719
  77.6 24.6 %collective-permute-start.26 = (bf16[8,64,512]{2,1,0:T(8,128)(2,1)S(1)}, bf16[8,64,512]{2,1,0:T(8,128)(2,1)S(1)}, u32[]{:S(2)}, u32[]{:S(2)}) collective-permute-start(bf16[8,64,512]{2,1,0:T(8,128)(2,1)S(1)} %pad_maximum_fusion.4.refs_0_), channel_id=1, source_target_pairs={{0,2},{1,3},{2,0},{3,1},{4,6},{5,7},{6,4},{7,5},{8,10},{9,11},{10,... | collective-permute-start | bytes 1572872 | tf_op jit(solution)/shard_map/ppermute | solution.py:719
  79.2 25.2 %collective-permute-start.25 = (bf16[8,64,512]{2,1,0:T(8,128)(2,1)S(1)}, bf16[8,64,512]{2,1,0:T(8,128)(2,1)S(1)}, u32[]{:S(2)}, u32[]{:S(2)}) collective-permute-start(bf16[8,64,512]{2,1,0:T(8,128)(2,1)S(1)} %pad_maximum_fusion.4.refs_0_), channel_id=1, source_target_pairs={{0,1},{1,0},{2,3},{3,2},{4,5},{5,4},{6,7},{7,6},{8,9},{9,8},{10,11... | collective-permute-start | bytes 1572872 | tf_op jit(solution)/shard_map/ppermute | solution.py:719
  81.9 25.0 %collective-permute-start.27 = (bf16[4,2,64,512]{3,2,1,0:T(8,128)(2,1)S(1)}, bf16[4,2,64,512]{3,2,1,0:T(8,128)(2,1)S(1)}, u32[]{:S(2)}, u32[]{:S(2)}) collective-permute-start(bf16[4,2,64,512]{3,2,1,0:T(8,128)(2,1)S(1)} %get-tuple-element.193), channel_id=1, source_target_pairs={{0,8},{4,12},{8,0},{12,4},{16,24},{20,28},{24,16},{28,20},{1,9},{5... | collective-permute-start | bytes 1572872 | tf_op jit(solution)/shard_map/ppermute | solution.py:719
  82.8 24.4 %collective-permute-start.28 = (bf16[4,2,64,512]{3,2,1,0:T(8,128)(2,1)S(1)}, bf16[4,2,64,512]{3,2,1,0:T(8,128)(2,1)S(1)}, u32[]{:S(2)}, u32[]{:S(2)}) collective-permute-start(bf16[4,2,64,512]{3,2,1,0:T(8,128)(2,1)S(1)} %get-tuple-element.194), channel_id=1, source_target_pairs={{0,16},{4,20},{8,24},{12,28},{16,0},{20,4},{24,8},{28,12},{1,17},{... | collective-permute-start | bytes 1572872 | tf_op jit(solution)/shard_map/ppermute | solution.py:719
  84.3 22.9 %collective-permute-start.29 = (bf16[4,2,64,512]{3,2,1,0:T(8,128)(2,1)S(1)}, bf16[4,2,64,512]{3,2,1,0:T(8,128)(2,1)S(1)}, u32[]{:S(2)}, u32[]{:S(2)}) collective-permute-start(bf16[4,2,64,512]{3,2,1,0:T(8,128)(2,1)S(1)} %get-tuple-element.195), channel_id=1, source_target_pairs={{0,24},{4,28},{8,16},{12,20},{16,8},{20,12},{24,0},{28,4},{1,25},{... | collective-permute-start | bytes 1572872 | tf_op jit(solution)/shard_map/ppermute | solution.py:719
  107.2 4.6 %collective-permute-start.30 = (bf16[4,272,512]{2,1,0:T(8,128)(2,1)S(1)}, bf16[4,272,512]{2,1,0:T(8,128)(2,1)S(1)}, u32[]{:S(2)}, u32[]{:S(2)}) collective-permute-start(bf16[4,272,512]{2,1,0:T(8,128)(2,1)S(1)} %get-tuple-element.201), channel_id=1, source_target_pairs={{0,4},{4,0},{8,12},{12,8},{16,20},{20,16},{24,28},{28,24},{1,5},{5... | collective-permute-start | bytes 3342344 | tf_op jit(solution)/shard_map/ppermute | solution.py:719
  107.3 16.2 %collective-permute-start.34 = (bf16[8,64,512]{2,1,0:T(8,128)(2,1)S(1)}, bf16[8,64,512]{2,1,0:T(8,128)(2,1)S(1)}, u32[]{:S(2)}, u32[]{:S(2)}) collective-permute-start(bf16[8,64,512]{2,1,0:T(8,128)(2,1)S(1)} %pad_maximum_fusion.4.refs_0_), channel_id=1, source_target_pairs={{1,2},{2,1},{5,6},{6,5},{9,10},{10,9},{13,14},{14,13},{17,18},{18,... | collective-permute-start | bytes 1572872 | tf_op jit(solution)/shard_map/ppermute | solution.py:770
  109.9 14.7 %collective-permute-start.35 = (bf16[8,64,512]{2,1,0:T(8,128)(2,1)S(1)}, bf16[8,64,512]{2,1,0:T(8,128)(2,1)S(1)}, u32[]{:S(2)}, u32[]{:S(2)}) collective-permute-start(bf16[8,64,512]{2,1,0:T(8,128)(2,1)S(1)} %collective-permute-done.26.refs_2_), channel_id=1, source_target_pairs={{1,0},{2,3},{5,4},{6,7},{9,8},{10,11},{13,12},{14,15},{17,16},{18,... | collective-permute-start | bytes 1572872 | tf_op jit(solution)/shard_map/ppermute | solution.py:771
  111.7 23.1 %collective-permute-start.36 = (bf16[512,512]{1,0:T(8,128)(2,1)S(1)}, bf16[512,512]{1,0:T(8,128)(2,1)S(1)}, u32[]{:S(2)}, u32[]{:S(2)}) collective-permute-start(bf16[512,512]{1,0:T(8,128)(2,1)S(1)} %get-tuple-element.214.refs_0_), channel_id=1, source_target_pairs={{0,1},{1,0},{2,3},{3,2},{4,5},{5,4},{6,7},{7,6},{8,9},{9,8},{10,11... | collective-permute-start | bytes 1572872 | tf_op jit(solution)/shard_map/ppermute | solution.py:719
  112.2 22.7 %collective-permute-start.33 = (bf16[272,512]{1,0:T(8,128)(2,1)S(1)}, bf16[272,512]{1,0:T(8,128)(2,1)S(1)}, u32[]{:S(2)}, u32[]{:S(2)}) collective-permute-start(bf16[272,512]{1,0:T(8,128)(2,1)S(1)} %get-tuple-element.233), channel_id=1, source_target_pairs={{0,24},{4,28},{8,16},{12,20},{16,8},{20,12},{24,0},{28,4},{1,25},{... | collective-permute-start | bytes 835592 | tf_op jit(solution)/shard_map/ppermute | solution.py:719
  113.6 21.2 %collective-permute-start.32 = (bf16[272,512]{1,0:T(8,128)(2,1)S(1)}, bf16[272,512]{1,0:T(8,128)(2,1)S(1)}, u32[]{:S(2)}, u32[]{:S(2)}) collective-permute-start(bf16[272,512]{1,0:T(8,128)(2,1)S(1)} %get-tuple-element.234), channel_id=1, source_target_pairs={{0,16},{4,20},{8,24},{12,28},{16,0},{20,4},{24,8},{28,12},{1,17},{... | collective-permute-start | bytes 835592 | tf_op jit(solution)/shard_map/ppermute | solution.py:719
  123.5 11.4 %collective-permute-start.31 = (bf16[272,512]{1,0:T(8,128)(2,1)S(1)}, bf16[272,512]{1,0:T(8,128)(2,1)S(1)}, u32[]{:S(2)}, u32[]{:S(2)}) collective-permute-start(bf16[272,512]{1,0:T(8,128)(2,1)S(1)} %get-tuple-element.235), channel_id=1, source_target_pairs={{0,8},{4,12},{8,0},{12,4},{16,24},{20,28},{24,16},{28,20},{1,9},{5... | collective-permute-start | bytes 835592 | tf_op jit(solution)/shard_map/ppermute | solution.py:719
  124.6 23.6 %collective-permute-start.37 = (bf16[512,512]{1,0:T(8,128)(2,1)S(1)}, bf16[512,512]{1,0:T(8,128)(2,1)S(1)}, u32[]{:S(2)}, u32[]{:S(2)}) collective-permute-start(bf16[512,512]{1,0:T(8,128)(2,1)S(1)} %get-tuple-element.214.refs_0_), channel_id=1, source_target_pairs={{0,2},{1,3},{2,0},{3,1},{4,6},{5,7},{6,4},{7,5},{8,10},{9,11},{10,... | collective-permute-start | bytes 1572872 | tf_op jit(solution)/shard_map/ppermute | solution.py:719
  138.4 46.9 %all-to-all-start = ((bf16[8,2,2,64,512]{4,3,2,1,0:T(8,128)(2,1)}), bf16[8,2,2,64,512]{4,3,2,1,0:T(8,128)(2,1)}, u32[]{:S(2)}, u32[]{:S(2)}) async-start(bf16[8,2,2,64,512]{4,3,2,1,0:T(8,128)(2,1)} %shard_map.326), calls=%async_computation | async-start | bytes 4194304 | tf_op jit(solution)/shard_map/all_to_all | solution.py:710
  148.3 12.5 %collective-permute-start.38 = (bf16[208,512]{1,0:T(8,128)(2,1)S(1)}, bf16[208,512]{1,0:T(8,128)(2,1)S(1)}, u32[]{:S(2)}, u32[]{:S(2)}) collective-permute-start(bf16[208,512]{1,0:T(8,128)(2,1)S(1)} %get-tuple-element.254), channel_id=1, source_target_pairs={{0,1},{1,0},{2,3},{3,2},{4,5},{5,4},{6,7},{7,6},{8,9},{9,8},{10,11... | collective-permute-start | bytes 638984 | tf_op jit(solution)/shard_map/ppermute | solution.py:719
  151.6 15.1 %collective-permute-start.39 = (bf16[208,512]{1,0:T(8,128)(2,1)S(1)}, bf16[208,512]{1,0:T(8,128)(2,1)S(1)}, u32[]{:S(2)}, u32[]{:S(2)}) collective-permute-start(bf16[208,512]{1,0:T(8,128)(2,1)S(1)} %get-tuple-element.255), channel_id=1, source_target_pairs={{0,2},{1,3},{2,0},{3,1},{4,6},{5,7},{6,4},{7,5},{8,10},{9,11},{10,... | collective-permute-start | bytes 638984 | tf_op jit(solution)/shard_map/ppermute | solution.py:719
  151.9 21.2 %collective-permute-start.40 = (bf16[208,512]{1,0:T(8,128)(2,1)S(1)}, bf16[208,512]{1,0:T(8,128)(2,1)S(1)}, u32[]{:S(2)}, u32[]{:S(2)}) collective-permute-start(bf16[208,512]{1,0:T(8,128)(2,1)S(1)} %pad_maximum_fusion.8), channel_id=1, source_target_pairs={{0,3},{1,2},{2,1},{3,0},{4,7},{5,6},{6,5},{7,4},{8,11},{9,10},{10,... | collective-permute-start | bytes 638984 | tf_op jit(solution)/shard_map/ppermute | solution.py:719
  153.3 30.2 %collective-permute-start.45 = (bf16[512,512]{1,0:T(8,128)(2,1)S(1)}, bf16[512,512]{1,0:T(8,128)(2,1)S(1)}, u32[]{:S(2)}, u32[]{:S(2)}) collective-permute-start(bf16[512,512]{1,0:T(8,128)(2,1)S(1)} %collective-permute-done.37.refs_2_), channel_id=1, source_target_pairs={{1,0},{2,3},{5,4},{6,7},{9,8},{10,11},{13,12},{14,15},{17,16},{18,... | collective-permute-start | bytes 1572872 | tf_op jit(solution)/shard_map/ppermute | solution.py:771
  158.0 25.4 %collective-permute-start.44 = (bf16[512,512]{1,0:T(8,128)(2,1)S(1)}, bf16[512,512]{1,0:T(8,128)(2,1)S(1)}, u32[]{:S(2)}, u32[]{:S(2)}) collective-permute-start(bf16[512,512]{1,0:T(8,128)(2,1)S(1)} %get-tuple-element.214.refs_0_), channel_id=1, source_target_pairs={{1,2},{2,1},{5,6},{6,5},{9,10},{10,9},{13,14},{14,13},{17,18},{18,... | collective-permute-start | bytes 1572872 | tf_op jit(solution)/shard_map/ppermute | solution.py:770
  173.2 8.3 %collective-permute-start.43 = (bf16[3,64,512]{2,1,0:T(8,128)(2,1)S(1)}, bf16[3,64,512]{2,1,0:T(8,128)(2,1)S(1)}, u32[]{:S(2)}, u32[]{:S(2)}) collective-permute-start(bf16[3,64,512]{2,1,0:T(8,128)(2,1)S(1)} %bitcast.85), channel_id=1, source_target_pairs={{0,24},{4,28},{8,16},{12,20},{16,8},{20,12},{24,0},{28,4},{1,25},{... | collective-permute-start | bytes 589832 | tf_op jit(solution)/shard_map/ppermute | solution.py:719
  174.8 8.5 %collective-permute-start.42 = (bf16[3,64,512]{2,1,0:T(8,128)(2,1)S(1)}, bf16[3,64,512]{2,1,0:T(8,128)(2,1)S(1)}, u32[]{:S(2)}, u32[]{:S(2)}) collective-permute-start(bf16[3,64,512]{2,1,0:T(8,128)(2,1)S(1)} %bitcast.86), channel_id=1, source_target_pairs={{0,16},{4,20},{8,24},{12,28},{16,0},{20,4},{24,8},{28,12},{1,17},{... | collective-permute-start | bytes 589832 | tf_op jit(solution)/shard_map/ppermute | solution.py:719
  175.5 7.8 %collective-permute-start.41 = (bf16[3,64,512]{2,1,0:T(8,128)(2,1)S(1)}, bf16[3,64,512]{2,1,0:T(8,128)(2,1)S(1)}, u32[]{:S(2)}, u32[]{:S(2)}) collective-permute-start(bf16[3,64,512]{2,1,0:T(8,128)(2,1)S(1)} %bitcast.87), channel_id=1, source_target_pairs={{0,8},{4,12},{8,0},{12,4},{16,24},{20,28},{24,16},{28,20},{1,9},{5... | collective-permute-start | bytes 589832 | tf_op jit(solution)/shard_map/ppermute | solution.py:719
  185.3 4.9 %collective-permute-start.46 = (bf16[4,3,64,512]{3,2,1,0:T(8,128)(2,1)S(1)}, bf16[4,3,64,512]{3,2,1,0:T(8,128)(2,1)S(1)}, u32[]{:S(2)}, u32[]{:S(2)}) collective-permute-start(bf16[4,3,64,512]{3,2,1,0:T(8,128)(2,1)S(1)} %pad_maximum_fusion.1.near_ref), channel_id=1, source_target_pairs={{0,4},{4,0},{8,12},{12,8},{16,20},{20,16},{24,28},{28,24},{1,5},{5... | collective-permute-start | bytes 2359304 | tf_op jit(solution)/shard_map/ppermute | solution.py:719
  (20 other events, 325.9 us)

commit v8 on v7

--- a/solution.py
+++ b/solution.py
@@ -945,10 +945,24 @@
     chunks = line_second(chunks)
     attn_far, ffn_parts = lax.optimization_barrier((attn_far, ffn_parts))
     attn_far = swap(attn_far, "dp", 1)
-    attn_parts = plane_parts(core_sums(attn_near, attn_far))
-    attn_parts, chunks, row_pieces[1] = lax.optimization_barrier(
-        (attn_parts, chunks, row_pieces[1])
-    )
+    cut = (nt * chunk + 16) // 2 // 16 * 16
+
+    def chip_sum(o, rows_of):
+        return (attn_near[o, rows_of].astype(F32) + attn_far[o, rows_of].astype(F32)).astype(BF16)
+
+    fore, rest = slice(0, cut), slice(cut, None)
+    fore_kept = [chip_sum(o, fore) for o in range(0, outer, 2)]
+    fore_got = swap(jnp.stack([chip_sum(o, fore) for o in range(1, outer, 2)]), "dp", 2)
+    rest_kept = [chip_sum(o, rest) for o in range(2)]
+    rest_got = [
+        swap(jnp.stack([chip_sum(2 * o, rest), chip_sum(2 * o + 1, rest)]), "dp", 4 * o)
+        for o in range(1, outer // 2)
+    ]
+    fore_parts = [total_of([kept, fore_got[o]]) for o, kept in enumerate(fore_kept)]
+    rest_parts = [total_of([rest_kept[o]] + [each[o] for each in rest_got]) for o in range(2)]
+    fore_parts = [fore_parts[0]] + [swap(fore_parts[o], "dp", 4 * o) for o in range(1, outer // 2)]
+    rest_parts = [rest_parts[0], swap(rest_parts[1], "dp", 2)]
+    fore_parts, rest_parts, chunks = lax.optimization_barrier((fore_parts, rest_parts, chunks))
     (dealt,) = call(
         deal_kernel,
         [((dp, seq_dev, nt // seq_dev, piece, width), BF16)],
@@ -957,7 +971,7 @@
         scratch=[pltpu.VMEM((nt, dp, piece, width), BF16)],
     )
     dealt = exchange(dealt, "dp")
-    attn_parts = total_of(attn_parts)
+    attn_parts = jnp.concatenate([total_of(fore_parts), total_of(rest_parts)])
     attn_parts, row_pieces[2] = lax.optimization_barrier((attn_parts, row_pieces[2]))
     ffn_parts = total_of(ffn_parts)
     grads = [
@@ -969,6 +983,12 @@
     ]
     grads = total_of([grads[0]] + [swap(grads[z], "tensor", z) for z in range(1, nt)])
     vectors = grads[3 * chunk :].astype(F32)
+    base = 4 + nt
+    g_b_up = lax.dynamic_index_in_dim(vectors[4:base], t, 0, keepdims=False)
+    g_b_q = lax.dynamic_index_in_dim(vectors[base + 2].reshape(nt, TILE), t, 0, keepdims=False)
+    g_b_v = lax.dynamic_index_in_dim(vectors[base + 3].reshape(nt, TILE), t, 0, keepdims=False)
+    vectors = [vectors[i] for i in (0, 1, 2, 3, base, base + 1)]
+    grads, row_pieces[1] = lax.optimization_barrier((grads, row_pieces[1]))
     row_pieces = line_second(row_pieces)
     near = jnp.stack(plane_pieces(grads[: 3 * chunk].reshape(3, chunk, width)))
     (grad_tokens,) = call(
@@ -980,7 +1000,9 @@
         off_chip=True,
     )
     grad_tokens = grad_tokens.reshape(seq_dev, length, width)
-    near, grad_tokens, dealt = lax.optimization_barrier((near, grad_tokens, dealt))
+    near, grad_tokens, dealt, vectors, g_b_up, g_b_q, g_b_v = lax.optimization_barrier(
+        (near, grad_tokens, dealt, vectors, g_b_up, g_b_q, g_b_v)
+    )
     grads = near, swap(near, "dp", 1)
     g_up, g_down, g_query, g_key, g_value, g_out = call(
         place_grads_kernel,
@@ -998,15 +1020,11 @@
         [pltpu.with_memory_space_constraint(dealt, pltpu.HBM)],
     )
     output = output.reshape(seq_dev, length, width)
-    base = 4 + nt
-    g_b_up = lax.dynamic_index_in_dim(vectors[4:base], t, 0, keepdims=False)
-    g_b_q = lax.dynamic_index_in_dim(vectors[base + 2].reshape(nt, TILE), t, 0, keepdims=False)
-    g_b_v = lax.dynamic_index_in_dim(vectors[base + 3].reshape(nt, TILE), t, 0, keepdims=False)
     return (
         output,
         grad_tokens,
-        vectors[base],
-        vectors[base + 1],
+        vectors[4],
+        vectors[5],
         g_query,
         g_b_q,
         g_key,

time: 194 us -> 191 us (0.985)
    ppermute x3, waiting for transfers between devices: 10.8 us -> 3.33 us  [line_second(): three = lax.ppermute(after(piece, two), 'tensor', [(1, 2), (2, 1)])]
    ppermute x41 -> x42, waiting for transfers between devices: 53.3 us -> 59.7 us  [swap(): return lax.ppermute(piece, axis, [(i, i ^ distance) for i in range(size)])]
    ppermute x41 -> x42, starting transfers between devices: 45.1 us -> 44.3 us  [swap(): return lax.ppermute(piece, axis, [(i, i ^ distance) for i in range(size)])]
  transfers between devices with their start and end apart: 48 -> 49, of which waited for: 24 -> 29; matrix products, arithmetic and copies ran while one was open for 3% -> 3% of each run, Pallas kernels for 20% -> 20%
where the time goes in v8:
time: 191 us; the launch traced here: 190 us
  starting transfers between devices  67.7 us (35%)
  waiting for transfers between devices  63.9 us (33%)
  Pallas kernels  51.1 us (27%)
  local copies, waits for them, and re-layouts  4.43 us (2%)
  other arithmetic  2.08 us (1%)
    ppermute x42, waiting for transfers between devices, swap(): return lax.ppermute(piece, axis, [(i, i ^ distance) for i in range(size)])  59.7 us
    pallas_call x14, Pallas kernels, call(): pl.pallas_call(kernel, out_shape=[jax.ShapeDtypeStruct(shape, dtype) for...  48.5 us
    ppermute x42, starting transfers between devices, swap(): return lax.ppermute(piece, axis, [(i, i ^ distance) for i in range(size)])  44.3 us
    ppermute x3, starting transfers between devices, line_second(): passed = lax.ppermute(two, 'tensor', [(1, 0), (2, 3)])  11.6 us
    ppermute x3, starting transfers between devices, line_second(): three = lax.ppermute(after(piece, two), 'tensor', [(1, 2), (2, 1)])  7.26 us
    all_to_all x1, starting transfers between devices, exchange(): lax.all_to_all(pieces, axis, 0, 0, tiled=True, axis_index_groups=groups)  4.47 us
  transfers between devices with their start and end apart: 49, of which 29 were waited for; matrix products, arithmetic and copies ran while one was open for 3% of the time, Pallas kernels for 20%

profile of v8, /device:TPU:8, one launch (start us, length us, event | category | flops | bytes accessed | tf_op | source)
XLA Modules:
  0.0 190.4 jit_solution(10394108733477277059)
XLA Ops:
  1.3 2.5 %shard_map.315 = (bf16[80,512]{1,0:T(8,128)(2,1)}, bf16[2,64,512]{2,1,0:T(8,128)(2,1)}) custom-call(s32[6]{0:T(128)} %stack.82.info, bf16[512,128]{1,0:T(8,128)(2,1)} %q_ref.1, bf16[512,128]{1,0:T(8,128)(2,1)} %k_ref.1, bf16[512,128]{1,0:T(8,128)(2,1)} %v_ref.1, bf16[128,512]{1,0:T(8,128)(2,1)} %o_ref.1, bf16[512,512]{1,0:T(8,128)(2,1)} %up_ref.1, ...), custom_call_target="tpu_custom_call" | custom-call | tf_op jit(solution)/shard_map/pallas_call | solution.py:783
  3.9 1.6 collective-permute-start.2
  6.6 1.4 collective-permute-start
  8.0 2.9 %collective-permute-start.7 = (bf16[2,64,512]{2,1,0:T(8,128)(2,1)}, bf16[2,64,512]{2,1,0:T(8,128)(2,1)S(1)}, u32[]{:S(2)}, u32[]{:S(2)}) collective-permute-start(bf16[2,64,512]{2,1,0:T(8,128)(2,1)} %get-tuple-element.142.refs_0_), channel_id=1, source_target_pairs={{0,2},{1,3},{2,0},{3,1},{4,6},{5,7},{6,4},{7,5},{8,10},{9,11},{10,... | collective-permute-start | bytes 393224 | tf_op jit(solution)/shard_map/ppermute | solution.py:719
  14.1 2.0 %collective-permute-done.1.refs_2_ = bf16[80,512]{1,0:T(8,128)(2,1)S(1)} collective-permute-done((bf16[80,512]{1,0:T(8,128)(2,1)}, bf16[80,512]{1,0:T(8,128)(2,1)S(1)}, u32[]{:S(2)}, u32[]{:S(2)}) %collective-permute-start.1) | collective-permute-done | bytes 81952 | tf_op jit(solution)/shard_map/ppermute | solution.py:719
  16.1 2.5 %collective-permute-start.5 = (bf16[4,64,512]{2,1,0:T(8,128)(2,1)S(1)}, bf16[4,64,512]{2,1,0:T(8,128)(2,1)S(1)}, u32[]{:S(2)}, u32[]{:S(2)}) collective-permute-start(bf16[4,64,512]{2,1,0:T(8,128)(2,1)S(1)} %get-tuple-element.148), channel_id=1, source_target_pairs={{0,24},{4,28},{8,16},{12,20},{16,8},{20,12},{24,0},{28,4},{1,25},{... | collective-permute-start | bytes 786440 | tf_op jit(solution)/shard_map/ppermute | solution.py:719
  19.7 2.1 %collective-permute-start.8 = (bf16[2,64,512]{2,1,0:T(8,128)(2,1)S(1)}, bf16[2,64,512]{2,1,0:T(8,128)(2,1)S(1)}, u32[]{:S(2)}, u32[]{:S(2)}) collective-permute-start(bf16[2,64,512]{2,1,0:T(8,128)(2,1)S(1)} %copy-done.2), channel_id=1, source_target_pairs={{1,2},{2,1},{5,6},{6,5},{9,10},{10,9},{13,14},{14,13},{17,18},{18,... | collective-permute-start | bytes 393224 | tf_op jit(solution)/shard_map/ppermute | solution.py:770
  21.8 3.1 %collective-permute-start.9 = (bf16[2,64,512]{2,1,0:T(8,128)(2,1)S(1)}, bf16[2,64,512]{2,1,0:T(8,128)(2,1)S(1)}, u32[]{:S(2)}, u32[]{:S(2)}) collective-permute-start(bf16[2,64,512]{2,1,0:T(8,128)(2,1)S(1)} %collective-permute-done.7.refs_2_), channel_id=1, source_target_pairs={{1,0},{2,3},{5,4},{6,7},{9,8},{10,11},{13,12},{14,15},{17,16},{18,... | collective-permute-start | bytes 393224 | tf_op jit(solution)/shard_map/ppermute | solution.py:771
  24.9 1.7 collective-permute-done.8.refs_3_
  30.9 6.0 %collective-permute-done.12 = bf16[4,64,512]{2,1,0:T(8,128)(2,1)S(1)} collective-permute-done((bf16[4,64,512]{2,1,0:T(8,128)(2,1)S(1)}, bf16[4,64,512]{2,1,0:T(8,128)(2,1)S(1)}, u32[]{:S(2)}, u32[]{:S(2)}) %collective-permute-start.12) | collective-permute-done | bytes 262176 | tf_op jit(solution)/shard_map/ppermute | solution.py:719
  37.0 1.5 collective-permute-start.13
  39.8 7.8 %shard_map.318 = (bf16[4,512,128]{2,1,0:T(8,128)(2,1)S(1)}, f32[4,512,128]{2,1,0:T(8,128)S(1)}, f32[4,512,128]{2,1,0:T(8,128)S(1)}, bf16[4,1024,128]{2,1,0:T(8,1...) custom-call(s32[6]{0:T(128)S(1)} %copy-done.4, ...), custom_call_target="tpu_custom_call" | custom-call | flops 10000000000 | bytes 1 | tf_op jit(solution)/shard_map/pallas_call | solution.py:696
  47.6 2.9 %collective-permute-done.13.refs_3_ = bf16[2,4,64,512]{3,2,1,0:T(8,128)(2,1)S(1)} collective-permute-done((bf16[2,4,64,512]{3,2,1,0:T(8,128)(2,1)S(1)}, bf16[2,4,64,512]{3,2,1,0:T(8,128)(2,1)S(1)}, u32[]{:S(2)}, u32[]{:S(2)}) %collective-permute-start.13) | collective-permute-done | bytes 524320 | tf_op jit(solution)/shard_map/ppermute | solution.py:719
  56.0 5.1 %shard_map.319 = (f32[512,512]{1,0:T(8,128)S(1)}, bf16[512,512]{1,0:T(8,128)(2,1)S(1)}, bf16[4,512,512]{2,1,0:T(8,128)(2,1)S(1)}, bf16[4,512,512]{2,1,0:T(8,128)...) custom-call(s32[6]{0:T(128)S(1)} %copy-done.4, ...), custom_call_target="tpu_custom_call" | custom-call | flops 1 | bytes 1 | tf_op jit(solution)/shard_map/pallas_call | solution.py:696
  61.3 1.4 collective-permute-done.19.far_ref
  64.7 1.6 collective-permute-start.22
  66.3 4.6 %shard_map.321 = (bf16[4,512,512]{2,1,0:T(8,128)(2,1)S(1)}, f32[512,512]{1,0:T(8,128)S(1)}, bf16[512,512]{1,0:T(8,128)(2,1)S(1)}, f32[4,512,128]{2,1,0:T(8,128)S...) custom-call(bf16[512,512]{1,0:T(8,128)(2,1)S(1)} %dynamic-slice_bitc, ...), custom_call_target="tpu_custom_call" | custom-call | flops 1 | bytes 1 | tf_op jit(solution)/shard_map/pallas_call | solution.py:696
  71.9 3.0 %shard_map.322 = (bf16[4,4,2,64,512]{4,3,2,1,0:T(8,128)(2,1)S(1)}, bf16[4,4,2,64,512]{4,3,2,1,0:T(8,128)(2,1)S(1)}) custom-call(s32[6]{0:T(128)S(1)} %copy-done.4, bf16[512,512]{1,0:T(8,128)(2,1)S(1)} %get-tuple-element.174.normed_ref, bf16[4,512,512]{2,1,0:T(8,128)(2,1)S(1)} %get-tuple-element.175.act_ref, ...), custom_call_target="tpu_custom_call" | custom-call | flops 1 | bytes 1 | tf_op jit(solution)/shard_map/pallas_call | solution.py:696
  75.0 2.6 %collective-permute-start.24 = (f32[4,32,128]{2,1,0:T(8,128)S(1)}, f32[4,32,128]{2,1,0:T(8,128)S(1)}, u32[]{:S(2)}, u32[]{:S(2)}) collective-permute-start(f32[4,32,128]{2,1,0:T(8,128)S(1)} %get-tuple-element.184), channel_id=1, source_target_pairs={{0,1},{1,0},{2,3},{3,2},{4,5},{5,4},{6,7},{7,6},{8,9},{9,8},{10,11... | collective-permute-start | bytes 196616 | tf_op jit(solution)/shard_map/ppermute | solution.py:719
  77.6 1.5 collective-permute-start.26
  79.1 1.9 %collective-permute-start.25 = (bf16[8,64,512]{2,1,0:T(8,128)(2,1)S(1)}, bf16[8,64,512]{2,1,0:T(8,128)(2,1)S(1)}, u32[]{:S(2)}, u32[]{:S(2)}) collective-permute-start(bf16[8,64,512]{2,1,0:T(8,128)(2,1)S(1)} %pad_maximum_fusion.4.refs_0_), channel_id=1, source_target_pairs={{0,1},{1,0},{2,3},{3,2},{4,5},{5,4},{6,7},{7,6},{8,9},{9,8},{10,11... | collective-permute-start | bytes 1572872 | tf_op jit(solution)/shard_map/ppermute | solution.py:719
  82.7 1.5 collective-permute-start.28
  85.3 14.0 %shard_map.323 = (bf16[4,512,384]{2,1,0:T(8,128)(2,1)S(1)}, f32[4,2,128]{2,1,0:T(2,128)S(1)}, bf16[512,512]{1,0:T(8,128)(2,1)S(1)}, f32[2,512]{1,0:T(2,128)S(1)}) custom-call(s32[6]{0:T(128)S(1)} %copy-done.4, s32[16]{0:T(128)S(1)} %copy-done.11, f32[4,512,128]{2,1,0:T(8,128)S(1)} %get-tuple-element.172.numer_ref, ...), custom_call_target="tpu_custom_call" | custom-call | flops 10000000000 | bytes 1 | tf_op jit(solution)/shard_map/pallas_call | solution.py:696
  99.3 2.8 %collective-permute-done.26.refs_2_ = bf16[8,64,512]{2,1,0:T(8,128)(2,1)S(1)} collective-permute-done((bf16[8,64,512]{2,1,0:T(8,128)(2,1)S(1)}, bf16[8,64,512]{2,1,0:T(8,128)(2,1)S(1)}, u32[]{:S(2)}, u32[]{:S(2)}) %collective-permute-start.26) | collective-permute-done | bytes 524320 | tf_op jit(solution)/shard_map/ppermute | solution.py:719
  102.1 2.2 %collective-permute-done.25.refs_1_ = bf16[8,64,512]{2,1,0:T(8,128)(2,1)S(1)} collective-permute-done((bf16[8,64,512]{2,1,0:T(8,128)(2,1)S(1)}, bf16[8,64,512]{2,1,0:T(8,128)(2,1)S(1)}, u32[]{:S(2)}, u32[]{:S(2)}) %collective-permute-start.25) | collective-permute-done | bytes 524320 | tf_op jit(solution)/shard_map/ppermute | solution.py:719
  104.3 2.5 %shard_map.324 = (bf16[4,272,512]{2,1,0:T(8,128)(2,1)S(1)}, bf16[4,272,512]{2,1,0:T(8,128)(2,1)S(1)}) custom-call(s32[6]{0:T(128)S(1)} %copy-done.4, bf16[512,512]{1,0:T(8,128)(2,1)S(1)} %get-tuple-element.135.normed_ref, bf16[4,512,384]{2,1,0:T(8,128)(2,1)S(1)} %get-tuple-element.192.grads_ref, bf16[512,512]{1,0:T(8,128)(2,1)S(1)} %get-tuple-element.196.grad_hidden_ref, ...), custom_call_target="tpu_custom_call" | custom-call | flops 1 | bytes 1 | tf_op jit(solution)/shard_map/pallas_call | solution.py:696
  107.0 3.7 %collective-permute-start.36 = (bf16[8,64,512]{2,1,0:T(8,128)(2,1)S(1)}, bf16[8,64,512]{2,1,0:T(8,128)(2,1)S(1)}, u32[]{:S(2)}, u32[]{:S(2)}) collective-permute-start(bf16[8,64,512]{2,1,0:T(8,128)(2,1)S(1)} %collective-permute-done.26.refs_2_), channel_id=1, source_target_pairs={{1,0},{2,3},{5,4},{6,7},{9,8},{10,11},{13,12},{14,15},{17,16},{18,... | collective-permute-start | bytes 1572872 | tf_op jit(solution)/shard_map/ppermute | solution.py:771
  110.8 3.2 %collective-permute-start.35 = (bf16[8,64,512]{2,1,0:T(8,128)(2,1)S(1)}, bf16[8,64,512]{2,1,0:T(8,128)(2,1)S(1)}, u32[]{:S(2)}, u32[]{:S(2)}) collective-permute-start(bf16[8,64,512]{2,1,0:T(8,128)(2,1)S(1)} %pad_maximum_fusion.4.refs_0_), channel_id=1, source_target_pairs={{1,2},{2,1},{5,6},{6,5},{9,10},{10,9},{13,14},{14,13},{17,18},{18,... | collective-permute-start | bytes 1572872 | tf_op jit(solution)/shard_map/ppermute | solution.py:770
  116.9 5.6 %collective-permute-done.31 = bf16[2,128,512]{2,1,0:T(8,128)(2,1)S(1)} collective-permute-done((bf16[2,128,512]{2,1,0:T(8,128)(2,1)S(1)}, bf16[2,128,512]{2,1,0:T(8,128)(2,1)S(1)}, u32[]{:S(2)}, u32[]{:S(2)}) %collective-permute-start.31) | collective-permute-done | bytes 262176 | tf_op jit(solution)/shard_map/ppermute | solution.py:719
  122.6 1.6 collective-permute-start.32
  125.3 1.4 collective-permute-done.35.refs_3_
  127.6 2.0 %collective-permute-done.34 = bf16[144,512]{1,0:T(8,128)(2,1)S(1)} collective-permute-done((bf16[144,512]{1,0:T(8,128)(2,1)S(1)}, bf16[144,512]{1,0:T(8,128)(2,1)S(1)}, u32[]{:S(2)}, u32[]{:S(2)}) %collective-permute-start.34) | collective-permute-done | bytes 147488 | tf_op jit(solution)/shard_map/ppermute | solution.py:719
  130.3 2.1 %shard_map.326 = bf16[8,2,2,64,512]{4,3,2,1,0:T(8,128)(2,1)} custom-call(s32[6]{0:T(128)S(1)} %copy-done.4, s32[16]{0:T(128)S(1)} %copy-done.12, bf16[8,64,512]{2,1,0:T(8,128)(2,1)S(1)} %pad_maximum_fusion.4.refs_0_, bf16[8,64,512]{2,1,0:T(8,128)(2,1)S(1)} %collective-permute-done.25.refs_1_, bf16[8,64,512]{2,1,0:T(8,128)(2,1)S(1)} %collective-permute-done.26.refs_2_, ...), custom_call_target="tpu_custom_call" | custom-call | flops 1 | bytes 1 | tf_op jit(solution)/shard_map/pallas_call | solution.py:696
  132.4 4.5 %all-to-all-start = ((bf16[8,2,2,64,512]{4,3,2,1,0:T(8,128)(2,1)}), bf16[8,2,2,64,512]{4,3,2,1,0:T(8,128)(2,1)}, u32[]{:S(2)}, u32[]{:S(2)}) async-start(bf16[8,2,2,64,512]{4,3,2,1,0:T(8,128)(2,1)} %shard_map.326), calls=%async_computation | async-start | bytes 4194304 | tf_op jit(solution)/shard_map/all_to_all | solution.py:710
  137.1 12.0 %collective-permute-done.37.refs_2_ = bf16[512,512]{1,0:T(8,128)(2,1)S(1)} collective-permute-done((bf16[512,512]{1,0:T(8,128)(2,1)S(1)}, bf16[512,512]{1,0:T(8,128)(2,1)S(1)}, u32[]{:S(2)}, u32[]{:S(2)}) %collective-permute-start.37) | collective-permute-done | bytes 524320 | tf_op jit(solution)/shard_map/ppermute | solution.py:719
  149.1 3.3 %collective-permute-start.38 = (bf16[208,512]{1,0:T(8,128)(2,1)S(1)}, bf16[208,512]{1,0:T(8,128)(2,1)S(1)}, u32[]{:S(2)}, u32[]{:S(2)}) collective-permute-start(bf16[208,512]{1,0:T(8,128)(2,1)S(1)} %get-tuple-element.278), channel_id=1, source_target_pairs={{0,1},{1,0},{2,3},{3,2},{4,5},{5,4},{6,7},{7,6},{8,9},{9,8},{10,11... | collective-permute-start | bytes 638984 | tf_op jit(solution)/shard_map/ppermute | solution.py:719
  152.7 1.4 collective-permute-start.40
  154.1 4.8 %collective-permute-start.46 = (bf16[512,512]{1,0:T(8,128)(2,1)S(1)}, bf16[512,512]{1,0:T(8,128)(2,1)S(1)}, u32[]{:S(2)}, u32[]{:S(2)}) collective-permute-start(bf16[512,512]{1,0:T(8,128)(2,1)S(1)} %collective-permute-done.37.refs_2_), channel_id=1, source_target_pairs={{1,0},{2,3},{5,4},{6,7},{9,8},{10,11},{13,12},{14,15},{17,16},{18,... | collective-permute-start | bytes 1572872 | tf_op jit(solution)/shard_map/ppermute | solution.py:771
  158.9 2.7 %collective-permute-done.38 = bf16[208,512]{1,0:T(8,128)(2,1)S(1)} collective-permute-done((bf16[208,512]{1,0:T(8,128)(2,1)S(1)}, bf16[208,512]{1,0:T(8,128)(2,1)S(1)}, u32[]{:S(2)}, u32[]{:S(2)}) %collective-permute-start.38) | collective-permute-done | bytes 213024 | tf_op jit(solution)/shard_map/ppermute | solution.py:719
  161.6 1.9 %collective-permute-start.45 = (bf16[512,512]{1,0:T(8,128)(2,1)S(1)}, bf16[512,512]{1,0:T(8,128)(2,1)S(1)}, u32[]{:S(2)}, u32[]{:S(2)}) collective-permute-start(bf16[512,512]{1,0:T(8,128)(2,1)S(1)} %get-tuple-element.225.refs_0_), channel_id=1, source_target_pairs={{1,2},{2,1},{5,6},{6,5},{9,10},{10,9},{13,14},{14,13},{17,18},{18,... | collective-permute-start | bytes 1572872 | tf_op jit(solution)/shard_map/ppermute | solution.py:770
  163.5 3.9 %collective-permute-done.39 = bf16[208,512]{1,0:T(8,128)(2,1)S(1)} collective-permute-done((bf16[208,512]{1,0:T(8,128)(2,1)S(1)}, bf16[208,512]{1,0:T(8,128)(2,1)S(1)}, u32[]{:S(2)}, u32[]{:S(2)}) %collective-permute-start.39) | collective-permute-done | bytes 213024 | tf_op jit(solution)/shard_map/ppermute | solution.py:719
  167.4 5.9 %collective-permute-done.40 = bf16[208,512]{1,0:T(8,128)(2,1)S(1)} collective-permute-done((bf16[208,512]{1,0:T(8,128)(2,1)S(1)}, bf16[208,512]{1,0:T(8,128)(2,1)S(1)}, u32[]{:S(2)}, u32[]{:S(2)}) %collective-permute-start.40) | collective-permute-done | bytes 213024 | tf_op jit(solution)/shard_map/ppermute | solution.py:719
  173.4 1.6 collective-permute-start.44
  178.7 1.5 collective-permute-done.44
  180.2 2.0 %collective-permute-done.43 = bf16[3,64,512]{2,1,0:T(8,128)(2,1)S(1)} collective-permute-done((bf16[3,64,512]{2,1,0:T(8,128)(2,1)S(1)}, bf16[3,64,512]{2,1,0:T(8,128)(2,1)S(1)}, u32[]{:S(2)}, u32[]{:S(2)}) %collective-permute-start.43) | collective-permute-done | bytes 196640 | tf_op jit(solution)/shard_map/ppermute | solution.py:719
  182.8 1.9 shard_map.325
  184.8 3.2 %shard_map.327 = bf16[2,2,8,64,512]{4,3,2,1,0:T(8,128)(2,1)} custom-call(bf16[8,2,2,64,512]{4,3,2,1,0:T(8,128)(2,1)} %all-to-all-done.pieces_ref), custom_call_target="tpu_custom_call" | custom-call | flops 1 | bytes 1 | tf_op jit(solution)/shard_map/pallas_call | solution.py:696
  188.0 2.4 %shard_map.328 = (f32[512,512]{1,0:T(8,128)}, f32[512,512]{1,0:T(8,128)}, f32[512,128]{1,0:T(8,128)}, f32[512,128]{1,0:T(8,128)}, f32[512,128]{1,0:T(8,128)}, /*index=5*/f32[128,512]{1,0:T(8,128)}) custom-call(s32[6]{0:T(128)S(1)} %copy-done.4, bf16[4,3,64,512]{3,2,1,0:T(8,128)(2,1)S(1)} %pad_maximum_fusion.1.near_ref, ...), custom_call_target="tpu_custom_call" | custom-call | flops 1 | bytes 1 | tf_op jit(solution)/shard_map/pallas_call | solution.py:696
  (131 shorter events, 33.9 us)
Async XLA Ops:
  3.9 10.2 %collective-permute-start.2 = (bf16[80,512]{1,0:T(8,128)(2,1)}, bf16[80,512]{1,0:T(8,128)(2,1)S(1)}, u32[]{:S(2)}, u32[]{:S(2)}) collective-permute-start(bf16[80,512]{1,0:T(8,128)(2,1)} %get-tuple-element.136.refs_0_), channel_id=1, source_target_pairs={{0,3},{1,2},{2,1},{3,0},{4,7},{5,6},{6,5},{7,4},{8,11},{9,10},{10,... | collective-permute-start | bytes 245768 | tf_op jit(solution)/shard_map/ppermute | solution.py:719
  5.5 10.6 %collective-permute-start.1 = (bf16[80,512]{1,0:T(8,128)(2,1)}, bf16[80,512]{1,0:T(8,128)(2,1)S(1)}, u32[]{:S(2)}, u32[]{:S(2)}) collective-permute-start(bf16[80,512]{1,0:T(8,128)(2,1)} %get-tuple-element.136.refs_0_), channel_id=1, source_target_pairs={{0,2},{1,3},{2,0},{3,1},{4,6},{5,7},{6,4},{7,5},{8,10},{9,11},{10,... | collective-permute-start | bytes 245768 | tf_op jit(solution)/shard_map/ppermute | solution.py:719
  6.6 9.5 %collective-permute-start = (bf16[80,512]{1,0:T(8,128)(2,1)}, bf16[80,512]{1,0:T(8,128)(2,1)S(1)}, u32[]{:S(2)}, u32[]{:S(2)}) collective-permute-start(bf16[80,512]{1,0:T(8,128)(2,1)} %get-tuple-element.136.refs_0_), channel_id=1, source_target_pairs={{0,1},{1,0},{2,3},{3,2},{4,5},{5,4},{6,7},{7,6},{8,9},{9,8},{10,11... | collective-permute-start | bytes 245768 | tf_op jit(solution)/shard_map/ppermute | solution.py:719
  8.0 11.7 %collective-permute-start.7 = (bf16[2,64,512]{2,1,0:T(8,128)(2,1)}, bf16[2,64,512]{2,1,0:T(8,128)(2,1)S(1)}, u32[]{:S(2)}, u32[]{:S(2)}) collective-permute-start(bf16[2,64,512]{2,1,0:T(8,128)(2,1)} %get-tuple-element.142.refs_0_), channel_id=1, source_target_pairs={{0,2},{1,3},{2,0},{3,1},{4,6},{5,7},{6,4},{7,5},{8,10},{9,11},{10,... | collective-permute-start | bytes 393224 | tf_op jit(solution)/shard_map/ppermute | solution.py:719
  10.9 10.9 %collective-permute-start.6 = (bf16[2,64,512]{2,1,0:T(8,128)(2,1)}, bf16[2,64,512]{2,1,0:T(8,128)(2,1)S(1)}, u32[]{:S(2)}, u32[]{:S(2)}) collective-permute-start(bf16[2,64,512]{2,1,0:T(8,128)(2,1)} %get-tuple-element.142.refs_0_), channel_id=1, source_target_pairs={{0,1},{1,0},{2,3},{3,2},{4,5},{5,4},{6,7},{7,6},{8,9},{9,8},{10,11... | collective-permute-start | bytes 393224 | tf_op jit(solution)/shard_map/ppermute | solution.py:719
  16.1 11.8 %collective-permute-start.5 = (bf16[4,64,512]{2,1,0:T(8,128)(2,1)S(1)}, bf16[4,64,512]{2,1,0:T(8,128)(2,1)S(1)}, u32[]{:S(2)}, u32[]{:S(2)}) collective-permute-start(bf16[4,64,512]{2,1,0:T(8,128)(2,1)S(1)} %get-tuple-element.148), channel_id=1, source_target_pairs={{0,24},{4,28},{8,16},{12,20},{16,8},{20,12},{24,0},{28,4},{1,25},{... | collective-permute-start | bytes 786440 | tf_op jit(solution)/shard_map/ppermute | solution.py:719
  18.6 9.4 %collective-permute-start.4 = (bf16[4,64,512]{2,1,0:T(8,128)(2,1)S(1)}, bf16[4,64,512]{2,1,0:T(8,128)(2,1)S(1)}, u32[]{:S(2)}, u32[]{:S(2)}) collective-permute-start(bf16[4,64,512]{2,1,0:T(8,128)(2,1)S(1)} %get-tuple-element.148), channel_id=1, source_target_pairs={{0,16},{4,20},{8,24},{12,28},{16,0},{20,4},{24,8},{28,12},{1,17},{... | collective-permute-start | bytes 786440 | tf_op jit(solution)/shard_map/ppermute | solution.py:719
  19.1 8.9 %collective-permute-start.3 = (bf16[4,64,512]{2,1,0:T(8,128)(2,1)S(1)}, bf16[4,64,512]{2,1,0:T(8,128)(2,1)S(1)}, u32[]{:S(2)}, u32[]{:S(2)}) collective-permute-start(bf16[4,64,512]{2,1,0:T(8,128)(2,1)S(1)} %get-tuple-element.148), channel_id=1, source_target_pairs={{0,8},{4,12},{8,0},{12,4},{16,24},{20,28},{24,16},{28,20},{1,9},{5... | collective-permute-start | bytes 786440 | tf_op jit(solution)/shard_map/ppermute | solution.py:719
  19.7 6.9 %collective-permute-start.8 = (bf16[2,64,512]{2,1,0:T(8,128)(2,1)S(1)}, bf16[2,64,512]{2,1,0:T(8,128)(2,1)S(1)}, u32[]{:S(2)}, u32[]{:S(2)}) collective-permute-start(bf16[2,64,512]{2,1,0:T(8,128)(2,1)S(1)} %copy-done.2), channel_id=1, source_target_pairs={{1,2},{2,1},{5,6},{6,5},{9,10},{10,9},{13,14},{14,13},{17,18},{18,... | collective-permute-start | bytes 393224 | tf_op jit(solution)/shard_map/ppermute | solution.py:770
  21.8 5.6 %collective-permute-start.9 = (bf16[2,64,512]{2,1,0:T(8,128)(2,1)S(1)}, bf16[2,64,512]{2,1,0:T(8,128)(2,1)S(1)}, u32[]{:S(2)}, u32[]{:S(2)}) collective-permute-start(bf16[2,64,512]{2,1,0:T(8,128)(2,1)S(1)} %collective-permute-done.7.refs_2_), channel_id=1, source_target_pairs={{1,0},{2,3},{5,4},{6,7},{9,8},{10,11},{13,12},{14,15},{17,16},{18,... | collective-permute-start | bytes 393224 | tf_op jit(solution)/shard_map/ppermute | solution.py:771
  28.1 11.7 %collective-permute-start.14 = (bf16[4,4,64,512]{3,2,1,0:T(8,128)(2,1)S(1)}, bf16[4,4,64,512]{3,2,1,0:T(8,128)(2,1)S(1)}, u32[]{:S(2)}, u32[]{:S(2)}) collective-permute-start(bf16[4,4,64,512]{3,2,1,0:T(8,128)(2,1)S(1)} %pad_maximum_fusion.near_ref), channel_id=1, source_target_pairs={{0,4},{4,0},{8,12},{12,8},{16,20},{20,16},{24,28},{28,24},{1,5},{5... | collective-permute-start | bytes 3145736 | tf_op jit(solution)/shard_map/ppermute | solution.py:719
  28.2 8.7 %collective-permute-start.12 = (bf16[4,64,512]{2,1,0:T(8,128)(2,1)S(1)}, bf16[4,64,512]{2,1,0:T(8,128)(2,1)S(1)}, u32[]{:S(2)}, u32[]{:S(2)}) collective-permute-start(bf16[4,64,512]{2,1,0:T(8,128)(2,1)S(1)} %get-tuple-element.146), channel_id=1, source_target_pairs={{0,16},{4,20},{8,24},{12,28},{16,0},{20,4},{24,8},{28,12},{1,17},{... | collective-permute-start | bytes 786440 | tf_op jit(solution)/shard_map/ppermute | solution.py:719
  29.6 8.9 %collective-permute-start.10 = (bf16[4,64,512]{2,1,0:T(8,128)(2,1)S(1)}, bf16[4,64,512]{2,1,0:T(8,128)(2,1)S(1)}, u32[]{:S(2)}, u32[]{:S(2)}) collective-permute-start(bf16[4,64,512]{2,1,0:T(8,128)(2,1)S(1)} %get-tuple-element.145), channel_id=1, source_target_pairs={{0,8},{4,12},{8,0},{12,4},{16,24},{20,28},{24,16},{28,20},{1,9},{5... | collective-permute-start | bytes 786440 | tf_op jit(solution)/shard_map/ppermute | solution.py:719
  37.0 13.6 %collective-permute-start.13 = (bf16[2,4,64,512]{3,2,1,0:T(8,128)(2,1)S(1)}, bf16[2,4,64,512]{3,2,1,0:T(8,128)(2,1)S(1)}, u32[]{:S(2)}, u32[]{:S(2)}) collective-permute-start(bf16[2,4,64,512]{3,2,1,0:T(8,128)(2,1)S(1)} %pad_maximum_fusion.3.refs_2_), channel_id=1, source_target_pairs={{0,8},{4,12},{8,0},{12,4},{16,24},{20,28},{24,16},{28,20},{1,9},{5... | collective-permute-start | bytes 1572872 | tf_op jit(solution)/shard_map/ppermute | solution.py:719
  38.5 13.3 %collective-permute-start.11 = (bf16[2,4,64,512]{3,2,1,0:T(8,128)(2,1)S(1)}, bf16[2,4,64,512]{3,2,1,0:T(8,128)(2,1)S(1)}, u32[]{:S(2)}, u32[]{:S(2)}) collective-permute-start(bf16[2,4,64,512]{3,2,1,0:T(8,128)(2,1)S(1)} %pad_maximum_fusion.2.refs_0_), channel_id=1, source_target_pairs={{0,16},{4,20},{8,24},{12,28},{16,0},{20,4},{24,8},{28,12},{1,17},{... | collective-permute-start | bytes 1572872 | tf_op jit(solution)/shard_map/ppermute | solution.py:719
  51.8 1.9 %collective-permute-start.15 = (bf16[2,4,64,512]{3,2,1,0:T(8,128)(2,1)S(1)}, bf16[2,4,64,512]{3,2,1,0:T(8,128)(2,1)S(1)}, u32[]{:S(2)}, u32[]{:S(2)}) collective-permute-start(bf16[2,4,64,512]{3,2,1,0:T(8,128)(2,1)S(1)} %pad_maximum_fusion.2.refs_0_), channel_id=1, source_target_pairs={{0,4},{4,0},{8,12},{12,8},{16,20},{20,16},{24,28},{28,24},{1,5},{5... | collective-permute-start | bytes 1572872 | tf_op jit(solution)/shard_map/ppermute | solution.py:719
  51.8 2.7 %collective-permute-start.16 = (bf16[2,4,64,512]{3,2,1,0:T(8,128)(2,1)S(1)}, bf16[2,4,64,512]{3,2,1,0:T(8,128)(2,1)S(1)}, u32[]{:S(2)}, u32[]{:S(2)}) collective-permute-start(bf16[2,4,64,512]{3,2,1,0:T(8,128)(2,1)S(1)} %collective-permute-done.11.refs_1_), channel_id=1, source_target_pairs={{0,4},{4,0},{8,12},{12,8},{16,20},{20,16},{24,28},{28,24},{1,5},{5... | collective-permute-start | bytes 1572872 | tf_op jit(solution)/shard_map/ppermute | solution.py:719
  52.3 2.9 %collective-permute-start.17 = (bf16[2,4,64,512]{3,2,1,0:T(8,128)(2,1)S(1)}, bf16[2,4,64,512]{3,2,1,0:T(8,128)(2,1)S(1)}, u32[]{:S(2)}, u32[]{:S(2)}) collective-permute-start(bf16[2,4,64,512]{3,2,1,0:T(8,128)(2,1)S(1)} %pad_maximum_fusion.3.refs_2_), channel_id=1, source_target_pairs={{0,4},{4,0},{8,12},{12,8},{16,20},{20,16},{24,28},{28,24},{1,5},{5... | collective-permute-start | bytes 1572872 | tf_op jit(solution)/shard_map/ppermute | solution.py:719
  52.3 3.6 %collective-permute-start.18 = (bf16[2,4,64,512]{3,2,1,0:T(8,128)(2,1)S(1)}, bf16[2,4,64,512]{3,2,1,0:T(8,128)(2,1)S(1)}, u32[]{:S(2)}, u32[]{:S(2)}) collective-permute-start(bf16[2,4,64,512]{3,2,1,0:T(8,128)(2,1)S(1)} %collective-permute-done.13.refs_3_), channel_id=1, source_target_pairs={{0,4},{4,0},{8,12},{12,8},{16,20},{20,16},{24,28},{28,24},{1,5},{5... | collective-permute-start | bytes 1572872 | tf_op jit(solution)/shard_map/ppermute | solution.py:719
  62.8 8.1 %collective-permute-start.20 = (bf16[2,64,512]{2,1,0:T(8,128)(2,1)S(1)}, bf16[2,64,512]{2,1,0:T(8,128)(2,1)S(1)}, u32[]{:S(2)}, u32[]{:S(2)}) collective-permute-start(bf16[2,64,512]{2,1,0:T(8,128)(2,1)S(1)} %get-tuple-element.177), channel_id=1, source_target_pairs={{0,8},{4,12},{8,0},{12,4},{16,24},{20,28},{24,16},{28,20},{1,9},{5... | collective-permute-start | bytes 393224 | tf_op jit(solution)/shard_map/ppermute | solution.py:719
  63.6 7.3 %collective-permute-start.21 = (bf16[2,64,512]{2,1,0:T(8,128)(2,1)S(1)}, bf16[2,64,512]{2,1,0:T(8,128)(2,1)S(1)}, u32[]{:S(2)}, u32[]{:S(2)}) collective-permute-start(bf16[2,64,512]{2,1,0:T(8,128)(2,1)S(1)} %get-tuple-element.178), channel_id=1, source_target_pairs={{0,16},{4,20},{8,24},{12,28},{16,0},{20,4},{24,8},{28,12},{1,17},{... | collective-permute-start | bytes 393224 | tf_op jit(solution)/shard_map/ppermute | solution.py:719
  64.7 7.1 %collective-permute-start.22 = (bf16[2,64,512]{2,1,0:T(8,128)(2,1)S(1)}, bf16[2,64,512]{2,1,0:T(8,128)(2,1)S(1)}, u32[]{:S(2)}, u32[]{:S(2)}) collective-permute-start(bf16[2,64,512]{2,1,0:T(8,128)(2,1)S(1)} %get-tuple-element.179), channel_id=1, source_target_pairs={{0,24},{4,28},{8,16},{12,20},{16,8},{20,12},{24,0},{28,4},{1,25},{... | collective-permute-start | bytes 393224 | tf_op jit(solution)/shard_map/ppermute | solution.py:719
  74.9 6.1 %collective-permute-start.23 = (bf16[4,4,2,64,512]{4,3,2,1,0:T(8,128)(2,1)S(1)}, bf16[4,4,2,64,512]{4,3,2,1,0:T(8,128)(2,1)S(1)}, u32[]{:S(2)}, u32[]{:S(2)}) collective-permute-start(bf16[4,4,2,64,512]{4,3,2,1,0:T(8,128)(2,1)S(1)} %get-tuple-element.183), channel_id=1, source_target_pairs={{0,4},{4,0},{8,12},{12,8},{16,20},{20,16},{24,28},{28,24},{1,5},{5... | collective-permute-start | bytes 6291464 | tf_op jit(solution)/shard_map/ppermute | solution.py:719
  75.0 6.8 %collective-permute-start.24 = (f32[4,32,128]{2,1,0:T(8,128)S(1)}, f32[4,32,128]{2,1,0:T(8,128)S(1)}, u32[]{:S(2)}, u32[]{:S(2)}) collective-permute-start(f32[4,32,128]{2,1,0:T(8,128)S(1)} %get-tuple-element.184), channel_id=1, source_target_pairs={{0,1},{1,0},{2,3},{3,2},{4,5},{5,4},{6,7},{7,6},{8,9},{9,8},{10,11... | collective-permute-start | bytes 196616 | tf_op jit(solution)/shard_map/ppermute | solution.py:719
  77.6 24.5 %collective-permute-start.26 = (bf16[8,64,512]{2,1,0:T(8,128)(2,1)S(1)}, bf16[8,64,512]{2,1,0:T(8,128)(2,1)S(1)}, u32[]{:S(2)}, u32[]{:S(2)}) collective-permute-start(bf16[8,64,512]{2,1,0:T(8,128)(2,1)S(1)} %pad_maximum_fusion.4.refs_0_), channel_id=1, source_target_pairs={{0,2},{1,3},{2,0},{3,1},{4,6},{5,7},{6,4},{7,5},{8,10},{9,11},{10,... | collective-permute-start | bytes 1572872 | tf_op jit(solution)/shard_map/ppermute | solution.py:719
  79.1 25.2 %collective-permute-start.25 = (bf16[8,64,512]{2,1,0:T(8,128)(2,1)S(1)}, bf16[8,64,512]{2,1,0:T(8,128)(2,1)S(1)}, u32[]{:S(2)}, u32[]{:S(2)}) collective-permute-start(bf16[8,64,512]{2,1,0:T(8,128)(2,1)S(1)} %pad_maximum_fusion.4.refs_0_), channel_id=1, source_target_pairs={{0,1},{1,0},{2,3},{3,2},{4,5},{5,4},{6,7},{7,6},{8,9},{9,8},{10,11... | collective-permute-start | bytes 1572872 | tf_op jit(solution)/shard_map/ppermute | solution.py:719
  81.8 25.1 %collective-permute-start.27 = (bf16[4,2,64,512]{3,2,1,0:T(8,128)(2,1)S(1)}, bf16[4,2,64,512]{3,2,1,0:T(8,128)(2,1)S(1)}, u32[]{:S(2)}, u32[]{:S(2)}) collective-permute-start(bf16[4,2,64,512]{3,2,1,0:T(8,128)(2,1)S(1)} %get-tuple-element.203), channel_id=1, source_target_pairs={{0,8},{4,12},{8,0},{12,4},{16,24},{20,28},{24,16},{28,20},{1,9},{5... | collective-permute-start | bytes 1572872 | tf_op jit(solution)/shard_map/ppermute | solution.py:719
  82.7 24.4 %collective-permute-start.28 = (bf16[4,2,64,512]{3,2,1,0:T(8,128)(2,1)S(1)}, bf16[4,2,64,512]{3,2,1,0:T(8,128)(2,1)S(1)}, u32[]{:S(2)}, u32[]{:S(2)}) collective-permute-start(bf16[4,2,64,512]{3,2,1,0:T(8,128)(2,1)S(1)} %get-tuple-element.204), channel_id=1, source_target_pairs={{0,16},{4,20},{8,24},{12,28},{16,0},{20,4},{24,8},{28,12},{1,17},{... | collective-permute-start | bytes 1572872 | tf_op jit(solution)/shard_map/ppermute | solution.py:719
  84.2 22.9 %collective-permute-start.29 = (bf16[4,2,64,512]{3,2,1,0:T(8,128)(2,1)S(1)}, bf16[4,2,64,512]{3,2,1,0:T(8,128)(2,1)S(1)}, u32[]{:S(2)}, u32[]{:S(2)}) collective-permute-start(bf16[4,2,64,512]{3,2,1,0:T(8,128)(2,1)S(1)} %get-tuple-element.205), channel_id=1, source_target_pairs={{0,24},{4,28},{8,16},{12,20},{16,8},{20,12},{24,0},{28,4},{1,25},{... | collective-permute-start | bytes 1572872 | tf_op jit(solution)/shard_map/ppermute | solution.py:719
  107.0 7.1 %collective-permute-start.30 = (bf16[4,272,512]{2,1,0:T(8,128)(2,1)S(1)}, bf16[4,272,512]{2,1,0:T(8,128)(2,1)S(1)}, u32[]{:S(2)}, u32[]{:S(2)}) collective-permute-start(bf16[4,272,512]{2,1,0:T(8,128)(2,1)S(1)} %get-tuple-element.211), channel_id=1, source_target_pairs={{0,4},{4,0},{8,12},{12,8},{16,20},{20,16},{24,28},{28,24},{1,5},{5... | collective-permute-start | bytes 3342344 | tf_op jit(solution)/shard_map/ppermute | solution.py:719
  107.0 20.2 %collective-permute-start.36 = (bf16[8,64,512]{2,1,0:T(8,128)(2,1)S(1)}, bf16[8,64,512]{2,1,0:T(8,128)(2,1)S(1)}, u32[]{:S(2)}, u32[]{:S(2)}) collective-permute-start(bf16[8,64,512]{2,1,0:T(8,128)(2,1)S(1)} %collective-permute-done.26.refs_2_), channel_id=1, source_target_pairs={{1,0},{2,3},{5,4},{6,7},{9,8},{10,11},{13,12},{14,15},{17,16},{18,... | collective-permute-start | bytes 1572872 | tf_op jit(solution)/shard_map/ppermute | solution.py:771
  110.8 15.9 %collective-permute-start.35 = (bf16[8,64,512]{2,1,0:T(8,128)(2,1)S(1)}, bf16[8,64,512]{2,1,0:T(8,128)(2,1)S(1)}, u32[]{:S(2)}, u32[]{:S(2)}) collective-permute-start(bf16[8,64,512]{2,1,0:T(8,128)(2,1)S(1)} %pad_maximum_fusion.4.refs_0_), channel_id=1, source_target_pairs={{1,2},{2,1},{5,6},{6,5},{9,10},{10,9},{13,14},{14,13},{17,18},{18,... | collective-permute-start | bytes 1572872 | tf_op jit(solution)/shard_map/ppermute | solution.py:770
  114.0 59.3 %collective-permute-start.41 = (bf16[512,512]{1,0:T(8,128)(2,1)S(1)}, bf16[512,512]{1,0:T(8,128)(2,1)S(1)}, u32[]{:S(2)}, u32[]{:S(2)}) collective-permute-start(bf16[512,512]{1,0:T(8,128)(2,1)S(1)} %get-tuple-element.225.refs_0_), channel_id=1, source_target_pairs={{0,1},{1,0},{2,3},{3,2},{4,5},{5,4},{6,7},{7,6},{8,9},{9,8},{10,11... | collective-permute-start | bytes 1572872 | tf_op jit(solution)/shard_map/ppermute | solution.py:719
  114.2 8.2 %collective-permute-start.31 = (bf16[2,128,512]{2,1,0:T(8,128)(2,1)S(1)}, bf16[2,128,512]{2,1,0:T(8,128)(2,1)S(1)}, u32[]{:S(2)}, u32[]{:S(2)}) collective-permute-start(bf16[2,128,512]{2,1,0:T(8,128)(2,1)S(1)} %pad_maximum_fusion.10), channel_id=1, source_target_pairs={{0,8},{4,12},{8,0},{12,4},{16,24},{20,28},{24,16},{28,20},{1,9},{5... | collective-permute-start | bytes 786440 | tf_op jit(solution)/shard_map/ppermute | solution.py:719
  115.7 8.6 %collective-permute-start.33 = (bf16[2,144,512]{2,1,0:T(8,128)(2,1)S(1)}, bf16[2,144,512]{2,1,0:T(8,128)(2,1)S(1)}, u32[]{:S(2)}, u32[]{:S(2)}) collective-permute-start(bf16[2,144,512]{2,1,0:T(8,128)(2,1)S(1)} %pad_maximum_fusion.8), channel_id=1, source_target_pairs={{0,16},{4,20},{8,24},{12,28},{16,0},{20,4},{24,8},{28,12},{1,17},{... | collective-permute-start | bytes 884744 | tf_op jit(solution)/shard_map/ppermute | solution.py:719
  122.6 5.0 %collective-permute-start.32 = (bf16[128,512]{1,0:T(8,128)(2,1)S(1)}, bf16[128,512]{1,0:T(8,128)(2,1)S(1)}, u32[]{:S(2)}, u32[]{:S(2)}) collective-permute-start(bf16[128,512]{1,0:T(8,128)(2,1)S(1)} %get-tuple-element.255), channel_id=1, source_target_pairs={{0,16},{4,20},{8,24},{12,28},{16,0},{20,4},{24,8},{28,12},{1,17},{... | collective-permute-start | bytes 393224 | tf_op jit(solution)/shard_map/ppermute | solution.py:719
  124.4 5.2 %collective-permute-start.34 = (bf16[144,512]{1,0:T(8,128)(2,1)S(1)}, bf16[144,512]{1,0:T(8,128)(2,1)S(1)}, u32[]{:S(2)}, u32[]{:S(2)}) collective-permute-start(bf16[144,512]{1,0:T(8,128)(2,1)S(1)} %get-tuple-element.253), channel_id=1, source_target_pairs={{0,8},{4,12},{8,0},{12,4},{16,24},{20,28},{24,16},{28,20},{1,9},{5... | collective-permute-start | bytes 442376 | tf_op jit(solution)/shard_map/ppermute | solution.py:719
  126.7 22.3 %collective-permute-start.37 = (bf16[512,512]{1,0:T(8,128)(2,1)S(1)}, bf16[512,512]{1,0:T(8,128)(2,1)S(1)}, u32[]{:S(2)}, u32[]{:S(2)}) collective-permute-start(bf16[512,512]{1,0:T(8,128)(2,1)S(1)} %get-tuple-element.225.refs_0_), channel_id=1, source_target_pairs={{0,2},{1,3},{2,0},{3,1},{4,6},{5,7},{6,4},{7,5},{8,10},{9,11},{10,... | collective-permute-start | bytes 1572872 | tf_op jit(solution)/shard_map/ppermute | solution.py:719
  132.4 52.3 %all-to-all-start = ((bf16[8,2,2,64,512]{4,3,2,1,0:T(8,128)(2,1)}), bf16[8,2,2,64,512]{4,3,2,1,0:T(8,128)(2,1)}, u32[]{:S(2)}, u32[]{:S(2)}) async-start(bf16[8,2,2,64,512]{4,3,2,1,0:T(8,128)(2,1)} %shard_map.326), calls=%async_computation | async-start | bytes 4194304 | tf_op jit(solution)/shard_map/all_to_all | solution.py:710
  149.1 12.4 %collective-permute-start.38 = (bf16[208,512]{1,0:T(8,128)(2,1)S(1)}, bf16[208,512]{1,0:T(8,128)(2,1)S(1)}, u32[]{:S(2)}, u32[]{:S(2)}) collective-permute-start(bf16[208,512]{1,0:T(8,128)(2,1)S(1)} %get-tuple-element.278), channel_id=1, source_target_pairs={{0,1},{1,0},{2,3},{3,2},{4,5},{5,4},{6,7},{7,6},{8,9},{9,8},{10,11... | collective-permute-start | bytes 638984 | tf_op jit(solution)/shard_map/ppermute | solution.py:719
  152.5 14.9 %collective-permute-start.39 = (bf16[208,512]{1,0:T(8,128)(2,1)S(1)}, bf16[208,512]{1,0:T(8,128)(2,1)S(1)}, u32[]{:S(2)}, u32[]{:S(2)}) collective-permute-start(bf16[208,512]{1,0:T(8,128)(2,1)S(1)} %get-tuple-element.279), channel_id=1, source_target_pairs={{0,2},{1,3},{2,0},{3,1},{4,6},{5,7},{6,4},{7,5},{8,10},{9,11},{10,... | collective-permute-start | bytes 638984 | tf_op jit(solution)/shard_map/ppermute | solution.py:719
  152.7 20.6 %collective-permute-start.40 = (bf16[208,512]{1,0:T(8,128)(2,1)S(1)}, bf16[208,512]{1,0:T(8,128)(2,1)S(1)}, u32[]{:S(2)}, u32[]{:S(2)}) collective-permute-start(bf16[208,512]{1,0:T(8,128)(2,1)S(1)} %pad_maximum_fusion.11), channel_id=1, source_target_pairs={{0,3},{1,2},{2,1},{3,0},{4,7},{5,6},{6,5},{7,4},{8,11},{9,10},{10,... | collective-permute-start | bytes 638984 | tf_op jit(solution)/shard_map/ppermute | solution.py:719
  154.1 28.7 %collective-permute-start.46 = (bf16[512,512]{1,0:T(8,128)(2,1)S(1)}, bf16[512,512]{1,0:T(8,128)(2,1)S(1)}, u32[]{:S(2)}, u32[]{:S(2)}) collective-permute-start(bf16[512,512]{1,0:T(8,128)(2,1)S(1)} %collective-permute-done.37.refs_2_), channel_id=1, source_target_pairs={{1,0},{2,3},{5,4},{6,7},{9,8},{10,11},{13,12},{14,15},{17,16},{18,... | collective-permute-start | bytes 1572872 | tf_op jit(solution)/shard_map/ppermute | solution.py:771
  161.6 21.2 %collective-permute-start.45 = (bf16[512,512]{1,0:T(8,128)(2,1)S(1)}, bf16[512,512]{1,0:T(8,128)(2,1)S(1)}, u32[]{:S(2)}, u32[]{:S(2)}) collective-permute-start(bf16[512,512]{1,0:T(8,128)(2,1)S(1)} %get-tuple-element.225.refs_0_), channel_id=1, source_target_pairs={{1,2},{2,1},{5,6},{6,5},{9,10},{10,9},{13,14},{14,13},{17,18},{18,... | collective-permute-start | bytes 1572872 | tf_op jit(solution)/shard_map/ppermute | solution.py:770
  173.4 6.7 %collective-permute-start.44 = (bf16[3,64,512]{2,1,0:T(8,128)(2,1)S(1)}, bf16[3,64,512]{2,1,0:T(8,128)(2,1)S(1)}, u32[]{:S(2)}, u32[]{:S(2)}) collective-permute-start(bf16[3,64,512]{2,1,0:T(8,128)(2,1)S(1)} %bitcast.85), channel_id=1, source_target_pairs={{0,24},{4,28},{8,16},{12,20},{16,8},{20,12},{24,0},{28,4},{1,25},{... | collective-permute-start | bytes 589832 | tf_op jit(solution)/shard_map/ppermute | solution.py:719
  175.0 7.1 %collective-permute-start.43 = (bf16[3,64,512]{2,1,0:T(8,128)(2,1)S(1)}, bf16[3,64,512]{2,1,0:T(8,128)(2,1)S(1)}, u32[]{:S(2)}, u32[]{:S(2)}) collective-permute-start(bf16[3,64,512]{2,1,0:T(8,128)(2,1)S(1)} %bitcast.86), channel_id=1, source_target_pairs={{0,16},{4,20},{8,24},{12,28},{16,0},{20,4},{24,8},{28,12},{1,17},{... | collective-permute-start | bytes 589832 | tf_op jit(solution)/shard_map/ppermute | solution.py:719
  176.2 6.2 %collective-permute-start.42 = (bf16[3,64,512]{2,1,0:T(8,128)(2,1)S(1)}, bf16[3,64,512]{2,1,0:T(8,128)(2,1)S(1)}, u32[]{:S(2)}, u32[]{:S(2)}) collective-permute-start(bf16[3,64,512]{2,1,0:T(8,128)(2,1)S(1)} %bitcast.87), channel_id=1, source_target_pairs={{0,8},{4,12},{8,0},{12,4},{16,24},{20,28},{24,16},{28,20},{1,9},{5... | collective-permute-start | bytes 589832 | tf_op jit(solution)/shard_map/ppermute | solution.py:719
  184.7 3.3 %collective-permute-start.47 = (bf16[4,3,64,512]{3,2,1,0:T(8,128)(2,1)S(1)}, bf16[4,3,64,512]{3,2,1,0:T(8,128)(2,1)S(1)}, u32[]{:S(2)}, u32[]{:S(2)}) collective-permute-start(bf16[4,3,64,512]{3,2,1,0:T(8,128)(2,1)S(1)} %pad_maximum_fusion.1.near_ref), channel_id=1, source_target_pairs={{0,4},{4,0},{8,12},{12,8},{16,20},{20,16},{24,28},{28,24},{1,5},{5... | collective-permute-start | bytes 2359304 | tf_op jit(solution)/shard_map/ppermute | solution.py:719
  (18 other events, 231.6 us)
